TPU v7x, 32 devices: a whole 2x2x4 slice. The times are simulated.
32 devices in a mesh: dp: 8 (over z, x), band: 4 (over y, core).
Axes of the slice: x: 2, y: 2, z: 4, core: 2. Of those that a mesh axis runs over, the one named last changes fastest.
Arguments:
- inputs: bfloat16 [2, 8, 2048, 768], P(None, 'dp', 'band'), may hold values from -6 to 6
- segments: int32 [2, 8, 2048], P(None, 'dp', 'band'), may hold values from 0 to 6, as said below
- cotangent: bfloat16 [2, 8, 2048, 768], P(None, 'dp', 'band'), may hold values from -6 to 6
- ln1_gain: bfloat16 [768], P('band'), may hold values from 0.5 to 1.5
- ln1_bias: bfloat16 [768], P('band'), may hold values from -3 to 3
- w_qkv: bfloat16 [768, 2304], P('band'), may hold values from -0.21875 to 0.21875
- b_qv: bfloat16 [1536], P('band'), may hold values from -0.4375 to 0.4375
- w_out: bfloat16 [768, 768], P('band'), may hold values from -2.5 to 2.5
- b_out: bfloat16 [768], P('band'), may hold values from -3 to 3
- ln2_gain: bfloat16 [768], P('band'), may hold values from 0.5 to 1.5
- ln2_bias: bfloat16 [768], P('band'), may hold values from -3 to 3
- w_up: bfloat16 [768, 3072], P('band'), may hold values from -0.21875 to 0.21875
- b_up: bfloat16 [3072], P('band'), may hold values from -3 to 3
- w_down: bfloat16 [3072, 768], P('band'), may hold values from -0.109375 to 0.109375
- b_down: bfloat16 [768], P('band'), may hold values from -3 to 3
Outputs:
- output: bfloat16 [2, 8, 2048, 768], P(None, 'dp', 'band')
- input_grad: bfloat16 [2, 8, 2048, 768], P(None, 'dp', 'band')
- grad_ln1_gain: float32 [768], P('band')
- grad_ln1_bias: float32 [768], P('band')
- grad_w_qkv: float32 [768, 2304], P('band')
- grad_b_qv: float32 [1536], P('band')
- grad_w_out: float32 [768, 768], P('band')
- grad_b_out: float32 [768], P('band')
- grad_ln2_gain: float32 [768], P('band')
- grad_ln2_bias: float32 [768], P('band')
- grad_w_up: float32 [768, 3072], P('band')
- grad_b_up: float32 [3072], P('band')
- grad_w_down: float32 [3072, 768], P('band')
- grad_b_down: float32 [768], P('band')
Inputs may be any that keep to these rules, and one draw needn't show every extreme that they name: `segments`: each sequence's 2048 slots are consecutive blocks of 512 slots that carry the same ids in the same order. In a block, ids never fall: tiles 1, 2, 3 and so on are contiguous runs, and padding (0) fills the end of the block, at most 51 slots.
All inputs are finite; a program needn't handle non-finite values.
Results may differ from a plain program's by a relative error of at most 0.02.
Values may be sent and summed in bfloat16 or wider, within the bound.
No kernel may reach another device: no remote copies, remote signals or barrier semaphores. Data moves between devices by JAX's collectives and lax.ppermute only.
A program may use at most 192 MiB of HBM per device.

v0:
```python
import functools

import jax
import jax.numpy as jnp
from jax import lax
from jax.sharding import PartitionSpec as P
from jax.experimental import pallas as pl
from jax.experimental.pallas import tpu as pltpu
bf=jnp.bfloat16; f32=jnp.float32
HD=64


def nt(a,b): return lax.dot_general(a,b,(((1,),(1,)),((),())),preferred_element_type=f32)


def nn(a,b): return lax.dot_general(a,b,(((1,),(0,)),((),())),preferred_element_type=f32)


def tn(a,b): return lax.dot_general(a,b,(((0,),(0,)),((),())),preferred_element_type=f32)


def lanes(shape): return lax.broadcasted_iota(jnp.int32,shape,1)


NEG=-1e30


def mask_feats_q(seg, base):
    l=lanes((seg.shape[0],2*HD))
    return (l==seg+base).astype(f32)


def mask_feats_k(seg, base):
    l=lanes((seg.shape[0],2*HD))
    inr=(l>=base)&(l<base+8)
    return jnp.where(inr&(l!=seg+base),NEG,0.0)


def both_masks(k, segk):
    low = lanes(k.shape) < HD
    return [
        jnp.where(low, k, mask_feats_k(segk, HD).astype(bf)),
        jnp.where(low, mask_feats_k(segk, 0).astype(bf), k),
    ]


def fwd_kernel(*refs, tq, parts):
    q_ref, seg_ref = refs[0], refs[1]
    k_refs, v_refs = refs[2 : 2 + parts], refs[2 + parts : 2 + 2 * parts]
    o_ref, lse_ref = refs[2 + 2 * parts :]
    n = q_ref.shape[0]
    v = jnp.concatenate([r[...] for r in v_refs])
    seg = seg_ref[...]
    ks = [jnp.concatenate(x) for x in zip(*[both_masks(r[...], seg) for r in k_refs])]
    for t in range(n // tq):
        rows = pl.ds(t * tq, tq)
        q = q_ref[rows, :] * jnp.asarray(0.125, bf)
        lq = lanes(q.shape) < HD
        segq = seg_ref[rows, :]
        outs, lses = [], []
        for h in range(2):
            feats = mask_feats_q(segq, HD if h == 0 else 0).astype(bf)
            qq = jnp.where(lq, q, feats) if h == 0 else jnp.where(lq, feats, q)
            s = nt(qq, ks[h])
            m = jnp.max(s, axis=-1, keepdims=True)
            p = jnp.exp(s - m)
            l = jnp.sum(p, axis=-1, keepdims=True)
            o = nn(p.astype(bf), v)
            outs.append(o / l)
            lses.append(m + jnp.log(l))
        o_ref[rows, :] = jnp.where(lq, outs[0], outs[1]).astype(bf)
        lse_ref[rows, :] = jnp.where(
            lq, jnp.broadcast_to(lses[0], q.shape), jnp.broadcast_to(lses[1], q.shape)
        )


def specs(n, d, first=0):
    col = pl.BlockSpec((n, 2 * HD), lambda h: (0, h + first))
    val = pl.BlockSpec((n, 2 * HD), lambda h: (0, h + first + d // (2 * HD)))
    seg = pl.BlockSpec((n, 1), lambda h: (0, 0))
    return col, val, seg


def attn_fwd(q, blocks, seg, tq=256):
    n, d = q.shape
    parts = len(blocks)
    col, val, one = specs(n, d)
    return pl.pallas_call(
        functools.partial(fwd_kernel, tq=min(tq, n), parts=parts),
        grid=(d // (2 * HD),),
        in_specs=[col, one] + [col] * parts + [val] * parts,
        out_specs=[col, col],
        out_shape=[jax.ShapeDtypeStruct((n, d), bf), jax.ShapeDtypeStruct((n, d), f32)],
        cost_estimate=pl.CostEstimate(
            flops=16 * n * n * parts * d, bytes_accessed=n * d * (8 + 4 * parts), transcendentals=0
        ),
        name="attn_fwd",
    )(q, seg[:, None], *blocks, *blocks)


def bwd_kernel(*refs, tq, parts):
    q_ref, do_ref, o_ref, lse_ref, seg_ref = refs[:5]
    k_refs, v_refs = refs[5 : 5 + parts], refs[5 + parts : 5 + 2 * parts]
    dq_ref = refs[5 + 2 * parts]
    dkv_refs = refs[6 + 2 * parts : 6 + 3 * parts]
    acc_ref = refs[6 + 3 * parts]
    n = q_ref.shape[0]
    seg = seg_ref[...]
    group = min(2, parts)
    for c in range(0, parts, group):
        k = jnp.concatenate([r[...] for r in k_refs[c : c + group]])
        v = jnp.concatenate([r[...] for r in v_refs[c : c + group]])
        ks = both_masks(k, jnp.concatenate([seg] * group))
        lk = lanes(k.shape) < HD
        z = jnp.zeros_like(k)
        km = [jnp.where(lk, k, z), jnp.where(lk, z, k)]
        dk = jnp.zeros(k.shape, f32)
        dv = jnp.zeros(k.shape, f32)
        for t in range(n // tq):
            rows = pl.ds(t * tq, tq)
            q = q_ref[rows, :] * jnp.asarray(0.125, bf)
            do = do_ref[rows, :]
            lq = lanes(q.shape) < HD
            zq = jnp.zeros_like(q)
            segq = seg_ref[rows, :]
            lse = lse_ref[rows, :]
            prod = do.astype(f32) * o_ref[rows, :].astype(f32)
            dqs = None
            for h in range(2):
                own = lq if h == 0 else ~lq
                qq = jnp.where(own, q, mask_feats_q(segq, HD if h == 0 else 0).astype(bf))
                qm = jnp.where(own, q, zq)
                dom = jnp.where(own, do, zq)
                dd = jnp.sum(jnp.where(own, prod, 0.0), axis=-1, keepdims=True)
                ls = lse[:, :1] if h == 0 else lse[:, HD : HD + 1]
                p = jnp.exp(nt(qq, ks[h]) - ls)
                ds = (p * (nt(dom, v) - dd)).astype(bf)
                dv = dv + tn(p.astype(bf), dom)
                dk = dk + tn(ds, qm)
                x = nn(ds, km[h])
                dqs = x if dqs is None else dqs + x
            if c == 0:
                acc_ref[rows, :] = dqs
            else:
                acc_ref[rows, :] += dqs
        for i in range(group):
            dkv_refs[c + i][0] = dk[i * n : (i + 1) * n].astype(bf)
            dkv_refs[c + i][1] = dv[i * n : (i + 1) * n].astype(bf)
    dq_ref[...] = (acc_ref[...] * 0.125).astype(bf)


def attn_bwd(q, blocks, do, o, lse, seg, first, count, tq=256):
    n, d = q.shape
    parts = len(blocks)
    wide = count * 2 * HD
    col, val, one = specs(n, d, first)
    out = pl.BlockSpec((n, 2 * HD), lambda h: (0, h))
    pair = pl.BlockSpec((2, n, 2 * HD), lambda h: (0, 0, h))
    return pl.pallas_call(
        functools.partial(bwd_kernel, tq=min(tq, n), parts=parts),
        grid=(count,),
        in_specs=[col, col, col, col, one] + [col] * parts + [val] * parts,
        out_specs=[out] + [pair] * parts,
        out_shape=[jax.ShapeDtypeStruct((n, wide), bf)] + [jax.ShapeDtypeStruct((2, n, wide), bf)] * parts,
        scratch_shapes=[pltpu.VMEM((n, 2 * HD), f32)],
        cost_estimate=pl.CostEstimate(
            flops=40 * n * n * parts * wide, bytes_accessed=n * wide * (12 + 8 * parts), transcendentals=0
        ),
        name="attn_bwd",
    )(q, do, o, lse, seg[:, None], *blocks, *blocks)


def normed(value, gain, shift):
    center = value - jnp.mean(value, axis=-1, keepdims=True)
    spread = jnp.mean(center * center, axis=-1, keepdims=True)
    return center * lax.rsqrt(spread + 1e-06) * gain + shift


def gelu_tanh(value):
    return jax.nn.gelu(value, approximate=True)


def swap(x, flip):
    parts = lax.axis_size("band")
    return lax.ppermute(x, "band", [(i, i ^ flip) for i in range(parts)])


def gather_relative(x):
    return spread([x], lax.axis_size("band") // 2)


def spread(blocks, flip):
    while flip >= 1:
        blocks = blocks + [swap(block, flip) for block in blocks]
        flip //= 2
    return blocks


def tie(first, second):
    return lax.optimization_barrier((first, second))


def fold(blocks, flip):
    half = len(blocks) // 2
    return [
        (near.astype(f32) + swap(far, flip).astype(f32)).astype(bf)
        for near, far in zip(blocks[:half], blocks[half:])
    ]


def reduce_relative(blocks, flip=1):
    while len(blocks) > 1:
        blocks = fold(blocks, flip)
        flip *= 2
    return blocks[0]


def gather_vectors(shards):
    packed = jnp.concatenate(shards)
    whole = lax.all_gather(packed, "band", axis=0, tiled=False)
    out, at = [], 0
    for shard in shards:
        out.append(whole[:, at : at + shard.shape[0]].reshape(-1).astype(f32))
        at += shard.shape[0]
    return out


def relative_rows(array):
    me = lax.axis_index("band")
    order = [0]
    flip = lax.axis_size("band") // 2
    while flip >= 1:
        order = order + [i ^ flip for i in order]
        flip //= 2
    return [lax.dynamic_index_in_dim(array, me ^ i, 0, keepdims=False) for i in order]


def reduce_last(matrix, grads, shards):
    parts, columns = lax.axis_size("band"), matrix.shape[1]
    packed = jnp.concatenate([g.reshape(parts, -1) for g in grads], axis=1).astype(bf)
    rows = -(-packed.shape[1] // (16 * columns)) * 16
    packed = jnp.pad(packed, ((0, 0), (0, rows * columns - packed.shape[1])))
    mine = reduce_relative(relative_rows(matrix.astype(bf).reshape(parts, -1, columns)))
    extra = reduce_relative(relative_rows(packed.reshape(parts, rows, columns)))
    total = finish(mine, 1)
    vector = sum_small(extra).reshape(-1)
    out, at = [], 0
    for shard in shards:
        out.append(vector[at : at + shard.shape[0]])
        at += shard.shape[0]
    return total, out


def gather_matrix(shard):
    return lax.all_gather(shard, "band", axis=0, tiled=True)


def reduce_band(grad):
    blocks = grad.reshape(lax.axis_size("band"), -1, grad.shape[1])
    return reduce_relative(relative_rows(blocks))


def trade(x, flip):
    size = lax.axis_size("dp")
    return lax.ppermute(x, "dp", [(i, i ^ flip) for i in range(size)])


def halve(x, flip):
    bit = lax.rem(lax.axis_index("dp") // flip, 2)
    halves = x.reshape(2, -1, x.shape[1])
    near = lax.dynamic_index_in_dim(halves, bit, 0, keepdims=False)
    far = lax.dynamic_index_in_dim(halves, 1 - bit, 0, keepdims=False)
    return (near.astype(f32) + trade(far, flip).astype(f32)).astype(bf)


def join(x, flip):
    bit = lax.rem(lax.axis_index("dp") // flip, 2)
    other = trade(x, flip)
    return jnp.where(bit == 0, jnp.concatenate([x, other]), jnp.concatenate([other, x]))


def finish(x, flip):
    size = lax.axis_size("dp")
    while flip < size:
        x = halve(x, flip)
        flip *= 2
    while flip > 1:
        flip //= 2
        x = join(x, flip)
    return x.astype(f32)


def sum_small(x):
    flip = 1
    while flip < lax.axis_size("dp"):
        x = (x.astype(f32) + trade(x, flip).astype(f32)).astype(bf)
        flip *= 2
    return x.astype(f32)


def layer(inputs, segments, cotangent, ln1_gain, ln1_bias, w_qkv, b_qv, w_out, b_out, ln2_gain, ln2_bias, w_up, b_up, w_down, b_down):
    micro, tokens, width = inputs.shape[0], inputs.shape[2], inputs.shape[3]
    vectors = (ln1_gain, ln1_bias, b_qv, b_out, ln2_gain, ln2_bias, b_up, b_down)
    gain_one, shift_one, bias_qv, bias_out, gain_two, shift_two, bias_up, bias_down = gather_vectors(vectors)
    w_proj = gather_matrix(w_qkv)

    value = inputs.reshape(micro * tokens, width).astype(f32)
    seg = segments.reshape(micro, tokens)
    normed_in, pull_one = jax.vjp(normed, value, gain_one, shift_one)
    normed_low = normed_in.astype(bf)
    projected = nn(normed_low, w_proj)
    query = (projected[:, :width] + bias_qv[:width]).astype(bf)
    pairs = jnp.concatenate(
        [projected[:, width : 2 * width], projected[:, 2 * width :] + bias_qv[width:]], axis=1
    ).astype(bf)

    gathered = [gather_relative(pairs[:tokens])]
    far = lax.axis_size("band") // 2
    started = []
    for m in range(1, micro):
        own = pairs[m * tokens : (m + 1) * tokens]
        started.append([own, swap(own, far)])
    gathered[0], (w_out, w_up, w_down) = tie(gathered[0], (w_out, w_up, w_down))
    w_mix = gather_matrix(w_out)
    w_rise = gather_matrix(w_up)
    w_fall = gather_matrix(w_down)

    saved, mixes = [], []
    for m in range(micro):
        rows = slice(m * tokens, (m + 1) * tokens)
        if m > 0:
            blocks, mixes[m - 1] = tie(started[m - 1], mixes[m - 1])
            gathered.append(spread(blocks, far // 2))
        mix, log_total = attn_fwd(query[rows], gathered[m], seg[m])
        mixes.append(mix)
        saved.append((query[rows], gathered[m], mix, log_total, seg[m]))
    mixed = jnp.concatenate(mixes)

    hidden = value + (nn(mixed, w_mix) + bias_out)
    normed_mid, pull_two = jax.vjp(normed, hidden, gain_two, shift_two)
    mid_low = normed_mid.astype(bf)
    upward = nn(mid_low, w_rise) + bias_up
    active, pull_gelu = jax.vjp(gelu_tanh, upward)
    active_low = active.astype(bf)
    output = (hidden + (nn(active_low, w_fall) + bias_down)).astype(bf)

    real = (seg.reshape(-1, 1) != 0).astype(f32)
    grad_y = cotangent.reshape(micro * tokens, width).astype(f32) * real
    grad_m = grad_y.astype(bf)
    grad_w_fall = tn(active_low, grad_m)
    grad_b_fall = jnp.sum(grad_m.astype(f32), axis=0)
    low_fall, grad_m = tie(grad_w_fall.astype(bf), grad_m)
    grad_up = pull_gelu(nt(grad_m, w_fall))[0].astype(bf)
    grad_w_rise = tn(mid_low, grad_up)
    grad_b_rise = jnp.sum(grad_up.astype(f32), axis=0)
    grad_mid, grad_gain_two, grad_shift_two = pull_two(nt(grad_up, w_rise))
    grad_hidden = grad_y + grad_mid
    grad_a = grad_hidden.astype(bf)
    grad_w_mix = tn(mixed, grad_a)
    grad_b_mix = jnp.sum(grad_a.astype(f32), axis=0)
    grad_mixed = nt(grad_a, w_mix).astype(bf)

    grad_mixed, *rest = lax.optimization_barrier((grad_mixed, grad_w_rise.astype(bf), grad_w_mix.astype(bf)))
    large = [low_fall, *rest]
    large = [reduce_band(grad) for grad in large]

    count = width // (4 * HD)
    calls = [(m, first) for m in range(micro) for first in range(0, 2 * count, count)]
    halves, grads_q = [], []
    for i, (m, first) in enumerate(calls):
        q, blocks, mix, log_total, seg_q = saved[m]
        grad_out = grad_mixed[m * tokens : (m + 1) * tokens]
        if i >= 2:
            halves[i - 2], grad_out = tie(halves[i - 2], grad_out)
        if i in (1, 2):
            large[i - 1], grad_out = tie(large[i - 1], grad_out)
        if i == 3:
            (large[2], halved), grad_out = tie((large[2], halve(large[0], 1)), grad_out)
        grad_q, *grad_blocks = attn_bwd(q, blocks, grad_out, mix, log_total, seg_q, first, count)
        halves.append(fold(grad_blocks, 1))
        grads_q.append(grad_q)
    pairs = []
    for half in halves:
        pairs.append(reduce_relative(half, 2))
    pairs, grads_q = tie(pairs, grads_q)
    wide = [finish(halved, 2), finish(large[1], 1), finish(large[2], 1)]
    grad_qkv = jnp.concatenate(
        [
            jnp.concatenate(
                [grads_q[i], grads_q[i + 1], pairs[i][0], pairs[i + 1][0], pairs[i][1], pairs[i + 1][1]], axis=1
            )
            for i in range(0, 2 * micro, 2)
        ]
    )
    grad_qkv = lax.optimization_barrier(grad_qkv)
    grad_w_proj = tn(normed_low, grad_qkv)
    sums = jnp.sum(grad_qkv.astype(f32), axis=0)
    grad_b_proj = jnp.concatenate([sums[:width], sums[2 * width :]])
    grad_norm_in, grad_gain_one, grad_shift_one = pull_one(nt(grad_qkv, w_proj))
    input_grad = (grad_hidden + grad_norm_in).astype(bf)

    last, small = reduce_last(
        grad_w_proj,
        (grad_gain_one, grad_shift_one, grad_b_proj, grad_b_mix, grad_gain_two, grad_shift_two, grad_b_rise, grad_b_fall),
        vectors,
    )
    return (
        output.reshape(inputs.shape),
        input_grad.reshape(inputs.shape),
        small[0],
        small[1],
        last,
        small[2],
        wide[2],
        small[3],
        small[4],
        small[5],
        wide[1],
        small[6],
        wide[0],
        small[7],
    )


def solution(mesh):
    split = P(None, "dp", "band", None)
    rows, vector = P("band", None), P("band")
    weights = (vector, vector, rows, vector, rows, vector, vector, vector, rows, vector, rows, vector)
    return jax.shard_map(
        layer,
        mesh=mesh,
        in_specs=(split, P(None, "dp", "band"), split) + weights,
        out_specs=(split, split) + weights,
        check_vma=False,
    )
```

profile of v0, /device:TPU:0, one launch (start us, length us, event | category | flops | bytes accessed | tf_op | source)
XLA Modules:
  0.0 631.5 jit_solution(3759316371854391678)
XLA Ops:
  8.0 5.5 concatenate.100
  13.4 6.2 all-gather.1
  23.7 19.3 %all-gather.7.cloned.1.call-done = bf16[768,2304]{1,0:T(8,128)(2,1)} async-done(((bf16[192,2304]{1,0:T(8,128)(2,1)}), bf16[768,2304]{1,0:T(8,128)(2,1)}) %all-gather.7.cloned.1.call-update) | async-done | bytes 3538960 | tf_op jit(solution)/shard_map/all_gather | solution.py:255
  43.1 5.8 fusion.66
  53.6 35.2 %collective-permute-done.1.refs_3_.refs_7_.refs_6_.refs_10_ = bf16[512,1536]{1,0:T(8,128)(2,1)S(1)} collective-permute-done((bf16[512,1536]{1,0:T(8,128)(2,1)S(1)}, bf16[512,1536]{1,0:T(8,128)(2,1)S(1)}, u32[]{:S(2)}, u32[]{:S(2)}) %collective-permute-start.1) | collective-permute-done | bytes 1572896 | tf_op jit(solution)/shard_map/ppermute | solution.py:185
  95.9 24.1 %attn_fwd.2 = (bf16[512,768]{1,0:T(8,128)(2,1)}, f32[512,768]{1,0:T(8,128)}) custom-call(bf16[512,768]{1,0:T(8,128)(2,1)} %get-tuple-element.200.refs_0_, s32[512,1]{1,0:T(8,128)} %copy.39.refs_1_.refs_4_, bf16[512,1536]{1,0:T(8,128)(2,1)} %copy-done.18, bf16[512,1536]{1,0:T(8,128)(2,1)} %copy-done.51, bf16[512,1536]{1,0:T(8,128)(2,1)} %copy-done.52, ...), custom_call_target="tpu_custom_call" | custom-call | flops 12884901888 | bytes 9437184 | tf_op jit(solution)/shard_map/attn_fwd/pallas_call | solution.py:88
  120.0 25.1 %collective-permute-done.refs_3_.refs_7_.refs_6_.refs_10_ = bf16[512,1536]{1,0:T(8,128)(2,1)} collective-permute-done((bf16[512,1536]{1,0:T(8,128)(2,1)}, bf16[512,1536]{1,0:T(8,128)(2,1)}, u32[]{:S(2)}, u32[]{:S(2)}) %collective-permute-start) | collective-permute-done | bytes 1572896 | tf_op jit(solution)/shard_map/ppermute | solution.py:185
  151.5 24.1 %attn_fwd.3 = (bf16[512,768]{1,0:T(8,128)(2,1)}, f32[512,768]{1,0:T(8,128)}) custom-call(bf16[512,768]{1,0:T(8,128)(2,1)} %get-tuple-element.199.refs_0_, s32[512,1]{1,0:T(8,128)} %copy.40.refs_1_.refs_4_, bf16[512,1536]{1,0:T(8,128)(2,1)} %get-tuple-element.80.refs_2_.refs_6_.refs_5_.refs_9_, ...), custom_call_target="tpu_custom_call" | custom-call | flops 12884901888 | bytes 9437184 | tf_op jit(solution)/shard_map/attn_fwd/pallas_call | solution.py:88
  177.7 3.3 fusion.64
  183.2 8.5 %fusion.54 = f32[1024,3072]{1,0:T(8,128)S(1)} fusion(bf16[768,3072]{1,0:T(8,128)(2,1)} %all-gather.11.cloned.1.call-done, f32[1024,768]{1,0:T(8,128)} %copy-done.6, f32[768]{0:T(1024)S(1)} %reshape.404, f32[768]{0:T(1024)S(1)} %reshape.403, f32[1024]{0:T(1024)S(1)} %fusion.51, f32[1024]{0:T(1024)S(1)} %broadcast_multiply_fusion), kind=kOutput, calls=%fused_computation.197 | convolution fusion | flops 4835770368 | bytes 20461568 | tf_op jit(solution)/shard_map/dot_general | solution.py:16
  191.7 8.1 %convolution_convert_fusion.1 = bf16[3072,768]{1,0:T(8,128)(2,1)S(1)} fusion(bf16[1024,768]{1,0:T(8,128)(2,1)S(1)} %copy-done.17, f32[1024,3072]{1,0:T(8,128)S(1)} %fusion.54, f32[3072]{0:T(1024)S(1)} %reshape.405), kind=kOutput, calls=%fused_computation.11 | convolution fusion | flops 4865654784 | bytes 18886656 | tf_op jit(solution)/shard_map/dot_general | solution.py:19
  203.2 15.5 %fusion.65 = (bf16[3072]{0:T(1024)(128)(2,1)}, bf16[1024,3072]{1,0:T(8,128)(2,1)S(1)}) fusion(f32[1024,3072]{1,0:T(8,128)} %copy-done.55, f32[3072]{0:T(1024)S(1)} %reshape.405, bf16[1024,768]{1,0:T(8,128)(2,1)S(1)} %copy-done.17, bf16[3072,768]{1,0:T(8,128)(2,1)} %all-gather.13.cloned.1.call-done), kind=kOutput, calls=%fused_computation.207 | convolution fusion | flops 4901041152 | bytes 25184256 | tf_op jit(solution)/shard_map/dot_general | solution.py:13
  218.7 8.2 %convolution_convert_fusion = bf16[768,3072]{1,0:T(8,128)(2,1)} fusion(bf16[1024,3072]{1,0:T(8,128)(2,1)S(1)} %get-tuple-element.230, f32[1024,768]{1,0:T(8,128)S(1)} %copy-done.7, f32[768]{0:T(1024)S(1)} %reshape.404, f32[768]{0:T(1024)S(1)} %reshape.403, f32[1024]{0:T(1024)S(1)} %fusion.51, f32[1024]{0:T(1024)S(1)} %broadcast_multiply_fusion), kind=kOutput, calls=%fused_computation.10 | convolution fusion | flops 4838129664 | bytes 14170112 | tf_op jit(solution)/shard_map/dot_general | solution.py:19
  226.8 8.6 %multiply_reduce_fusion = (bf16[768]{0:T(1024)(128)(2,1)}, f32[1024]{0:T(1024)S(1)}, bf16[768]{0:T(1024)(128)(2,1)}, f32[1024,768]{1,0:T(8,128)S(1)}) fusion(f32[1024,768]{1,0:T(8,128)S(1)} %copy-done.7, f32[1024]{0:T(1024)S(1)} %fusion.51, f32[1024]{0:T(1024)S(1)} %broadcast_multiply_fusion, f32[768]{0:T(1024)S(1)} %reshape.403, ...), kind=kOutput, calls=%fused_computation.40 | convolution fusion | flops 4838126592 | bytes 17319936 | tf_op jit(solution)/shard_map/dot_general | solution.py:13
  244.8 21.6 %attn_bwd.4 = (bf16[512,384]{1,0:T(8,128)(2,1)}, bf16[2,512,384]{2,1,0:T(8,128)(2,1)}, bf16[2,512,384]{2,1,0:T(8,128)(2,1)}, bf16[2,512,384]{2,1,0:T(8,128)(2,1)}, bf16[2,512,384]{2,1,0:T(8,128)(2,1)}) custom-call(bf16[512,768]{1,0:T(8,128)(2,1)} %get-tuple-element.200.refs_0_, bf16[512,768]{1,0:T(8,128)(2,1)} %get-tuple-element.96.refs_1_, ...), custom_call_target="tpu_custom_call" | custom-call | flops 16106127360 | bytes 8650752 | tf_op jit(solution)/shard_map/attn_bwd/pallas_call | solution.py:159
  267.0 13.6 %add_convert_fusion.1 = bf16[1024,768]{1,0:T(8,128)(2,1)} fusion(f32[1024,768]{1,0:T(8,128)} %copy-done.6, bf16[3072,768]{1,0:T(8,128)(2,1)} %all-gather.13.cloned.1.call-done, f32[768]{0:T(1024)S(1)} %reshape.406, f32[1024,3072]{1,0:T(8,128)} %copy-done.55, f32[3072]{0:T(1024)} %copy-done.45), kind=kOutput, calls=%fused_computation.44 | convolution fusion | flops 4865654784 | bytes 22035456 | tf_op jit(solution)/shard_map/dot_general | solution.py:16
  284.6 2.9 dynamic-slice_bitcast_fusion.1
  294.9 5.6 collective-permute-done.23
  301.8 2.8 fusion.21
  306.1 11.2 %collective-permute-done.8 = bf16[2,512,384]{2,1,0:T(8,128)(2,1)S(1)} collective-permute-done((bf16[2,512,384]{2,1,0:T(8,128)(2,1)S(1)}, bf16[2,512,384]{2,1,0:T(8,128)(2,1)S(1)}, u32[]{:S(2)}, u32[]{:S(2)}) %collective-permute-start.8) | collective-permute-done | bytes 786464 | tf_op jit(solution)/shard_map/ppermute | solution.py:185
  317.5 25.1 %collective-permute-done.11 = bf16[768,768]{1,0:T(8,128)(2,1)S(1)} collective-permute-done((bf16[768,768]{1,0:T(8,128)(2,1)S(1)}, bf16[768,768]{1,0:T(8,128)(2,1)S(1)}, u32[]{:S(2)}, u32[]{:S(2)}) %collective-permute-start.11) | collective-permute-done | bytes 1179680 | tf_op jit(solution)/shard_map/ppermute | solution.py:185
  347.1 21.2 %attn_bwd.5 = (bf16[512,384]{1,0:T(8,128)(2,1)}, bf16[2,512,384]{2,1,0:T(8,128)(2,1)}, bf16[2,512,384]{2,1,0:T(8,128)(2,1)}, bf16[2,512,384]{2,1,0:T(8,128)(2,1)}, bf16[2,512,384]{2,1,0:T(8,128)(2,1)}) custom-call(bf16[512,768]{1,0:T(8,128)(2,1)} %get-tuple-element.200.refs_0_, bf16[512,768]{1,0:T(8,128)(2,1)} %get-tuple-element.96.refs_1_, ...), custom_call_target="tpu_custom_call" | custom-call | flops 16106127360 | bytes 8650752 | tf_op jit(solution)/shard_map/attn_bwd/pallas_call | solution.py:159
  368.8 2.6 add_convert_fusion.3
  373.8 21.8 %attn_bwd.6 = (bf16[512,384]{1,0:T(8,128)(2,1)}, bf16[2,512,384]{2,1,0:T(8,128)(2,1)}, bf16[2,512,384]{2,1,0:T(8,128)(2,1)}, bf16[2,512,384]{2,1,0:T(8,128)(2,1)}, bf16[2,512,384]{2,1,0:T(8,128)(2,1)}) custom-call(bf16[512,768]{1,0:T(8,128)(2,1)} %get-tuple-element.199.refs_0_, bf16[512,768]{1,0:T(8,128)(2,1)} %get-tuple-element.114.refs_1_, ...), custom_call_target="tpu_custom_call" | custom-call | flops 16106127360 | bytes 8650752 | tf_op jit(solution)/shard_map/attn_bwd/pallas_call | solution.py:159
  408.3 21.3 %attn_bwd.7 = (bf16[512,384]{1,0:T(8,128)(2,1)}, bf16[2,512,384]{2,1,0:T(8,128)(2,1)}, bf16[2,512,384]{2,1,0:T(8,128)(2,1)}, bf16[2,512,384]{2,1,0:T(8,128)(2,1)}, bf16[2,512,384]{2,1,0:T(8,128)(2,1)}) custom-call(bf16[512,768]{1,0:T(8,128)(2,1)} %get-tuple-element.199.refs_0_, bf16[512,768]{1,0:T(8,128)(2,1)} %get-tuple-element.114.refs_1_, ...), custom_call_target="tpu_custom_call" | custom-call | flops 16106127360 | bytes 8650752 | tf_op jit(solution)/shard_map/attn_bwd/pallas_call | solution.py:159
  433.6 3.1 collective-permute-done.44
  439.2 6.9 %collective-permute-done.51 = bf16[24,3072]{1,0:T(8,128)(2,1)S(1)} collective-permute-done((bf16[24,3072]{1,0:T(8,128)(2,1)S(1)}, bf16[24,3072]{1,0:T(8,128)(2,1)S(1)}, u32[]{:S(2)}, u32[]{:S(2)}) %collective-permute-start.51) | collective-permute-done | bytes 147488 | tf_op jit(solution)/shard_map/ppermute | solution.py:265
  446.2 5.3 collective-permute-done.45
  451.5 3.0 collective-permute-start.46
  455.5 4.5 collective-permute-done.46
  461.2 4.4 collective-permute-done.47
  466.3 7.3 %collective-permute-done.56 = bf16[96,768]{1,0:T(8,128)(2,1)S(1)} collective-permute-done((bf16[96,768]{1,0:T(8,128)(2,1)S(1)}, bf16[96,768]{1,0:T(8,128)(2,1)S(1)}, u32[]{:S(2)}, u32[]{:S(2)}) %collective-permute-start.56) | collective-permute-done | bytes 147488 | tf_op jit(solution)/shard_map/ppermute | solution.py:265
  477.9 3.6 collective-permute-done.57
  483.3 13.5 %collective-permute-done.20 = bf16[2,512,384]{2,1,0:T(8,128)(2,1)S(1)} collective-permute-done((bf16[2,512,384]{2,1,0:T(8,128)(2,1)S(1)}, bf16[2,512,384]{2,1,0:T(8,128)(2,1)S(1)}, u32[]{:S(2)}, u32[]{:S(2)}) %collective-permute-start.20) | collective-permute-done | bytes 786464 | tf_op jit(solution)/shard_map/ppermute | solution.py:185
  499.8 13.9 %collective-permute-done.14 = bf16[2,512,384]{2,1,0:T(8,128)(2,1)S(1)} collective-permute-done((bf16[2,512,384]{2,1,0:T(8,128)(2,1)S(1)}, bf16[2,512,384]{2,1,0:T(8,128)(2,1)S(1)}, u32[]{:S(2)}, u32[]{:S(2)}) %collective-permute-start.14) | collective-permute-done | bytes 786464 | tf_op jit(solution)/shard_map/ppermute | solution.py:185
  517.2 8.0 %collective-permute-done.27 = bf16[2,512,384]{2,1,0:T(8,128)(2,1)S(1)} collective-permute-done((bf16[2,512,384]{2,1,0:T(8,128)(2,1)S(1)}, bf16[2,512,384]{2,1,0:T(8,128)(2,1)S(1)}, u32[]{:S(2)}, u32[]{:S(2)}) %collective-permute-start.27) | collective-permute-done | bytes 786464 | tf_op jit(solution)/shard_map/ppermute | solution.py:185
  528.5 4.4 convolution_convert_fusion.2
  536.6 5.7 fusion.55
  542.2 3.0 reduce.5
  545.3 3.0 fusion.16
  552.7 20.1 %collective-permute-done.36 = bf16[192,2304]{1,0:T(8,128)(2,1)} collective-permute-done((bf16[192,2304]{1,0:T(8,128)(2,1)}, bf16[192,2304]{1,0:T(8,128)(2,1)}, u32[]{:S(2)}, u32[]{:S(2)}) %collective-permute-start.36) | collective-permute-done | bytes 884768 | tf_op jit(solution)/shard_map/ppermute | solution.py:185
  575.5 3.9 add_convert_fusion
  579.4 6.7 %collective-permute-done.37 = bf16[96,2304]{1,0:T(8,128)(2,1)S(1)} collective-permute-done((bf16[96,2304]{1,0:T(8,128)(2,1)S(1)}, bf16[96,2304]{1,0:T(8,128)(2,1)S(1)}, u32[]{:S(2)}, u32[]{:S(2)}) %collective-permute-start.37) | collective-permute-done | bytes 442400 | tf_op jit(solution)/shard_map/ppermute | solution.py:265
  587.4 4.9 collective-permute-done.38
  593.4 7.9 %collective-permute-done.39 = bf16[24,2304]{1,0:T(8,128)(2,1)S(1)} collective-permute-done((bf16[24,2304]{1,0:T(8,128)(2,1)S(1)}, bf16[24,2304]{1,0:T(8,128)(2,1)S(1)}, u32[]{:S(2)}, u32[]{:S(2)}) %collective-permute-start.39) | collective-permute-done | bytes 110624 | tf_op jit(solution)/shard_map/ppermute | solution.py:265
  602.0 6.1 collective-permute-done.40
  608.9 6.0 collective-permute-done.41
  617.6 5.8 collective-permute-done.42
  (359 shorter events, 118.2 us)
Async XLA Ops:
  7.2 35.9 %all-gather.7.cloned.1.call-start = ((), (), s32[]{:S(2)}) async-start(), calls=%async_computation | async-start | bytes 4423680 | tf_op jit(solution)/shard_map/all_gather | solution.py:255
  7.9 169.7 %all-gather.9.cloned.1.call-start = ((), (), s32[]{:S(2)}) async-start(), calls=%async_computation.1 | async-start | bytes 1474560 | tf_op jit(solution)/shard_map/all_gather | solution.py:255
  52.3 36.5 %collective-permute-start.1 = (bf16[512,1536]{1,0:T(8,128)(2,1)S(1)}, bf16[512,1536]{1,0:T(8,128)(2,1)S(1)}, u32[]{:S(2)}, u32[]{:S(2)}) collective-permute-start(bf16[512,1536]{1,0:T(8,128)(2,1)S(1)} %get-tuple-element.74.refs_2_.refs_6_.refs_5_.refs_9_), channel_id=1, source_target_pairs={{0,2},{1,3},{2,0},{3,1},{4,6},{5,7},{6,4},{7,5},{8,10},{9,11},{10,... | collective-permute-start | bytes 4718600 | tf_op jit(solution)/shard_map/ppermute | solution.py:185
  53.4 35.4 %collective-permute-start.2 = (bf16[512,1536]{1,0:T(8,128)(2,1)S(1)}, bf16[512,1536]{1,0:T(8,128)(2,1)S(1)}, u32[]{:S(2)}, u32[]{:S(2)}) collective-permute-start(bf16[512,1536]{1,0:T(8,128)(2,1)S(1)} %get-tuple-element.74.refs_2_.refs_6_.refs_5_.refs_9_), channel_id=1, source_target_pairs={{0,1},{1,0},{2,3},{3,2},{4,5},{5,4},{6,7},{7,6},{8,9},{9,8},{10,11... | collective-permute-start | bytes 4718600 | tf_op jit(solution)/shard_map/ppermute | solution.py:185
  92.4 90.8 %all-gather.11.cloned.1.call-start = ((), (), s32[]{:S(2)}) async-start(), calls=%async_computation.2 | async-start | bytes 5898240 | tf_op jit(solution)/shard_map/all_gather | solution.py:255
  93.1 110.1 %all-gather.13.cloned.1.call-start = ((), (), s32[]{:S(2)}) async-start(), calls=%async_computation.3 | async-start | bytes 5898240 | tf_op jit(solution)/shard_map/all_gather | solution.py:255
  93.3 51.8 %collective-permute-start = (bf16[512,1536]{1,0:T(8,128)(2,1)}, bf16[512,1536]{1,0:T(8,128)(2,1)}, u32[]{:S(2)}, u32[]{:S(2)}) collective-permute-start(bf16[512,1536]{1,0:T(8,128)(2,1)} %get-tuple-element.80.refs_2_.refs_6_.refs_5_.refs_9_), channel_id=1, source_target_pairs={{0,2},{1,3},{2,0},{3,1},{4,6},{5,7},{6,4},{7,5},{8,10},{9,11},{10,... | collective-permute-start | bytes 4718600 | tf_op jit(solution)/shard_map/ppermute | solution.py:185
  202.7 88.5 %collective-permute-start.10 = (bf16[768,768]{1,0:T(8,128)(2,1)}, bf16[768,768]{1,0:T(8,128)(2,1)}, u32[]{:S(2)}, u32[]{:S(2)}) collective-permute-start(bf16[768,768]{1,0:T(8,128)(2,1)} %get-tuple-element.192), channel_id=1, source_target_pairs={{0,1},{1,0},{2,3},{3,2},{4,5},{5,4},{6,7},{7,6},{8,9},{9,8},{10,11... | collective-permute-start | bytes 3538952 | tf_op jit(solution)/shard_map/ppermute | solution.py:185
  203.0 114.5 %collective-permute-start.9 = (bf16[768,768]{1,0:T(8,128)(2,1)}, bf16[768,768]{1,0:T(8,128)(2,1)}, u32[]{:S(2)}, u32[]{:S(2)}) collective-permute-start(bf16[768,768]{1,0:T(8,128)(2,1)} %get-tuple-element.191), channel_id=1, source_target_pairs={{0,1},{1,0},{2,3},{3,2},{4,5},{5,4},{6,7},{7,6},{8,9},{9,8},{10,11... | collective-permute-start | bytes 3538952 | tf_op jit(solution)/shard_map/ppermute | solution.py:185
  244.5 43.0 %collective-permute-start.22 = (bf16[192,768]{1,0:T(8,128)(2,1)}, bf16[192,768]{1,0:T(8,128)(2,1)}, u32[]{:S(2)}, u32[]{:S(2)}) collective-permute-start(bf16[192,768]{1,0:T(8,128)(2,1)} %get-tuple-element.202), channel_id=1, source_target_pairs={{0,1},{1,0},{2,3},{3,2},{4,5},{5,4},{6,7},{7,6},{8,9},{9,8},{10,11... | collective-permute-start | bytes 884744 | tf_op jit(solution)/shard_map/ppermute | solution.py:185
  266.4 22.4 %collective-permute-start.7 = (bf16[2,512,384]{2,1,0:T(8,128)(2,1)}, bf16[2,512,384]{2,1,0:T(8,128)(2,1)}, u32[]{:S(2)}, u32[]{:S(2)}) collective-permute-start(bf16[2,512,384]{2,1,0:T(8,128)(2,1)} %get-tuple-element.92), channel_id=1, source_target_pairs={{0,1},{1,0},{2,3},{3,2},{4,5},{5,4},{6,7},{7,6},{8,9},{9,8},{10,11... | collective-permute-start | bytes 2359304 | tf_op jit(solution)/shard_map/ppermute | solution.py:185
  266.7 23.8 %collective-permute-start.6 = (bf16[2,512,384]{2,1,0:T(8,128)(2,1)}, bf16[2,512,384]{2,1,0:T(8,128)(2,1)S(1)}, u32[]{:S(2)}, u32[]{:S(2)}) collective-permute-start(bf16[2,512,384]{2,1,0:T(8,128)(2,1)} %get-tuple-element.90), channel_id=1, source_target_pairs={{0,1},{1,0},{2,3},{3,2},{4,5},{5,4},{6,7},{7,6},{8,9},{9,8},{10,11... | collective-permute-start | bytes 2359304 | tf_op jit(solution)/shard_map/ppermute | solution.py:185
  287.5 14.2 %collective-permute-start.16 = (bf16[192,3072]{1,0:T(8,128)(2,1)S(1)}, bf16[192,3072]{1,0:T(8,128)(2,1)S(1)}, u32[]{:S(2)}, u32[]{:S(2)}) collective-permute-start(bf16[192,3072]{1,0:T(8,128)(2,1)S(1)} %get-tuple-element.190), channel_id=1, source_target_pairs={{0,1},{1,0},{2,3},{3,2},{4,5},{5,4},{6,7},{7,6},{8,9},{9,8},{10,11... | collective-permute-start | bytes 3538952 | tf_op jit(solution)/shard_map/ppermute | solution.py:185
  290.5 9.9 %collective-permute-start.23 = (bf16[192,768]{1,0:T(8,128)(2,1)S(1)}, bf16[192,768]{1,0:T(8,128)(2,1)S(1)}, u32[]{:S(2)}, u32[]{:S(2)}) collective-permute-start(bf16[192,768]{1,0:T(8,128)(2,1)S(1)} %fusion.38), channel_id=1, source_target_pairs={{0,2},{1,3},{2,0},{3,1},{4,6},{5,7},{6,4},{7,5},{8,10},{9,11},{10,... | collective-permute-start | bytes 884744 | tf_op jit(solution)/shard_map/ppermute | solution.py:185
  291.2 77.6 %collective-permute-start.15 = (bf16[192,3072]{1,0:T(8,128)(2,1)}, bf16[192,3072]{1,0:T(8,128)(2,1)}, u32[]{:S(2)}, u32[]{:S(2)}) collective-permute-start(bf16[192,3072]{1,0:T(8,128)(2,1)} %get-tuple-element.189), channel_id=1, source_target_pairs={{0,1},{1,0},{2,3},{3,2},{4,5},{5,4},{6,7},{7,6},{8,9},{9,8},{10,11... | collective-permute-start | bytes 3538952 | tf_op jit(solution)/shard_map/ppermute | solution.py:185
  293.3 24.0 %collective-permute-start.8 = (bf16[2,512,384]{2,1,0:T(8,128)(2,1)S(1)}, bf16[2,512,384]{2,1,0:T(8,128)(2,1)S(1)}, u32[]{:S(2)}, u32[]{:S(2)}) collective-permute-start(bf16[2,512,384]{2,1,0:T(8,128)(2,1)S(1)} %add_convert_fusion.16), channel_id=1, source_target_pairs={{0,2},{1,3},{2,0},{3,1},{4,6},{5,7},{6,4},{7,5},{8,10},{9,11},{10,... | collective-permute-start | bytes 2359304 | tf_op jit(solution)/shard_map/ppermute | solution.py:185
  300.4 42.1 %collective-permute-start.11 = (bf16[768,768]{1,0:T(8,128)(2,1)S(1)}, bf16[768,768]{1,0:T(8,128)(2,1)S(1)}, u32[]{:S(2)}, u32[]{:S(2)}) collective-permute-start(bf16[768,768]{1,0:T(8,128)(2,1)S(1)} %fusion.23), channel_id=1, source_target_pairs={{0,2},{1,3},{2,0},{3,1},{4,6},{5,7},{6,4},{7,5},{8,10},{9,11},{10,... | collective-permute-start | bytes 3538952 | tf_op jit(solution)/shard_map/ppermute | solution.py:185
  304.5 64.3 %collective-permute-start.17 = (bf16[192,3072]{1,0:T(8,128)(2,1)}, bf16[192,3072]{1,0:T(8,128)(2,1)}, u32[]{:S(2)}, u32[]{:S(2)}) collective-permute-start(bf16[192,3072]{1,0:T(8,128)(2,1)} %fusion.21), channel_id=1, source_target_pairs={{0,2},{1,3},{2,0},{3,1},{4,6},{5,7},{6,4},{7,5},{8,10},{9,11},{10,... | collective-permute-start | bytes 3538952 | tf_op jit(solution)/shard_map/ppermute | solution.py:185
  345.6 52.8 %collective-permute-start.24 = (bf16[384,768]{1,0:T(8,128)(2,1)}, bf16[384,768]{1,0:T(8,128)(2,1)}, u32[]{:S(2)}, u32[]{:S(2)}) collective-permute-start(bf16[384,768]{1,0:T(8,128)(2,1)} %dynamic-slice_bitcast_fusion.7), channel_id=1, source_target_pairs={{0,4},{4,0},{8,12},{12,8},{16,20},{20,16},{24,28},{28,24},{1,5},{5... | collective-permute-start | bytes 1769480 | tf_op jit(solution)/shard_map/ppermute | solution.py:265
  368.2 32.8 %collective-permute-start.13 = (bf16[2,512,384]{2,1,0:T(8,128)(2,1)}, bf16[2,512,384]{2,1,0:T(8,128)(2,1)}, u32[]{:S(2)}, u32[]{:S(2)}) collective-permute-start(bf16[2,512,384]{2,1,0:T(8,128)(2,1)} %get-tuple-element.100), channel_id=1, source_target_pairs={{0,1},{1,0},{2,3},{3,2},{4,5},{5,4},{6,7},{7,6},{8,9},{9,8},{10,11... | collective-permute-start | bytes 2359304 | tf_op jit(solution)/shard_map/ppermute | solution.py:185
  368.3 35.2 %collective-permute-start.12 = (bf16[2,512,384]{2,1,0:T(8,128)(2,1)}, bf16[2,512,384]{2,1,0:T(8,128)(2,1)}, u32[]{:S(2)}, u32[]{:S(2)}) collective-permute-start(bf16[2,512,384]{2,1,0:T(8,128)(2,1)} %get-tuple-element.98), channel_id=1, source_target_pairs={{0,1},{1,0},{2,3},{3,2},{4,5},{5,4},{6,7},{7,6},{8,9},{9,8},{10,11... | collective-permute-start | bytes 2359304 | tf_op jit(solution)/shard_map/ppermute | solution.py:185
  373.3 22.4 %collective-permute-start.49 = (bf16[96,3072]{1,0:T(8,128)(2,1)}, bf16[96,3072]{1,0:T(8,128)(2,1)}, u32[]{:S(2)}, u32[]{:S(2)}) collective-permute-start(bf16[96,3072]{1,0:T(8,128)(2,1)} %dynamic-slice_bitcast_fusion.6), channel_id=1, source_target_pairs={{0,4},{4,0},{8,12},{12,8},{16,20},{20,16},{24,28},{28,24},{1,5},{5... | collective-permute-start | bytes 1769480 | tf_op jit(solution)/shard_map/ppermute | solution.py:265
  395.6 78.0 %collective-permute-start.19 = (bf16[2,512,384]{2,1,0:T(8,128)(2,1)}, bf16[2,512,384]{2,1,0:T(8,128)(2,1)}, u32[]{:S(2)}, u32[]{:S(2)}) collective-permute-start(bf16[2,512,384]{2,1,0:T(8,128)(2,1)} %get-tuple-element.110), channel_id=1, source_target_pairs={{0,1},{1,0},{2,3},{3,2},{4,5},{5,4},{6,7},{7,6},{8,9},{9,8},{10,11... | collective-permute-start | bytes 2359304 | tf_op jit(solution)/shard_map/ppermute | solution.py:185
  395.7 87.3 %collective-permute-start.18 = (bf16[2,512,384]{2,1,0:T(8,128)(2,1)}, bf16[2,512,384]{2,1,0:T(8,128)(2,1)}, u32[]{:S(2)}, u32[]{:S(2)}) collective-permute-start(bf16[2,512,384]{2,1,0:T(8,128)(2,1)} %get-tuple-element.108), channel_id=1, source_target_pairs={{0,1},{1,0},{2,3},{3,2},{4,5},{5,4},{6,7},{7,6},{8,9},{9,8},{10,11... | collective-permute-start | bytes 2359304 | tf_op jit(solution)/shard_map/ppermute | solution.py:185
  398.4 31.3 %collective-permute-start.50 = (bf16[48,3072]{1,0:T(8,128)(2,1)}, bf16[48,3072]{1,0:T(8,128)(2,1)}, u32[]{:S(2)}, u32[]{:S(2)}) collective-permute-start(bf16[48,3072]{1,0:T(8,128)(2,1)} %dynamic-slice_bitcast_fusion.10), channel_id=1, source_target_pairs={{0,8},{4,12},{8,0},{12,4},{16,24},{20,28},{24,16},{28,20},{1,9},{5... | collective-permute-start | bytes 884744 | tf_op jit(solution)/shard_map/ppermute | solution.py:265
  405.6 45.9 %collective-permute-start.55 = (bf16[192,768]{1,0:T(8,128)(2,1)}, bf16[192,768]{1,0:T(8,128)(2,1)}, u32[]{:S(2)}, u32[]{:S(2)}) collective-permute-start(bf16[192,768]{1,0:T(8,128)(2,1)} %dynamic-slice_bitcast_fusion.9), channel_id=1, source_target_pairs={{0,8},{4,12},{8,0},{12,4},{16,24},{20,28},{24,16},{28,20},{1,9},{5... | collective-permute-start | bytes 884744 | tf_op jit(solution)/shard_map/ppermute | solution.py:265
  406.8 24.1 %collective-permute-start.43 = (bf16[96,768]{1,0:T(8,128)(2,1)}, bf16[96,768]{1,0:T(8,128)(2,1)}, u32[]{:S(2)}, u32[]{:S(2)}) collective-permute-start(bf16[96,768]{1,0:T(8,128)(2,1)} %dynamic-slice_bitcast_fusion.16), channel_id=1, source_target_pairs={{0,4},{4,0},{8,12},{12,8},{16,20},{20,16},{24,28},{28,24},{1,5},{5... | collective-permute-start | bytes 442376 | tf_op jit(solution)/shard_map/ppermute | solution.py:265
  429.6 53.0 %collective-permute-start.26 = (bf16[2,512,384]{2,1,0:T(8,128)(2,1)}, bf16[2,512,384]{2,1,0:T(8,128)(2,1)S(1)}, u32[]{:S(2)}, u32[]{:S(2)}) collective-permute-start(bf16[2,512,384]{2,1,0:T(8,128)(2,1)} %get-tuple-element.118), channel_id=1, source_target_pairs={{0,1},{1,0},{2,3},{3,2},{4,5},{5,4},{6,7},{7,6},{8,9},{9,8},{10,11... | collective-permute-start | bytes 2359304 | tf_op jit(solution)/shard_map/ppermute | solution.py:185
  436.7 9.4 %collective-permute-start.51 = (bf16[24,3072]{1,0:T(8,128)(2,1)S(1)}, bf16[24,3072]{1,0:T(8,128)(2,1)S(1)}, u32[]{:S(2)}, u32[]{:S(2)}) collective-permute-start(bf16[24,3072]{1,0:T(8,128)(2,1)S(1)} %dynamic-slice_bitcast_fusion.15), channel_id=1, source_target_pairs={{0,16},{4,20},{8,24},{12,28},{16,0},{20,4},{24,8},{28,12},{1,17},{... | collective-permute-start | bytes 442376 | tf_op jit(solution)/shard_map/ppermute | solution.py:265
  451.5 14.1 %collective-permute-start.52 = (bf16[24,3072]{1,0:T(8,128)(2,1)S(1)}, bf16[24,3072]{1,0:T(8,128)(2,1)S(1)}, u32[]{:S(2)}, u32[]{:S(2)}) collective-permute-start(bf16[24,3072]{1,0:T(8,128)(2,1)S(1)} %fusion.43), channel_id=1, source_target_pairs={{0,16},{4,20},{8,24},{12,28},{16,0},{20,4},{24,8},{28,12},{1,17},{... | collective-permute-start | bytes 442376 | tf_op jit(solution)/shard_map/ppermute | solution.py:265
  451.5 8.5 %collective-permute-start.46 = (bf16[24,768]{1,0:T(8,128)(2,1)S(1)}, bf16[24,768]{1,0:T(8,128)(2,1)S(1)}, u32[]{:S(2)}, u32[]{:S(2)}) collective-permute-start(bf16[24,768]{1,0:T(8,128)(2,1)S(1)} %fusion.50), channel_id=1, source_target_pairs={{0,16},{4,20},{8,24},{12,28},{16,0},{20,4},{24,8},{28,12},{1,17},{... | collective-permute-start | bytes 110600 | tf_op jit(solution)/shard_map/ppermute | solution.py:265
  465.6 10.7 %collective-permute-start.48 = (bf16[96,768]{1,0:T(8,128)(2,1)S(1)}, bf16[96,768]{1,0:T(8,128)(2,1)S(1)}, u32[]{:S(2)}, u32[]{:S(2)}) collective-permute-start(bf16[96,768]{1,0:T(8,128)(2,1)S(1)} %maximum_select_fusion.10), channel_id=1, source_target_pairs={{0,4},{4,0},{8,12},{12,8},{16,20},{20,16},{24,28},{28,24},{1,5},{5... | collective-permute-start | bytes 442376 | tf_op jit(solution)/shard_map/ppermute | solution.py:265
  476.4 20.5 %collective-permute-start.20 = (bf16[2,512,384]{2,1,0:T(8,128)(2,1)S(1)}, bf16[2,512,384]{2,1,0:T(8,128)(2,1)S(1)}, u32[]{:S(2)}, u32[]{:S(2)}) collective-permute-start(bf16[2,512,384]{2,1,0:T(8,128)(2,1)S(1)} %add_convert_fusion.10), channel_id=1, source_target_pairs={{0,2},{1,3},{2,0},{3,1},{4,6},{5,7},{6,4},{7,5},{8,10},{9,11},{10,... | collective-permute-start | bytes 2359304 | tf_op jit(solution)/shard_map/ppermute | solution.py:185
  481.5 35.8 %collective-permute-start.25 = (bf16[2,512,384]{2,1,0:T(8,128)(2,1)S(1)}, bf16[2,512,384]{2,1,0:T(8,128)(2,1)S(1)}, u32[]{:S(2)}, u32[]{:S(2)}) collective-permute-start(bf16[2,512,384]{2,1,0:T(8,128)(2,1)S(1)} %copy-done.54), channel_id=1, source_target_pairs={{0,1},{1,0},{2,3},{3,2},{4,5},{5,4},{6,7},{7,6},{8,9},{9,8},{10,11... | collective-permute-start | bytes 2359304 | tf_op jit(solution)/shard_map/ppermute | solution.py:185
  481.9 31.8 %collective-permute-start.14 = (bf16[2,512,384]{2,1,0:T(8,128)(2,1)S(1)}, bf16[2,512,384]{2,1,0:T(8,128)(2,1)S(1)}, u32[]{:S(2)}, u32[]{:S(2)}) collective-permute-start(bf16[2,512,384]{2,1,0:T(8,128)(2,1)S(1)} %copy-done.23), channel_id=1, source_target_pairs={{0,2},{1,3},{2,0},{3,1},{4,6},{5,7},{6,4},{7,5},{8,10},{9,11},{10,... | collective-permute-start | bytes 2359304 | tf_op jit(solution)/shard_map/ppermute | solution.py:185
  482.6 16.3 %collective-permute-start.58 = (bf16[192,768]{1,0:T(8,128)(2,1)S(1)}, bf16[192,768]{1,0:T(8,128)(2,1)S(1)}, u32[]{:S(2)}, u32[]{:S(2)}) collective-permute-start(bf16[192,768]{1,0:T(8,128)(2,1)S(1)} %maximum_select_fusion.8), channel_id=1, source_target_pairs={{0,8},{4,12},{8,0},{12,4},{16,24},{20,28},{24,16},{28,20},{1,9},{5... | collective-permute-start | bytes 884744 | tf_op jit(solution)/shard_map/ppermute | solution.py:265
  483.0 30.9 %collective-permute-start.54 = (bf16[96,3072]{1,0:T(8,128)(2,1)S(1)}, bf16[96,3072]{1,0:T(8,128)(2,1)S(1)}, u32[]{:S(2)}, u32[]{:S(2)}) collective-permute-start(bf16[96,3072]{1,0:T(8,128)(2,1)S(1)} %maximum_select_fusion.3), channel_id=1, source_target_pairs={{0,4},{4,0},{8,12},{12,8},{16,20},{20,16},{24,28},{28,24},{1,5},{5... | collective-permute-start | bytes 1769480 | tf_op jit(solution)/shard_map/ppermute | solution.py:265
  496.8 28.4 %collective-permute-start.27 = (bf16[2,512,384]{2,1,0:T(8,128)(2,1)S(1)}, bf16[2,512,384]{2,1,0:T(8,128)(2,1)S(1)}, u32[]{:S(2)}, u32[]{:S(2)}) collective-permute-start(bf16[2,512,384]{2,1,0:T(8,128)(2,1)S(1)} %add_convert_fusion.7), channel_id=1, source_target_pairs={{0,2},{1,3},{2,0},{3,1},{4,6},{5,7},{6,4},{7,5},{8,10},{9,11},{10,... | collective-permute-start | bytes 2359304 | tf_op jit(solution)/shard_map/ppermute | solution.py:185
  499.1 16.5 %collective-permute-start.59 = (bf16[384,768]{1,0:T(8,128)(2,1)S(1)}, bf16[384,768]{1,0:T(8,128)(2,1)S(1)}, u32[]{:S(2)}, u32[]{:S(2)}) collective-permute-start(bf16[384,768]{1,0:T(8,128)(2,1)S(1)} %maximum_select_fusion.4), channel_id=1, source_target_pairs={{0,4},{4,0},{8,12},{12,8},{16,20},{20,16},{24,28},{28,24},{1,5},{5... | collective-permute-start | bytes 1769480 | tf_op jit(solution)/shard_map/ppermute | solution.py:265
  536.0 12.3 %collective-permute-start.35 = (bf16[192,2304]{1,0:T(8,128)(2,1)}, bf16[192,2304]{1,0:T(8,128)(2,1)}, u32[]{:S(2)}, u32[]{:S(2)}) collective-permute-start(bf16[192,2304]{1,0:T(8,128)(2,1)} %get-tuple-element.194), channel_id=1, source_target_pairs={{0,1},{1,0},{2,3},{3,2},{4,5},{5,4},{6,7},{7,6},{8,9},{9,8},{10,11... | collective-permute-start | bytes 2654216 | tf_op jit(solution)/shard_map/ppermute | solution.py:185
  536.0 16.6 %collective-permute-start.34 = (bf16[192,2304]{1,0:T(8,128)(2,1)}, bf16[192,2304]{1,0:T(8,128)(2,1)}, u32[]{:S(2)}, u32[]{:S(2)}) collective-permute-start(bf16[192,2304]{1,0:T(8,128)(2,1)} %get-tuple-element.193), channel_id=1, source_target_pairs={{0,1},{1,0},{2,3},{3,2},{4,5},{5,4},{6,7},{7,6},{8,9},{9,8},{10,11... | collective-permute-start | bytes 2654216 | tf_op jit(solution)/shard_map/ppermute | solution.py:185
  550.9 21.9 %collective-permute-start.36 = (bf16[192,2304]{1,0:T(8,128)(2,1)}, bf16[192,2304]{1,0:T(8,128)(2,1)}, u32[]{:S(2)}, u32[]{:S(2)}) collective-permute-start(bf16[192,2304]{1,0:T(8,128)(2,1)} %fusion.26), channel_id=1, source_target_pairs={{0,2},{1,3},{2,0},{3,1},{4,6},{5,7},{6,4},{7,5},{8,10},{9,11},{10,... | collective-permute-start | bytes 2654216 | tf_op jit(solution)/shard_map/ppermute | solution.py:185
  552.1 34.6 %collective-permute-start.29 = (bf16[16,2304]{1,0:T(8,128)(2,1)S(1)}, bf16[16,2304]{1,0:T(8,128)(2,1)S(1)}, u32[]{:S(2)}, u32[]{:S(2)}) collective-permute-start(bf16[16,2304]{1,0:T(8,128)(2,1)S(1)} %get-tuple-element.204), channel_id=1, source_target_pairs={{0,1},{1,0},{2,3},{3,2},{4,5},{5,4},{6,7},{7,6},{8,9},{9,8},{10,11... | collective-permute-start | bytes 221192 | tf_op jit(solution)/shard_map/ppermute | solution.py:185
  552.2 40.6 %collective-permute-start.28 = (bf16[16,2304]{1,0:T(8,128)(2,1)S(1)}, bf16[16,2304]{1,0:T(8,128)(2,1)S(1)}, u32[]{:S(2)}, u32[]{:S(2)}) collective-permute-start(bf16[16,2304]{1,0:T(8,128)(2,1)S(1)} %get-tuple-element.203), channel_id=1, source_target_pairs={{0,1},{1,0},{2,3},{3,2},{4,5},{5,4},{6,7},{7,6},{8,9},{9,8},{10,11... | collective-permute-start | bytes 221192 | tf_op jit(solution)/shard_map/ppermute | solution.py:185
  574.9 11.3 %collective-permute-start.37 = (bf16[96,2304]{1,0:T(8,128)(2,1)S(1)}, bf16[96,2304]{1,0:T(8,128)(2,1)S(1)}, u32[]{:S(2)}, u32[]{:S(2)}) collective-permute-start(bf16[96,2304]{1,0:T(8,128)(2,1)S(1)} %dynamic-slice_bitcast_fusion.8), channel_id=1, source_target_pairs={{0,4},{4,0},{8,12},{12,8},{16,20},{20,16},{24,28},{28,24},{1,5},{5... | collective-permute-start | bytes 1327112 | tf_op jit(solution)/shard_map/ppermute | solution.py:265
  592.4 9.0 %collective-permute-start.39 = (bf16[24,2304]{1,0:T(8,128)(2,1)S(1)}, bf16[24,2304]{1,0:T(8,128)(2,1)S(1)}, u32[]{:S(2)}, u32[]{:S(2)}) collective-permute-start(bf16[24,2304]{1,0:T(8,128)(2,1)S(1)} %dynamic-slice_bitcast_fusion.17), channel_id=1, source_target_pairs={{0,16},{4,20},{8,24},{12,28},{16,0},{20,4},{24,8},{28,12},{1,17},{... | collective-permute-start | bytes 331784 | tf_op jit(solution)/shard_map/ppermute | solution.py:265
  592.8 8.7 %collective-permute-start.31 = (bf16[16,2304]{1,0:T(8,128)(2,1)S(1)}, bf16[16,2304]{1,0:T(8,128)(2,1)S(1)}, u32[]{:S(2)}, u32[]{:S(2)}) collective-permute-start(bf16[16,2304]{1,0:T(8,128)(2,1)S(1)} %add_convert_fusion.22), channel_id=1, source_target_pairs={{0,4},{4,0},{8,12},{12,8},{16,20},{20,16},{24,28},{28,24},{1,5},{5... | collective-permute-start | bytes 221192 | tf_op jit(solution)/shard_map/ppermute | solution.py:265
  615.0 8.4 %collective-permute-start.42 = (bf16[96,2304]{1,0:T(8,128)(2,1)S(1)}, bf16[96,2304]{1,0:T(8,128)(2,1)S(1)}, u32[]{:S(2)}, u32[]{:S(2)}) collective-permute-start(bf16[96,2304]{1,0:T(8,128)(2,1)S(1)} %maximum_select_fusion.5), channel_id=1, source_target_pairs={{0,4},{4,0},{8,12},{12,8},{16,20},{20,16},{24,28},{28,24},{1,5},{5... | collective-permute-start | bytes 1327112 | tf_op jit(solution)/shard_map/ppermute | solution.py:265
  (72 other events, 703.8 us)
Sparse Core Ops, SparseCore 0:
  9.6 33.4 all-gather.6
  92.5 23.8 all-gather.8
  117.9 45.2 all-gather.10
  164.7 37.4 all-gather.12
where the time goes:
time: 637 us; the launch traced here: 631 us
  waiting for transfers between devices  254 us (40%)
  Pallas kernels  134 us (21%)
  matrix products  84.4 us (13%)
  other arithmetic  58.6 us (9%)
  local copies, waits for them, and re-layouts  45.1 us (7%)
  starting transfers between devices  33.6 us (5%)
  between operations  15.3 us (2%)
    ppermute x33, waiting for transfers between devices, swap(): return lax.ppermute(x, 'band', [(i, i ^ flip) for i in range(parts)])  160 us
    pallas_call x4, Pallas kernels, attn_bwd(): pl.pallas_call(functools.partial(bwd_kernel, tq=min(tq, n), parts=parts),...  85.8 us
    ppermute x27, waiting for transfers between devices, trade(): return lax.ppermute(x, 'dp', [(i, i ^ flip) for i in range(size)])  73.4 us
    pallas_call x2, Pallas kernels, attn_fwd(): pl.pallas_call(functools.partial(fwd_kernel, tq=min(tq, n), parts=parts),...  48.2 us
    dot_general x4, matrix products, nn(): lax.dot_general(a, b, (((1,), (0,)), ((), ())), preferred_element_type=f32)  31.2 us
    dot_general x4, matrix products, nt(): lax.dot_general(a, b, (((1,), (1,)), ((), ())), preferred_element_type=f32)  31.1 us
    convert_element_type x20, other arithmetic, fold(): (near.astype(f32) + swap(far, flip).astype(f32)).astype(bf)  25 us
    dot_general x4, matrix products, tn(): lax.dot_general(a, b, (((0,), (0,)), ((), ())), preferred_element_type=f32)  22.1 us
  transfers between devices with their start and end apart: 64, of which 27 were waited for; matrix products, arithmetic and copies ran while one was open for 25% of the time, Pallas kernels for 21%

commit v1 on v0

--- a/solution.py
+++ b/solution.py
@@ -255,9 +255,13 @@
     return lax.all_gather(shard, "band", axis=0, tiled=True)
 
 
-def reduce_band(grad):
+def reduce_core(grad):
     blocks = grad.reshape(lax.axis_size("band"), -1, grad.shape[1])
-    return reduce_relative(relative_rows(blocks))
+    return fold(relative_rows(blocks), 1)
+
+
+def reduce_chip(blocks):
+    return reduce_relative(blocks, 2)
 
 
 def trade(x, flip):
@@ -350,7 +354,10 @@
     grad_w_fall = tn(active_low, grad_m)
     grad_b_fall = jnp.sum(grad_m.astype(f32), axis=0)
     low_fall, grad_m = tie(grad_w_fall.astype(bf), grad_m)
+    fall = reduce_core(low_fall)
     grad_up = pull_gelu(nt(grad_m, w_fall))[0].astype(bf)
+    fall, grad_up = tie(fall, grad_up)
+    fall = reduce_chip(fall)
     grad_w_rise = tn(mid_low, grad_up)
     grad_b_rise = jnp.sum(grad_up.astype(f32), axis=0)
     grad_mid, grad_gain_two, grad_shift_two = pull_two(nt(grad_up, w_rise))
@@ -361,8 +368,7 @@
     grad_mixed = nt(grad_a, w_mix).astype(bf)
 
     grad_mixed, *rest = lax.optimization_barrier((grad_mixed, grad_w_rise.astype(bf), grad_w_mix.astype(bf)))
-    large = [low_fall, *rest]
-    large = [reduce_band(grad) for grad in large]
+    rise, out_grad = reduce_core(rest[0]), reduce_core(rest[1])
 
     count = width // (4 * HD)
     calls = [(m, first) for m in range(micro) for first in range(0, 2 * count, count)]
@@ -372,10 +378,13 @@
         grad_out = grad_mixed[m * tokens : (m + 1) * tokens]
         if i >= 2:
             halves[i - 2], grad_out = tie(halves[i - 2], grad_out)
-        if i in (1, 2):
-            large[i - 1], grad_out = tie(large[i - 1], grad_out)
+        if i == 1:
+            (fall, rise, out_grad), grad_out = tie((fall, rise, out_grad), grad_out)
+            rise, out_grad = reduce_chip(rise), reduce_chip(out_grad)
+            fall = halve(fall, 1)
         if i == 3:
-            (large[2], halved), grad_out = tie((large[2], halve(large[0], 1)), grad_out)
+            (fall, rise, out_grad), grad_out = tie((fall, rise, out_grad), grad_out)
+            rise = halve(rise, 1)
         grad_q, *grad_blocks = attn_bwd(q, blocks, grad_out, mix, log_total, seg_q, first, count)
         halves.append(fold(grad_blocks, 1))
         grads_q.append(grad_q)
@@ -383,7 +392,7 @@
     for half in halves:
         pairs.append(reduce_relative(half, 2))
     pairs, grads_q = tie(pairs, grads_q)
-    wide = [finish(halved, 2), finish(large[1], 1), finish(large[2], 1)]
+    wide = [finish(fall, 2), finish(rise, 2), finish(out_grad, 1)]
     grad_qkv = jnp.concatenate(
         [
             jnp.concatenate(

time: 637 us -> 602 us (0.945)
  waiting for transfers between devices: 254 us -> 199 us
  starting transfers between devices: 33.6 us -> 48.1 us
  other arithmetic: 58.6 us -> 68.4 us
    ppermute x33, waiting for transfers between devices: 160 us -> 90.2 us  [swap(): return lax.ppermute(x, 'band', [(i, i ^ flip) for i in range(parts)])]
    ppermute x27, waiting for transfers between devices: 73.4 us -> 88.6 us  [trade(): return lax.ppermute(x, 'dp', [(i, i ^ flip) for i in range(size)])]
    ppermute x27, starting transfers between devices: 20.1 us -> 33.5 us  [trade(): return lax.ppermute(x, 'dp', [(i, i ^ flip) for i in range(size)])]
    convert_element_type x20, other arithmetic: 25 us -> 33.4 us  [fold(): (near.astype(f32) + swap(far, flip).astype(f32)).astype(bf)]
    unnamed x129 -> x135, local copies, waits for them, and re-layouts: 14.6 us -> 15.9 us
  transfers between devices with their start and end apart: 64 -> 64, of which waited for: 27 -> 27; matrix products, arithmetic and copies ran while one was open for 25% -> 24% of each run, Pallas kernels for 21% -> 19%
where the time goes in v1:
time: 602 us; the launch traced here: 596 us
  waiting for transfers between devices  199 us (33%)
  Pallas kernels  134 us (22%)
  matrix products  81.6 us (14%)
  other arithmetic  68.4 us (11%)
  starting transfers between devices  48.1 us (8%)
  local copies, waits for them, and re-layouts  43 us (7%)
  between operations  15.6 us (3%)
  blocking collectives  6.24 us (1%)
    ppermute x33, waiting for transfers between devices, swap(): return lax.ppermute(x, 'band', [(i, i ^ flip) for i in range(parts)])  90.2 us
    ppermute x27, waiting for transfers between devices, trade(): return lax.ppermute(x, 'dp', [(i, i ^ flip) for i in range(size)])  88.6 us
    pallas_call x4, Pallas kernels, attn_bwd(): pl.pallas_call(functools.partial(bwd_kernel, tq=min(tq, n), parts=parts),...  85.9 us
    pallas_call x2, Pallas kernels, attn_fwd(): pl.pallas_call(functools.partial(fwd_kernel, tq=min(tq, n), parts=parts),...  48.2 us
    ppermute x27, starting transfers between devices, trade(): return lax.ppermute(x, 'dp', [(i, i ^ flip) for i in range(size)])  33.5 us
    convert_element_type x20, other arithmetic, fold(): (near.astype(f32) + swap(far, flip).astype(f32)).astype(bf)  33.4 us
    dot_general x4, matrix products, nn(): lax.dot_general(a, b, (((1,), (0,)), ((), ())), preferred_element_type=f32)  31.6 us
    dot_general x4, matrix products, nt(): lax.dot_general(a, b, (((1,), (1,)), ((), ())), preferred_element_type=f32)  27 us
  transfers between devices with their start and end apart: 64, of which 27 were waited for; matrix products, arithmetic and copies ran while one was open for 24% of the time, Pallas kernels for 19%

profile of v1, /device:TPU:0, one launch (start us, length us, event | category | flops | bytes accessed | tf_op | source)
XLA Modules:
  0.0 596.3 jit_solution(11376730930969921042)
XLA Ops:
  8.0 5.5 concatenate.100
  13.4 6.2 %all-gather.1 = bf16[4,1,2304]{2,1,0:T(2,128)(2,1)S(1)} all-gather(bf16[1,1,2304]{2,1,0:T(2,128)(2,1)S(1)} %reshape.435), channel_id=2, replica_groups=mesh['dp'=8,'band'=4] {'band'}, dimensions={0}, use_global_device_ids=true | all-gather | bytes 23040 | tf_op jit(solution)/shard_map/all_gather | solution.py:220
  23.8 19.3 %all-gather.7.cloned.1.call-done = bf16[768,2304]{1,0:T(8,128)(2,1)} async-done(((bf16[192,2304]{1,0:T(8,128)(2,1)}), bf16[768,2304]{1,0:T(8,128)(2,1)}) %all-gather.7.cloned.1.call-update) | async-done | bytes 3538960 | tf_op jit(solution)/shard_map/all_gather | solution.py:255
  43.1 5.8 fusion.65
  52.5 35.2 %collective-permute-done.1.refs_3_.refs_7_.refs_6_.refs_10_ = bf16[512,1536]{1,0:T(8,128)(2,1)S(1)} collective-permute-done((bf16[512,1536]{1,0:T(8,128)(2,1)S(1)}, bf16[512,1536]{1,0:T(8,128)(2,1)S(1)}, u32[]{:S(2)}, u32[]{:S(2)}) %collective-permute-start.1) | collective-permute-done | bytes 1572896 | tf_op jit(solution)/shard_map/ppermute | solution.py:185
  94.8 24.1 %attn_fwd.2 = (bf16[512,768]{1,0:T(8,128)(2,1)}, f32[512,768]{1,0:T(8,128)}) custom-call(bf16[512,768]{1,0:T(8,128)(2,1)} %get-tuple-element.216.refs_0_, s32[512,1]{1,0:T(8,128)} %copy.39.refs_1_.refs_4_, bf16[512,1536]{1,0:T(8,128)(2,1)} %copy-done.18, bf16[512,1536]{1,0:T(8,128)(2,1)} %copy-done.51, bf16[512,1536]{1,0:T(8,128)(2,1)} %copy-done.52, ...), custom_call_target="tpu_custom_call" | custom-call | flops 12884901888 | bytes 9437184 | tf_op jit(solution)/shard_map/attn_fwd/pallas_call | solution.py:88
  118.9 25.1 %collective-permute-done.refs_3_.refs_7_.refs_6_.refs_10_ = bf16[512,1536]{1,0:T(8,128)(2,1)} collective-permute-done((bf16[512,1536]{1,0:T(8,128)(2,1)}, bf16[512,1536]{1,0:T(8,128)(2,1)}, u32[]{:S(2)}, u32[]{:S(2)}) %collective-permute-start) | collective-permute-done | bytes 1572896 | tf_op jit(solution)/shard_map/ppermute | solution.py:185
  150.4 24.0 %attn_fwd.3 = (bf16[512,768]{1,0:T(8,128)(2,1)}, f32[512,768]{1,0:T(8,128)}) custom-call(bf16[512,768]{1,0:T(8,128)(2,1)} %get-tuple-element.215.refs_0_, s32[512,1]{1,0:T(8,128)} %copy.40.refs_1_.refs_4_, bf16[512,1536]{1,0:T(8,128)(2,1)} %get-tuple-element.86.refs_2_.refs_6_.refs_5_.refs_9_, ...), custom_call_target="tpu_custom_call" | custom-call | flops 12884901888 | bytes 9437184 | tf_op jit(solution)/shard_map/attn_fwd/pallas_call | solution.py:88
  176.5 3.3 fusion.64
  182.0 8.6 %fusion.54 = f32[1024,3072]{1,0:T(8,128)S(1)} fusion(bf16[768,3072]{1,0:T(8,128)(2,1)} %all-gather.11.cloned.1.call-done, f32[1024,768]{1,0:T(8,128)} %copy-done.6, f32[768]{0:T(1024)S(1)} %reshape.404, f32[768]{0:T(1024)S(1)} %reshape.403, f32[1024]{0:T(1024)S(1)} %fusion.51, f32[1024]{0:T(1024)S(1)} %broadcast_multiply_fusion), kind=kOutput, calls=%fused_computation.197 | convolution fusion | flops 4835770368 | bytes 20461568 | tf_op jit(solution)/shard_map/dot_general | solution.py:16
  190.7 8.1 %convolution_convert_fusion.1 = bf16[3072,768]{1,0:T(8,128)(2,1)S(1)} fusion(bf16[1024,768]{1,0:T(8,128)(2,1)S(1)} %copy-done.17, f32[1024,3072]{1,0:T(8,128)S(1)} %fusion.54, f32[3072]{0:T(1024)S(1)} %reshape.405), kind=kOutput, calls=%fused_computation.11 | convolution fusion | flops 4865654784 | bytes 18886656 | tf_op jit(solution)/shard_map/dot_general | solution.py:19
  202.2 14.2 %fusion.6 = bf16[1024,3072]{1,0:T(8,128)(2,1)S(1)} fusion(f32[1024,3072]{1,0:T(8,128)} %copy-done.56, f32[3072]{0:T(1024)S(1)} %reshape.405, bf16[1024,768]{1,0:T(8,128)(2,1)S(1)} %copy-done.17, bf16[3072,768]{1,0:T(8,128)(2,1)} %all-gather.13.cloned.1.call-done), kind=kOutput, calls=%fused_computation.8 | convolution fusion | flops 4897898496 | bytes 25178112 | tf_op jit(solution)/shard_map/dot_general | solution.py:13
  216.5 6.6 %fusion.23 = (bf16[768,768]{1,0:T(8,128)(2,1)}, bf16[768,768]{1,0:T(8,128)(2,1)}) fusion(bf16[768,768]{1,0:T(8,128)(2,1)} %collective-permute-done.7, bf16[4,768,768]{2,1,0:T(8,128)(2,1)} %bitcast.234, s32[]{:T(128)S(6)} %select_n.206, bf16[768,768]{1,0:T(8,128)(2,1)} %collective-permute-done.6, s32[]{:T(128)S(6)} %select_n.204), kind=kLoop, calls=%fused_computation.53 | loop fusion | flops 4718592 | bytes 7077896 | tf_op jit(solution)/shard_map/convert_element_type | solution.py:206
  223.1 8.1 %convolution_convert_fusion = bf16[768,3072]{1,0:T(8,128)(2,1)} fusion(bf16[1024,3072]{1,0:T(8,128)(2,1)S(1)} %fusion.6, f32[1024,768]{1,0:T(8,128)S(1)} %copy-done.7, f32[768]{0:T(1024)S(1)} %reshape.404, f32[768]{0:T(1024)S(1)} %reshape.403, f32[1024]{0:T(1024)S(1)} %fusion.51, f32[1024]{0:T(1024)S(1)} %broadcast_multiply_fusion), kind=kOutput, calls=%fused_computation.10 | convolution fusion | flops 4838129664 | bytes 14170112 | tf_op jit(solution)/shard_map/dot_general | solution.py:19
  231.2 5.6 multiply_reduce_fusion
  246.1 21.6 %attn_bwd.4 = (bf16[512,384]{1,0:T(8,128)(2,1)}, bf16[2,512,384]{2,1,0:T(8,128)(2,1)}, bf16[2,512,384]{2,1,0:T(8,128)(2,1)}, bf16[2,512,384]{2,1,0:T(8,128)(2,1)}, bf16[2,512,384]{2,1,0:T(8,128)(2,1)}) custom-call(bf16[512,768]{1,0:T(8,128)(2,1)} %get-tuple-element.216.refs_0_, bf16[512,768]{1,0:T(8,128)(2,1)} %get-tuple-element.107.refs_1_, ...), custom_call_target="tpu_custom_call" | custom-call | flops 16106127360 | bytes 8650752 | tf_op jit(solution)/shard_map/attn_bwd/pallas_call | solution.py:159
  268.0 13.8 %add_convert_fusion.1 = bf16[1024,768]{1,0:T(8,128)(2,1)} fusion(f32[1024,768]{1,0:T(8,128)} %copy-done.6, bf16[3072,768]{1,0:T(8,128)(2,1)} %all-gather.13.cloned.1.call-done, f32[768]{0:T(1024)S(1)} %reshape.406, f32[1024,3072]{1,0:T(8,128)} %copy-done.56, f32[3072]{0:T(1024)S(1)} %reshape.405), kind=kOutput, calls=%fused_computation.44 | convolution fusion | flops 4865654784 | bytes 22035456 | tf_op jit(solution)/shard_map/dot_general | solution.py:16
  286.0 3.7 reduce.7
  289.7 3.3 dynamic-slice_bitcast_fusion
  302.1 21.4 %attn_bwd.6 = (bf16[512,384]{1,0:T(8,128)(2,1)}, bf16[2,512,384]{2,1,0:T(8,128)(2,1)}, bf16[2,512,384]{2,1,0:T(8,128)(2,1)}, bf16[2,512,384]{2,1,0:T(8,128)(2,1)}, bf16[2,512,384]{2,1,0:T(8,128)(2,1)}) custom-call(bf16[512,768]{1,0:T(8,128)(2,1)} %get-tuple-element.215.refs_0_, bf16[512,768]{1,0:T(8,128)(2,1)} %get-tuple-element.126.refs_1_, ...), custom_call_target="tpu_custom_call" | custom-call | flops 16106127360 | bytes 8650752 | tf_op jit(solution)/shard_map/attn_bwd/pallas_call | solution.py:159
  327.1 4.7 fusion.21
  332.3 21.4 %attn_bwd.5 = (bf16[512,384]{1,0:T(8,128)(2,1)}, bf16[2,512,384]{2,1,0:T(8,128)(2,1)}, bf16[2,512,384]{2,1,0:T(8,128)(2,1)}, bf16[2,512,384]{2,1,0:T(8,128)(2,1)}, bf16[2,512,384]{2,1,0:T(8,128)(2,1)}) custom-call(bf16[512,768]{1,0:T(8,128)(2,1)} %get-tuple-element.216.refs_0_, bf16[512,768]{1,0:T(8,128)(2,1)} %get-tuple-element.107.refs_1_, ...), custom_call_target="tpu_custom_call" | custom-call | flops 16106127360 | bytes 8650752 | tf_op jit(solution)/shard_map/attn_bwd/pallas_call | solution.py:159
  361.4 8.2 %collective-permute-done.22 = bf16[384,768]{1,0:T(8,128)(2,1)S(1)} collective-permute-done((bf16[384,768]{1,0:T(8,128)(2,1)S(1)}, bf16[384,768]{1,0:T(8,128)(2,1)S(1)}, u32[]{:S(2)}, u32[]{:S(2)}) %collective-permute-start.22) | collective-permute-done | bytes 589856 | tf_op jit(solution)/shard_map/ppermute | solution.py:269
  374.8 10.6 %collective-permute-done.23 = bf16[192,3072]{1,0:T(8,128)(2,1)S(1)} collective-permute-done((bf16[192,3072]{1,0:T(8,128)(2,1)}, bf16[192,3072]{1,0:T(8,128)(2,1)S(1)}, u32[]{:S(2)}, u32[]{:S(2)}) %collective-permute-start.23) | collective-permute-done | bytes 1179680 | tf_op jit(solution)/shard_map/ppermute | solution.py:185
  385.8 21.4 %attn_bwd.7 = (bf16[512,384]{1,0:T(8,128)(2,1)}, bf16[2,512,384]{2,1,0:T(8,128)(2,1)}, bf16[2,512,384]{2,1,0:T(8,128)(2,1)}, bf16[2,512,384]{2,1,0:T(8,128)(2,1)}, bf16[2,512,384]{2,1,0:T(8,128)(2,1)}) custom-call(bf16[512,768]{1,0:T(8,128)(2,1)} %get-tuple-element.215.refs_0_, bf16[512,768]{1,0:T(8,128)(2,1)} %get-tuple-element.126.refs_1_, ...), custom_call_target="tpu_custom_call" | custom-call | flops 16106127360 | bytes 8650752 | tf_op jit(solution)/shard_map/attn_bwd/pallas_call | solution.py:159
  408.8 5.7 collective-permute-done.43
  428.5 2.6 collective-permute-start.46
  437.9 3.3 collective-permute-done.56
  442.9 3.3 collective-permute-done.50
  449.3 7.6 %collective-permute-done.57 = bf16[96,768]{1,0:T(8,128)(2,1)S(1)} collective-permute-done((bf16[96,768]{1,0:T(8,128)(2,1)S(1)}, bf16[96,768]{1,0:T(8,128)(2,1)S(1)}, u32[]{:S(2)}, u32[]{:S(2)}) %collective-permute-start.57) | collective-permute-done | bytes 147488 | tf_op jit(solution)/shard_map/ppermute | solution.py:269
  459.4 2.7 collective-permute-start.52
  462.3 8.4 %collective-permute-done.58 = bf16[192,768]{1,0:T(8,128)(2,1)S(1)} collective-permute-done((bf16[192,768]{1,0:T(8,128)(2,1)S(1)}, bf16[192,768]{1,0:T(8,128)(2,1)S(1)}, u32[]{:S(2)}, u32[]{:S(2)}) %collective-permute-start.58) | collective-permute-done | bytes 294944 | tf_op jit(solution)/shard_map/ppermute | solution.py:269
  476.3 5.1 collective-permute-done.53
  483.4 5.7 collective-permute-done.59
  494.6 4.4 convolution_convert_fusion.2
  502.2 5.7 fusion.55
  507.9 3.0 reduce.5
  511.0 3.0 fusion.16
  517.8 3.9 add_convert_fusion
  521.7 16.9 %collective-permute-done.36 = bf16[192,2304]{1,0:T(8,128)(2,1)S(1)} collective-permute-done((bf16[192,2304]{1,0:T(8,128)(2,1)S(1)}, bf16[192,2304]{1,0:T(8,128)(2,1)S(1)}, u32[]{:S(2)}, u32[]{:S(2)}) %collective-permute-start.36) | collective-permute-done | bytes 884768 | tf_op jit(solution)/shard_map/ppermute | solution.py:185
  541.9 9.5 %collective-permute-done.37 = bf16[96,2304]{1,0:T(8,128)(2,1)S(1)} collective-permute-done((bf16[96,2304]{1,0:T(8,128)(2,1)S(1)}, bf16[96,2304]{1,0:T(8,128)(2,1)S(1)}, u32[]{:S(2)}, u32[]{:S(2)}) %collective-permute-start.37) | collective-permute-done | bytes 442400 | tf_op jit(solution)/shard_map/ppermute | solution.py:269
  552.7 4.8 collective-permute-done.38
  559.9 7.1 %collective-permute-done.39 = bf16[24,2304]{1,0:T(8,128)(2,1)S(1)} collective-permute-done((bf16[24,2304]{1,0:T(8,128)(2,1)S(1)}, bf16[24,2304]{1,0:T(8,128)(2,1)S(1)}, u32[]{:S(2)}, u32[]{:S(2)}) %collective-permute-start.39) | collective-permute-done | bytes 110624 | tf_op jit(solution)/shard_map/ppermute | solution.py:269
  567.1 3.0 collective-permute-start.33
  570.1 3.4 collective-permute-done.40
  574.4 5.2 collective-permute-done.41
  581.6 3.3 fusion.30
  585.0 3.0 collective-permute-done.42
  (367 shorter events, 129.9 us)
Async XLA Ops:
  7.2 35.9 %all-gather.7.cloned.1.call-start = ((), (), s32[]{:S(2)}) async-start(), calls=%async_computation | async-start | bytes 4423680 | tf_op jit(solution)/shard_map/all_gather | solution.py:255
  7.9 168.6 %all-gather.9.cloned.1.call-start = ((), (), s32[]{:S(2)}) async-start(), calls=%async_computation.1 | async-start | bytes 1474560 | tf_op jit(solution)/shard_map/all_gather | solution.py:255
  51.1 36.5 %collective-permute-start.1 = (bf16[512,1536]{1,0:T(8,128)(2,1)S(1)}, bf16[512,1536]{1,0:T(8,128)(2,1)S(1)}, u32[]{:S(2)}, u32[]{:S(2)}) collective-permute-start(bf16[512,1536]{1,0:T(8,128)(2,1)S(1)} %get-tuple-element.80.refs_2_.refs_6_.refs_5_.refs_9_), channel_id=1, source_target_pairs={{0,2},{1,3},{2,0},{3,1},{4,6},{5,7},{6,4},{7,5},{8,10},{9,11},{10,... | collective-permute-start | bytes 4718600 | tf_op jit(solution)/shard_map/ppermute | solution.py:185
  52.2 35.4 %collective-permute-start.2 = (bf16[512,1536]{1,0:T(8,128)(2,1)S(1)}, bf16[512,1536]{1,0:T(8,128)(2,1)S(1)}, u32[]{:S(2)}, u32[]{:S(2)}) collective-permute-start(bf16[512,1536]{1,0:T(8,128)(2,1)S(1)} %get-tuple-element.80.refs_2_.refs_6_.refs_5_.refs_9_), channel_id=1, source_target_pairs={{0,1},{1,0},{2,3},{3,2},{4,5},{5,4},{6,7},{7,6},{8,9},{9,8},{10,11... | collective-permute-start | bytes 4718600 | tf_op jit(solution)/shard_map/ppermute | solution.py:185
  91.2 90.8 %all-gather.11.cloned.1.call-start = ((), (), s32[]{:S(2)}) async-start(), calls=%async_computation.2 | async-start | bytes 5898240 | tf_op jit(solution)/shard_map/all_gather | solution.py:255
  91.9 110.2 %all-gather.13.cloned.1.call-start = ((), (), s32[]{:S(2)}) async-start(), calls=%async_computation.3 | async-start | bytes 5898240 | tf_op jit(solution)/shard_map/all_gather | solution.py:255
  92.2 51.8 %collective-permute-start = (bf16[512,1536]{1,0:T(8,128)(2,1)}, bf16[512,1536]{1,0:T(8,128)(2,1)}, u32[]{:S(2)}, u32[]{:S(2)}) collective-permute-start(bf16[512,1536]{1,0:T(8,128)(2,1)} %get-tuple-element.86.refs_2_.refs_6_.refs_5_.refs_9_), channel_id=1, source_target_pairs={{0,2},{1,3},{2,0},{3,1},{4,6},{5,7},{6,4},{7,5},{8,10},{9,11},{10,... | collective-permute-start | bytes 4718600 | tf_op jit(solution)/shard_map/ppermute | solution.py:185
  201.7 14.8 %collective-permute-start.7 = (bf16[768,768]{1,0:T(8,128)(2,1)}, bf16[768,768]{1,0:T(8,128)(2,1)}, u32[]{:S(2)}, u32[]{:S(2)}) collective-permute-start(bf16[768,768]{1,0:T(8,128)(2,1)} %get-tuple-element.207), channel_id=1, source_target_pairs={{0,1},{1,0},{2,3},{3,2},{4,5},{5,4},{6,7},{7,6},{8,9},{9,8},{10,11... | collective-permute-start | bytes 3538952 | tf_op jit(solution)/shard_map/ppermute | solution.py:185
  201.9 14.6 %collective-permute-start.6 = (bf16[768,768]{1,0:T(8,128)(2,1)}, bf16[768,768]{1,0:T(8,128)(2,1)}, u32[]{:S(2)}, u32[]{:S(2)}) collective-permute-start(bf16[768,768]{1,0:T(8,128)(2,1)} %get-tuple-element.208), channel_id=1, source_target_pairs={{0,1},{1,0},{2,3},{3,2},{4,5},{5,4},{6,7},{7,6},{8,9},{9,8},{10,11... | collective-permute-start | bytes 3538952 | tf_op jit(solution)/shard_map/ppermute | solution.py:185
  267.7 28.4 %collective-permute-start.8 = (bf16[2,512,384]{2,1,0:T(8,128)(2,1)}, bf16[2,512,384]{2,1,0:T(8,128)(2,1)}, u32[]{:S(2)}, u32[]{:S(2)}) collective-permute-start(bf16[2,512,384]{2,1,0:T(8,128)(2,1)} %get-tuple-element.98), channel_id=1, source_target_pairs={{0,1},{1,0},{2,3},{3,2},{4,5},{5,4},{6,7},{7,6},{8,9},{9,8},{10,11... | collective-permute-start | bytes 2359304 | tf_op jit(solution)/shard_map/ppermute | solution.py:185
  281.9 16.5 %collective-permute-start.9 = (bf16[2,512,384]{2,1,0:T(8,128)(2,1)}, bf16[2,512,384]{2,1,0:T(8,128)(2,1)}, u32[]{:S(2)}, u32[]{:S(2)}) collective-permute-start(bf16[2,512,384]{2,1,0:T(8,128)(2,1)} %get-tuple-element.100), channel_id=1, source_target_pairs={{0,1},{1,0},{2,3},{3,2},{4,5},{5,4},{6,7},{7,6},{8,9},{9,8},{10,11... | collective-permute-start | bytes 2359304 | tf_op jit(solution)/shard_map/ppermute | solution.py:185
  282.2 41.5 %collective-permute-start.11 = (bf16[768,768]{1,0:T(8,128)(2,1)}, bf16[768,768]{1,0:T(8,128)(2,1)S(1)}, u32[]{:S(2)}, u32[]{:S(2)}) collective-permute-start(bf16[768,768]{1,0:T(8,128)(2,1)} %get-tuple-element.104), channel_id=1, source_target_pairs={{0,2},{1,3},{2,0},{3,1},{4,6},{5,7},{6,4},{7,5},{8,10},{9,11},{10,... | collective-permute-start | bytes 3538952 | tf_op jit(solution)/shard_map/ppermute | solution.py:185
  283.5 9.5 %collective-permute-start.15 = (bf16[192,768]{1,0:T(8,128)(2,1)}, bf16[192,768]{1,0:T(8,128)(2,1)S(1)}, u32[]{:S(2)}, u32[]{:S(2)}) collective-permute-start(bf16[192,768]{1,0:T(8,128)(2,1)} %get-tuple-element.219), channel_id=1, source_target_pairs={{0,1},{1,0},{2,3},{3,2},{4,5},{5,4},{6,7},{7,6},{8,9},{9,8},{10,11... | collective-permute-start | bytes 884744 | tf_op jit(solution)/shard_map/ppermute | solution.py:185
  283.5 9.6 %collective-permute-start.14 = (bf16[192,768]{1,0:T(8,128)(2,1)}, bf16[192,768]{1,0:T(8,128)(2,1)S(1)}, u32[]{:S(2)}, u32[]{:S(2)}) collective-permute-start(bf16[192,768]{1,0:T(8,128)(2,1)} %get-tuple-element.220), channel_id=1, source_target_pairs={{0,1},{1,0},{2,3},{3,2},{4,5},{5,4},{6,7},{7,6},{8,9},{9,8},{10,11... | collective-permute-start | bytes 884744 | tf_op jit(solution)/shard_map/ppermute | solution.py:185
  293.1 34.0 %collective-permute-start.13 = (bf16[192,3072]{1,0:T(8,128)(2,1)}, bf16[192,3072]{1,0:T(8,128)(2,1)}, u32[]{:S(2)}, u32[]{:S(2)}) collective-permute-start(bf16[192,3072]{1,0:T(8,128)(2,1)} %get-tuple-element.203), channel_id=1, source_target_pairs={{0,1},{1,0},{2,3},{3,2},{4,5},{5,4},{6,7},{7,6},{8,9},{9,8},{10,11... | collective-permute-start | bytes 3538952 | tf_op jit(solution)/shard_map/ppermute | solution.py:185
  293.8 33.3 %collective-permute-start.12 = (bf16[192,3072]{1,0:T(8,128)(2,1)}, bf16[192,3072]{1,0:T(8,128)(2,1)}, u32[]{:S(2)}, u32[]{:S(2)}) collective-permute-start(bf16[192,3072]{1,0:T(8,128)(2,1)} %get-tuple-element.204), channel_id=1, source_target_pairs={{0,1},{1,0},{2,3},{3,2},{4,5},{5,4},{6,7},{7,6},{8,9},{9,8},{10,11... | collective-permute-start | bytes 3538952 | tf_op jit(solution)/shard_map/ppermute | solution.py:185
  300.6 55.7 %collective-permute-start.10 = (bf16[2,512,384]{2,1,0:T(8,128)(2,1)}, bf16[2,512,384]{2,1,0:T(8,128)(2,1)}, u32[]{:S(2)}, u32[]{:S(2)}) collective-permute-start(bf16[2,512,384]{2,1,0:T(8,128)(2,1)} %add_convert_fusion.16), channel_id=1, source_target_pairs={{0,2},{1,3},{2,0},{3,1},{4,6},{5,7},{6,4},{7,5},{8,10},{9,11},{10,... | collective-permute-start | bytes 2359304 | tf_op jit(solution)/shard_map/ppermute | solution.py:185
  323.6 35.4 %collective-permute-start.20 = (bf16[2,512,384]{2,1,0:T(8,128)(2,1)}, bf16[2,512,384]{2,1,0:T(8,128)(2,1)}, u32[]{:S(2)}, u32[]{:S(2)}) collective-permute-start(bf16[2,512,384]{2,1,0:T(8,128)(2,1)} %get-tuple-element.119), channel_id=1, source_target_pairs={{0,1},{1,0},{2,3},{3,2},{4,5},{5,4},{6,7},{7,6},{8,9},{9,8},{10,11... | collective-permute-start | bytes 2359304 | tf_op jit(solution)/shard_map/ppermute | solution.py:185
  324.7 95.6 %collective-permute-start.19 = (bf16[2,512,384]{2,1,0:T(8,128)(2,1)}, bf16[2,512,384]{2,1,0:T(8,128)(2,1)}, u32[]{:S(2)}, u32[]{:S(2)}) collective-permute-start(bf16[2,512,384]{2,1,0:T(8,128)(2,1)} %get-tuple-element.117), channel_id=1, source_target_pairs={{0,1},{1,0},{2,3},{3,2},{4,5},{5,4},{6,7},{7,6},{8,9},{9,8},{10,11... | collective-permute-start | bytes 2359304 | tf_op jit(solution)/shard_map/ppermute | solution.py:185
  331.8 22.0 %collective-permute-start.24 = (bf16[192,768]{1,0:T(8,128)(2,1)}, bf16[192,768]{1,0:T(8,128)(2,1)S(1)}, u32[]{:S(2)}, u32[]{:S(2)}) collective-permute-start(bf16[192,768]{1,0:T(8,128)(2,1)} %get-tuple-element.124), channel_id=1, source_target_pairs={{0,2},{1,3},{2,0},{3,1},{4,6},{5,7},{6,4},{7,5},{8,10},{9,11},{10,... | collective-permute-start | bytes 884744 | tf_op jit(solution)/shard_map/ppermute | solution.py:185
  353.7 18.4 %collective-permute-start.16 = (bf16[2,512,384]{2,1,0:T(8,128)(2,1)}, bf16[2,512,384]{2,1,0:T(8,128)(2,1)S(1)}, u32[]{:S(2)}, u32[]{:S(2)}) collective-permute-start(bf16[2,512,384]{2,1,0:T(8,128)(2,1)} %get-tuple-element.109), channel_id=1, source_target_pairs={{0,1},{1,0},{2,3},{3,2},{4,5},{5,4},{6,7},{7,6},{8,9},{9,8},{10,11... | collective-permute-start | bytes 2359304 | tf_op jit(solution)/shard_map/ppermute | solution.py:185
  353.8 15.8 %collective-permute-start.22 = (bf16[384,768]{1,0:T(8,128)(2,1)S(1)}, bf16[384,768]{1,0:T(8,128)(2,1)S(1)}, u32[]{:S(2)}, u32[]{:S(2)}) collective-permute-start(bf16[384,768]{1,0:T(8,128)(2,1)S(1)} %dynamic-slice_bitcast_fusion.7), channel_id=1, source_target_pairs={{0,4},{4,0},{8,12},{12,8},{16,20},{20,16},{24,28},{28,24},{1,5},{5... | collective-permute-start | bytes 1769480 | tf_op jit(solution)/shard_map/ppermute | solution.py:269
  356.3 29.1 %collective-permute-start.23 = (bf16[192,3072]{1,0:T(8,128)(2,1)}, bf16[192,3072]{1,0:T(8,128)(2,1)S(1)}, u32[]{:S(2)}, u32[]{:S(2)}) collective-permute-start(bf16[192,3072]{1,0:T(8,128)(2,1)} %get-tuple-element.122), channel_id=1, source_target_pairs={{0,2},{1,3},{2,0},{3,1},{4,6},{5,7},{6,4},{7,5},{8,10},{9,11},{10,... | collective-permute-start | bytes 3538952 | tf_op jit(solution)/shard_map/ppermute | solution.py:185
  359.0 14.2 %collective-permute-start.17 = (bf16[2,512,384]{2,1,0:T(8,128)(2,1)S(1)}, bf16[2,512,384]{2,1,0:T(8,128)(2,1)S(1)}, u32[]{:S(2)}, u32[]{:S(2)}) collective-permute-start(bf16[2,512,384]{2,1,0:T(8,128)(2,1)S(1)} %copy-done.55), channel_id=1, source_target_pairs={{0,1},{1,0},{2,3},{3,2},{4,5},{5,4},{6,7},{7,6},{8,9},{9,8},{10,11... | collective-permute-start | bytes 2359304 | tf_op jit(solution)/shard_map/ppermute | solution.py:185
  369.6 52.4 %collective-permute-start.21 = (bf16[2,512,384]{2,1,0:T(8,128)(2,1)}, bf16[2,512,384]{2,1,0:T(8,128)(2,1)}, u32[]{:S(2)}, u32[]{:S(2)}) collective-permute-start(bf16[2,512,384]{2,1,0:T(8,128)(2,1)} %add_convert_fusion.10), channel_id=1, source_target_pairs={{0,2},{1,3},{2,0},{3,1},{4,6},{5,7},{6,4},{7,5},{8,10},{9,11},{10,... | collective-permute-start | bytes 2359304 | tf_op jit(solution)/shard_map/ppermute | solution.py:185
  374.3 99.6 %collective-permute-start.18 = (bf16[2,512,384]{2,1,0:T(8,128)(2,1)}, bf16[2,512,384]{2,1,0:T(8,128)(2,1)}, u32[]{:S(2)}, u32[]{:S(2)}) collective-permute-start(bf16[2,512,384]{2,1,0:T(8,128)(2,1)} %add_convert_fusion.13), channel_id=1, source_target_pairs={{0,2},{1,3},{2,0},{3,1},{4,6},{5,7},{6,4},{7,5},{8,10},{9,11},{10,... | collective-permute-start | bytes 2359304 | tf_op jit(solution)/shard_map/ppermute | solution.py:185
  407.2 52.2 %collective-permute-start.26 = (bf16[2,512,384]{2,1,0:T(8,128)(2,1)}, bf16[2,512,384]{2,1,0:T(8,128)(2,1)S(1)}, u32[]{:S(2)}, u32[]{:S(2)}) collective-permute-start(bf16[2,512,384]{2,1,0:T(8,128)(2,1)} %get-tuple-element.130), channel_id=1, source_target_pairs={{0,1},{1,0},{2,3},{3,2},{4,5},{5,4},{6,7},{7,6},{8,9},{9,8},{10,11... | collective-permute-start | bytes 2359304 | tf_op jit(solution)/shard_map/ppermute | solution.py:185
  419.9 13.8 %collective-permute-start.49 = (bf16[96,3072]{1,0:T(8,128)(2,1)S(1)}, bf16[96,3072]{1,0:T(8,128)(2,1)S(1)}, u32[]{:S(2)}, u32[]{:S(2)}) collective-permute-start(bf16[96,3072]{1,0:T(8,128)(2,1)S(1)} %dynamic-slice_bitcast_fusion.6), channel_id=1, source_target_pairs={{0,4},{4,0},{8,12},{12,8},{16,20},{20,16},{24,28},{28,24},{1,5},{5... | collective-permute-start | bytes 1769480 | tf_op jit(solution)/shard_map/ppermute | solution.py:269
  420.4 8.1 %collective-permute-start.55 = (bf16[192,768]{1,0:T(8,128)(2,1)S(1)}, bf16[192,768]{1,0:T(8,128)(2,1)S(1)}, u32[]{:S(2)}, u32[]{:S(2)}) collective-permute-start(bf16[192,768]{1,0:T(8,128)(2,1)S(1)} %dynamic-slice_bitcast_fusion.9), channel_id=1, source_target_pairs={{0,8},{4,12},{8,0},{12,4},{16,24},{20,28},{24,16},{28,20},{1,9},{5... | collective-permute-start | bytes 884744 | tf_op jit(solution)/shard_map/ppermute | solution.py:269
  427.6 63.1 %collective-permute-start.25 = (bf16[2,512,384]{2,1,0:T(8,128)(2,1)S(1)}, bf16[2,512,384]{2,1,0:T(8,128)(2,1)S(1)}, u32[]{:S(2)}, u32[]{:S(2)}) collective-permute-start(bf16[2,512,384]{2,1,0:T(8,128)(2,1)S(1)} %copy-done.54), channel_id=1, source_target_pairs={{0,1},{1,0},{2,3},{3,2},{4,5},{5,4},{6,7},{7,6},{8,9},{9,8},{10,11... | collective-permute-start | bytes 2359304 | tf_op jit(solution)/shard_map/ppermute | solution.py:185
  436.3 9.8 %collective-permute-start.50 = (bf16[48,3072]{1,0:T(8,128)(2,1)S(1)}, bf16[48,3072]{1,0:T(8,128)(2,1)S(1)}, u32[]{:S(2)}, u32[]{:S(2)}) collective-permute-start(bf16[48,3072]{1,0:T(8,128)(2,1)S(1)} %dynamic-slice_bitcast_fusion.10), channel_id=1, source_target_pairs={{0,8},{4,12},{8,0},{12,4},{16,24},{20,28},{24,16},{28,20},{1,9},{5... | collective-permute-start | bytes 884744 | tf_op jit(solution)/shard_map/ppermute | solution.py:269
  446.1 10.8 %collective-permute-start.57 = (bf16[96,768]{1,0:T(8,128)(2,1)S(1)}, bf16[96,768]{1,0:T(8,128)(2,1)S(1)}, u32[]{:S(2)}, u32[]{:S(2)}) collective-permute-start(bf16[96,768]{1,0:T(8,128)(2,1)S(1)} %fusion.42), channel_id=1, source_target_pairs={{0,16},{4,20},{8,24},{12,28},{16,0},{20,4},{24,8},{28,12},{1,17},{... | collective-permute-start | bytes 442376 | tf_op jit(solution)/shard_map/ppermute | solution.py:269
  446.9 12.4 %collective-permute-start.51 = (bf16[24,3072]{1,0:T(8,128)(2,1)S(1)}, bf16[24,3072]{1,0:T(8,128)(2,1)S(1)}, u32[]{:S(2)}, u32[]{:S(2)}) collective-permute-start(bf16[24,3072]{1,0:T(8,128)(2,1)S(1)} %dynamic-slice_bitcast_fusion.15), channel_id=1, source_target_pairs={{0,16},{4,20},{8,24},{12,28},{16,0},{20,4},{24,8},{28,12},{1,17},{... | collective-permute-start | bytes 442376 | tf_op jit(solution)/shard_map/ppermute | solution.py:269
  456.9 18.5 %collective-permute-start.48 = (bf16[96,768]{1,0:T(8,128)(2,1)S(1)}, bf16[96,768]{1,0:T(8,128)(2,1)S(1)}, u32[]{:S(2)}, u32[]{:S(2)}) collective-permute-start(bf16[96,768]{1,0:T(8,128)(2,1)S(1)} %maximum_select_fusion.10), channel_id=1, source_target_pairs={{0,4},{4,0},{8,12},{12,8},{16,20},{20,16},{24,28},{28,24},{1,5},{5... | collective-permute-start | bytes 442376 | tf_op jit(solution)/shard_map/ppermute | solution.py:269
  459.3 11.4 %collective-permute-start.58 = (bf16[192,768]{1,0:T(8,128)(2,1)S(1)}, bf16[192,768]{1,0:T(8,128)(2,1)S(1)}, u32[]{:S(2)}, u32[]{:S(2)}) collective-permute-start(bf16[192,768]{1,0:T(8,128)(2,1)S(1)} %maximum_select_fusion.8), channel_id=1, source_target_pairs={{0,8},{4,12},{8,0},{12,4},{16,24},{20,28},{24,16},{28,20},{1,9},{5... | collective-permute-start | bytes 884744 | tf_op jit(solution)/shard_map/ppermute | solution.py:269
  459.4 13.5 %collective-permute-start.52 = (bf16[24,3072]{1,0:T(8,128)(2,1)S(1)}, bf16[24,3072]{1,0:T(8,128)(2,1)S(1)}, u32[]{:S(2)}, u32[]{:S(2)}) collective-permute-start(bf16[24,3072]{1,0:T(8,128)(2,1)S(1)} %fusion.43), channel_id=1, source_target_pairs={{0,16},{4,20},{8,24},{12,28},{16,0},{20,4},{24,8},{28,12},{1,17},{... | collective-permute-start | bytes 442376 | tf_op jit(solution)/shard_map/ppermute | solution.py:269
  470.7 20.0 %collective-permute-start.27 = (bf16[2,512,384]{2,1,0:T(8,128)(2,1)S(1)}, bf16[2,512,384]{2,1,0:T(8,128)(2,1)S(1)}, u32[]{:S(2)}, u32[]{:S(2)}) collective-permute-start(bf16[2,512,384]{2,1,0:T(8,128)(2,1)S(1)} %add_convert_fusion.7), channel_id=1, source_target_pairs={{0,2},{1,3},{2,0},{3,1},{4,6},{5,7},{6,4},{7,5},{8,10},{9,11},{10,... | collective-permute-start | bytes 2359304 | tf_op jit(solution)/shard_map/ppermute | solution.py:185
  472.8 16.3 %collective-permute-start.59 = (bf16[384,768]{1,0:T(8,128)(2,1)S(1)}, bf16[384,768]{1,0:T(8,128)(2,1)S(1)}, u32[]{:S(2)}, u32[]{:S(2)}) collective-permute-start(bf16[384,768]{1,0:T(8,128)(2,1)S(1)} %maximum_select_fusion.4), channel_id=1, source_target_pairs={{0,4},{4,0},{8,12},{12,8},{16,20},{20,16},{24,28},{28,24},{1,5},{5... | collective-permute-start | bytes 1769480 | tf_op jit(solution)/shard_map/ppermute | solution.py:269
  482.4 99.3 %collective-permute-start.54 = (bf16[96,3072]{1,0:T(8,128)(2,1)}, bf16[96,3072]{1,0:T(8,128)(2,1)}, u32[]{:S(2)}, u32[]{:S(2)}) collective-permute-start(bf16[96,3072]{1,0:T(8,128)(2,1)} %maximum_select_fusion.3), channel_id=1, source_target_pairs={{0,4},{4,0},{8,12},{12,8},{16,20},{20,16},{24,28},{28,24},{1,5},{5... | collective-permute-start | bytes 1769480 | tf_op jit(solution)/shard_map/ppermute | solution.py:269
  502.2 13.0 %collective-permute-start.35 = (bf16[192,2304]{1,0:T(8,128)(2,1)}, bf16[192,2304]{1,0:T(8,128)(2,1)}, u32[]{:S(2)}, u32[]{:S(2)}) collective-permute-start(bf16[192,2304]{1,0:T(8,128)(2,1)} %get-tuple-element.210), channel_id=1, source_target_pairs={{0,1},{1,0},{2,3},{3,2},{4,5},{5,4},{6,7},{7,6},{8,9},{9,8},{10,11... | collective-permute-start | bytes 2654216 | tf_op jit(solution)/shard_map/ppermute | solution.py:185
  517.0 21.5 %collective-permute-start.36 = (bf16[192,2304]{1,0:T(8,128)(2,1)S(1)}, bf16[192,2304]{1,0:T(8,128)(2,1)S(1)}, u32[]{:S(2)}, u32[]{:S(2)}) collective-permute-start(bf16[192,2304]{1,0:T(8,128)(2,1)S(1)} %fusion.26), channel_id=1, source_target_pairs={{0,2},{1,3},{2,0},{3,1},{4,6},{5,7},{6,4},{7,5},{8,10},{9,11},{10,... | collective-permute-start | bytes 2654216 | tf_op jit(solution)/shard_map/ppermute | solution.py:185
  517.2 24.0 %collective-permute-start.29 = (bf16[16,2304]{1,0:T(8,128)(2,1)S(1)}, bf16[16,2304]{1,0:T(8,128)(2,1)S(1)}, u32[]{:S(2)}, u32[]{:S(2)}) collective-permute-start(bf16[16,2304]{1,0:T(8,128)(2,1)S(1)} %get-tuple-element.222), channel_id=1, source_target_pairs={{0,1},{1,0},{2,3},{3,2},{4,5},{5,4},{6,7},{7,6},{8,9},{9,8},{10,11... | collective-permute-start | bytes 221192 | tf_op jit(solution)/shard_map/ppermute | solution.py:185
  517.3 34.3 %collective-permute-start.28 = (bf16[16,2304]{1,0:T(8,128)(2,1)S(1)}, bf16[16,2304]{1,0:T(8,128)(2,1)S(1)}, u32[]{:S(2)}, u32[]{:S(2)}) collective-permute-start(bf16[16,2304]{1,0:T(8,128)(2,1)S(1)} %get-tuple-element.221), channel_id=1, source_target_pairs={{0,1},{1,0},{2,3},{3,2},{4,5},{5,4},{6,7},{7,6},{8,9},{9,8},{10,11... | collective-permute-start | bytes 221192 | tf_op jit(solution)/shard_map/ppermute | solution.py:185
  540.1 11.2 %collective-permute-start.37 = (bf16[96,2304]{1,0:T(8,128)(2,1)S(1)}, bf16[96,2304]{1,0:T(8,128)(2,1)S(1)}, u32[]{:S(2)}, u32[]{:S(2)}) collective-permute-start(bf16[96,2304]{1,0:T(8,128)(2,1)S(1)} %dynamic-slice_bitcast_fusion.8), channel_id=1, source_target_pairs={{0,4},{4,0},{8,12},{12,8},{16,20},{20,16},{24,28},{28,24},{1,5},{5... | collective-permute-start | bytes 1327112 | tf_op jit(solution)/shard_map/ppermute | solution.py:269
  541.2 10.4 %collective-permute-start.30 = (bf16[16,2304]{1,0:T(8,128)(2,1)S(1)}, bf16[16,2304]{1,0:T(8,128)(2,1)S(1)}, u32[]{:S(2)}, u32[]{:S(2)}) collective-permute-start(bf16[16,2304]{1,0:T(8,128)(2,1)S(1)} %fusion.47), channel_id=1, source_target_pairs={{0,2},{1,3},{2,0},{3,1},{4,6},{5,7},{6,4},{7,5},{8,10},{9,11},{10,... | collective-permute-start | bytes 221192 | tf_op jit(solution)/shard_map/ppermute | solution.py:185
  557.6 9.4 %collective-permute-start.39 = (bf16[24,2304]{1,0:T(8,128)(2,1)S(1)}, bf16[24,2304]{1,0:T(8,128)(2,1)S(1)}, u32[]{:S(2)}, u32[]{:S(2)}) collective-permute-start(bf16[24,2304]{1,0:T(8,128)(2,1)S(1)} %dynamic-slice_bitcast_fusion.17), channel_id=1, source_target_pairs={{0,16},{4,20},{8,24},{12,28},{16,0},{20,4},{24,8},{28,12},{1,17},{... | collective-permute-start | bytes 331784 | tf_op jit(solution)/shard_map/ppermute | solution.py:269
  557.8 9.3 %collective-permute-start.32 = (bf16[16,2304]{1,0:T(8,128)(2,1)S(1)}, bf16[16,2304]{1,0:T(8,128)(2,1)S(1)}, u32[]{:S(2)}, u32[]{:S(2)}) collective-permute-start(bf16[16,2304]{1,0:T(8,128)(2,1)S(1)} %add_convert_fusion.21), channel_id=1, source_target_pairs={{0,8},{4,12},{8,0},{12,4},{16,24},{20,28},{24,16},{28,20},{1,9},{5... | collective-permute-start | bytes 221192 | tf_op jit(solution)/shard_map/ppermute | solution.py:269
  579.6 8.4 %collective-permute-start.42 = (bf16[96,2304]{1,0:T(8,128)(2,1)S(1)}, bf16[96,2304]{1,0:T(8,128)(2,1)S(1)}, u32[]{:S(2)}, u32[]{:S(2)}) collective-permute-start(bf16[96,2304]{1,0:T(8,128)(2,1)S(1)} %maximum_select_fusion.5), channel_id=1, source_target_pairs={{0,4},{4,0},{8,12},{12,8},{16,20},{20,16},{24,28},{28,24},{1,5},{5... | collective-permute-start | bytes 1327112 | tf_op jit(solution)/shard_map/ppermute | solution.py:269
  (75 other events, 628.1 us)
Sparse Core Ops, SparseCore 0:
  9.6 33.4 all-gather.6
  91.3 23.8 all-gather.8
  116.8 45.3 all-gather.10
  163.6 37.4 all-gather.12

commit v2 on v1

--- a/solution.py
+++ b/solution.py
@@ -74,22 +74,23 @@
         )
 
 
-def specs(n, d, first=0):
-    col = pl.BlockSpec((n, 2 * HD), lambda h: (0, h + first))
-    val = pl.BlockSpec((n, 2 * HD), lambda h: (0, h + first + d // (2 * HD)))
+def specs(n, first, count):
+    wide = pl.BlockSpec((n, 2 * HD), lambda h: (0, h + first))
+    key = pl.BlockSpec((n, 2 * HD), lambda h: (0, h))
+    val = pl.BlockSpec((n, 2 * HD), lambda h: (0, h + count))
     seg = pl.BlockSpec((n, 1), lambda h: (0, 0))
-    return col, val, seg
-
-
-def attn_fwd(q, blocks, seg, tq=256):
-    n, d = q.shape
-    parts = len(blocks)
-    col, val, one = specs(n, d)
+    return wide, key, val, seg
+
+
+def attn_fwd(q, blocks, seg, first, count, tq=256):
+    n = q.shape[0]
+    parts, d = len(blocks), count * 2 * HD
+    wide, key, val, one = specs(n, first, count)
     return pl.pallas_call(
         functools.partial(fwd_kernel, tq=min(tq, n), parts=parts),
-        grid=(d // (2 * HD),),
-        in_specs=[col, one] + [col] * parts + [val] * parts,
-        out_specs=[col, col],
+        grid=(count,),
+        in_specs=[wide, one] + [key] * parts + [val] * parts,
+        out_specs=[key, key],
         out_shape=[jax.ShapeDtypeStruct((n, d), bf), jax.ShapeDtypeStruct((n, d), f32)],
         cost_estimate=pl.CostEstimate(
             flops=16 * n * n * parts * d, bytes_accessed=n * d * (8 + 4 * parts), transcendentals=0
@@ -150,21 +151,19 @@
 
 
 def attn_bwd(q, blocks, do, o, lse, seg, first, count, tq=256):
-    n, d = q.shape
-    parts = len(blocks)
-    wide = count * 2 * HD
-    col, val, one = specs(n, d, first)
-    out = pl.BlockSpec((n, 2 * HD), lambda h: (0, h))
+    n = q.shape[0]
+    parts, d = len(blocks), count * 2 * HD
+    wide, key, val, one = specs(n, first, count)
     pair = pl.BlockSpec((2, n, 2 * HD), lambda h: (0, 0, h))
     return pl.pallas_call(
         functools.partial(bwd_kernel, tq=min(tq, n), parts=parts),
         grid=(count,),
-        in_specs=[col, col, col, col, one] + [col] * parts + [val] * parts,
-        out_specs=[out] + [pair] * parts,
-        out_shape=[jax.ShapeDtypeStruct((n, wide), bf)] + [jax.ShapeDtypeStruct((2, n, wide), bf)] * parts,
+        in_specs=[wide, wide, key, key, one] + [key] * parts + [val] * parts,
+        out_specs=[key] + [pair] * parts,
+        out_shape=[jax.ShapeDtypeStruct((n, d), bf)] + [jax.ShapeDtypeStruct((2, n, d), bf)] * parts,
         scratch_shapes=[pltpu.VMEM((n, 2 * HD), f32)],
         cost_estimate=pl.CostEstimate(
-            flops=40 * n * n * parts * wide, bytes_accessed=n * wide * (12 + 8 * parts), transcendentals=0
+            flops=40 * n * n * parts * d, bytes_accessed=n * d * (12 + 8 * parts), transcendentals=0
         ),
         name="attn_bwd",
     )(q, do, o, lse, seg[:, None], *blocks, *blocks)
@@ -183,10 +182,6 @@
 def swap(x, flip):
     parts = lax.axis_size("band")
     return lax.ppermute(x, "band", [(i, i ^ flip) for i in range(parts)])
-
-
-def gather_relative(x):
-    return spread([x], lax.axis_size("band") // 2)
 
 
 def spread(blocks, flip):
@@ -240,10 +235,10 @@
     packed = jnp.concatenate([g.reshape(parts, -1) for g in grads], axis=1).astype(bf)
     rows = -(-packed.shape[1] // (16 * columns)) * 16
     packed = jnp.pad(packed, ((0, 0), (0, rows * columns - packed.shape[1])))
-    mine = reduce_relative(relative_rows(matrix.astype(bf).reshape(parts, -1, columns)))
+    mine = reduce_chip(reduce_core(matrix.astype(bf)))
     extra = reduce_relative(relative_rows(packed.reshape(parts, rows, columns)))
+    vector = sum_small(extra).reshape(-1)
     total = finish(mine, 1)
-    vector = sum_small(extra).reshape(-1)
     out, at = [], 0
     for shard in shards:
         out.append(vector[at : at + shard.shape[0]])
@@ -304,6 +299,7 @@
 
 def layer(inputs, segments, cotangent, ln1_gain, ln1_bias, w_qkv, b_qv, w_out, b_out, ln2_gain, ln2_bias, w_up, b_up, w_down, b_down):
     micro, tokens, width = inputs.shape[0], inputs.shape[2], inputs.shape[3]
+    parts = lax.axis_size("band")
     vectors = (ln1_gain, ln1_bias, b_qv, b_out, ln2_gain, ln2_bias, b_up, b_down)
     gain_one, shift_one, bias_qv, bias_out, gain_two, shift_two, bias_up, bias_down = gather_vectors(vectors)
     w_proj = gather_matrix(w_qkv)
@@ -314,31 +310,41 @@
     normed_low = normed_in.astype(bf)
     projected = nn(normed_low, w_proj)
     query = (projected[:, :width] + bias_qv[:width]).astype(bf)
-    pairs = jnp.concatenate(
-        [projected[:, width : 2 * width], projected[:, 2 * width :] + bias_qv[width:]], axis=1
-    ).astype(bf)
-
-    gathered = [gather_relative(pairs[:tokens])]
-    far = lax.axis_size("band") // 2
+    keys = projected[:, width : 2 * width].astype(bf)
+    values = (projected[:, 2 * width :] + bias_qv[width:]).astype(bf)
+
+    count = width // (4 * HD)
+    half = width // 2
+    far = parts // 2
+    units = [(m, first) for m in range(micro) for first in (0, count)]
     started = []
-    for m in range(1, micro):
-        own = pairs[m * tokens : (m + 1) * tokens]
-        started.append([own, swap(own, far)])
-    gathered[0], (w_out, w_up, w_down) = tie(gathered[0], (w_out, w_up, w_down))
-    w_mix = gather_matrix(w_out)
-    w_rise = gather_matrix(w_up)
-    w_fall = gather_matrix(w_down)
+    for i, (m, first) in enumerate(units):
+        rows, cols = slice(m * tokens, (m + 1) * tokens), slice(first * 2 * HD, first * 2 * HD + half)
+        own = jnp.concatenate([keys[rows, cols], values[rows, cols]], axis=1)
+        if i > 0:
+            started[i - 1], own = tie(started[i - 1], own)
+        started.append(own)
+    for i, own in enumerate(started):
+        started[i] = [own, swap(own, far)]
 
     saved, mixes = [], []
-    for m in range(micro):
-        rows = slice(m * tokens, (m + 1) * tokens)
-        if m > 0:
-            blocks, mixes[m - 1] = tie(started[m - 1], mixes[m - 1])
-            gathered.append(spread(blocks, far // 2))
-        mix, log_total = attn_fwd(query[rows], gathered[m], seg[m])
+    for i, (m, first) in enumerate(units):
+        blocks = started[i]
+        if i > 0:
+            blocks, mixes[i - 1] = tie(blocks, mixes[i - 1])
+        blocks = spread(blocks, far // 2)
+        if i == 0:
+            blocks, (w_out, w_up, w_down) = tie(blocks, (w_out, w_up, w_down))
+            w_mix = gather_matrix(w_out)
+            w_rise = gather_matrix(w_up)
+            w_fall = gather_matrix(w_down)
+        q = query[m * tokens : (m + 1) * tokens]
+        mix, log_total = attn_fwd(q, blocks, seg[m], first, count)
         mixes.append(mix)
-        saved.append((query[rows], gathered[m], mix, log_total, seg[m]))
-    mixed = jnp.concatenate(mixes)
+        saved.append((q, blocks, mix, log_total, seg[m]))
+    mixed = jnp.concatenate(
+        [jnp.concatenate(mixes[i : i + 2], axis=1) for i in range(0, 2 * micro, 2)]
+    )
 
     hidden = value + (nn(mixed, w_mix) + bias_out)
     normed_mid, pull_two = jax.vjp(normed, hidden, gain_two, shift_two)
@@ -346,7 +352,6 @@
     upward = nn(mid_low, w_rise) + bias_up
     active, pull_gelu = jax.vjp(gelu_tanh, upward)
     active_low = active.astype(bf)
-    output = (hidden + (nn(active_low, w_fall) + bias_down)).astype(bf)
 
     real = (seg.reshape(-1, 1) != 0).astype(f32)
     grad_y = cotangent.reshape(micro * tokens, width).astype(f32) * real
@@ -359,7 +364,6 @@
     fall, grad_up = tie(fall, grad_up)
     fall = reduce_chip(fall)
     grad_w_rise = tn(mid_low, grad_up)
-    grad_b_rise = jnp.sum(grad_up.astype(f32), axis=0)
     grad_mid, grad_gain_two, grad_shift_two = pull_two(nt(grad_up, w_rise))
     grad_hidden = grad_y + grad_mid
     grad_a = grad_hidden.astype(bf)
@@ -370,11 +374,9 @@
     grad_mixed, *rest = lax.optimization_barrier((grad_mixed, grad_w_rise.astype(bf), grad_w_mix.astype(bf)))
     rise, out_grad = reduce_core(rest[0]), reduce_core(rest[1])
 
-    count = width // (4 * HD)
-    calls = [(m, first) for m in range(micro) for first in range(0, 2 * count, count)]
     halves, grads_q = [], []
-    for i, (m, first) in enumerate(calls):
-        q, blocks, mix, log_total, seg_q = saved[m]
+    for i, (m, first) in enumerate(units):
+        q, blocks, mix, log_total, seg_q = saved[i]
         grad_out = grad_mixed[m * tokens : (m + 1) * tokens]
         if i >= 2:
             halves[i - 2], grad_out = tie(halves[i - 2], grad_out)
@@ -388,11 +390,13 @@
         grad_q, *grad_blocks = attn_bwd(q, blocks, grad_out, mix, log_total, seg_q, first, count)
         halves.append(fold(grad_blocks, 1))
         grads_q.append(grad_q)
+    halves[-1], (active_low, grad_up) = tie(halves[-1], (active_low, grad_up))
+    output = (hidden + (nn(active_low, w_fall) + bias_down)).astype(bf)
+    grad_b_rise = jnp.sum(grad_up.astype(f32), axis=0)
     pairs = []
     for half in halves:
         pairs.append(reduce_relative(half, 2))
     pairs, grads_q = tie(pairs, grads_q)
-    wide = [finish(fall, 2), finish(rise, 2), finish(out_grad, 1)]
     grad_qkv = jnp.concatenate(
         [
             jnp.concatenate(
@@ -401,7 +405,8 @@
             for i in range(0, 2 * micro, 2)
         ]
     )
-    grad_qkv = lax.optimization_barrier(grad_qkv)
+    (fall, rise, out_grad), grad_qkv = tie((fall, rise, out_grad), grad_qkv)
+    wide = [finish(fall, 2), finish(rise, 2), finish(out_grad, 1)]
     grad_w_proj = tn(normed_low, grad_qkv)
     sums = jnp.sum(grad_qkv.astype(f32), axis=0)
     grad_b_proj = jnp.concatenate([sums[:width], sums[2 * width :]])

time: 602 us -> 627 us (1.042)
  other arithmetic: 68.4 us -> 83 us
    ppermute x33 -> x39, waiting for transfers between devices: 90.2 us -> 101 us  [swap(): return lax.ppermute(x, 'band', [(i, i ^ flip) for i in range(parts)])]
    ppermute x27, waiting for transfers between devices: 88.6 us -> 78.6 us  [trade(): return lax.ppermute(x, 'dp', [(i, i ^ flip) for i in range(size)])]
    convert_element_type x20 -> x21, other arithmetic: 33.4 us -> 39.1 us  [fold(): (near.astype(f32) + swap(far, flip).astype(f32)).astype(bf)]
    unnamed x135 -> x164, local copies, waits for them, and re-layouts: 15.9 us -> 10.6 us
    pallas_call x2 -> x4, Pallas kernels: 48.2 us -> 53.4 us  [attn_fwd(): pl.pallas_call(functools.partial(fwd_kernel, tq=min(tq, n), parts=parts),...]
    ppermute x33 -> x39, starting transfers between devices: 14.2 us -> 16 us  [swap(): return lax.ppermute(x, 'band', [(i, i ^ flip) for i in range(parts)])]
  transfers between devices with their start and end apart: 64 -> 70, of which waited for: 27 -> 31; matrix products, arithmetic and copies ran while one was open for 24% -> 22% of each run, Pallas kernels for 19% -> 19%
where the time goes in v2:
time: 627 us; the launch traced here: 621 us
  waiting for transfers between devices  200 us (32%)
  Pallas kernels  140 us (22%)
  matrix products  83.1 us (13%)
  other arithmetic  83 us (13%)
  starting transfers between devices  49.1 us (8%)
  local copies, waits for them, and re-layouts  43.5 us (7%)
  between operations  15.7 us (3%)
    ppermute x39, waiting for transfers between devices, swap(): return lax.ppermute(x, 'band', [(i, i ^ flip) for i in range(parts)])  101 us
    pallas_call x4, Pallas kernels, attn_bwd(): pl.pallas_call(functools.partial(bwd_kernel, tq=min(tq, n), parts=parts),...  86.5 us
    ppermute x27, waiting for transfers between devices, trade(): return lax.ppermute(x, 'dp', [(i, i ^ flip) for i in range(size)])  78.6 us
    pallas_call x4, Pallas kernels, attn_fwd(): pl.pallas_call(functools.partial(fwd_kernel, tq=min(tq, n), parts=parts),...  53.4 us
    convert_element_type x21, other arithmetic, fold(): (near.astype(f32) + swap(far, flip).astype(f32)).astype(bf)  39.1 us
    ppermute x27, starting transfers between devices, trade(): return lax.ppermute(x, 'dp', [(i, i ^ flip) for i in range(size)])  33 us
    dot_general x4, matrix products, nn(): lax.dot_general(a, b, (((1,), (0,)), ((), ())), preferred_element_type=f32)  32.9 us
    dot_general x4, matrix products, nt(): lax.dot_general(a, b, (((1,), (1,)), ((), ())), preferred_element_type=f32)  25.7 us
  transfers between devices with their start and end apart: 70, of which 31 were waited for; matrix products, arithmetic and copies ran while one was open for 22% of the time, Pallas kernels for 19%

profile of v2, /device:TPU:0, one launch (start us, length us, event | category | flops | bytes accessed | tf_op | source)
XLA Modules:
  0.0 620.9 jit_solution(15852463894725346179)
XLA Ops:
  8.0 5.5 concatenate.114
  13.4 6.2 %all-gather.1 = bf16[4,1,2304]{2,1,0:T(2,128)(2,1)S(1)} all-gather(bf16[1,1,2304]{2,1,0:T(2,128)(2,1)S(1)} %reshape.435), channel_id=2, replica_groups=mesh['dp'=8,'band'=4] {'band'}, dimensions={0}, use_global_device_ids=true | all-gather | bytes 23040 | tf_op jit(solution)/shard_map/all_gather | solution.py:215
  23.8 19.3 %all-gather.7.cloned.1.call-done = bf16[768,2304]{1,0:T(8,128)(2,1)} async-done(((bf16[192,2304]{1,0:T(8,128)(2,1)}), bf16[768,2304]{1,0:T(8,128)(2,1)}) %all-gather.7.cloned.1.call-update) | async-done | bytes 3538960 | tf_op jit(solution)/shard_map/all_gather | solution.py:250
  43.1 5.8 fusion.67
  53.6 18.6 %collective-permute-done.1.refs_3_.refs_7_.refs_6_.refs_10_ = bf16[512,768]{1,0:T(8,128)(2,1)S(1)} collective-permute-done((bf16[512,768]{1,0:T(8,128)(2,1)S(1)}, bf16[512,768]{1,0:T(8,128)(2,1)S(1)}, u32[]{:S(2)}, u32[]{:S(2)}) %collective-permute-start.1) | collective-permute-done | bytes 786464 | tf_op jit(solution)/shard_map/ppermute | solution.py:184
  82.3 13.4 %attn_fwd.4 = (bf16[512,384]{1,0:T(8,128)(2,1)}, f32[512,384]{1,0:T(8,128)}) custom-call(bf16[512,768]{1,0:T(8,128)(2,1)} %get-tuple-element.265.refs_0_, s32[512,1]{1,0:T(8,128)} %copy.41.refs_1_.refs_4_, bf16[512,768]{1,0:T(8,128)(2,1)} %copy-done.33, bf16[512,768]{1,0:T(8,128)(2,1)} %copy-done.61, bf16[512,768]{1,0:T(8,128)(2,1)} %copy-done.62, ...), custom_call_target="tpu_custom_call" | custom-call | flops 6442450944 | bytes 4718592 | tf_op jit(solution)/shard_map/attn_fwd/pallas_call | solution.py:89
  95.8 11.1 %collective-permute-done.refs_3_.refs_7_.refs_6_.refs_10_ = bf16[512,768]{1,0:T(8,128)(2,1)} collective-permute-done((bf16[512,768]{1,0:T(8,128)(2,1)}, bf16[512,768]{1,0:T(8,128)(2,1)}, u32[]{:S(2)}, u32[]{:S(2)}) %collective-permute-start) | collective-permute-done | bytes 786464 | tf_op jit(solution)/shard_map/ppermute | solution.py:184
  112.1 13.1 %attn_fwd.5 = (bf16[512,384]{1,0:T(8,128)(2,1)}, f32[512,384]{1,0:T(8,128)}) custom-call(bf16[512,768]{1,0:T(8,128)(2,1)} %get-tuple-element.265.refs_0_, s32[512,1]{1,0:T(8,128)} %copy.41.refs_1_.refs_4_, bf16[512,768]{1,0:T(8,128)(2,1)} %get-tuple-element.115.refs_2_.refs_6_.refs_5_.refs_9_, ...), custom_call_target="tpu_custom_call" | custom-call | flops 6442450944 | bytes 4718592 | tf_op jit(solution)/shard_map/attn_fwd/pallas_call | solution.py:89
  125.2 18.7 %collective-permute-done.4.refs_3_.refs_7_.refs_6_.refs_10_ = bf16[512,768]{1,0:T(8,128)(2,1)} collective-permute-done((bf16[512,768]{1,0:T(8,128)(2,1)S(1)}, bf16[512,768]{1,0:T(8,128)(2,1)}, u32[]{:S(2)}, u32[]{:S(2)}) %collective-permute-start.4) | collective-permute-done | bytes 786464 | tf_op jit(solution)/shard_map/ppermute | solution.py:184
  147.6 13.3 %attn_fwd.6 = (bf16[512,384]{1,0:T(8,128)(2,1)}, f32[512,384]{1,0:T(8,128)}) custom-call(bf16[512,768]{1,0:T(8,128)(2,1)} %get-tuple-element.266.refs_0_, s32[512,1]{1,0:T(8,128)} %copy.43.refs_1_.refs_4_, bf16[512,768]{1,0:T(8,128)(2,1)} %get-tuple-element.120.refs_2_.refs_6_.refs_5_.refs_9_, ...), custom_call_target="tpu_custom_call" | custom-call | flops 6442450944 | bytes 4718592 | tf_op jit(solution)/shard_map/attn_fwd/pallas_call | solution.py:89
  160.9 8.3 %collective-permute-done.7.refs_3_.refs_7_.refs_6_.refs_10_ = bf16[512,768]{1,0:T(8,128)(2,1)} collective-permute-done((bf16[512,768]{1,0:T(8,128)(2,1)}, bf16[512,768]{1,0:T(8,128)(2,1)}, u32[]{:S(2)}, u32[]{:S(2)}) %collective-permute-start.7) | collective-permute-done | bytes 786464 | tf_op jit(solution)/shard_map/ppermute | solution.py:184
  173.1 13.6 %attn_fwd.7 = (bf16[512,384]{1,0:T(8,128)(2,1)}, f32[512,384]{1,0:T(8,128)}) custom-call(bf16[512,768]{1,0:T(8,128)(2,1)} %get-tuple-element.266.refs_0_, s32[512,1]{1,0:T(8,128)} %copy.43.refs_1_.refs_4_, bf16[512,768]{1,0:T(8,128)(2,1)} %get-tuple-element.124.refs_2_.refs_6_.refs_5_.refs_9_, ...), custom_call_target="tpu_custom_call" | custom-call | flops 6442450944 | bytes 4718592 | tf_op jit(solution)/shard_map/attn_fwd/pallas_call | solution.py:89
  186.7 3.0 fusion.68
  191.9 13.9 %multiply_convert_fusion = (bf16[1024,3072]{1,0:T(8,128)(2,1)S(1)}, f32[1024,3072]{1,0:T(8,128)}) fusion(f32[3072]{0:T(1024)S(1)} %reshape.405, bf16[768,3072]{1,0:T(8,128)(2,1)} %all-gather.11.cloned.1.call-done, f32[1024,768]{1,0:T(8,128)} %copy-done.6, f32[768]{0:T(1024)S(1)} %reshape.404, f32[768]{0:T(1024)S(1)} %reshape.403, f32[1024]{0:T(1024)S(1)} %fusion.50, ...), kind=kOutput, calls=%fused_computation.9 | convolution fusion | flops 4867227648 | bytes 26765312 | tf_op jit(solution)/shard_map/dot_general | solution.py:16
  205.9 5.5 convolution_convert_fusion.1
  214.4 14.5 %fusion.6 = bf16[1024,3072]{1,0:T(8,128)(2,1)S(1)} fusion(f32[1024,3072]{1,0:T(8,128)} %get-tuple-element.302, f32[3072]{0:T(1024)S(1)} %reshape.405, bf16[1024,768]{1,0:T(8,128)(2,1)S(1)} %copy-done.25, bf16[3072,768]{1,0:T(8,128)(2,1)} %all-gather.13.cloned.1.call-done), kind=kOutput, calls=%fused_computation.8 | convolution fusion | flops 4897898496 | bytes 25178112 | tf_op jit(solution)/shard_map/dot_general | solution.py:13
  229.0 5.7 fusion.23
  234.7 7.9 %convolution_convert_fusion = bf16[768,3072]{1,0:T(8,128)(2,1)} fusion(bf16[1024,3072]{1,0:T(8,128)(2,1)S(1)} %fusion.6, f32[1024,768]{1,0:T(8,128)S(1)} %copy-done.7, f32[768]{0:T(1024)S(1)} %reshape.404, f32[768]{0:T(1024)S(1)} %reshape.403, f32[1024]{0:T(1024)S(1)} %fusion.50, f32[1024]{0:T(1024)S(1)} %broadcast_multiply_fusion), kind=kOutput, calls=%fused_computation.10 | convolution fusion | flops 4838129664 | bytes 14170112 | tf_op jit(solution)/shard_map/dot_general | solution.py:19
  242.6 5.6 multiply_reduce_fusion
  256.4 21.5 %attn_bwd.6 = (bf16[512,384]{1,0:T(8,128)(2,1)}, bf16[2,512,384]{2,1,0:T(8,128)(2,1)}, bf16[2,512,384]{2,1,0:T(8,128)(2,1)}, bf16[2,512,384]{2,1,0:T(8,128)(2,1)}, bf16[2,512,384]{2,1,0:T(8,128)(2,1)}) custom-call(bf16[512,768]{1,0:T(8,128)(2,1)} %get-tuple-element.265.refs_0_, bf16[512,768]{1,0:T(8,128)(2,1)} %get-tuple-element.143.refs_1_, ...), custom_call_target="tpu_custom_call" | custom-call | flops 16106127360 | bytes 8650752 | tf_op jit(solution)/shard_map/attn_bwd/pallas_call | solution.py:158
  284.5 3.3 dynamic-slice_bitcast_fusion
  295.2 21.9 %attn_bwd.7 = (bf16[512,384]{1,0:T(8,128)(2,1)}, bf16[2,512,384]{2,1,0:T(8,128)(2,1)}, bf16[2,512,384]{2,1,0:T(8,128)(2,1)}, bf16[2,512,384]{2,1,0:T(8,128)(2,1)}, bf16[2,512,384]{2,1,0:T(8,128)(2,1)}) custom-call(bf16[512,768]{1,0:T(8,128)(2,1)} %get-tuple-element.266.refs_0_, bf16[512,768]{1,0:T(8,128)(2,1)} %get-tuple-element.169.refs_1_, ...), custom_call_target="tpu_custom_call" | custom-call | flops 16106127360 | bytes 8650752 | tf_op jit(solution)/shard_map/attn_bwd/pallas_call | solution.py:158
  319.7 5.1 fusion.21
  328.8 21.5 %attn_bwd.4 = (bf16[512,384]{1,0:T(8,128)(2,1)}, bf16[2,512,384]{2,1,0:T(8,128)(2,1)}, bf16[2,512,384]{2,1,0:T(8,128)(2,1)}, bf16[2,512,384]{2,1,0:T(8,128)(2,1)}, bf16[2,512,384]{2,1,0:T(8,128)(2,1)}) custom-call(bf16[512,768]{1,0:T(8,128)(2,1)} %get-tuple-element.265.refs_0_, bf16[512,768]{1,0:T(8,128)(2,1)} %get-tuple-element.143.refs_1_, ...), custom_call_target="tpu_custom_call" | custom-call | flops 16106127360 | bytes 8650752 | tf_op jit(solution)/shard_map/attn_bwd/pallas_call | solution.py:158
  364.4 15.6 %collective-permute-done.20 = bf16[192,3072]{1,0:T(8,128)(2,1)S(1)} collective-permute-done((bf16[192,3072]{1,0:T(8,128)(2,1)}, bf16[192,3072]{1,0:T(8,128)(2,1)S(1)}, u32[]{:S(2)}, u32[]{:S(2)}) %collective-permute-start.20) | collective-permute-done | bytes 1179680 | tf_op jit(solution)/shard_map/ppermute | solution.py:184
  382.8 21.5 %attn_bwd.5 = (bf16[512,384]{1,0:T(8,128)(2,1)}, bf16[2,512,384]{2,1,0:T(8,128)(2,1)}, bf16[2,512,384]{2,1,0:T(8,128)(2,1)}, bf16[2,512,384]{2,1,0:T(8,128)(2,1)}, bf16[2,512,384]{2,1,0:T(8,128)(2,1)}) custom-call(bf16[512,768]{1,0:T(8,128)(2,1)} %get-tuple-element.266.refs_0_, bf16[512,768]{1,0:T(8,128)(2,1)} %get-tuple-element.169.refs_1_, ...), custom_call_target="tpu_custom_call" | custom-call | flops 16106127360 | bytes 8650752 | tf_op jit(solution)/shard_map/attn_bwd/pallas_call | solution.py:158
  404.9 2.9 add_convert_fusion.7
  407.8 4.6 collective-permute-done.30
  419.8 3.7 reduce.7
  423.5 10.2 %add_convert_fusion.1 = bf16[1024,768]{1,0:T(8,128)(2,1)} fusion(f32[1024,768]{1,0:T(8,128)} %copy-done.6, bf16[1024,3072]{1,0:T(8,128)(2,1)} %copy-done.64, bf16[3072,768]{1,0:T(8,128)(2,1)} %all-gather.13.cloned.1.call-done, f32[768]{0:T(1024)S(1)} %reshape.415), kind=kOutput, calls=%fused_computation.39 | convolution fusion | flops 4834197504 | bytes 15731712 | tf_op jit(solution)/shard_map/dot_general | solution.py:16
  433.7 3.7 collective-permute-done.34
  443.2 3.0 reduce.5
  446.3 8.7 %convolution_convert_fusion.2 = bf16[768,2304]{1,0:T(8,128)(2,1)} fusion(bf16[1024,768]{1,0:T(8,128)(2,1)} %copy-done.24, bf16[1024,2304]{1,0:T(8,128)(2,1)} %pad_maximum_fusion), kind=kOutput, calls=%fused_computation.12 | convolution fusion | flops 3625648128 | bytes 9830400 | tf_op jit(solution)/shard_map/dot_general | solution.py:19
  455.0 4.1 fusion.56
  470.0 3.6 collective-permute-done.50
  479.5 5.5 collective-permute-done.51
  495.9 2.9 collective-permute-start.53
  506.8 8.8 %collective-permute-done.40 = bf16[16,2304]{1,0:T(8,128)(2,1)S(1)} collective-permute-done((bf16[16,2304]{1,0:T(8,128)(2,1)S(1)}, bf16[16,2304]{1,0:T(8,128)(2,1)S(1)}, u32[]{:S(2)}, u32[]{:S(2)}) %collective-permute-start.40) | collective-permute-done | bytes 73760 | tf_op jit(solution)/shard_map/ppermute | solution.py:264
  525.3 11.6 %collective-permute-done.43 = bf16[192,2304]{1,0:T(8,128)(2,1)} collective-permute-done((bf16[192,2304]{1,0:T(8,128)(2,1)}, bf16[192,2304]{1,0:T(8,128)(2,1)}, u32[]{:S(2)}, u32[]{:S(2)}) %collective-permute-start.43) | collective-permute-done | bytes 884768 | tf_op jit(solution)/shard_map/ppermute | solution.py:184
  542.6 3.0 collective-permute-start.63
  545.5 4.0 collective-permute-done.44
  552.0 6.1 collective-permute-done.45
  559.6 5.6 collective-permute-done.46
  566.3 8.8 %collective-permute-done.64 = bf16[192,768]{1,0:T(8,128)(2,1)S(1)} collective-permute-done((bf16[192,768]{1,0:T(8,128)(2,1)S(1)}, bf16[192,768]{1,0:T(8,128)(2,1)S(1)}, u32[]{:S(2)}, u32[]{:S(2)}) %collective-permute-start.64) | collective-permute-done | bytes 294944 | tf_op jit(solution)/shard_map/ppermute | solution.py:264
  578.6 4.0 collective-permute-done.48
  584.5 7.1 %collective-permute-done.65 = bf16[384,768]{1,0:T(8,128)(2,1)S(1)} collective-permute-done((bf16[384,768]{1,0:T(8,128)(2,1)S(1)}, bf16[384,768]{1,0:T(8,128)(2,1)S(1)}, u32[]{:S(2)}, u32[]{:S(2)}) %collective-permute-start.65) | collective-permute-done | bytes 589856 | tf_op jit(solution)/shard_map/ppermute | solution.py:264
  593.2 11.0 %collective-permute-done.60 = bf16[96,3072]{1,0:T(8,128)(2,1)S(1)} collective-permute-done((bf16[96,3072]{1,0:T(8,128)(2,1)S(1)}, bf16[96,3072]{1,0:T(8,128)(2,1)S(1)}, u32[]{:S(2)}, u32[]{:S(2)}) %collective-permute-start.60) | collective-permute-done | bytes 589856 | tf_op jit(solution)/shard_map/ppermute | solution.py:264
  605.9 6.6 %collective-permute-done.49 = bf16[96,2304]{1,0:T(8,128)(2,1)S(1)} collective-permute-done((bf16[96,2304]{1,0:T(8,128)(2,1)S(1)}, bf16[96,2304]{1,0:T(8,128)(2,1)S(1)}, u32[]{:S(2)}, u32[]{:S(2)}) %collective-permute-start.49) | collective-permute-done | bytes 442400 | tf_op jit(solution)/shard_map/ppermute | solution.py:264
  (413 shorter events, 162.0 us)
Async XLA Ops:
  7.2 35.9 %all-gather.7.cloned.1.call-start = ((), (), s32[]{:S(2)}) async-start(), calls=%async_computation | async-start | bytes 4423680 | tf_op jit(solution)/shard_map/all_gather | solution.py:250
  7.9 178.8 %all-gather.9.cloned.1.call-start = ((), (), s32[]{:S(2)}) async-start(), calls=%async_computation.1 | async-start | bytes 1474560 | tf_op jit(solution)/shard_map/all_gather | solution.py:250
  52.5 19.7 %collective-permute-start.1 = (bf16[512,768]{1,0:T(8,128)(2,1)S(1)}, bf16[512,768]{1,0:T(8,128)(2,1)S(1)}, u32[]{:S(2)}, u32[]{:S(2)}) collective-permute-start(bf16[512,768]{1,0:T(8,128)(2,1)S(1)} %get-tuple-element.107.refs_2_.refs_6_.refs_5_.refs_9_), channel_id=1, source_target_pairs={{0,2},{1,3},{2,0},{3,1},{4,6},{5,7},{6,4},{7,5},{8,10},{9,11},{10,... | collective-permute-start | bytes 2359304 | tf_op jit(solution)/shard_map/ppermute | solution.py:184
  53.4 18.8 %collective-permute-start.2 = (bf16[512,768]{1,0:T(8,128)(2,1)S(1)}, bf16[512,768]{1,0:T(8,128)(2,1)S(1)}, u32[]{:S(2)}, u32[]{:S(2)}) collective-permute-start(bf16[512,768]{1,0:T(8,128)(2,1)S(1)} %get-tuple-element.107.refs_2_.refs_6_.refs_5_.refs_9_), channel_id=1, source_target_pairs={{0,1},{1,0},{2,3},{3,2},{4,5},{5,4},{6,7},{7,6},{8,9},{9,8},{10,11... | collective-permute-start | bytes 2359304 | tf_op jit(solution)/shard_map/ppermute | solution.py:184
  74.6 117.3 %all-gather.11.cloned.1.call-start = ((), (), s32[]{:S(2)}) async-start(), calls=%async_computation.2 | async-start | bytes 5898240 | tf_op jit(solution)/shard_map/all_gather | solution.py:250
  75.4 139.0 %all-gather.13.cloned.1.call-start = ((), (), s32[]{:S(2)}) async-start(), calls=%async_computation.3 | async-start | bytes 5898240 | tf_op jit(solution)/shard_map/all_gather | solution.py:250
  80.7 26.2 %collective-permute-start = (bf16[512,768]{1,0:T(8,128)(2,1)}, bf16[512,768]{1,0:T(8,128)(2,1)}, u32[]{:S(2)}, u32[]{:S(2)}) collective-permute-start(bf16[512,768]{1,0:T(8,128)(2,1)} %get-tuple-element.115.refs_2_.refs_6_.refs_5_.refs_9_), channel_id=1, source_target_pairs={{0,2},{1,3},{2,0},{3,1},{4,6},{5,7},{6,4},{7,5},{8,10},{9,11},{10,... | collective-permute-start | bytes 2359304 | tf_op jit(solution)/shard_map/ppermute | solution.py:184
  107.4 36.4 %collective-permute-start.4 = (bf16[512,768]{1,0:T(8,128)(2,1)S(1)}, bf16[512,768]{1,0:T(8,128)(2,1)}, u32[]{:S(2)}, u32[]{:S(2)}) collective-permute-start(bf16[512,768]{1,0:T(8,128)(2,1)S(1)} %copy-done.32), channel_id=1, source_target_pairs={{0,2},{1,3},{2,0},{3,1},{4,6},{5,7},{6,4},{7,5},{8,10},{9,11},{10,... | collective-permute-start | bytes 2359304 | tf_op jit(solution)/shard_map/ppermute | solution.py:184
  144.4 24.8 %collective-permute-start.7 = (bf16[512,768]{1,0:T(8,128)(2,1)}, bf16[512,768]{1,0:T(8,128)(2,1)}, u32[]{:S(2)}, u32[]{:S(2)}) collective-permute-start(bf16[512,768]{1,0:T(8,128)(2,1)} %get-tuple-element.124.refs_2_.refs_6_.refs_5_.refs_9_), channel_id=1, source_target_pairs={{0,2},{1,3},{2,0},{3,1},{4,6},{5,7},{6,4},{7,5},{8,10},{9,11},{10,... | collective-permute-start | bytes 2359304 | tf_op jit(solution)/shard_map/ppermute | solution.py:184
  213.9 15.1 %collective-permute-start.13 = (bf16[768,768]{1,0:T(8,128)(2,1)}, bf16[768,768]{1,0:T(8,128)(2,1)}, u32[]{:S(2)}, u32[]{:S(2)}) collective-permute-start(bf16[768,768]{1,0:T(8,128)(2,1)} %get-tuple-element.255), channel_id=1, source_target_pairs={{0,1},{1,0},{2,3},{3,2},{4,5},{5,4},{6,7},{7,6},{8,9},{9,8},{10,11... | collective-permute-start | bytes 3538952 | tf_op jit(solution)/shard_map/ppermute | solution.py:184
  214.0 14.9 %collective-permute-start.12 = (bf16[768,768]{1,0:T(8,128)(2,1)S(1)}, bf16[768,768]{1,0:T(8,128)(2,1)}, u32[]{:S(2)}, u32[]{:S(2)}) collective-permute-start(bf16[768,768]{1,0:T(8,128)(2,1)S(1)} %get-tuple-element.256), channel_id=1, source_target_pairs={{0,1},{1,0},{2,3},{3,2},{4,5},{5,4},{6,7},{7,6},{8,9},{9,8},{10,11... | collective-permute-start | bytes 3538952 | tf_op jit(solution)/shard_map/ppermute | solution.py:184
  278.0 12.3 %collective-permute-start.27 = (bf16[2,512,384]{2,1,0:T(8,128)(2,1)}, bf16[2,512,384]{2,1,0:T(8,128)(2,1)}, u32[]{:S(2)}, u32[]{:S(2)}) collective-permute-start(bf16[2,512,384]{2,1,0:T(8,128)(2,1)} %get-tuple-element.162), channel_id=1, source_target_pairs={{0,1},{1,0},{2,3},{3,2},{4,5},{5,4},{6,7},{7,6},{8,9},{9,8},{10,11... | collective-permute-start | bytes 2359304 | tf_op jit(solution)/shard_map/ppermute | solution.py:184
  280.2 37.2 %collective-permute-start.14 = (bf16[768,768]{1,0:T(8,128)(2,1)}, bf16[768,768]{1,0:T(8,128)(2,1)}, u32[]{:S(2)}, u32[]{:S(2)}) collective-permute-start(bf16[768,768]{1,0:T(8,128)(2,1)} %get-tuple-element.133), channel_id=1, source_target_pairs={{0,2},{1,3},{2,0},{3,1},{4,6},{5,7},{6,4},{7,5},{8,10},{9,11},{10,... | collective-permute-start | bytes 3538952 | tf_op jit(solution)/shard_map/ppermute | solution.py:184
  287.8 31.9 %collective-permute-start.16 = (bf16[192,3072]{1,0:T(8,128)(2,1)}, bf16[192,3072]{1,0:T(8,128)(2,1)}, u32[]{:S(2)}, u32[]{:S(2)}) collective-permute-start(bf16[192,3072]{1,0:T(8,128)(2,1)} %get-tuple-element.251), channel_id=1, source_target_pairs={{0,1},{1,0},{2,3},{3,2},{4,5},{5,4},{6,7},{7,6},{8,9},{9,8},{10,11... | collective-permute-start | bytes 3538952 | tf_op jit(solution)/shard_map/ppermute | solution.py:184
  288.2 31.5 %collective-permute-start.15 = (bf16[192,3072]{1,0:T(8,128)(2,1)}, bf16[192,3072]{1,0:T(8,128)(2,1)}, u32[]{:S(2)}, u32[]{:S(2)}) collective-permute-start(bf16[192,3072]{1,0:T(8,128)(2,1)} %get-tuple-element.252), channel_id=1, source_target_pairs={{0,1},{1,0},{2,3},{3,2},{4,5},{5,4},{6,7},{7,6},{8,9},{9,8},{10,11... | collective-permute-start | bytes 3538952 | tf_op jit(solution)/shard_map/ppermute | solution.py:184
  294.8 58.1 %collective-permute-start.29 = (bf16[2,512,384]{2,1,0:T(8,128)(2,1)}, bf16[2,512,384]{2,1,0:T(8,128)(2,1)}, u32[]{:S(2)}, u32[]{:S(2)}) collective-permute-start(bf16[2,512,384]{2,1,0:T(8,128)(2,1)} %add_convert_fusion.12), channel_id=1, source_target_pairs={{0,2},{1,3},{2,0},{3,1},{4,6},{5,7},{6,4},{7,5},{8,10},{9,11},{10,... | collective-permute-start | bytes 2359304 | tf_op jit(solution)/shard_map/ppermute | solution.py:184
  317.2 38.4 %collective-permute-start.32 = (bf16[2,512,384]{2,1,0:T(8,128)(2,1)}, bf16[2,512,384]{2,1,0:T(8,128)(2,1)}, u32[]{:S(2)}, u32[]{:S(2)}) collective-permute-start(bf16[2,512,384]{2,1,0:T(8,128)(2,1)} %get-tuple-element.174), channel_id=1, source_target_pairs={{0,1},{1,0},{2,3},{3,2},{4,5},{5,4},{6,7},{7,6},{8,9},{9,8},{10,11... | collective-permute-start | bytes 2359304 | tf_op jit(solution)/shard_map/ppermute | solution.py:184
  317.4 87.0 %collective-permute-start.31 = (bf16[2,512,384]{2,1,0:T(8,128)(2,1)}, bf16[2,512,384]{2,1,0:T(8,128)(2,1)}, u32[]{:S(2)}, u32[]{:S(2)}) collective-permute-start(bf16[2,512,384]{2,1,0:T(8,128)(2,1)} %get-tuple-element.172), channel_id=1, source_target_pairs={{0,1},{1,0},{2,3},{3,2},{4,5},{5,4},{6,7},{7,6},{8,9},{9,8},{10,11... | collective-permute-start | bytes 2359304 | tf_op jit(solution)/shard_map/ppermute | solution.py:184
  325.6 32.6 %collective-permute-start.19 = (bf16[384,768]{1,0:T(8,128)(2,1)}, bf16[384,768]{1,0:T(8,128)(2,1)}, u32[]{:S(2)}, u32[]{:S(2)}) collective-permute-start(bf16[384,768]{1,0:T(8,128)(2,1)} %dynamic-slice_bitcast_fusion.7), channel_id=1, source_target_pairs={{0,4},{4,0},{8,12},{12,8},{16,20},{20,16},{24,28},{28,24},{1,5},{5... | collective-permute-start | bytes 1769480 | tf_op jit(solution)/shard_map/ppermute | solution.py:264
  327.4 22.8 %collective-permute-start.21 = (bf16[192,768]{1,0:T(8,128)(2,1)}, bf16[192,768]{1,0:T(8,128)(2,1)S(1)}, u32[]{:S(2)}, u32[]{:S(2)}) collective-permute-start(bf16[192,768]{1,0:T(8,128)(2,1)} %get-tuple-element.142), channel_id=1, source_target_pairs={{0,2},{1,3},{2,0},{3,1},{4,6},{5,7},{6,4},{7,5},{8,10},{9,11},{10,... | collective-permute-start | bytes 884744 | tf_op jit(solution)/shard_map/ppermute | solution.py:184
  351.0 29.1 %collective-permute-start.20 = (bf16[192,3072]{1,0:T(8,128)(2,1)}, bf16[192,3072]{1,0:T(8,128)(2,1)S(1)}, u32[]{:S(2)}, u32[]{:S(2)}) collective-permute-start(bf16[192,3072]{1,0:T(8,128)(2,1)} %get-tuple-element.140), channel_id=1, source_target_pairs={{0,2},{1,3},{2,0},{3,1},{4,6},{5,7},{6,4},{7,5},{8,10},{9,11},{10,... | collective-permute-start | bytes 3538952 | tf_op jit(solution)/shard_map/ppermute | solution.py:184
  358.2 46.7 %collective-permute-start.33 = (bf16[2,512,384]{2,1,0:T(8,128)(2,1)}, bf16[2,512,384]{2,1,0:T(8,128)(2,1)}, u32[]{:S(2)}, u32[]{:S(2)}) collective-permute-start(bf16[2,512,384]{2,1,0:T(8,128)(2,1)} %add_convert_fusion.8), channel_id=1, source_target_pairs={{0,2},{1,3},{2,0},{3,1},{4,6},{5,7},{6,4},{7,5},{8,10},{9,11},{10,... | collective-permute-start | bytes 2359304 | tf_op jit(solution)/shard_map/ppermute | solution.py:184
  363.7 48.7 %collective-permute-start.30 = (bf16[2,512,384]{2,1,0:T(8,128)(2,1)}, bf16[2,512,384]{2,1,0:T(8,128)(2,1)}, u32[]{:S(2)}, u32[]{:S(2)}) collective-permute-start(bf16[2,512,384]{2,1,0:T(8,128)(2,1)} %add_convert_fusion.16), channel_id=1, source_target_pairs={{0,2},{1,3},{2,0},{3,1},{4,6},{5,7},{6,4},{7,5},{8,10},{9,11},{10,... | collective-permute-start | bytes 2359304 | tf_op jit(solution)/shard_map/ppermute | solution.py:184
  382.4 32.3 %collective-permute-start.26 = (bf16[96,3072]{1,0:T(8,128)(2,1)}, bf16[96,3072]{1,0:T(8,128)(2,1)}, u32[]{:S(2)}, u32[]{:S(2)}) collective-permute-start(bf16[96,3072]{1,0:T(8,128)(2,1)} %dynamic-slice_bitcast_fusion.6), channel_id=1, source_target_pairs={{0,4},{4,0},{8,12},{12,8},{16,20},{20,16},{24,28},{28,24},{1,5},{5... | collective-permute-start | bytes 1769480 | tf_op jit(solution)/shard_map/ppermute | solution.py:264
  404.3 12.5 %collective-permute-start.24 = (bf16[2,512,384]{2,1,0:T(8,128)(2,1)}, bf16[2,512,384]{2,1,0:T(8,128)(2,1)S(1)}, u32[]{:S(2)}, u32[]{:S(2)}) collective-permute-start(bf16[2,512,384]{2,1,0:T(8,128)(2,1)} %get-tuple-element.153), channel_id=1, source_target_pairs={{0,1},{1,0},{2,3},{3,2},{4,5},{5,4},{6,7},{7,6},{8,9},{9,8},{10,11... | collective-permute-start | bytes 2359304 | tf_op jit(solution)/shard_map/ppermute | solution.py:184
  404.4 13.5 %collective-permute-start.25 = (bf16[2,512,384]{2,1,0:T(8,128)(2,1)}, bf16[2,512,384]{2,1,0:T(8,128)(2,1)S(1)}, u32[]{:S(2)}, u32[]{:S(2)}) collective-permute-start(bf16[2,512,384]{2,1,0:T(8,128)(2,1)} %get-tuple-element.155), channel_id=1, source_target_pairs={{0,1},{1,0},{2,3},{3,2},{4,5},{5,4},{6,7},{7,6},{8,9},{9,8},{10,11... | collective-permute-start | bytes 2359304 | tf_op jit(solution)/shard_map/ppermute | solution.py:184
  419.0 18.4 %collective-permute-start.34 = (bf16[2,512,384]{2,1,0:T(8,128)(2,1)}, bf16[2,512,384]{2,1,0:T(8,128)(2,1)}, u32[]{:S(2)}, u32[]{:S(2)}) collective-permute-start(bf16[2,512,384]{2,1,0:T(8,128)(2,1)} %add_convert_fusion.14), channel_id=1, source_target_pairs={{0,2},{1,3},{2,0},{3,1},{4,6},{5,7},{6,4},{7,5},{8,10},{9,11},{10,... | collective-permute-start | bytes 2359304 | tf_op jit(solution)/shard_map/ppermute | solution.py:184
  464.3 11.2 %collective-permute-start.35 = (bf16[16,2304]{1,0:T(8,128)(2,1)S(1)}, bf16[16,2304]{1,0:T(8,128)(2,1)S(1)}, u32[]{:S(2)}, u32[]{:S(2)}) collective-permute-start(bf16[16,2304]{1,0:T(8,128)(2,1)S(1)} %get-tuple-element.275), channel_id=1, source_target_pairs={{0,1},{1,0},{2,3},{3,2},{4,5},{5,4},{6,7},{7,6},{8,9},{9,8},{10,11... | collective-permute-start | bytes 221192 | tf_op jit(solution)/shard_map/ppermute | solution.py:184
  467.2 38.4 %collective-permute-start.42 = (bf16[192,2304]{1,0:T(8,128)(2,1)S(1)}, bf16[192,2304]{1,0:T(8,128)(2,1)S(1)}, u32[]{:S(2)}, u32[]{:S(2)}) collective-permute-start(bf16[192,2304]{1,0:T(8,128)(2,1)S(1)} %get-tuple-element.262), channel_id=1, source_target_pairs={{0,1},{1,0},{2,3},{3,2},{4,5},{5,4},{6,7},{7,6},{8,9},{9,8},{10,11... | collective-permute-start | bytes 2654216 | tf_op jit(solution)/shard_map/ppermute | solution.py:184
  467.3 58.0 %collective-permute-start.41 = (bf16[192,2304]{1,0:T(8,128)(2,1)}, bf16[192,2304]{1,0:T(8,128)(2,1)}, u32[]{:S(2)}, u32[]{:S(2)}) collective-permute-start(bf16[192,2304]{1,0:T(8,128)(2,1)} %get-tuple-element.261), channel_id=1, source_target_pairs={{0,1},{1,0},{2,3},{3,2},{4,5},{5,4},{6,7},{7,6},{8,9},{9,8},{10,11... | collective-permute-start | bytes 2654216 | tf_op jit(solution)/shard_map/ppermute | solution.py:184
  468.4 27.5 %collective-permute-start.56 = (bf16[48,3072]{1,0:T(8,128)(2,1)S(1)}, bf16[48,3072]{1,0:T(8,128)(2,1)S(1)}, u32[]{:S(2)}, u32[]{:S(2)}) collective-permute-start(bf16[48,3072]{1,0:T(8,128)(2,1)S(1)} %dynamic-slice_bitcast_fusion.10), channel_id=1, source_target_pairs={{0,8},{4,12},{8,0},{12,4},{16,24},{20,28},{24,16},{28,20},{1,9},{5... | collective-permute-start | bytes 884744 | tf_op jit(solution)/shard_map/ppermute | solution.py:264
  475.5 24.1 %collective-permute-start.61 = (bf16[192,768]{1,0:T(8,128)(2,1)S(1)}, bf16[192,768]{1,0:T(8,128)(2,1)S(1)}, u32[]{:S(2)}, u32[]{:S(2)}) collective-permute-start(bf16[192,768]{1,0:T(8,128)(2,1)S(1)} %dynamic-slice_bitcast_fusion.9), channel_id=1, source_target_pairs={{0,8},{4,12},{8,0},{12,4},{16,24},{20,28},{24,16},{28,20},{1,9},{5... | collective-permute-start | bytes 884744 | tf_op jit(solution)/shard_map/ppermute | solution.py:264
  495.9 9.1 %collective-permute-start.53 = (bf16[24,768]{1,0:T(8,128)(2,1)S(1)}, bf16[24,768]{1,0:T(8,128)(2,1)S(1)}, u32[]{:S(2)}, u32[]{:S(2)}) collective-permute-start(bf16[24,768]{1,0:T(8,128)(2,1)S(1)} %fusion.49), channel_id=1, source_target_pairs={{0,16},{4,20},{8,24},{12,28},{16,0},{20,4},{24,8},{28,12},{1,17},{... | collective-permute-start | bytes 110600 | tf_op jit(solution)/shard_map/ppermute | solution.py:264
  499.6 41.0 %collective-permute-start.57 = (bf16[24,3072]{1,0:T(8,128)(2,1)}, bf16[24,3072]{1,0:T(8,128)(2,1)}, u32[]{:S(2)}, u32[]{:S(2)}) collective-permute-start(bf16[24,3072]{1,0:T(8,128)(2,1)} %dynamic-slice_bitcast_fusion.15), channel_id=1, source_target_pairs={{0,16},{4,20},{8,24},{12,28},{16,0},{20,4},{24,8},{28,12},{1,17},{... | collective-permute-start | bytes 442376 | tf_op jit(solution)/shard_map/ppermute | solution.py:264
  501.2 40.4 %collective-permute-start.62 = (bf16[96,768]{1,0:T(8,128)(2,1)}, bf16[96,768]{1,0:T(8,128)(2,1)}, u32[]{:S(2)}, u32[]{:S(2)}) collective-permute-start(bf16[96,768]{1,0:T(8,128)(2,1)} %dynamic-slice_bitcast_fusion.14), channel_id=1, source_target_pairs={{0,16},{4,20},{8,24},{12,28},{16,0},{20,4},{24,8},{28,12},{1,17},{... | collective-permute-start | bytes 442376 | tf_op jit(solution)/shard_map/ppermute | solution.py:264
  505.0 10.6 %collective-permute-start.40 = (bf16[16,2304]{1,0:T(8,128)(2,1)S(1)}, bf16[16,2304]{1,0:T(8,128)(2,1)S(1)}, u32[]{:S(2)}, u32[]{:S(2)}) collective-permute-start(bf16[16,2304]{1,0:T(8,128)(2,1)S(1)} %add_convert_fusion.20), channel_id=1, source_target_pairs={{0,16},{4,20},{8,24},{12,28},{16,0},{20,4},{24,8},{28,12},{1,17},{... | collective-permute-start | bytes 221192 | tf_op jit(solution)/shard_map/ppermute | solution.py:264
  505.6 15.3 %collective-permute-start.54 = (bf16[48,768]{1,0:T(8,128)(2,1)}, bf16[48,768]{1,0:T(8,128)(2,1)}, u32[]{:S(2)}, u32[]{:S(2)}) collective-permute-start(bf16[48,768]{1,0:T(8,128)(2,1)} %maximum_select_fusion.11), channel_id=1, source_target_pairs={{0,8},{4,12},{8,0},{12,4},{16,24},{20,28},{24,16},{28,20},{1,9},{5... | collective-permute-start | bytes 221192 | tf_op jit(solution)/shard_map/ppermute | solution.py:264
  515.5 21.4 %collective-permute-start.43 = (bf16[192,2304]{1,0:T(8,128)(2,1)}, bf16[192,2304]{1,0:T(8,128)(2,1)}, u32[]{:S(2)}, u32[]{:S(2)}) collective-permute-start(bf16[192,2304]{1,0:T(8,128)(2,1)} %fusion.26), channel_id=1, source_target_pairs={{0,2},{1,3},{2,0},{3,1},{4,6},{5,7},{6,4},{7,5},{8,10},{9,11},{10,... | collective-permute-start | bytes 2654216 | tf_op jit(solution)/shard_map/ppermute | solution.py:184
  522.0 55.8 %collective-permute-start.55 = (bf16[96,768]{1,0:T(8,128)(2,1)S(1)}, bf16[96,768]{1,0:T(8,128)(2,1)S(1)}, u32[]{:S(2)}, u32[]{:S(2)}) collective-permute-start(bf16[96,768]{1,0:T(8,128)(2,1)S(1)} %maximum_select_fusion.10), channel_id=1, source_target_pairs={{0,4},{4,0},{8,12},{12,8},{16,20},{20,16},{24,28},{28,24},{1,5},{5... | collective-permute-start | bytes 442376 | tf_op jit(solution)/shard_map/ppermute | solution.py:264
  538.7 10.9 %collective-permute-start.44 = (bf16[96,2304]{1,0:T(8,128)(2,1)S(1)}, bf16[96,2304]{1,0:T(8,128)(2,1)S(1)}, u32[]{:S(2)}, u32[]{:S(2)}) collective-permute-start(bf16[96,2304]{1,0:T(8,128)(2,1)S(1)} %dynamic-slice_bitcast_fusion.8), channel_id=1, source_target_pairs={{0,4},{4,0},{8,12},{12,8},{16,20},{20,16},{24,28},{28,24},{1,5},{5... | collective-permute-start | bytes 1327112 | tf_op jit(solution)/shard_map/ppermute | solution.py:264
  541.5 9.3 %collective-permute-start.58 = (bf16[24,3072]{1,0:T(8,128)(2,1)S(1)}, bf16[24,3072]{1,0:T(8,128)(2,1)S(1)}, u32[]{:S(2)}, u32[]{:S(2)}) collective-permute-start(bf16[24,3072]{1,0:T(8,128)(2,1)S(1)} %fusion.42), channel_id=1, source_target_pairs={{0,16},{4,20},{8,24},{12,28},{16,0},{20,4},{24,8},{28,12},{1,17},{... | collective-permute-start | bytes 442376 | tf_op jit(solution)/shard_map/ppermute | solution.py:264
  542.6 15.7 %collective-permute-start.63 = (bf16[96,768]{1,0:T(8,128)(2,1)S(1)}, bf16[96,768]{1,0:T(8,128)(2,1)S(1)}, u32[]{:S(2)}, u32[]{:S(2)}) collective-permute-start(bf16[96,768]{1,0:T(8,128)(2,1)S(1)} %fusion.41), channel_id=1, source_target_pairs={{0,16},{4,20},{8,24},{12,28},{16,0},{20,4},{24,8},{28,12},{1,17},{... | collective-permute-start | bytes 442376 | tf_op jit(solution)/shard_map/ppermute | solution.py:264
  550.9 25.0 %collective-permute-start.59 = (bf16[48,3072]{1,0:T(8,128)(2,1)S(1)}, bf16[48,3072]{1,0:T(8,128)(2,1)S(1)}, u32[]{:S(2)}, u32[]{:S(2)}) collective-permute-start(bf16[48,3072]{1,0:T(8,128)(2,1)S(1)} %maximum_select_fusion.7), channel_id=1, source_target_pairs={{0,8},{4,12},{8,0},{12,4},{16,24},{20,28},{24,16},{28,20},{1,9},{5... | collective-permute-start | bytes 884744 | tf_op jit(solution)/shard_map/ppermute | solution.py:264
  558.3 16.8 %collective-permute-start.64 = (bf16[192,768]{1,0:T(8,128)(2,1)S(1)}, bf16[192,768]{1,0:T(8,128)(2,1)S(1)}, u32[]{:S(2)}, u32[]{:S(2)}) collective-permute-start(bf16[192,768]{1,0:T(8,128)(2,1)S(1)} %maximum_select_fusion.8), channel_id=1, source_target_pairs={{0,8},{4,12},{8,0},{12,4},{16,24},{20,28},{24,16},{28,20},{1,9},{5... | collective-permute-start | bytes 884744 | tf_op jit(solution)/shard_map/ppermute | solution.py:264
  565.2 10.5 %collective-permute-start.47 = (bf16[24,2304]{1,0:T(8,128)(2,1)S(1)}, bf16[24,2304]{1,0:T(8,128)(2,1)S(1)}, u32[]{:S(2)}, u32[]{:S(2)}) collective-permute-start(bf16[24,2304]{1,0:T(8,128)(2,1)S(1)} %fusion.44), channel_id=1, source_target_pairs={{0,16},{4,20},{8,24},{12,28},{16,0},{20,4},{24,8},{28,12},{1,17},{... | collective-permute-start | bytes 331784 | tf_op jit(solution)/shard_map/ppermute | solution.py:264
  575.4 16.3 %collective-permute-start.65 = (bf16[384,768]{1,0:T(8,128)(2,1)S(1)}, bf16[384,768]{1,0:T(8,128)(2,1)S(1)}, u32[]{:S(2)}, u32[]{:S(2)}) collective-permute-start(bf16[384,768]{1,0:T(8,128)(2,1)S(1)} %maximum_select_fusion.4), channel_id=1, source_target_pairs={{0,4},{4,0},{8,12},{12,8},{16,20},{20,16},{24,28},{28,24},{1,5},{5... | collective-permute-start | bytes 1769480 | tf_op jit(solution)/shard_map/ppermute | solution.py:264
  576.0 28.3 %collective-permute-start.60 = (bf16[96,3072]{1,0:T(8,128)(2,1)S(1)}, bf16[96,3072]{1,0:T(8,128)(2,1)S(1)}, u32[]{:S(2)}, u32[]{:S(2)}) collective-permute-start(bf16[96,3072]{1,0:T(8,128)(2,1)S(1)} %maximum_select_fusion.3), channel_id=1, source_target_pairs={{0,4},{4,0},{8,12},{12,8},{16,20},{20,16},{24,28},{28,24},{1,5},{5... | collective-permute-start | bytes 1769480 | tf_op jit(solution)/shard_map/ppermute | solution.py:264
  582.8 29.8 %collective-permute-start.49 = (bf16[96,2304]{1,0:T(8,128)(2,1)S(1)}, bf16[96,2304]{1,0:T(8,128)(2,1)S(1)}, u32[]{:S(2)}, u32[]{:S(2)}) collective-permute-start(bf16[96,2304]{1,0:T(8,128)(2,1)S(1)} %maximum_select_fusion.5), channel_id=1, source_target_pairs={{0,4},{4,0},{8,12},{12,8},{16,20},{20,16},{24,28},{28,24},{1,5},{5... | collective-permute-start | bytes 1327112 | tf_op jit(solution)/shard_map/ppermute | solution.py:264
  (96 other events, 846.1 us)
Sparse Core Ops, SparseCore 0:
  9.6 33.4 all-gather.6
  74.8 23.8 all-gather.8
  100.2 58.2 all-gather.10
  159.9 37.4 all-gather.12

commit v3 on v2

--- a/solution.py
+++ b/solution.py
@@ -383,10 +383,9 @@
         if i == 1:
             (fall, rise, out_grad), grad_out = tie((fall, rise, out_grad), grad_out)
             rise, out_grad = reduce_chip(rise), reduce_chip(out_grad)
-            fall = halve(fall, 1)
         if i == 3:
             (fall, rise, out_grad), grad_out = tie((fall, rise, out_grad), grad_out)
-            rise = halve(rise, 1)
+            wide = [lax.psum(part, "dp") for part in (fall, rise, out_grad)]
         grad_q, *grad_blocks = attn_bwd(q, blocks, grad_out, mix, log_total, seg_q, first, count)
         halves.append(fold(grad_blocks, 1))
         grads_q.append(grad_q)
@@ -405,8 +404,8 @@
             for i in range(0, 2 * micro, 2)
         ]
     )
-    (fall, rise, out_grad), grad_qkv = tie((fall, rise, out_grad), grad_qkv)
-    wide = [finish(fall, 2), finish(rise, 2), finish(out_grad, 1)]
+    grad_qkv = lax.optimization_barrier(grad_qkv)
+    wide = [part.astype(f32) for part in wide]
     grad_w_proj = tn(normed_low, grad_qkv)
     sums = jnp.sum(grad_qkv.astype(f32), axis=0)
     grad_b_proj = jnp.concatenate([sums[:width], sums[2 * width :]])

time: 627 us -> 568 us (0.906)
  waiting for transfers between devices: 200 us -> 169 us
  starting transfers between devices: 49.1 us -> 34.1 us
  other arithmetic: 83 us -> 76.7 us
    ppermute x27 -> x9, waiting for transfers between devices: 78.6 us -> 28.2 us  [trade(): return lax.ppermute(x, 'dp', [(i, i ^ flip) for i in range(size)])]
    ppermute x39, waiting for transfers between devices: 101 us -> 120 us  [swap(): return lax.ppermute(x, 'band', [(i, i ^ flip) for i in range(parts)])]
    ppermute x27 -> x9, starting transfers between devices: 33 us -> 14.9 us  [trade(): return lax.ppermute(x, 'dp', [(i, i ^ flip) for i in range(size)])]
    convert_element_type x12 -> x3, other arithmetic: 7.37 us -> 0.19 us  [halve(): return (near.astype(f32) + trade(far, flip).astype(f32)).astype(bf)]
    convert_element_type x0 -> x3, other arithmetic: none -> 6.42 us  [layer(): wide = [part.astype(f32) for part in wide]]
    unnamed x164 -> x134, local copies, waits for them, and re-layouts: 10.6 us -> 12.6 us
  transfers between devices with their start and end apart: 70 -> 53, of which waited for: 31 -> 22; matrix products, arithmetic and copies ran while one was open for 22% -> 26% of each run, Pallas kernels for 19% -> 21%
where the time goes in v3:
time: 568 us; the launch traced here: 562 us
  waiting for transfers between devices  169 us (30%)
  Pallas kernels  140 us (25%)
  matrix products  81.4 us (14%)
  other arithmetic  76.7 us (14%)
  local copies, waits for them, and re-layouts  39.8 us (7%)
  starting transfers between devices  34.1 us (6%)
  between operations  15.1 us (3%)
  blocking collectives  6.24 us (1%)
    ppermute x39, waiting for transfers between devices, swap(): return lax.ppermute(x, 'band', [(i, i ^ flip) for i in range(parts)])  120 us
    pallas_call x4, Pallas kernels, attn_bwd(): pl.pallas_call(functools.partial(bwd_kernel, tq=min(tq, n), parts=parts),...  86.6 us
    pallas_call x4, Pallas kernels, attn_fwd(): pl.pallas_call(functools.partial(fwd_kernel, tq=min(tq, n), parts=parts),...  52.9 us
    convert_element_type x21, other arithmetic, fold(): (near.astype(f32) + swap(far, flip).astype(f32)).astype(bf)  40.8 us
    dot_general x4, matrix products, nn(): lax.dot_general(a, b, (((1,), (0,)), ((), ())), preferred_element_type=f32)  33.7 us
    ppermute x9, waiting for transfers between devices, trade(): return lax.ppermute(x, 'dp', [(i, i ^ flip) for i in range(size)])  28.2 us
    dot_general x4, matrix products, nt(): lax.dot_general(a, b, (((1,), (1,)), ((), ())), preferred_element_type=f32)  27.7 us
    dot_general x4, matrix products, tn(): lax.dot_general(a, b, (((0,), (0,)), ((), ())), preferred_element_type=f32)  20.1 us
  transfers between devices with their start and end apart: 53, of which 22 were waited for; matrix products, arithmetic and copies ran while one was open for 26% of the time, Pallas kernels for 21%

profile of v3, /device:TPU:0, one launch (start us, length us, event | category | flops | bytes accessed | tf_op | source)
XLA Modules:
  0.0 561.6 jit_solution(12477777822636113527)
XLA Ops:
  8.0 5.5 concatenate.60
  13.4 6.2 %all-gather.1 = bf16[4,1,2304]{2,1,0:T(2,128)(2,1)S(1)} all-gather(bf16[1,1,2304]{2,1,0:T(2,128)(2,1)S(1)} %reshape.372), channel_id=2, replica_groups=mesh['dp'=8,'band'=4] {'band'}, dimensions={0}, use_global_device_ids=true | all-gather | bytes 23040 | tf_op jit(solution)/shard_map/all_gather | solution.py:215
  24.3 18.8 %all-gather.7.cloned.1.call-done = bf16[768,2304]{1,0:T(8,128)(2,1)} async-done(((bf16[192,2304]{1,0:T(8,128)(2,1)}), bf16[768,2304]{1,0:T(8,128)(2,1)}) %all-gather.7.cloned.1.call-update) | async-done | bytes 3538960 | tf_op jit(solution)/shard_map/all_gather | solution.py:250
  43.1 5.8 %fusion.55 = (bf16[1024,2304]{1,0:T(8,128)(2,1)S(1)}, f32[1024,2304]{1,0:T(8,128)S(1)}) fusion(bf16[1024,768]{1,0:T(8,128)(2,1)S(1)} %fusion.15, bf16[768,2304]{1,0:T(8,128)(2,1)} %all-gather.7.cloned.1.call-done), kind=kOutput, calls=%fused_computation.169 | convolution fusion | flops 3626237952 | bytes 19267584 | tf_op jit(solution)/shard_map/dot_general | solution.py:16
  53.6 18.6 %collective-permute-done.1.refs_3_.refs_7_.refs_6_.refs_10_ = bf16[512,768]{1,0:T(8,128)(2,1)S(1)} collective-permute-done((bf16[512,768]{1,0:T(8,128)(2,1)S(1)}, bf16[512,768]{1,0:T(8,128)(2,1)S(1)}, u32[]{:S(2)}, u32[]{:S(2)}) %collective-permute-start.1) | collective-permute-done | bytes 786464 | tf_op jit(solution)/shard_map/ppermute | solution.py:184
  81.9 13.3 %attn_fwd.4 = (bf16[512,384]{1,0:T(8,128)(2,1)}, f32[512,384]{1,0:T(8,128)}) custom-call(bf16[512,768]{1,0:T(8,128)(2,1)} %get-tuple-element.260.refs_0_, s32[512,1]{1,0:T(8,128)} %copy.41.refs_1_.refs_4_, bf16[512,768]{1,0:T(8,128)(2,1)} %copy-done.20, bf16[512,768]{1,0:T(8,128)(2,1)} %copy-done.49, bf16[512,768]{1,0:T(8,128)(2,1)} %copy-done.50, ...), custom_call_target="tpu_custom_call" | custom-call | flops 6442450944 | bytes 4718592 | tf_op jit(solution)/shard_map/attn_fwd/pallas_call | solution.py:89
  95.2 11.3 %collective-permute-done.refs_3_.refs_7_.refs_6_.refs_10_ = bf16[512,768]{1,0:T(8,128)(2,1)} collective-permute-done((bf16[512,768]{1,0:T(8,128)(2,1)}, bf16[512,768]{1,0:T(8,128)(2,1)}, u32[]{:S(2)}, u32[]{:S(2)}) %collective-permute-start) | collective-permute-done | bytes 786464 | tf_op jit(solution)/shard_map/ppermute | solution.py:184
  111.2 13.2 %attn_fwd.5 = (bf16[512,384]{1,0:T(8,128)(2,1)}, f32[512,384]{1,0:T(8,128)}) custom-call(bf16[512,768]{1,0:T(8,128)(2,1)} %get-tuple-element.260.refs_0_, s32[512,1]{1,0:T(8,128)} %copy.41.refs_1_.refs_4_, bf16[512,768]{1,0:T(8,128)(2,1)} %get-tuple-element.111.refs_2_.refs_6_.refs_5_.refs_9_, ...), custom_call_target="tpu_custom_call" | custom-call | flops 6442450944 | bytes 4718592 | tf_op jit(solution)/shard_map/attn_fwd/pallas_call | solution.py:89
  124.4 18.9 %collective-permute-done.4.refs_3_.refs_7_.refs_6_.refs_10_ = bf16[512,768]{1,0:T(8,128)(2,1)} collective-permute-done((bf16[512,768]{1,0:T(8,128)(2,1)S(1)}, bf16[512,768]{1,0:T(8,128)(2,1)}, u32[]{:S(2)}, u32[]{:S(2)}) %collective-permute-start.4) | collective-permute-done | bytes 786464 | tf_op jit(solution)/shard_map/ppermute | solution.py:184
  147.0 13.3 %attn_fwd.6 = (bf16[512,384]{1,0:T(8,128)(2,1)}, f32[512,384]{1,0:T(8,128)}) custom-call(bf16[512,768]{1,0:T(8,128)(2,1)} %get-tuple-element.261.refs_0_, s32[512,1]{1,0:T(8,128)} %copy.43.refs_1_.refs_4_, bf16[512,768]{1,0:T(8,128)(2,1)} %get-tuple-element.116.refs_2_.refs_6_.refs_5_.refs_9_, ...), custom_call_target="tpu_custom_call" | custom-call | flops 6442450944 | bytes 4718592 | tf_op jit(solution)/shard_map/attn_fwd/pallas_call | solution.py:89
  160.3 8.5 %collective-permute-done.7.refs_3_.refs_7_.refs_6_.refs_10_ = bf16[512,768]{1,0:T(8,128)(2,1)} collective-permute-done((bf16[512,768]{1,0:T(8,128)(2,1)}, bf16[512,768]{1,0:T(8,128)(2,1)}, u32[]{:S(2)}, u32[]{:S(2)}) %collective-permute-start.7) | collective-permute-done | bytes 786464 | tf_op jit(solution)/shard_map/ppermute | solution.py:184
  172.6 13.1 %attn_fwd.7 = (bf16[512,384]{1,0:T(8,128)(2,1)}, f32[512,384]{1,0:T(8,128)}) custom-call(bf16[512,768]{1,0:T(8,128)(2,1)} %get-tuple-element.261.refs_0_, s32[512,1]{1,0:T(8,128)} %copy.43.refs_1_.refs_4_, bf16[512,768]{1,0:T(8,128)(2,1)} %get-tuple-element.120.refs_2_.refs_6_.refs_5_.refs_9_, ...), custom_call_target="tpu_custom_call" | custom-call | flops 6442450944 | bytes 4718592 | tf_op jit(solution)/shard_map/attn_fwd/pallas_call | solution.py:89
  185.8 3.4 fusion.56
  191.3 14.3 %multiply_convert_fusion = (bf16[1024,3072]{1,0:T(8,128)(2,1)S(1)}, f32[1024,3072]{1,0:T(8,128)}) fusion(f32[3072]{0:T(1024)S(1)} %reshape.351, bf16[768,3072]{1,0:T(8,128)(2,1)} %all-gather.11.cloned.1.call-done, f32[1024,768]{1,0:T(8,128)} %copy-done.6, f32[768]{0:T(1024)S(1)} %reshape.350, f32[768]{0:T(1024)S(1)} %reshape.349, f32[1024]{0:T(1024)S(1)} %fusion.38, ...), kind=kOutput, calls=%fused_computation.9 | convolution fusion | flops 4867227648 | bytes 26765312 | tf_op jit(solution)/shard_map/dot_general | solution.py:16
  205.6 5.5 convolution_convert_fusion.1
  215.3 14.4 %fusion.6 = bf16[1024,3072]{1,0:T(8,128)(2,1)S(1)} fusion(f32[1024,3072]{1,0:T(8,128)} %get-tuple-element.297, f32[3072]{0:T(1024)S(1)} %reshape.351, bf16[1024,768]{1,0:T(8,128)(2,1)S(1)} %copy-done.16, bf16[3072,768]{1,0:T(8,128)(2,1)} %all-gather.13.cloned.1.call-done), kind=kOutput, calls=%fused_computation.8 | convolution fusion | flops 4897898496 | bytes 25178112 | tf_op jit(solution)/shard_map/dot_general | solution.py:13
  229.7 5.3 fusion.23
  235.0 8.0 %convolution_convert_fusion = bf16[768,3072]{1,0:T(8,128)(2,1)} fusion(bf16[1024,3072]{1,0:T(8,128)(2,1)S(1)} %fusion.6, f32[1024,768]{1,0:T(8,128)S(1)} %copy-done.7, f32[768]{0:T(1024)S(1)} %reshape.350, f32[768]{0:T(1024)S(1)} %reshape.349, f32[1024]{0:T(1024)S(1)} %fusion.38, f32[1024]{0:T(1024)S(1)} %broadcast_multiply_fusion), kind=kOutput, calls=%fused_computation.10 | convolution fusion | flops 4838129664 | bytes 14170112 | tf_op jit(solution)/shard_map/dot_general | solution.py:19
  243.1 6.2 %multiply_reduce_fusion = (bf16[768]{0:T(1024)(128)(2,1)}, f32[1024]{0:T(1024)S(1)}, bf16[768]{0:T(1024)(128)(2,1)}, f32[1024,768]{1,0:T(8,128)S(1)}) fusion(f32[1024,768]{1,0:T(8,128)S(1)} %copy-done.7, f32[1024]{0:T(1024)S(1)} %fusion.38, f32[1024]{0:T(1024)S(1)} %broadcast_multiply_fusion, f32[768]{0:T(1024)S(1)} %reshape.349, ...), kind=kOutput, calls=%fused_computation.37 | convolution fusion | flops 4838126592 | bytes 17319936 | tf_op jit(solution)/shard_map/dot_general | solution.py:13
  258.4 21.6 %attn_bwd.6 = (bf16[512,384]{1,0:T(8,128)(2,1)}, bf16[2,512,384]{2,1,0:T(8,128)(2,1)}, bf16[2,512,384]{2,1,0:T(8,128)(2,1)}, bf16[2,512,384]{2,1,0:T(8,128)(2,1)}, bf16[2,512,384]{2,1,0:T(8,128)(2,1)}) custom-call(bf16[512,768]{1,0:T(8,128)(2,1)} %get-tuple-element.260.refs_0_, bf16[512,768]{1,0:T(8,128)(2,1)} %get-tuple-element.139.refs_1_, ...), custom_call_target="tpu_custom_call" | custom-call | flops 16106127360 | bytes 8650752 | tf_op jit(solution)/shard_map/attn_bwd/pallas_call | solution.py:158
  283.6 3.3 dynamic-slice_bitcast_fusion
  289.7 21.7 %attn_bwd.7 = (bf16[512,384]{1,0:T(8,128)(2,1)}, bf16[2,512,384]{2,1,0:T(8,128)(2,1)}, bf16[2,512,384]{2,1,0:T(8,128)(2,1)}, bf16[2,512,384]{2,1,0:T(8,128)(2,1)}, bf16[2,512,384]{2,1,0:T(8,128)(2,1)}) custom-call(bf16[512,768]{1,0:T(8,128)(2,1)} %get-tuple-element.261.refs_0_, bf16[512,768]{1,0:T(8,128)(2,1)} %get-tuple-element.162.refs_1_, ...), custom_call_target="tpu_custom_call" | custom-call | flops 16106127360 | bytes 8650752 | tf_op jit(solution)/shard_map/attn_bwd/pallas_call | solution.py:158
  311.8 2.6 add_convert_fusion.4
  314.4 4.3 fusion.21
  319.2 21.8 %attn_bwd.4 = (bf16[512,384]{1,0:T(8,128)(2,1)}, bf16[2,512,384]{2,1,0:T(8,128)(2,1)}, bf16[2,512,384]{2,1,0:T(8,128)(2,1)}, bf16[2,512,384]{2,1,0:T(8,128)(2,1)}, bf16[2,512,384]{2,1,0:T(8,128)(2,1)}) custom-call(bf16[512,768]{1,0:T(8,128)(2,1)} %get-tuple-element.260.refs_0_, bf16[512,768]{1,0:T(8,128)(2,1)} %get-tuple-element.139.refs_1_, ...), custom_call_target="tpu_custom_call" | custom-call | flops 16106127360 | bytes 8650752 | tf_op jit(solution)/shard_map/attn_bwd/pallas_call | solution.py:158
  358.4 11.9 %collective-permute-done.19 = bf16[192,3072]{1,0:T(8,128)(2,1)} collective-permute-done((bf16[192,3072]{1,0:T(8,128)(2,1)}, bf16[192,3072]{1,0:T(8,128)(2,1)}, u32[]{:S(2)}, u32[]{:S(2)}) %collective-permute-start.19) | collective-permute-done | bytes 1179680 | tf_op jit(solution)/shard_map/ppermute | solution.py:184
  370.3 2.7 add_convert_fusion.3
  372.9 21.5 %attn_bwd.5 = (bf16[512,384]{1,0:T(8,128)(2,1)}, bf16[2,512,384]{2,1,0:T(8,128)(2,1)}, bf16[2,512,384]{2,1,0:T(8,128)(2,1)}, bf16[2,512,384]{2,1,0:T(8,128)(2,1)}, bf16[2,512,384]{2,1,0:T(8,128)(2,1)}) custom-call(bf16[512,768]{1,0:T(8,128)(2,1)} %get-tuple-element.261.refs_0_, bf16[512,768]{1,0:T(8,128)(2,1)} %get-tuple-element.162.refs_1_, ...), custom_call_target="tpu_custom_call" | custom-call | flops 16106127360 | bytes 8650752 | tf_op jit(solution)/shard_map/attn_bwd/pallas_call | solution.py:158
  396.5 7.5 %collective-permute-done.31 = bf16[2,512,384]{2,1,0:T(8,128)(2,1)} collective-permute-done((bf16[2,512,384]{2,1,0:T(8,128)(2,1)}, bf16[2,512,384]{2,1,0:T(8,128)(2,1)}, u32[]{:S(2)}, u32[]{:S(2)}) %collective-permute-start.31) | collective-permute-done | bytes 786464 | tf_op jit(solution)/shard_map/ppermute | solution.py:184
  404.0 2.8 add_convert_fusion.7
  406.8 13.5 %collective-permute-done.28 = bf16[2,512,384]{2,1,0:T(8,128)(2,1)} collective-permute-done((bf16[2,512,384]{2,1,0:T(8,128)(2,1)}, bf16[2,512,384]{2,1,0:T(8,128)(2,1)}, u32[]{:S(2)}, u32[]{:S(2)}) %collective-permute-start.28) | collective-permute-done | bytes 786464 | tf_op jit(solution)/shard_map/ppermute | solution.py:184
  427.9 3.7 reduce.7
  431.6 10.2 %add_convert_fusion.1 = bf16[1024,768]{1,0:T(8,128)(2,1)} fusion(f32[1024,768]{1,0:T(8,128)} %copy-done.6, bf16[1024,3072]{1,0:T(8,128)(2,1)} %copy-done.52, bf16[3072,768]{1,0:T(8,128)(2,1)} %all-gather.13.cloned.1.call-done, f32[768]{0:T(1024)S(1)} %copy-done.45), kind=kOutput, calls=%fused_computation.39 | convolution fusion | flops 4834197504 | bytes 15731712 | tf_op jit(solution)/shard_map/dot_general | solution.py:16
  441.9 3.8 collective-permute-done.32
  449.8 4.2 convolution_convert_fusion.2
  457.2 5.7 %fusion.44 = (bf16[768]{0:T(1024)(128)(2,1)S(1)}, f32[1024]{0:T(1024)S(1)}, f32[1024,768]{1,0:T(8,128)}) fusion(f32[768]{0:T(1024)S(1)} %copy-done.33, f32[1024]{0:T(1024)S(1)} %bitcast.200, bf16[2,1,512,768]{3,2,1,0:T(8,128)(2,1)S(1)} %copy-done.1, bf16[1024,2304]{1,0:T(8,128)(2,1)S(1)} %pad_maximum_fusion, bf16[768,2304]{1,0:T(8,128)(2,1)S(1)} %copy-done.46), kind=kOutput, calls=%fused_computation.159 | convolution fusion | flops 3628595456 | bytes 12988928 | tf_op jit(solution)/shard_map/dot_general | solution.py:13
  462.9 3.1 reduce.5
  466.0 3.0 fusion.16
  469.7 2.6 fusion.26
  474.7 19.4 %collective-permute-done.41 = bf16[192,2304]{1,0:T(8,128)(2,1)} collective-permute-done((bf16[192,2304]{1,0:T(8,128)(2,1)}, bf16[192,2304]{1,0:T(8,128)(2,1)}, u32[]{:S(2)}, u32[]{:S(2)}) %collective-permute-start.41) | collective-permute-done | bytes 884768 | tf_op jit(solution)/shard_map/ppermute | solution.py:184
  498.1 3.9 add_convert_fusion
  502.0 5.6 collective-permute-done.42
  511.1 6.4 %collective-permute-done.43 = bf16[48,2304]{1,0:T(8,128)(2,1)S(1)} collective-permute-done((bf16[48,2304]{1,0:T(8,128)(2,1)S(1)}, bf16[48,2304]{1,0:T(8,128)(2,1)S(1)}, u32[]{:S(2)}, u32[]{:S(2)}) %collective-permute-start.43) | collective-permute-done | bytes 221216 | tf_op jit(solution)/shard_map/ppermute | solution.py:264
  521.5 3.7 collective-permute-done.44
  525.7 2.9 collective-permute-start.37
  528.7 4.6 collective-permute-done.45
  535.6 6.7 %collective-permute-done.46 = bf16[48,2304]{1,0:T(8,128)(2,1)S(1)} collective-permute-done((bf16[48,2304]{1,0:T(8,128)(2,1)S(1)}, bf16[48,2304]{1,0:T(8,128)(2,1)S(1)}, u32[]{:S(2)}, u32[]{:S(2)}) %collective-permute-start.46) | collective-permute-done | bytes 221216 | tf_op jit(solution)/shard_map/ppermute | solution.py:264
  547.8 2.9 convert_element_type.683
  (326 shorter events, 115.7 us)
Async XLA Ops:
  7.2 35.9 %all-gather.7.cloned.1.call-start = ((), (), s32[]{:S(2)}) async-start(), calls=%async_computation | async-start | bytes 4423680 | tf_op jit(solution)/shard_map/all_gather | solution.py:250
  7.9 177.8 %all-gather.9.cloned.1.call-start = ((), (), s32[]{:S(2)}) async-start(), calls=%async_computation.1 | async-start | bytes 1474560 | tf_op jit(solution)/shard_map/all_gather | solution.py:250
  52.5 19.7 %collective-permute-start.1 = (bf16[512,768]{1,0:T(8,128)(2,1)S(1)}, bf16[512,768]{1,0:T(8,128)(2,1)S(1)}, u32[]{:S(2)}, u32[]{:S(2)}) collective-permute-start(bf16[512,768]{1,0:T(8,128)(2,1)S(1)} %get-tuple-element.103.refs_2_.refs_6_.refs_5_.refs_9_), channel_id=1, source_target_pairs={{0,2},{1,3},{2,0},{3,1},{4,6},{5,7},{6,4},{7,5},{8,10},{9,11},{10,... | collective-permute-start | bytes 2359304 | tf_op jit(solution)/shard_map/ppermute | solution.py:184
  53.4 18.8 %collective-permute-start.2 = (bf16[512,768]{1,0:T(8,128)(2,1)S(1)}, bf16[512,768]{1,0:T(8,128)(2,1)S(1)}, u32[]{:S(2)}, u32[]{:S(2)}) collective-permute-start(bf16[512,768]{1,0:T(8,128)(2,1)S(1)} %get-tuple-element.103.refs_2_.refs_6_.refs_5_.refs_9_), channel_id=1, source_target_pairs={{0,1},{1,0},{2,3},{3,2},{4,5},{5,4},{6,7},{7,6},{8,9},{9,8},{10,11... | collective-permute-start | bytes 2359304 | tf_op jit(solution)/shard_map/ppermute | solution.py:184
  74.6 116.7 %all-gather.11.cloned.1.call-start = ((), (), s32[]{:S(2)}) async-start(), calls=%async_computation.2 | async-start | bytes 5898240 | tf_op jit(solution)/shard_map/all_gather | solution.py:250
  75.4 139.9 %all-gather.13.cloned.1.call-start = ((), (), s32[]{:S(2)}) async-start(), calls=%async_computation.3 | async-start | bytes 5898240 | tf_op jit(solution)/shard_map/all_gather | solution.py:250
  80.3 26.2 %collective-permute-start = (bf16[512,768]{1,0:T(8,128)(2,1)}, bf16[512,768]{1,0:T(8,128)(2,1)}, u32[]{:S(2)}, u32[]{:S(2)}) collective-permute-start(bf16[512,768]{1,0:T(8,128)(2,1)} %get-tuple-element.111.refs_2_.refs_6_.refs_5_.refs_9_), channel_id=1, source_target_pairs={{0,2},{1,3},{2,0},{3,1},{4,6},{5,7},{6,4},{7,5},{8,10},{9,11},{10,... | collective-permute-start | bytes 2359304 | tf_op jit(solution)/shard_map/ppermute | solution.py:184
  106.5 4.7 collective-permute-start.6
  107.0 36.2 %collective-permute-start.4 = (bf16[512,768]{1,0:T(8,128)(2,1)S(1)}, bf16[512,768]{1,0:T(8,128)(2,1)}, u32[]{:S(2)}, u32[]{:S(2)}) collective-permute-start(bf16[512,768]{1,0:T(8,128)(2,1)S(1)} %copy-done.19), channel_id=1, source_target_pairs={{0,2},{1,3},{2,0},{3,1},{4,6},{5,7},{6,4},{7,5},{8,10},{9,11},{10,... | collective-permute-start | bytes 2359304 | tf_op jit(solution)/shard_map/ppermute | solution.py:184
  143.8 402.1 %all-reduce.4.cloned.1.call-start = ((), (), s32[]{:S(2)}) async-start(), calls=%async_computation.4 | async-start | bytes 5308416 | tf_op jit(solution)/shard_map/psum | solution.py:388
  144.0 24.7 %collective-permute-start.7 = (bf16[512,768]{1,0:T(8,128)(2,1)}, bf16[512,768]{1,0:T(8,128)(2,1)}, u32[]{:S(2)}, u32[]{:S(2)}) collective-permute-start(bf16[512,768]{1,0:T(8,128)(2,1)} %get-tuple-element.120.refs_2_.refs_6_.refs_5_.refs_9_), channel_id=1, source_target_pairs={{0,2},{1,3},{2,0},{3,1},{4,6},{5,7},{6,4},{7,5},{8,10},{9,11},{10,... | collective-permute-start | bytes 2359304 | tf_op jit(solution)/shard_map/ppermute | solution.py:184
  168.8 3.8 collective-permute-start.11
  214.8 14.9 %collective-permute-start.13 = (bf16[768,768]{1,0:T(8,128)(2,1)}, bf16[768,768]{1,0:T(8,128)(2,1)}, u32[]{:S(2)}, u32[]{:S(2)}) collective-permute-start(bf16[768,768]{1,0:T(8,128)(2,1)} %get-tuple-element.250), channel_id=1, source_target_pairs={{0,1},{1,0},{2,3},{3,2},{4,5},{5,4},{6,7},{7,6},{8,9},{9,8},{10,11... | collective-permute-start | bytes 3538952 | tf_op jit(solution)/shard_map/ppermute | solution.py:184
  215.0 14.7 %collective-permute-start.12 = (bf16[768,768]{1,0:T(8,128)(2,1)}, bf16[768,768]{1,0:T(8,128)(2,1)}, u32[]{:S(2)}, u32[]{:S(2)}) collective-permute-start(bf16[768,768]{1,0:T(8,128)(2,1)} %get-tuple-element.251), channel_id=1, source_target_pairs={{0,1},{1,0},{2,3},{3,2},{4,5},{5,4},{6,7},{7,6},{8,9},{9,8},{10,11... | collective-permute-start | bytes 3538952 | tf_op jit(solution)/shard_map/ppermute | solution.py:184
  280.0 8.4 %collective-permute-start.25 = (bf16[2,512,384]{2,1,0:T(8,128)(2,1)}, bf16[2,512,384]{2,1,0:T(8,128)(2,1)S(1)}, u32[]{:S(2)}, u32[]{:S(2)}) collective-permute-start(bf16[2,512,384]{2,1,0:T(8,128)(2,1)} %get-tuple-element.155), channel_id=1, source_target_pairs={{0,1},{1,0},{2,3},{3,2},{4,5},{5,4},{6,7},{7,6},{8,9},{9,8},{10,11... | collective-permute-start | bytes 2359304 | tf_op jit(solution)/shard_map/ppermute | solution.py:184
  280.3 31.6 %collective-permute-start.14 = (bf16[768,768]{1,0:T(8,128)(2,1)}, bf16[768,768]{1,0:T(8,128)(2,1)}, u32[]{:S(2)}, u32[]{:S(2)}) collective-permute-start(bf16[768,768]{1,0:T(8,128)(2,1)} %get-tuple-element.129), channel_id=1, source_target_pairs={{0,2},{1,3},{2,0},{3,1},{4,6},{5,7},{6,4},{7,5},{8,10},{9,11},{10,... | collective-permute-start | bytes 3538952 | tf_op jit(solution)/shard_map/ppermute | solution.py:184
  282.9 4.0 collective-permute-start.18
  283.1 4.2 collective-permute-start.17
  283.5 5.1 collective-permute-start.26
  286.9 27.6 %collective-permute-start.16 = (bf16[192,3072]{1,0:T(8,128)(2,1)}, bf16[192,3072]{1,0:T(8,128)(2,1)}, u32[]{:S(2)}, u32[]{:S(2)}) collective-permute-start(bf16[192,3072]{1,0:T(8,128)(2,1)} %get-tuple-element.246), channel_id=1, source_target_pairs={{0,1},{1,0},{2,3},{3,2},{4,5},{5,4},{6,7},{7,6},{8,9},{9,8},{10,11... | collective-permute-start | bytes 3538952 | tf_op jit(solution)/shard_map/ppermute | solution.py:184
  287.3 27.2 %collective-permute-start.15 = (bf16[192,3072]{1,0:T(8,128)(2,1)}, bf16[192,3072]{1,0:T(8,128)(2,1)}, u32[]{:S(2)}, u32[]{:S(2)}) collective-permute-start(bf16[192,3072]{1,0:T(8,128)(2,1)} %get-tuple-element.247), channel_id=1, source_target_pairs={{0,1},{1,0},{2,3},{3,2},{4,5},{5,4},{6,7},{7,6},{8,9},{9,8},{10,11... | collective-permute-start | bytes 3538952 | tf_op jit(solution)/shard_map/ppermute | solution.py:184
  311.4 38.7 %collective-permute-start.30 = (bf16[2,512,384]{2,1,0:T(8,128)(2,1)}, bf16[2,512,384]{2,1,0:T(8,128)(2,1)}, u32[]{:S(2)}, u32[]{:S(2)}) collective-permute-start(bf16[2,512,384]{2,1,0:T(8,128)(2,1)} %get-tuple-element.167), channel_id=1, source_target_pairs={{0,1},{1,0},{2,3},{3,2},{4,5},{5,4},{6,7},{7,6},{8,9},{9,8},{10,11... | collective-permute-start | bytes 2359304 | tf_op jit(solution)/shard_map/ppermute | solution.py:184
  318.7 29.5 %collective-permute-start.20 = (bf16[192,768]{1,0:T(8,128)(2,1)}, bf16[192,768]{1,0:T(8,128)(2,1)}, u32[]{:S(2)}, u32[]{:S(2)}) collective-permute-start(bf16[192,768]{1,0:T(8,128)(2,1)} %get-tuple-element.138), channel_id=1, source_target_pairs={{0,2},{1,3},{2,0},{3,1},{4,6},{5,7},{6,4},{7,5},{8,10},{9,11},{10,... | collective-permute-start | bytes 884744 | tf_op jit(solution)/shard_map/ppermute | solution.py:184
  340.9 12.1 %collective-permute-start.21 = (bf16[2,512,384]{2,1,0:T(8,128)(2,1)}, bf16[2,512,384]{2,1,0:T(8,128)(2,1)}, u32[]{:S(2)}, u32[]{:S(2)}) collective-permute-start(bf16[2,512,384]{2,1,0:T(8,128)(2,1)} %get-tuple-element.142), channel_id=1, source_target_pairs={{0,1},{1,0},{2,3},{3,2},{4,5},{5,4},{6,7},{7,6},{8,9},{9,8},{10,11... | collective-permute-start | bytes 2359304 | tf_op jit(solution)/shard_map/ppermute | solution.py:184
  341.0 29.2 %collective-permute-start.19 = (bf16[192,3072]{1,0:T(8,128)(2,1)}, bf16[192,3072]{1,0:T(8,128)(2,1)}, u32[]{:S(2)}, u32[]{:S(2)}) collective-permute-start(bf16[192,3072]{1,0:T(8,128)(2,1)} %get-tuple-element.136), channel_id=1, source_target_pairs={{0,2},{1,3},{2,0},{3,1},{4,6},{5,7},{6,4},{7,5},{8,10},{9,11},{10,... | collective-permute-start | bytes 3538952 | tf_op jit(solution)/shard_map/ppermute | solution.py:184
  347.7 46.8 %collective-permute-start.27 = (bf16[2,512,384]{2,1,0:T(8,128)(2,1)}, bf16[2,512,384]{2,1,0:T(8,128)(2,1)}, u32[]{:S(2)}, u32[]{:S(2)}) collective-permute-start(bf16[2,512,384]{2,1,0:T(8,128)(2,1)} %add_convert_fusion.12), channel_id=1, source_target_pairs={{0,2},{1,3},{2,0},{3,1},{4,6},{5,7},{6,4},{7,5},{8,10},{9,11},{10,... | collective-permute-start | bytes 2359304 | tf_op jit(solution)/shard_map/ppermute | solution.py:184
  348.2 8.6 %collective-permute-start.22 = (bf16[2,512,384]{2,1,0:T(8,128)(2,1)}, bf16[2,512,384]{2,1,0:T(8,128)(2,1)S(1)}, u32[]{:S(2)}, u32[]{:S(2)}) collective-permute-start(bf16[2,512,384]{2,1,0:T(8,128)(2,1)} %get-tuple-element.144), channel_id=1, source_target_pairs={{0,1},{1,0},{2,3},{3,2},{4,5},{5,4},{6,7},{7,6},{8,9},{9,8},{10,11... | collective-permute-start | bytes 2359304 | tf_op jit(solution)/shard_map/ppermute | solution.py:184
  350.0 46.4 %collective-permute-start.29 = (bf16[2,512,384]{2,1,0:T(8,128)(2,1)}, bf16[2,512,384]{2,1,0:T(8,128)(2,1)}, u32[]{:S(2)}, u32[]{:S(2)}) collective-permute-start(bf16[2,512,384]{2,1,0:T(8,128)(2,1)} %get-tuple-element.165), channel_id=1, source_target_pairs={{0,1},{1,0},{2,3},{3,2},{4,5},{5,4},{6,7},{7,6},{8,9},{9,8},{10,11... | collective-permute-start | bytes 2359304 | tf_op jit(solution)/shard_map/ppermute | solution.py:184
  353.0 50.9 %collective-permute-start.31 = (bf16[2,512,384]{2,1,0:T(8,128)(2,1)}, bf16[2,512,384]{2,1,0:T(8,128)(2,1)}, u32[]{:S(2)}, u32[]{:S(2)}) collective-permute-start(bf16[2,512,384]{2,1,0:T(8,128)(2,1)} %add_convert_fusion.8), channel_id=1, source_target_pairs={{0,2},{1,3},{2,0},{3,1},{4,6},{5,7},{6,4},{7,5},{8,10},{9,11},{10,... | collective-permute-start | bytes 2359304 | tf_op jit(solution)/shard_map/ppermute | solution.py:184
  357.9 62.4 %collective-permute-start.28 = (bf16[2,512,384]{2,1,0:T(8,128)(2,1)}, bf16[2,512,384]{2,1,0:T(8,128)(2,1)}, u32[]{:S(2)}, u32[]{:S(2)}) collective-permute-start(bf16[2,512,384]{2,1,0:T(8,128)(2,1)} %add_convert_fusion.16), channel_id=1, source_target_pairs={{0,2},{1,3},{2,0},{3,1},{4,6},{5,7},{6,4},{7,5},{8,10},{9,11},{10,... | collective-permute-start | bytes 2359304 | tf_op jit(solution)/shard_map/ppermute | solution.py:184
  394.4 27.4 %collective-permute-start.23 = (bf16[2,512,384]{2,1,0:T(8,128)(2,1)}, bf16[2,512,384]{2,1,0:T(8,128)(2,1)}, u32[]{:S(2)}, u32[]{:S(2)}) collective-permute-start(bf16[2,512,384]{2,1,0:T(8,128)(2,1)} %get-tuple-element.149), channel_id=1, source_target_pairs={{0,1},{1,0},{2,3},{3,2},{4,5},{5,4},{6,7},{7,6},{8,9},{9,8},{10,11... | collective-permute-start | bytes 2359304 | tf_op jit(solution)/shard_map/ppermute | solution.py:184
  395.9 28.2 %collective-permute-start.24 = (bf16[2,512,384]{2,1,0:T(8,128)(2,1)}, bf16[2,512,384]{2,1,0:T(8,128)(2,1)}, u32[]{:S(2)}, u32[]{:S(2)}) collective-permute-start(bf16[2,512,384]{2,1,0:T(8,128)(2,1)} %get-tuple-element.151), channel_id=1, source_target_pairs={{0,1},{1,0},{2,3},{3,2},{4,5},{5,4},{6,7},{7,6},{8,9},{9,8},{10,11... | collective-permute-start | bytes 2359304 | tf_op jit(solution)/shard_map/ppermute | solution.py:184
  426.3 19.3 %collective-permute-start.32 = (bf16[2,512,384]{2,1,0:T(8,128)(2,1)}, bf16[2,512,384]{2,1,0:T(8,128)(2,1)}, u32[]{:S(2)}, u32[]{:S(2)}) collective-permute-start(bf16[2,512,384]{2,1,0:T(8,128)(2,1)} %add_convert_fusion.14), channel_id=1, source_target_pairs={{0,2},{1,3},{2,0},{3,1},{4,6},{5,7},{6,4},{7,5},{8,10},{9,11},{10,... | collective-permute-start | bytes 2359304 | tf_op jit(solution)/shard_map/ppermute | solution.py:184
  457.1 12.6 %collective-permute-start.40 = (bf16[192,2304]{1,0:T(8,128)(2,1)}, bf16[192,2304]{1,0:T(8,128)(2,1)}, u32[]{:S(2)}, u32[]{:S(2)}) collective-permute-start(bf16[192,2304]{1,0:T(8,128)(2,1)} %get-tuple-element.257), channel_id=1, source_target_pairs={{0,1},{1,0},{2,3},{3,2},{4,5},{5,4},{6,7},{7,6},{8,9},{9,8},{10,11... | collective-permute-start | bytes 2654216 | tf_op jit(solution)/shard_map/ppermute | solution.py:184
  469.2 5.5 collective-permute-start.39
  472.2 21.9 %collective-permute-start.41 = (bf16[192,2304]{1,0:T(8,128)(2,1)}, bf16[192,2304]{1,0:T(8,128)(2,1)}, u32[]{:S(2)}, u32[]{:S(2)}) collective-permute-start(bf16[192,2304]{1,0:T(8,128)(2,1)} %fusion.26), channel_id=1, source_target_pairs={{0,2},{1,3},{2,0},{3,1},{4,6},{5,7},{6,4},{7,5},{8,10},{9,11},{10,... | collective-permute-start | bytes 2654216 | tf_op jit(solution)/shard_map/ppermute | solution.py:184
  474.2 35.5 %collective-permute-start.34 = (bf16[16,2304]{1,0:T(8,128)(2,1)S(1)}, bf16[16,2304]{1,0:T(8,128)(2,1)S(1)}, u32[]{:S(2)}, u32[]{:S(2)}) collective-permute-start(bf16[16,2304]{1,0:T(8,128)(2,1)S(1)} %get-tuple-element.271), channel_id=1, source_target_pairs={{0,1},{1,0},{2,3},{3,2},{4,5},{5,4},{6,7},{7,6},{8,9},{9,8},{10,11... | collective-permute-start | bytes 221192 | tf_op jit(solution)/shard_map/ppermute | solution.py:184
  474.2 45.7 %collective-permute-start.33 = (bf16[16,2304]{1,0:T(8,128)(2,1)S(1)}, bf16[16,2304]{1,0:T(8,128)(2,1)S(1)}, u32[]{:S(2)}, u32[]{:S(2)}) collective-permute-start(bf16[16,2304]{1,0:T(8,128)(2,1)S(1)} %get-tuple-element.270), channel_id=1, source_target_pairs={{0,1},{1,0},{2,3},{3,2},{4,5},{5,4},{6,7},{7,6},{8,9},{9,8},{10,11... | collective-permute-start | bytes 221192 | tf_op jit(solution)/shard_map/ppermute | solution.py:184
  496.2 11.4 %collective-permute-start.42 = (bf16[96,2304]{1,0:T(8,128)(2,1)S(1)}, bf16[96,2304]{1,0:T(8,128)(2,1)S(1)}, u32[]{:S(2)}, u32[]{:S(2)}) collective-permute-start(bf16[96,2304]{1,0:T(8,128)(2,1)S(1)} %dynamic-slice_bitcast_fusion.6), channel_id=1, source_target_pairs={{0,4},{4,0},{8,12},{12,8},{16,20},{20,16},{24,28},{28,24},{1,5},{5... | collective-permute-start | bytes 1327112 | tf_op jit(solution)/shard_map/ppermute | solution.py:264
  507.8 9.7 %collective-permute-start.43 = (bf16[48,2304]{1,0:T(8,128)(2,1)S(1)}, bf16[48,2304]{1,0:T(8,128)(2,1)S(1)}, u32[]{:S(2)}, u32[]{:S(2)}) collective-permute-start(bf16[48,2304]{1,0:T(8,128)(2,1)S(1)} %dynamic-slice_bitcast_fusion.9), channel_id=1, source_target_pairs={{0,8},{4,12},{8,0},{12,4},{16,24},{20,28},{24,16},{28,20},{1,9},{5... | collective-permute-start | bytes 663560 | tf_op jit(solution)/shard_map/ppermute | solution.py:264
  509.6 10.3 %collective-permute-start.35 = (bf16[16,2304]{1,0:T(8,128)(2,1)S(1)}, bf16[16,2304]{1,0:T(8,128)(2,1)S(1)}, u32[]{:S(2)}, u32[]{:S(2)}) collective-permute-start(bf16[16,2304]{1,0:T(8,128)(2,1)S(1)} %fusion.35), channel_id=1, source_target_pairs={{0,2},{1,3},{2,0},{3,1},{4,6},{5,7},{6,4},{7,5},{8,10},{9,11},{10,... | collective-permute-start | bytes 221192 | tf_op jit(solution)/shard_map/ppermute | solution.py:184
  517.5 7.8 %collective-permute-start.44 = (bf16[24,2304]{1,0:T(8,128)(2,1)S(1)}, bf16[24,2304]{1,0:T(8,128)(2,1)S(1)}, u32[]{:S(2)}, u32[]{:S(2)}) collective-permute-start(bf16[24,2304]{1,0:T(8,128)(2,1)S(1)} %dynamic-slice_bitcast_fusion.10), channel_id=1, source_target_pairs={{0,16},{4,20},{8,24},{12,28},{16,0},{20,4},{24,8},{28,12},{1,17},{... | collective-permute-start | bytes 331784 | tf_op jit(solution)/shard_map/ppermute | solution.py:264
  520.0 5.7 %collective-permute-start.36 = (bf16[16,2304]{1,0:T(8,128)(2,1)S(1)}, bf16[16,2304]{1,0:T(8,128)(2,1)S(1)}, u32[]{:S(2)}, u32[]{:S(2)}) collective-permute-start(bf16[16,2304]{1,0:T(8,128)(2,1)S(1)} %add_convert_fusion.22), channel_id=1, source_target_pairs={{0,4},{4,0},{8,12},{12,8},{16,20},{20,16},{24,28},{28,24},{1,5},{5... | collective-permute-start | bytes 221192 | tf_op jit(solution)/shard_map/ppermute | solution.py:264
  525.3 7.9 %collective-permute-start.45 = (bf16[24,2304]{1,0:T(8,128)(2,1)S(1)}, bf16[24,2304]{1,0:T(8,128)(2,1)S(1)}, u32[]{:S(2)}, u32[]{:S(2)}) collective-permute-start(bf16[24,2304]{1,0:T(8,128)(2,1)S(1)} %fusion.34), channel_id=1, source_target_pairs={{0,16},{4,20},{8,24},{12,28},{16,0},{20,4},{24,8},{28,12},{1,17},{... | collective-permute-start | bytes 331784 | tf_op jit(solution)/shard_map/ppermute | solution.py:264
  525.7 7.6 %collective-permute-start.37 = (bf16[16,2304]{1,0:T(8,128)(2,1)S(1)}, bf16[16,2304]{1,0:T(8,128)(2,1)S(1)}, u32[]{:S(2)}, u32[]{:S(2)}) collective-permute-start(bf16[16,2304]{1,0:T(8,128)(2,1)S(1)} %add_convert_fusion.21), channel_id=1, source_target_pairs={{0,8},{4,12},{8,0},{12,4},{16,24},{20,28},{24,16},{28,20},{1,9},{5... | collective-permute-start | bytes 221192 | tf_op jit(solution)/shard_map/ppermute | solution.py:264
  533.3 8.9 %collective-permute-start.46 = (bf16[48,2304]{1,0:T(8,128)(2,1)S(1)}, bf16[48,2304]{1,0:T(8,128)(2,1)S(1)}, u32[]{:S(2)}, u32[]{:S(2)}) collective-permute-start(bf16[48,2304]{1,0:T(8,128)(2,1)S(1)} %maximum_select_fusion.2), channel_id=1, source_target_pairs={{0,8},{4,12},{8,0},{12,4},{16,24},{20,28},{24,16},{28,20},{1,9},{5... | collective-permute-start | bytes 663560 | tf_op jit(solution)/shard_map/ppermute | solution.py:264
  533.4 10.5 %collective-permute-start.38 = (bf16[16,2304]{1,0:T(8,128)(2,1)S(1)}, bf16[16,2304]{1,0:T(8,128)(2,1)S(1)}, u32[]{:S(2)}, u32[]{:S(2)}) collective-permute-start(bf16[16,2304]{1,0:T(8,128)(2,1)S(1)} %add_convert_fusion.20), channel_id=1, source_target_pairs={{0,16},{4,20},{8,24},{12,28},{16,0},{20,4},{24,8},{28,12},{1,17},{... | collective-permute-start | bytes 221192 | tf_op jit(solution)/shard_map/ppermute | solution.py:264
  542.3 11.2 %collective-permute-start.47 = (bf16[96,2304]{1,0:T(8,128)(2,1)S(1)}, bf16[96,2304]{1,0:T(8,128)(2,1)S(1)}, u32[]{:S(2)}, u32[]{:S(2)}) collective-permute-start(bf16[96,2304]{1,0:T(8,128)(2,1)S(1)} %maximum_select_fusion.1), channel_id=1, source_target_pairs={{0,4},{4,0},{8,12},{12,8},{16,20},{20,16},{24,28},{28,24},{1,5},{5... | collective-permute-start | bytes 1327112 | tf_op jit(solution)/shard_map/ppermute | solution.py:264
  (64 other events, 548.1 us)
Sparse Core Ops, SparseCore 0:
  9.6 33.4 all-gather.6
  74.8 23.8 all-gather.8
  100.2 57.7 all-gather.10
  159.4 37.4 all-gather.12
  396.6 117.7 all-reduce.3

commit v4 on v3

--- a/solution.py
+++ b/solution.py
@@ -235,7 +235,7 @@
     packed = jnp.concatenate([g.reshape(parts, -1) for g in grads], axis=1).astype(bf)
     rows = -(-packed.shape[1] // (16 * columns)) * 16
     packed = jnp.pad(packed, ((0, 0), (0, rows * columns - packed.shape[1])))
-    mine = reduce_chip(reduce_core(matrix.astype(bf)))
+    mine = reduce_chip(reduce_core(matrix))
     extra = reduce_relative(relative_rows(packed.reshape(parts, rows, columns)))
     vector = sum_small(extra).reshape(-1)
     total = finish(mine, 1)
@@ -364,6 +364,8 @@
     fall, grad_up = tie(fall, grad_up)
     fall = reduce_chip(fall)
     grad_w_rise = tn(mid_low, grad_up)
+    low_rise, grad_up = tie(grad_w_rise.astype(bf), grad_up)
+    rise = reduce_core(low_rise)
     grad_mid, grad_gain_two, grad_shift_two = pull_two(nt(grad_up, w_rise))
     grad_hidden = grad_y + grad_mid
     grad_a = grad_hidden.astype(bf)
@@ -371,8 +373,8 @@
     grad_b_mix = jnp.sum(grad_a.astype(f32), axis=0)
     grad_mixed = nt(grad_a, w_mix).astype(bf)
 
-    grad_mixed, *rest = lax.optimization_barrier((grad_mixed, grad_w_rise.astype(bf), grad_w_mix.astype(bf)))
-    rise, out_grad = reduce_core(rest[0]), reduce_core(rest[1])
+    (rise, low_out), grad_mixed = tie((rise, grad_w_mix.astype(bf)), grad_mixed)
+    rise, out_grad = reduce_chip(rise), reduce_core(low_out)
 
     halves, grads_q = [], []
     for i, (m, first) in enumerate(units):
@@ -381,8 +383,8 @@
         if i >= 2:
             halves[i - 2], grad_out = tie(halves[i - 2], grad_out)
         if i == 1:
-            (fall, rise, out_grad), grad_out = tie((fall, rise, out_grad), grad_out)
-            rise, out_grad = reduce_chip(rise), reduce_chip(out_grad)
+            (fall, out_grad), grad_out = tie((fall, out_grad), grad_out)
+            out_grad = reduce_chip(out_grad)
         if i == 3:
             (fall, rise, out_grad), grad_out = tie((fall, rise, out_grad), grad_out)
             wide = [lax.psum(part, "dp") for part in (fall, rise, out_grad)]
@@ -407,13 +409,14 @@
     grad_qkv = lax.optimization_barrier(grad_qkv)
     wide = [part.astype(f32) for part in wide]
     grad_w_proj = tn(normed_low, grad_qkv)
+    low_proj, grad_qkv = tie(grad_w_proj.astype(bf), grad_qkv)
     sums = jnp.sum(grad_qkv.astype(f32), axis=0)
     grad_b_proj = jnp.concatenate([sums[:width], sums[2 * width :]])
     grad_norm_in, grad_gain_one, grad_shift_one = pull_one(nt(grad_qkv, w_proj))
     input_grad = (grad_hidden + grad_norm_in).astype(bf)
 
     last, small = reduce_last(
-        grad_w_proj,
+        low_proj,
         (grad_gain_one, grad_shift_one, grad_b_proj, grad_b_mix, grad_gain_two, grad_shift_two, grad_b_rise, grad_b_fall),
         vectors,
     )

time: 568 us -> 551 us (0.970)
  waiting for transfers between devices: 169 us -> 155 us
    ppermute x39, waiting for transfers between devices: 120 us -> 94.2 us  [swap(): return lax.ppermute(x, 'band', [(i, i ^ flip) for i in range(parts)])]
    ppermute x9, waiting for transfers between devices: 28.2 us -> 39.8 us  [trade(): return lax.ppermute(x, 'dp', [(i, i ^ flip) for i in range(size)])]
    unnamed x134 -> x132, local copies, waits for them, and re-layouts: 12.6 us -> 14.6 us
  transfers between devices with their start and end apart: 53 -> 53, of which waited for: 22 -> 18; matrix products, arithmetic and copies ran while one was open for 26% -> 31% of each run, Pallas kernels for 21% -> 26%
where the time goes in v4:
time: 551 us; the launch traced here: 545 us
  waiting for transfers between devices  155 us (28%)
  Pallas kernels  139 us (25%)
  other arithmetic  80.1 us (15%)
  matrix products  79.5 us (14%)
  local copies, waits for them, and re-layouts  40.3 us (7%)
  starting transfers between devices  30 us (5%)
  between operations  15.2 us (3%)
  blocking collectives  6.24 us (1%)
    ppermute x39, waiting for transfers between devices, swap(): return lax.ppermute(x, 'band', [(i, i ^ flip) for i in range(parts)])  94.2 us
    pallas_call x4, Pallas kernels, attn_bwd(): pl.pallas_call(functools.partial(bwd_kernel, tq=min(tq, n), parts=parts),...  86.4 us
    pallas_call x4, Pallas kernels, attn_fwd(): pl.pallas_call(functools.partial(fwd_kernel, tq=min(tq, n), parts=parts),...  52.9 us
    convert_element_type x21, other arithmetic, fold(): (near.astype(f32) + swap(far, flip).astype(f32)).astype(bf)  44.4 us
    ppermute x9, waiting for transfers between devices, trade(): return lax.ppermute(x, 'dp', [(i, i ^ flip) for i in range(size)])  39.8 us
    dot_general x4, matrix products, nn(): lax.dot_general(a, b, (((1,), (0,)), ((), ())), preferred_element_type=f32)  33 us
    dot_general x4, matrix products, nt(): lax.dot_general(a, b, (((1,), (1,)), ((), ())), preferred_element_type=f32)  28.5 us
    all_gather x4, waiting for transfers between devices, gather_matrix(): return lax.all_gather(shard, 'band', axis=0, tiled=True)  19.3 us
  transfers between devices with their start and end apart: 53, of which 18 were waited for; matrix products, arithmetic and copies ran while one was open for 31% of the time, Pallas kernels for 26%

profile of v4, /device:TPU:0, one launch (start us, length us, event | category | flops | bytes accessed | tf_op | source)
XLA Modules:
  0.0 545.3 jit_solution(11375723850275691257)
XLA Ops:
  8.0 5.5 %concatenate.60 = bf16[2304]{0:T(1024)(128)(2,1)S(1)} concatenate(bf16[192]{0:T(256)(128)(2,1)} %param.18, bf16[192]{0:T(256)(128)(2,1)} %param.19, bf16[384]{0:T(512)(128)(2,1)} %param.21, bf16[192]{0:T(256)(128)(2,1)} %param.23, bf16[192]{0:T(256)(128)(2,1)} %param.24, bf16[192]{0:T(256)(128)(2,1)} %param.25, bf16[768]{0:T(1024)(128)(2,1)} %param.27, bf16[192]{0:T(256)(128)(2,1)} %param.29), dimensions={0} | concatenate | bytes 9216 | tf_op jit(solution)/shard_map/concatenate | solution.py:214
  13.4 6.2 %all-gather.1 = bf16[4,1,2304]{2,1,0:T(2,128)(2,1)S(1)} all-gather(bf16[1,1,2304]{2,1,0:T(2,128)(2,1)S(1)} %reshape.372), channel_id=2, replica_groups=mesh['dp'=8,'band'=4] {'band'}, dimensions={0}, use_global_device_ids=true | all-gather | bytes 23040 | tf_op jit(solution)/shard_map/all_gather | solution.py:215
  23.8 19.3 %all-gather.7.cloned.1.call-done = bf16[768,2304]{1,0:T(8,128)(2,1)} async-done(((bf16[192,2304]{1,0:T(8,128)(2,1)}), bf16[768,2304]{1,0:T(8,128)(2,1)}) %all-gather.7.cloned.1.call-update) | async-done | bytes 3538960 | tf_op jit(solution)/shard_map/all_gather | solution.py:250
  43.1 5.8 %fusion.55 = (bf16[1024,2304]{1,0:T(8,128)(2,1)S(1)}, f32[1024,2304]{1,0:T(8,128)S(1)}) fusion(bf16[1024,768]{1,0:T(8,128)(2,1)S(1)} %fusion.15, bf16[768,2304]{1,0:T(8,128)(2,1)} %all-gather.7.cloned.1.call-done), kind=kOutput, calls=%fused_computation.169 | convolution fusion | flops 3626237952 | bytes 19267584 | tf_op jit(solution)/shard_map/dot_general | solution.py:16
  53.7 18.5 %collective-permute-done.1.refs_3_.refs_7_.refs_6_.refs_10_ = bf16[512,768]{1,0:T(8,128)(2,1)S(1)} collective-permute-done((bf16[512,768]{1,0:T(8,128)(2,1)S(1)}, bf16[512,768]{1,0:T(8,128)(2,1)S(1)}, u32[]{:S(2)}, u32[]{:S(2)}) %collective-permute-start.1) | collective-permute-done | bytes 786464 | tf_op jit(solution)/shard_map/ppermute | solution.py:184
  78.4 2.5 pad_maximum_fusion.3
  82.5 13.2 %attn_fwd.4 = (bf16[512,384]{1,0:T(8,128)(2,1)}, f32[512,384]{1,0:T(8,128)}) custom-call(bf16[512,768]{1,0:T(8,128)(2,1)} %get-tuple-element.266.refs_0_, s32[512,1]{1,0:T(8,128)} %copy.41.refs_1_.refs_4_, bf16[512,768]{1,0:T(8,128)(2,1)} %copy-done.22, bf16[512,768]{1,0:T(8,128)(2,1)} %copy-done.49, bf16[512,768]{1,0:T(8,128)(2,1)} %copy-done.50, ...), custom_call_target="tpu_custom_call" | custom-call | flops 6442450944 | bytes 4718592 | tf_op jit(solution)/shard_map/attn_fwd/pallas_call | solution.py:89
  95.8 11.4 %collective-permute-done.refs_3_.refs_7_.refs_6_.refs_10_ = bf16[512,768]{1,0:T(8,128)(2,1)} collective-permute-done((bf16[512,768]{1,0:T(8,128)(2,1)}, bf16[512,768]{1,0:T(8,128)(2,1)}, u32[]{:S(2)}, u32[]{:S(2)}) %collective-permute-start) | collective-permute-done | bytes 786464 | tf_op jit(solution)/shard_map/ppermute | solution.py:184
  112.5 13.2 %attn_fwd.5 = (bf16[512,384]{1,0:T(8,128)(2,1)}, f32[512,384]{1,0:T(8,128)}) custom-call(bf16[512,768]{1,0:T(8,128)(2,1)} %get-tuple-element.266.refs_0_, s32[512,1]{1,0:T(8,128)} %copy.41.refs_1_.refs_4_, bf16[512,768]{1,0:T(8,128)(2,1)} %get-tuple-element.114.refs_2_.refs_6_.refs_5_.refs_9_, ...), custom_call_target="tpu_custom_call" | custom-call | flops 6442450944 | bytes 4718592 | tf_op jit(solution)/shard_map/attn_fwd/pallas_call | solution.py:89
  125.7 18.5 %collective-permute-done.4.refs_3_.refs_7_.refs_6_.refs_10_ = bf16[512,768]{1,0:T(8,128)(2,1)S(1)} collective-permute-done((bf16[512,768]{1,0:T(8,128)(2,1)S(1)}, bf16[512,768]{1,0:T(8,128)(2,1)S(1)}, u32[]{:S(2)}, u32[]{:S(2)}) %collective-permute-start.4) | collective-permute-done | bytes 786464 | tf_op jit(solution)/shard_map/ppermute | solution.py:184
  147.9 13.3 %attn_fwd.6 = (bf16[512,384]{1,0:T(8,128)(2,1)}, f32[512,384]{1,0:T(8,128)}) custom-call(bf16[512,768]{1,0:T(8,128)(2,1)} %get-tuple-element.267.refs_0_, s32[512,1]{1,0:T(8,128)} %copy.43.refs_1_.refs_4_, bf16[512,768]{1,0:T(8,128)(2,1)} %get-tuple-element.119.refs_2_.refs_6_.refs_5_.refs_9_, bf16[512,768]{1,0:T(8,128)(2,1)} %copy-done.48, ...), custom_call_target="tpu_custom_call" | custom-call | flops 6442450944 | bytes 4718592 | tf_op jit(solution)/shard_map/attn_fwd/pallas_call | solution.py:89
  161.2 8.2 %collective-permute-done.7.refs_3_.refs_7_.refs_6_.refs_10_ = bf16[512,768]{1,0:T(8,128)(2,1)} collective-permute-done((bf16[512,768]{1,0:T(8,128)(2,1)}, bf16[512,768]{1,0:T(8,128)(2,1)}, u32[]{:S(2)}, u32[]{:S(2)}) %collective-permute-start.7) | collective-permute-done | bytes 786464 | tf_op jit(solution)/shard_map/ppermute | solution.py:184
  174.2 13.2 %attn_fwd.7 = (bf16[512,384]{1,0:T(8,128)(2,1)}, f32[512,384]{1,0:T(8,128)}) custom-call(bf16[512,768]{1,0:T(8,128)(2,1)} %get-tuple-element.267.refs_0_, s32[512,1]{1,0:T(8,128)} %copy.43.refs_1_.refs_4_, bf16[512,768]{1,0:T(8,128)(2,1)} %get-tuple-element.123.refs_2_.refs_6_.refs_5_.refs_9_, ...), custom_call_target="tpu_custom_call" | custom-call | flops 6442450944 | bytes 4718592 | tf_op jit(solution)/shard_map/attn_fwd/pallas_call | solution.py:89
  187.4 3.3 fusion.56
  192.9 14.2 %multiply_convert_fusion = (bf16[1024,3072]{1,0:T(8,128)(2,1)S(1)}, f32[1024,3072]{1,0:T(8,128)}) fusion(f32[3072]{0:T(1024)S(1)} %reshape.351, bf16[768,3072]{1,0:T(8,128)(2,1)} %all-gather.11.cloned.1.call-done, f32[1024,768]{1,0:T(8,128)} %copy-done.6, f32[768]{0:T(1024)S(1)} %reshape.350, f32[768]{0:T(1024)S(1)} %reshape.349, f32[1024]{0:T(1024)S(1)} %fusion.38, ...), kind=kOutput, calls=%fused_computation.9 | convolution fusion | flops 4867227648 | bytes 26765312 | tf_op jit(solution)/shard_map/dot_general | solution.py:16
  207.1 5.5 %convolution_convert_fusion.1 = bf16[3072,768]{1,0:T(8,128)(2,1)S(1)} fusion(bf16[1024,3072]{1,0:T(8,128)(2,1)S(1)} %get-tuple-element.156, bf16[1024,768]{1,0:T(8,128)(2,1)S(1)} %copy-done.17), kind=kOutput, calls=%fused_computation.11 | convolution fusion | flops 4834197504 | bytes 12582912 | tf_op jit(solution)/shard_map/dot_general | solution.py:19
  216.8 14.4 %fusion.6 = bf16[1024,3072]{1,0:T(8,128)(2,1)S(1)} fusion(f32[1024,3072]{1,0:T(8,128)} %get-tuple-element.303, f32[3072]{0:T(1024)S(1)} %reshape.351, bf16[1024,768]{1,0:T(8,128)(2,1)S(1)} %copy-done.17, bf16[3072,768]{1,0:T(8,128)(2,1)} %all-gather.13.cloned.1.call-done), kind=kOutput, calls=%fused_computation.8 | convolution fusion | flops 4897898496 | bytes 25178112 | tf_op jit(solution)/shard_map/dot_general | solution.py:13
  231.2 5.8 %fusion.23 = (bf16[768,768]{1,0:T(8,128)(2,1)}, bf16[768,768]{1,0:T(8,128)(2,1)}) fusion(bf16[768,768]{1,0:T(8,128)(2,1)} %collective-permute-done.13, bf16[4,768,768]{2,1,0:T(8,128)(2,1)S(1)} %bitcast.176, s32[]{:T(128)S(6)} %select_n.92, bf16[768,768]{1,0:T(8,128)(2,1)} %collective-permute-done.12, s32[]{:T(128)S(6)} %select_n.90), kind=kLoop, calls=%fused_computation.50 | loop fusion | flops 4718592 | bytes 7077896 | tf_op jit(solution)/shard_map/convert_element_type | solution.py:201
  237.8 6.9 %convolution_convert_fusion = bf16[768,3072]{1,0:T(8,128)(2,1)S(1)} fusion(bf16[1024,3072]{1,0:T(8,128)(2,1)S(1)} %fusion.6, f32[1024,768]{1,0:T(8,128)S(1)} %copy-done.7, f32[768]{0:T(1024)S(1)} %reshape.350, f32[768]{0:T(1024)S(1)} %reshape.349, f32[1024]{0:T(1024)S(1)} %fusion.38, f32[1024]{0:T(1024)S(1)} %broadcast_multiply_fusion), kind=kOutput, calls=%fused_computation.10 | convolution fusion | flops 4838129664 | bytes 14170112 | tf_op jit(solution)/shard_map/dot_general | solution.py:19
  248.9 5.6 %multiply_reduce_fusion = (bf16[768]{0:T(1024)(128)(2,1)S(1)}, f32[1024]{0:T(1024)S(1)}, bf16[768]{0:T(1024)(128)(2,1)S(1)}, f32[1024,768]{1,0:T(8,128)S(1)}) fusion(f32[1024,768]{1,0:T(8,128)S(1)} %copy-done.7, f32[1024]{0:T(1024)S(1)} %fusion.38, f32[1024]{0:T(1024)S(1)} %broadcast_multiply_fusion, f32[768]{0:T(1024)S(1)} %reshape.349, ...), kind=kOutput, calls=%fused_computation.37 | convolution fusion | flops 4838126592 | bytes 17319936 | tf_op jit(solution)/shard_map/dot_general | solution.py:13
  259.8 2.8 convolution_convert_fusion.3
  264.2 4.7 fusion.21
  272.6 21.5 %attn_bwd.6 = (bf16[512,384]{1,0:T(8,128)(2,1)}, bf16[2,512,384]{2,1,0:T(8,128)(2,1)}, bf16[2,512,384]{2,1,0:T(8,128)(2,1)}, bf16[2,512,384]{2,1,0:T(8,128)(2,1)}, bf16[2,512,384]{2,1,0:T(8,128)(2,1)}) custom-call(bf16[512,768]{1,0:T(8,128)(2,1)} %get-tuple-element.266.refs_0_, bf16[512,768]{1,0:T(8,128)(2,1)} %get-tuple-element.143.refs_1_, ...), custom_call_target="tpu_custom_call" | custom-call | flops 16106127360 | bytes 8650752 | tf_op jit(solution)/shard_map/attn_bwd/pallas_call | solution.py:158
  294.6 2.9 add_convert_fusion.4
  300.2 21.5 %attn_bwd.4 = (bf16[512,384]{1,0:T(8,128)(2,1)}, bf16[2,512,384]{2,1,0:T(8,128)(2,1)}, bf16[2,512,384]{2,1,0:T(8,128)(2,1)}, bf16[2,512,384]{2,1,0:T(8,128)(2,1)}, bf16[2,512,384]{2,1,0:T(8,128)(2,1)}) custom-call(bf16[512,768]{1,0:T(8,128)(2,1)} %get-tuple-element.266.refs_0_, bf16[512,768]{1,0:T(8,128)(2,1)} %get-tuple-element.143.refs_1_, ...), custom_call_target="tpu_custom_call" | custom-call | flops 16106127360 | bytes 8650752 | tf_op jit(solution)/shard_map/attn_bwd/pallas_call | solution.py:158
  328.1 21.6 %attn_bwd.7 = (bf16[512,384]{1,0:T(8,128)(2,1)}, bf16[2,512,384]{2,1,0:T(8,128)(2,1)}, bf16[2,512,384]{2,1,0:T(8,128)(2,1)}, bf16[2,512,384]{2,1,0:T(8,128)(2,1)}, bf16[2,512,384]{2,1,0:T(8,128)(2,1)}) custom-call(bf16[512,768]{1,0:T(8,128)(2,1)} %get-tuple-element.267.refs_0_, bf16[512,768]{1,0:T(8,128)(2,1)} %get-tuple-element.166.refs_1_, ...), custom_call_target="tpu_custom_call" | custom-call | flops 16106127360 | bytes 8650752 | tf_op jit(solution)/shard_map/attn_bwd/pallas_call | solution.py:158
  350.4 2.5 add_convert_fusion.17
  352.9 2.5 add_convert_fusion.16
  356.1 2.7 add_convert_fusion.3
  358.8 21.8 %attn_bwd.5 = (bf16[512,384]{1,0:T(8,128)(2,1)}, bf16[2,512,384]{2,1,0:T(8,128)(2,1)}, bf16[2,512,384]{2,1,0:T(8,128)(2,1)}, bf16[2,512,384]{2,1,0:T(8,128)(2,1)}, bf16[2,512,384]{2,1,0:T(8,128)(2,1)}) custom-call(bf16[512,768]{1,0:T(8,128)(2,1)} %get-tuple-element.267.refs_0_, bf16[512,768]{1,0:T(8,128)(2,1)} %get-tuple-element.166.refs_1_, ...), custom_call_target="tpu_custom_call" | custom-call | flops 16106127360 | bytes 8650752 | tf_op jit(solution)/shard_map/attn_bwd/pallas_call | solution.py:158
  381.7 2.3 add_convert_fusion.8
  392.8 9.6 %add_convert_fusion.1 = bf16[1024,768]{1,0:T(8,128)(2,1)} fusion(f32[1024,768]{1,0:T(8,128)S(1)} %copy-done.8, bf16[1024,3072]{1,0:T(8,128)(2,1)} %copy-done.51, bf16[3072,768]{1,0:T(8,128)(2,1)} %all-gather.13.cloned.1.call-done, f32[768]{0:T(1024)S(1)} %copy-done.46), kind=kOutput, calls=%fused_computation.39 | convolution fusion | flops 4834197504 | bytes 15731712 | tf_op jit(solution)/shard_map/dot_general | solution.py:16
  402.4 4.4 reduce.7
  409.6 10.8 %collective-permute-done.32 = bf16[2,512,384]{2,1,0:T(8,128)(2,1)} collective-permute-done((bf16[2,512,384]{2,1,0:T(8,128)(2,1)}, bf16[2,512,384]{2,1,0:T(8,128)(2,1)}, u32[]{:S(2)}, u32[]{:S(2)}) %collective-permute-start.32) | collective-permute-done | bytes 786464 | tf_op jit(solution)/shard_map/ppermute | solution.py:184
  424.7 4.2 convolution_convert_fusion.2
  432.1 5.7 %fusion.44 = (bf16[768]{0:T(1024)(128)(2,1)S(1)}, f32[1024]{0:T(1024)S(1)}, f32[1024,768]{1,0:T(8,128)}) fusion(f32[768]{0:T(1024)S(1)} %copy-done.33, f32[1024]{0:T(1024)S(1)} %bitcast.200, bf16[2,1,512,768]{3,2,1,0:T(8,128)(2,1)S(1)} %copy-done.1, bf16[1024,2304]{1,0:T(8,128)(2,1)S(1)} %pad_maximum_fusion, bf16[768,2304]{1,0:T(8,128)(2,1)S(1)} %copy-done.47), kind=kOutput, calls=%fused_computation.159 | convolution fusion | flops 3628595456 | bytes 12988928 | tf_op jit(solution)/shard_map/dot_general | solution.py:13
  437.8 3.1 reduce.5
  440.9 3.0 fusion.16
  444.6 2.6 fusion.26
  449.2 19.9 %collective-permute-done.41 = bf16[192,2304]{1,0:T(8,128)(2,1)} collective-permute-done((bf16[192,2304]{1,0:T(8,128)(2,1)}, bf16[192,2304]{1,0:T(8,128)(2,1)}, u32[]{:S(2)}, u32[]{:S(2)}) %collective-permute-start.41) | collective-permute-done | bytes 884768 | tf_op jit(solution)/shard_map/ppermute | solution.py:184
  472.8 3.9 add_convert_fusion
  476.7 10.3 %collective-permute-done.42 = bf16[96,2304]{1,0:T(8,128)(2,1)S(1)} collective-permute-done((bf16[96,2304]{1,0:T(8,128)(2,1)S(1)}, bf16[96,2304]{1,0:T(8,128)(2,1)S(1)}, u32[]{:S(2)}, u32[]{:S(2)}) %collective-permute-start.42) | collective-permute-done | bytes 442400 | tf_op jit(solution)/shard_map/ppermute | solution.py:264
  490.3 11.1 %collective-permute-done.43 = bf16[48,2304]{1,0:T(8,128)(2,1)S(1)} collective-permute-done((bf16[48,2304]{1,0:T(8,128)(2,1)S(1)}, bf16[48,2304]{1,0:T(8,128)(2,1)S(1)}, u32[]{:S(2)}, u32[]{:S(2)}) %collective-permute-start.43) | collective-permute-done | bytes 221216 | tf_op jit(solution)/shard_map/ppermute | solution.py:264
  503.6 6.0 %collective-permute-done.44 = bf16[24,2304]{1,0:T(8,128)(2,1)S(1)} collective-permute-done((bf16[24,2304]{1,0:T(8,128)(2,1)S(1)}, bf16[24,2304]{1,0:T(8,128)(2,1)S(1)}, u32[]{:S(2)}, u32[]{:S(2)}) %collective-permute-start.44) | collective-permute-done | bytes 110624 | tf_op jit(solution)/shard_map/ppermute | solution.py:264
  512.0 4.9 collective-permute-done.45
  517.0 2.9 collective-permute-start.38
  519.9 6.0 %collective-permute-done.46 = bf16[48,2304]{1,0:T(8,128)(2,1)S(1)} collective-permute-done((bf16[48,2304]{1,0:T(8,128)(2,1)S(1)}, bf16[48,2304]{1,0:T(8,128)(2,1)S(1)}, u32[]{:S(2)}, u32[]{:S(2)}) %collective-permute-start.46) | collective-permute-done | bytes 221216 | tf_op jit(solution)/shard_map/ppermute | solution.py:264
  531.3 2.9 convert_element_type.683
  (324 shorter events, 107.6 us)
Async XLA Ops:
  7.2 35.9 %all-gather.7.cloned.1.call-start = ((), (), s32[]{:S(2)}) async-start(), calls=%async_computation | async-start | bytes 4423680 | tf_op jit(solution)/shard_map/all_gather | solution.py:250
  7.9 179.4 %all-gather.9.cloned.1.call-start = ((), (), s32[]{:S(2)}) async-start(), calls=%async_computation.1 | async-start | bytes 1474560 | tf_op jit(solution)/shard_map/all_gather | solution.py:250
  52.5 19.7 %collective-permute-start.1 = (bf16[512,768]{1,0:T(8,128)(2,1)S(1)}, bf16[512,768]{1,0:T(8,128)(2,1)S(1)}, u32[]{:S(2)}, u32[]{:S(2)}) collective-permute-start(bf16[512,768]{1,0:T(8,128)(2,1)S(1)} %get-tuple-element.106.refs_2_.refs_6_.refs_5_.refs_9_), channel_id=1, source_target_pairs={{0,2},{1,3},{2,0},{3,1},{4,6},{5,7},{6,4},{7,5},{8,10},{9,11},{10,... | collective-permute-start | bytes 2359304 | tf_op jit(solution)/shard_map/ppermute | solution.py:184
  53.5 18.8 %collective-permute-start.2 = (bf16[512,768]{1,0:T(8,128)(2,1)S(1)}, bf16[512,768]{1,0:T(8,128)(2,1)S(1)}, u32[]{:S(2)}, u32[]{:S(2)}) collective-permute-start(bf16[512,768]{1,0:T(8,128)(2,1)S(1)} %get-tuple-element.106.refs_2_.refs_6_.refs_5_.refs_9_), channel_id=1, source_target_pairs={{0,1},{1,0},{2,3},{3,2},{4,5},{5,4},{6,7},{7,6},{8,9},{9,8},{10,11... | collective-permute-start | bytes 2359304 | tf_op jit(solution)/shard_map/ppermute | solution.py:184
  74.7 118.2 %all-gather.11.cloned.1.call-start = ((), (), s32[]{:S(2)}) async-start(), calls=%async_computation.2 | async-start | bytes 5898240 | tf_op jit(solution)/shard_map/all_gather | solution.py:250
  75.4 141.4 %all-gather.13.cloned.1.call-start = ((), (), s32[]{:S(2)}) async-start(), calls=%async_computation.3 | async-start | bytes 5898240 | tf_op jit(solution)/shard_map/all_gather | solution.py:250
  80.9 26.2 %collective-permute-start = (bf16[512,768]{1,0:T(8,128)(2,1)}, bf16[512,768]{1,0:T(8,128)(2,1)}, u32[]{:S(2)}, u32[]{:S(2)}) collective-permute-start(bf16[512,768]{1,0:T(8,128)(2,1)} %get-tuple-element.114.refs_2_.refs_6_.refs_5_.refs_9_), channel_id=1, source_target_pairs={{0,2},{1,3},{2,0},{3,1},{4,6},{5,7},{6,4},{7,5},{8,10},{9,11},{10,... | collective-permute-start | bytes 2359304 | tf_op jit(solution)/shard_map/ppermute | solution.py:184
  107.2 5.4 collective-permute-start.6
  107.7 36.5 %collective-permute-start.4 = (bf16[512,768]{1,0:T(8,128)(2,1)S(1)}, bf16[512,768]{1,0:T(8,128)(2,1)S(1)}, u32[]{:S(2)}, u32[]{:S(2)}) collective-permute-start(bf16[512,768]{1,0:T(8,128)(2,1)S(1)} %copy-done.21), channel_id=1, source_target_pairs={{0,2},{1,3},{2,0},{3,1},{4,6},{5,7},{6,4},{7,5},{8,10},{9,11},{10,... | collective-permute-start | bytes 2359304 | tf_op jit(solution)/shard_map/ppermute | solution.py:184
  144.7 24.8 %collective-permute-start.7 = (bf16[512,768]{1,0:T(8,128)(2,1)}, bf16[512,768]{1,0:T(8,128)(2,1)}, u32[]{:S(2)}, u32[]{:S(2)}) collective-permute-start(bf16[512,768]{1,0:T(8,128)(2,1)} %get-tuple-element.123.refs_2_.refs_6_.refs_5_.refs_9_), channel_id=1, source_target_pairs={{0,2},{1,3},{2,0},{3,1},{4,6},{5,7},{6,4},{7,5},{8,10},{9,11},{10,... | collective-permute-start | bytes 2359304 | tf_op jit(solution)/shard_map/ppermute | solution.py:184
  145.0 384.4 %all-reduce.4.cloned.1.call-start = ((), (), s32[]{:S(2)}) async-start(), calls=%async_computation.4 | async-start | bytes 5308416 | tf_op jit(solution)/shard_map/psum | solution.py:390
  169.4 4.7 collective-permute-start.10
  216.3 14.9 %collective-permute-start.13 = (bf16[768,768]{1,0:T(8,128)(2,1)}, bf16[768,768]{1,0:T(8,128)(2,1)}, u32[]{:S(2)}, u32[]{:S(2)}) collective-permute-start(bf16[768,768]{1,0:T(8,128)(2,1)} %get-tuple-element.256), channel_id=1, source_target_pairs={{0,1},{1,0},{2,3},{3,2},{4,5},{5,4},{6,7},{7,6},{8,9},{9,8},{10,11... | collective-permute-start | bytes 3538952 | tf_op jit(solution)/shard_map/ppermute | solution.py:184
  216.3 14.9 %collective-permute-start.12 = (bf16[768,768]{1,0:T(8,128)(2,1)}, bf16[768,768]{1,0:T(8,128)(2,1)}, u32[]{:S(2)}, u32[]{:S(2)}) collective-permute-start(bf16[768,768]{1,0:T(8,128)(2,1)} %get-tuple-element.257), channel_id=1, source_target_pairs={{0,1},{1,0},{2,3},{3,2},{4,5},{5,4},{6,7},{7,6},{8,9},{9,8},{10,11... | collective-permute-start | bytes 3538952 | tf_op jit(solution)/shard_map/ppermute | solution.py:184
  237.0 57.1 %collective-permute-start.14 = (bf16[768,768]{1,0:T(8,128)(2,1)}, bf16[768,768]{1,0:T(8,128)(2,1)}, u32[]{:S(2)}, u32[]{:S(2)}) collective-permute-start(bf16[768,768]{1,0:T(8,128)(2,1)} %get-tuple-element.132), channel_id=1, source_target_pairs={{0,2},{1,3},{2,0},{3,1},{4,6},{5,7},{6,4},{7,5},{8,10},{9,11},{10,... | collective-permute-start | bytes 3538952 | tf_op jit(solution)/shard_map/ppermute | solution.py:184
  248.3 15.8 %collective-permute-start.16 = (bf16[192,3072]{1,0:T(8,128)(2,1)}, bf16[192,3072]{1,0:T(8,128)(2,1)}, u32[]{:S(2)}, u32[]{:S(2)}) collective-permute-start(bf16[192,3072]{1,0:T(8,128)(2,1)} %get-tuple-element.252), channel_id=1, source_target_pairs={{0,1},{1,0},{2,3},{3,2},{4,5},{5,4},{6,7},{7,6},{8,9},{9,8},{10,11... | collective-permute-start | bytes 3538952 | tf_op jit(solution)/shard_map/ppermute | solution.py:184
  248.3 15.8 %collective-permute-start.15 = (bf16[192,3072]{1,0:T(8,128)(2,1)}, bf16[192,3072]{1,0:T(8,128)(2,1)}, u32[]{:S(2)}, u32[]{:S(2)}) collective-permute-start(bf16[192,3072]{1,0:T(8,128)(2,1)} %get-tuple-element.253), channel_id=1, source_target_pairs={{0,1},{1,0},{2,3},{3,2},{4,5},{5,4},{6,7},{7,6},{8,9},{9,8},{10,11... | collective-permute-start | bytes 3538952 | tf_op jit(solution)/shard_map/ppermute | solution.py:184
  269.6 28.0 %collective-permute-start.18 = (bf16[192,768]{1,0:T(8,128)(2,1)}, bf16[192,768]{1,0:T(8,128)(2,1)S(1)}, u32[]{:S(2)}, u32[]{:S(2)}) collective-permute-start(bf16[192,768]{1,0:T(8,128)(2,1)} %get-tuple-element.274), channel_id=1, source_target_pairs={{0,1},{1,0},{2,3},{3,2},{4,5},{5,4},{6,7},{7,6},{8,9},{9,8},{10,11... | collective-permute-start | bytes 884744 | tf_op jit(solution)/shard_map/ppermute | solution.py:184
  269.6 27.9 %collective-permute-start.17 = (bf16[192,768]{1,0:T(8,128)(2,1)S(1)}, bf16[192,768]{1,0:T(8,128)(2,1)}, u32[]{:S(2)}, u32[]{:S(2)}) collective-permute-start(bf16[192,768]{1,0:T(8,128)(2,1)S(1)} %get-tuple-element.275), channel_id=1, source_target_pairs={{0,1},{1,0},{2,3},{3,2},{4,5},{5,4},{6,7},{7,6},{8,9},{9,8},{10,11... | collective-permute-start | bytes 884744 | tf_op jit(solution)/shard_map/ppermute | solution.py:184
  271.3 84.7 %collective-permute-start.19 = (bf16[192,3072]{1,0:T(8,128)(2,1)}, bf16[192,3072]{1,0:T(8,128)(2,1)}, u32[]{:S(2)}, u32[]{:S(2)}) collective-permute-start(bf16[192,3072]{1,0:T(8,128)(2,1)} %get-tuple-element.140), channel_id=1, source_target_pairs={{0,2},{1,3},{2,0},{3,1},{4,6},{5,7},{6,4},{7,5},{8,10},{9,11},{10,... | collective-permute-start | bytes 3538952 | tf_op jit(solution)/shard_map/ppermute | solution.py:184
  294.0 29.0 %collective-permute-start.25 = (bf16[2,512,384]{2,1,0:T(8,128)(2,1)}, bf16[2,512,384]{2,1,0:T(8,128)(2,1)}, u32[]{:S(2)}, u32[]{:S(2)}) collective-permute-start(bf16[2,512,384]{2,1,0:T(8,128)(2,1)} %get-tuple-element.159), channel_id=1, source_target_pairs={{0,1},{1,0},{2,3},{3,2},{4,5},{5,4},{6,7},{7,6},{8,9},{9,8},{10,11... | collective-permute-start | bytes 2359304 | tf_op jit(solution)/shard_map/ppermute | solution.py:184
  294.1 30.5 %collective-permute-start.26 = (bf16[2,512,384]{2,1,0:T(8,128)(2,1)}, bf16[2,512,384]{2,1,0:T(8,128)(2,1)}, u32[]{:S(2)}, u32[]{:S(2)}) collective-permute-start(bf16[2,512,384]{2,1,0:T(8,128)(2,1)} %get-tuple-element.161), channel_id=1, source_target_pairs={{0,1},{1,0},{2,3},{3,2},{4,5},{5,4},{6,7},{7,6},{8,9},{9,8},{10,11... | collective-permute-start | bytes 2359304 | tf_op jit(solution)/shard_map/ppermute | solution.py:184
  299.4 22.4 %collective-permute-start.20 = (bf16[192,768]{1,0:T(8,128)(2,1)}, bf16[192,768]{1,0:T(8,128)(2,1)S(1)}, u32[]{:S(2)}, u32[]{:S(2)}) collective-permute-start(bf16[192,768]{1,0:T(8,128)(2,1)} %get-tuple-element.142), channel_id=1, source_target_pairs={{0,2},{1,3},{2,0},{3,1},{4,6},{5,7},{6,4},{7,5},{8,10},{9,11},{10,... | collective-permute-start | bytes 884744 | tf_op jit(solution)/shard_map/ppermute | solution.py:184
  321.7 28.1 %collective-permute-start.21 = (bf16[2,512,384]{2,1,0:T(8,128)(2,1)}, bf16[2,512,384]{2,1,0:T(8,128)(2,1)}, u32[]{:S(2)}, u32[]{:S(2)}) collective-permute-start(bf16[2,512,384]{2,1,0:T(8,128)(2,1)} %get-tuple-element.146), channel_id=1, source_target_pairs={{0,1},{1,0},{2,3},{3,2},{4,5},{5,4},{6,7},{7,6},{8,9},{9,8},{10,11... | collective-permute-start | bytes 2359304 | tf_op jit(solution)/shard_map/ppermute | solution.py:184
  321.8 31.1 %collective-permute-start.22 = (bf16[2,512,384]{2,1,0:T(8,128)(2,1)}, bf16[2,512,384]{2,1,0:T(8,128)(2,1)}, u32[]{:S(2)}, u32[]{:S(2)}) collective-permute-start(bf16[2,512,384]{2,1,0:T(8,128)(2,1)} %get-tuple-element.148), channel_id=1, source_target_pairs={{0,1},{1,0},{2,3},{3,2},{4,5},{5,4},{6,7},{7,6},{8,9},{9,8},{10,11... | collective-permute-start | bytes 2359304 | tf_op jit(solution)/shard_map/ppermute | solution.py:184
  326.9 57.1 %collective-permute-start.27 = (bf16[2,512,384]{2,1,0:T(8,128)(2,1)}, bf16[2,512,384]{2,1,0:T(8,128)(2,1)}, u32[]{:S(2)}, u32[]{:S(2)}) collective-permute-start(bf16[2,512,384]{2,1,0:T(8,128)(2,1)} %add_convert_fusion.12), channel_id=1, source_target_pairs={{0,2},{1,3},{2,0},{3,1},{4,6},{5,7},{6,4},{7,5},{8,10},{9,11},{10,... | collective-permute-start | bytes 2359304 | tf_op jit(solution)/shard_map/ppermute | solution.py:184
  349.8 30.9 %collective-permute-start.30 = (bf16[2,512,384]{2,1,0:T(8,128)(2,1)}, bf16[2,512,384]{2,1,0:T(8,128)(2,1)}, u32[]{:S(2)}, u32[]{:S(2)}) collective-permute-start(bf16[2,512,384]{2,1,0:T(8,128)(2,1)} %get-tuple-element.171), channel_id=1, source_target_pairs={{0,1},{1,0},{2,3},{3,2},{4,5},{5,4},{6,7},{7,6},{8,9},{9,8},{10,11... | collective-permute-start | bytes 2359304 | tf_op jit(solution)/shard_map/ppermute | solution.py:184
  349.9 57.7 %collective-permute-start.29 = (bf16[2,512,384]{2,1,0:T(8,128)(2,1)}, bf16[2,512,384]{2,1,0:T(8,128)(2,1)}, u32[]{:S(2)}, u32[]{:S(2)}) collective-permute-start(bf16[2,512,384]{2,1,0:T(8,128)(2,1)} %get-tuple-element.169), channel_id=1, source_target_pairs={{0,1},{1,0},{2,3},{3,2},{4,5},{5,4},{6,7},{7,6},{8,9},{9,8},{10,11... | collective-permute-start | bytes 2359304 | tf_op jit(solution)/shard_map/ppermute | solution.py:184
  355.3 31.3 %collective-permute-start.28 = (bf16[2,512,384]{2,1,0:T(8,128)(2,1)}, bf16[2,512,384]{2,1,0:T(8,128)(2,1)}, u32[]{:S(2)}, u32[]{:S(2)}) collective-permute-start(bf16[2,512,384]{2,1,0:T(8,128)(2,1)} %add_convert_fusion.16), channel_id=1, source_target_pairs={{0,2},{1,3},{2,0},{3,1},{4,6},{5,7},{6,4},{7,5},{8,10},{9,11},{10,... | collective-permute-start | bytes 2359304 | tf_op jit(solution)/shard_map/ppermute | solution.py:184
  380.6 8.0 %collective-permute-start.23 = (bf16[2,512,384]{2,1,0:T(8,128)(2,1)}, bf16[2,512,384]{2,1,0:T(8,128)(2,1)}, u32[]{:S(2)}, u32[]{:S(2)}) collective-permute-start(bf16[2,512,384]{2,1,0:T(8,128)(2,1)} %get-tuple-element.153), channel_id=1, source_target_pairs={{0,1},{1,0},{2,3},{3,2},{4,5},{5,4},{6,7},{7,6},{8,9},{9,8},{10,11... | collective-permute-start | bytes 2359304 | tf_op jit(solution)/shard_map/ppermute | solution.py:184
  380.7 10.2 %collective-permute-start.24 = (bf16[2,512,384]{2,1,0:T(8,128)(2,1)}, bf16[2,512,384]{2,1,0:T(8,128)(2,1)S(1)}, u32[]{:S(2)}, u32[]{:S(2)}) collective-permute-start(bf16[2,512,384]{2,1,0:T(8,128)(2,1)} %get-tuple-element.155), channel_id=1, source_target_pairs={{0,1},{1,0},{2,3},{3,2},{4,5},{5,4},{6,7},{7,6},{8,9},{9,8},{10,11... | collective-permute-start | bytes 2359304 | tf_op jit(solution)/shard_map/ppermute | solution.py:184
  384.0 23.5 %collective-permute-start.31 = (bf16[2,512,384]{2,1,0:T(8,128)(2,1)}, bf16[2,512,384]{2,1,0:T(8,128)(2,1)}, u32[]{:S(2)}, u32[]{:S(2)}) collective-permute-start(bf16[2,512,384]{2,1,0:T(8,128)(2,1)} %add_convert_fusion.8), channel_id=1, source_target_pairs={{0,2},{1,3},{2,0},{3,1},{4,6},{5,7},{6,4},{7,5},{8,10},{9,11},{10,... | collective-permute-start | bytes 2359304 | tf_op jit(solution)/shard_map/ppermute | solution.py:184
  392.0 28.5 %collective-permute-start.32 = (bf16[2,512,384]{2,1,0:T(8,128)(2,1)}, bf16[2,512,384]{2,1,0:T(8,128)(2,1)}, u32[]{:S(2)}, u32[]{:S(2)}) collective-permute-start(bf16[2,512,384]{2,1,0:T(8,128)(2,1)} %add_convert_fusion.14), channel_id=1, source_target_pairs={{0,2},{1,3},{2,0},{3,1},{4,6},{5,7},{6,4},{7,5},{8,10},{9,11},{10,... | collective-permute-start | bytes 2359304 | tf_op jit(solution)/shard_map/ppermute | solution.py:184
  432.1 12.5 %collective-permute-start.40 = (bf16[192,2304]{1,0:T(8,128)(2,1)}, bf16[192,2304]{1,0:T(8,128)(2,1)}, u32[]{:S(2)}, u32[]{:S(2)}) collective-permute-start(bf16[192,2304]{1,0:T(8,128)(2,1)} %get-tuple-element.263), channel_id=1, source_target_pairs={{0,1},{1,0},{2,3},{3,2},{4,5},{5,4},{6,7},{7,6},{8,9},{9,8},{10,11... | collective-permute-start | bytes 2654216 | tf_op jit(solution)/shard_map/ppermute | solution.py:184
  444.1 5.1 collective-permute-start.39
  447.2 21.9 %collective-permute-start.41 = (bf16[192,2304]{1,0:T(8,128)(2,1)}, bf16[192,2304]{1,0:T(8,128)(2,1)}, u32[]{:S(2)}, u32[]{:S(2)}) collective-permute-start(bf16[192,2304]{1,0:T(8,128)(2,1)} %fusion.26), channel_id=1, source_target_pairs={{0,2},{1,3},{2,0},{3,1},{4,6},{5,7},{6,4},{7,5},{8,10},{9,11},{10,... | collective-permute-start | bytes 2654216 | tf_op jit(solution)/shard_map/ppermute | solution.py:184
  448.6 40.1 %collective-permute-start.34 = (bf16[16,2304]{1,0:T(8,128)(2,1)S(1)}, bf16[16,2304]{1,0:T(8,128)(2,1)S(1)}, u32[]{:S(2)}, u32[]{:S(2)}) collective-permute-start(bf16[16,2304]{1,0:T(8,128)(2,1)S(1)} %get-tuple-element.277), channel_id=1, source_target_pairs={{0,1},{1,0},{2,3},{3,2},{4,5},{5,4},{6,7},{7,6},{8,9},{9,8},{10,11... | collective-permute-start | bytes 221192 | tf_op jit(solution)/shard_map/ppermute | solution.py:184
  448.7 53.7 %collective-permute-start.33 = (bf16[16,2304]{1,0:T(8,128)(2,1)S(1)}, bf16[16,2304]{1,0:T(8,128)(2,1)S(1)}, u32[]{:S(2)}, u32[]{:S(2)}) collective-permute-start(bf16[16,2304]{1,0:T(8,128)(2,1)S(1)} %get-tuple-element.276), channel_id=1, source_target_pairs={{0,1},{1,0},{2,3},{3,2},{4,5},{5,4},{6,7},{7,6},{8,9},{9,8},{10,11... | collective-permute-start | bytes 221192 | tf_op jit(solution)/shard_map/ppermute | solution.py:184
  471.2 15.9 %collective-permute-start.42 = (bf16[96,2304]{1,0:T(8,128)(2,1)S(1)}, bf16[96,2304]{1,0:T(8,128)(2,1)S(1)}, u32[]{:S(2)}, u32[]{:S(2)}) collective-permute-start(bf16[96,2304]{1,0:T(8,128)(2,1)S(1)} %dynamic-slice_bitcast_fusion.6), channel_id=1, source_target_pairs={{0,4},{4,0},{8,12},{12,8},{16,20},{20,16},{24,28},{28,24},{1,5},{5... | collective-permute-start | bytes 1327112 | tf_op jit(solution)/shard_map/ppermute | solution.py:264
  487.2 14.3 %collective-permute-start.43 = (bf16[48,2304]{1,0:T(8,128)(2,1)S(1)}, bf16[48,2304]{1,0:T(8,128)(2,1)S(1)}, u32[]{:S(2)}, u32[]{:S(2)}) collective-permute-start(bf16[48,2304]{1,0:T(8,128)(2,1)S(1)} %dynamic-slice_bitcast_fusion.9), channel_id=1, source_target_pairs={{0,8},{4,12},{8,0},{12,4},{16,24},{20,28},{24,16},{28,20},{1,9},{5... | collective-permute-start | bytes 663560 | tf_op jit(solution)/shard_map/ppermute | solution.py:264
  488.7 13.7 %collective-permute-start.35 = (bf16[16,2304]{1,0:T(8,128)(2,1)S(1)}, bf16[16,2304]{1,0:T(8,128)(2,1)S(1)}, u32[]{:S(2)}, u32[]{:S(2)}) collective-permute-start(bf16[16,2304]{1,0:T(8,128)(2,1)S(1)} %fusion.35), channel_id=1, source_target_pairs={{0,2},{1,3},{2,0},{3,1},{4,6},{5,7},{6,4},{7,5},{8,10},{9,11},{10,... | collective-permute-start | bytes 221192 | tf_op jit(solution)/shard_map/ppermute | solution.py:184
  501.5 8.1 %collective-permute-start.44 = (bf16[24,2304]{1,0:T(8,128)(2,1)S(1)}, bf16[24,2304]{1,0:T(8,128)(2,1)S(1)}, u32[]{:S(2)}, u32[]{:S(2)}) collective-permute-start(bf16[24,2304]{1,0:T(8,128)(2,1)S(1)} %dynamic-slice_bitcast_fusion.10), channel_id=1, source_target_pairs={{0,16},{4,20},{8,24},{12,28},{16,0},{20,4},{24,8},{28,12},{1,17},{... | collective-permute-start | bytes 331784 | tf_op jit(solution)/shard_map/ppermute | solution.py:264
  502.5 7.2 %collective-permute-start.36 = (bf16[16,2304]{1,0:T(8,128)(2,1)S(1)}, bf16[16,2304]{1,0:T(8,128)(2,1)S(1)}, u32[]{:S(2)}, u32[]{:S(2)}) collective-permute-start(bf16[16,2304]{1,0:T(8,128)(2,1)S(1)} %add_convert_fusion.22), channel_id=1, source_target_pairs={{0,4},{4,0},{8,12},{12,8},{16,20},{20,16},{24,28},{28,24},{1,5},{5... | collective-permute-start | bytes 221192 | tf_op jit(solution)/shard_map/ppermute | solution.py:264
  509.6 7.2 %collective-permute-start.45 = (bf16[24,2304]{1,0:T(8,128)(2,1)S(1)}, bf16[24,2304]{1,0:T(8,128)(2,1)S(1)}, u32[]{:S(2)}, u32[]{:S(2)}) collective-permute-start(bf16[24,2304]{1,0:T(8,128)(2,1)S(1)} %fusion.34), channel_id=1, source_target_pairs={{0,16},{4,20},{8,24},{12,28},{16,0},{20,4},{24,8},{28,12},{1,17},{... | collective-permute-start | bytes 331784 | tf_op jit(solution)/shard_map/ppermute | solution.py:264
  509.7 7.2 %collective-permute-start.37 = (bf16[16,2304]{1,0:T(8,128)(2,1)S(1)}, bf16[16,2304]{1,0:T(8,128)(2,1)S(1)}, u32[]{:S(2)}, u32[]{:S(2)}) collective-permute-start(bf16[16,2304]{1,0:T(8,128)(2,1)S(1)} %add_convert_fusion.21), channel_id=1, source_target_pairs={{0,8},{4,12},{8,0},{12,4},{16,24},{20,28},{24,16},{28,20},{1,9},{5... | collective-permute-start | bytes 221192 | tf_op jit(solution)/shard_map/ppermute | solution.py:264
  516.9 9.0 %collective-permute-start.46 = (bf16[48,2304]{1,0:T(8,128)(2,1)S(1)}, bf16[48,2304]{1,0:T(8,128)(2,1)S(1)}, u32[]{:S(2)}, u32[]{:S(2)}) collective-permute-start(bf16[48,2304]{1,0:T(8,128)(2,1)S(1)} %maximum_select_fusion.2), channel_id=1, source_target_pairs={{0,8},{4,12},{8,0},{12,4},{16,24},{20,28},{24,16},{28,20},{1,9},{5... | collective-permute-start | bytes 663560 | tf_op jit(solution)/shard_map/ppermute | solution.py:264
  517.0 10.4 %collective-permute-start.38 = (bf16[16,2304]{1,0:T(8,128)(2,1)S(1)}, bf16[16,2304]{1,0:T(8,128)(2,1)S(1)}, u32[]{:S(2)}, u32[]{:S(2)}) collective-permute-start(bf16[16,2304]{1,0:T(8,128)(2,1)S(1)} %add_convert_fusion.20), channel_id=1, source_target_pairs={{0,16},{4,20},{8,24},{12,28},{16,0},{20,4},{24,8},{28,12},{1,17},{... | collective-permute-start | bytes 221192 | tf_op jit(solution)/shard_map/ppermute | solution.py:264
  526.0 11.3 %collective-permute-start.47 = (bf16[96,2304]{1,0:T(8,128)(2,1)S(1)}, bf16[96,2304]{1,0:T(8,128)(2,1)S(1)}, u32[]{:S(2)}, u32[]{:S(2)}) collective-permute-start(bf16[96,2304]{1,0:T(8,128)(2,1)S(1)} %maximum_select_fusion.1), channel_id=1, source_target_pairs={{0,4},{4,0},{8,12},{12,8},{16,20},{20,16},{24,28},{28,24},{1,5},{5... | collective-permute-start | bytes 1327112 | tf_op jit(solution)/shard_map/ppermute | solution.py:264
  (63 other events, 526.7 us)
Sparse Core Ops, SparseCore 0:
  9.6 33.4 all-gather.6
  74.8 23.8 all-gather.8
  100.2 58.5 all-gather.10
  160.2 37.4 all-gather.12
  380.8 119.6 all-reduce.3

commit v5 on v4

--- a/solution.py
+++ b/solution.py
@@ -1,4 +1,5 @@
 import functools
+import math
 
 import jax
 import jax.numpy as jnp
@@ -175,8 +176,7 @@
     return center * lax.rsqrt(spread + 1e-06) * gain + shift
 
 
-def gelu_tanh(value):
-    return jax.nn.gelu(value, approximate=True)
+GELU = (2 / math.pi) ** 0.5
 
 
 def swap(x, flip):
@@ -350,8 +350,10 @@
     normed_mid, pull_two = jax.vjp(normed, hidden, gain_two, shift_two)
     mid_low = normed_mid.astype(bf)
     upward = nn(mid_low, w_rise) + bias_up
-    active, pull_gelu = jax.vjp(gelu_tanh, upward)
-    active_low = active.astype(bf)
+    bent = jnp.tanh(GELU * (upward + 0.044715 * upward * upward * upward))
+    active_low = (0.5 * upward * (1 + bent)).astype(bf)
+    slope = 0.5 * (1 + bent) + 0.5 * upward * (1 - bent * bent) * (GELU * (1 + 3 * 0.044715 * upward * upward))
+    active_low, slope = lax.optimization_barrier((active_low, slope))
 
     real = (seg.reshape(-1, 1) != 0).astype(f32)
     grad_y = cotangent.reshape(micro * tokens, width).astype(f32) * real
@@ -360,7 +362,7 @@
     grad_b_fall = jnp.sum(grad_m.astype(f32), axis=0)
     low_fall, grad_m = tie(grad_w_fall.astype(bf), grad_m)
     fall = reduce_core(low_fall)
-    grad_up = pull_gelu(nt(grad_m, w_fall))[0].astype(bf)
+    grad_up = (nt(grad_m, w_fall) * slope).astype(bf)
     fall, grad_up = tie(fall, grad_up)
     fall = reduce_chip(fall)
     grad_w_rise = tn(mid_low, grad_up)
@@ -397,29 +399,36 @@
     pairs = []
     for half in halves:
         pairs.append(reduce_relative(half, 2))
-    pairs, grads_q = tie(pairs, grads_q)
-    grad_qkv = jnp.concatenate(
+    grad_query = jnp.concatenate(
+        [jnp.concatenate(grads_q[i : i + 2], axis=1) for i in range(0, 2 * micro, 2)]
+    )
+    low_query = tn(normed_low, grad_query).astype(bf)
+    query_part = reduce_chip(reduce_core(low_query))
+    query_part = finish(query_part, 1)
+
+    pairs = lax.optimization_barrier(pairs)
+    grad_pair = jnp.concatenate(
         [
-            jnp.concatenate(
-                [grads_q[i], grads_q[i + 1], pairs[i][0], pairs[i + 1][0], pairs[i][1], pairs[i + 1][1]], axis=1
-            )
+            jnp.concatenate([pairs[i][0], pairs[i + 1][0], pairs[i][1], pairs[i + 1][1]], axis=1)
             for i in range(0, 2 * micro, 2)
         ]
     )
-    grad_qkv = lax.optimization_barrier(grad_qkv)
+    grad_pair = lax.optimization_barrier(grad_pair)
     wide = [part.astype(f32) for part in wide]
-    grad_w_proj = tn(normed_low, grad_qkv)
-    low_proj, grad_qkv = tie(grad_w_proj.astype(bf), grad_qkv)
-    sums = jnp.sum(grad_qkv.astype(f32), axis=0)
-    grad_b_proj = jnp.concatenate([sums[:width], sums[2 * width :]])
-    grad_norm_in, grad_gain_one, grad_shift_one = pull_one(nt(grad_qkv, w_proj))
+    low_pair, grad_pair = tie(tn(normed_low, grad_pair).astype(bf), grad_pair)
+    grad_b_proj = jnp.concatenate(
+        [jnp.sum(grad_query.astype(f32), axis=0), jnp.sum(grad_pair[:, width:].astype(f32), axis=0)]
+    )
+    grad_norm = nt(grad_query, w_proj[:, :width]) + nt(grad_pair, w_proj[:, width:])
+    grad_norm_in, grad_gain_one, grad_shift_one = pull_one(grad_norm)
     input_grad = (grad_hidden + grad_norm_in).astype(bf)
 
     last, small = reduce_last(
-        low_proj,
+        low_pair,
         (grad_gain_one, grad_shift_one, grad_b_proj, grad_b_mix, grad_gain_two, grad_shift_two, grad_b_rise, grad_b_fall),
         vectors,
     )
+    last = jnp.concatenate([query_part, last], axis=1)
     return (
         output.reshape(inputs.shape),
         input_grad.reshape(inputs.shape),

time: 551 us -> 574 us (1.042)
  other arithmetic: 80.1 us -> 94.7 us
  starting transfers between devices: 30 us -> 36.2 us
    concatenate x2 -> x3, other arithmetic: 0.32 us -> 20.4 us  [the longest x1 19 us: layer(): jnp.concatenate([jnp.concatenate([pairs[i][0], pairs[i + 1][0], pairs[i][...]
    ppermute x9 -> x15, starting transfers between devices: 11.9 us -> 19.6 us  [trade(): return lax.ppermute(x, 'dp', [(i, i ^ flip) for i in range(size)])]
    convert_element_type x21 -> x23, other arithmetic: 44.4 us -> 39.7 us  [fold(): (near.astype(f32) + swap(far, flip).astype(f32)).astype(bf)]
    dot_general x4 -> x5, matrix products: 28.5 us -> 24 us  [nt(): lax.dot_general(a, b, (((1,), (1,)), ((), ())), preferred_element_type=f32)]
    unnamed x132 -> x134, local copies, waits for them, and re-layouts: 14.6 us -> 11.4 us
    ppermute x9 -> x15, waiting for transfers between devices: 39.8 us -> 42.8 us  [trade(): return lax.ppermute(x, 'dp', [(i, i ^ flip) for i in range(size)])]
    dot_general x4 -> x5, matrix products: 18 us -> 19.8 us  [tn(): lax.dot_general(a, b, (((0,), (0,)), ((), ())), preferred_element_type=f32)]
    ppermute x39 -> x42, starting transfers between devices: 17.5 us -> 15.9 us  [swap(): return lax.ppermute(x, 'band', [(i, i ^ flip) for i in range(parts)])]
  transfers between devices with their start and end apart: 53 -> 62, of which waited for: 18 -> 25; matrix products, arithmetic and copies ran while one was open for 31% -> 32% of each run, Pallas kernels for 26% -> 21%
where the time goes in v5:
time: 574 us; the launch traced here: 567 us
  waiting for transfers between devices  156 us (27%)
  Pallas kernels  139 us (24%)
  other arithmetic  94.7 us (16%)
  matrix products  80.6 us (14%)
  local copies, waits for them, and re-layouts  38.4 us (7%)
  starting transfers between devices  36.2 us (6%)
  between operations  15.6 us (3%)
  blocking collectives  6.24 us (1%)
    ppermute x42, waiting for transfers between devices, swap(): return lax.ppermute(x, 'band', [(i, i ^ flip) for i in range(parts)])  93.4 us
    pallas_call x4, Pallas kernels, attn_bwd(): pl.pallas_call(functools.partial(bwd_kernel, tq=min(tq, n), parts=parts),...  86.3 us
    pallas_call x4, Pallas kernels, attn_fwd(): pl.pallas_call(functools.partial(fwd_kernel, tq=min(tq, n), parts=parts),...  52.9 us
    ppermute x15, waiting for transfers between devices, trade(): return lax.ppermute(x, 'dp', [(i, i ^ flip) for i in range(size)])  42.8 us
    convert_element_type x23, other arithmetic, fold(): (near.astype(f32) + swap(far, flip).astype(f32)).astype(bf)  39.7 us
    dot_general x4, matrix products, nn(): lax.dot_general(a, b, (((1,), (0,)), ((), ())), preferred_element_type=f32)  36.8 us
    dot_general x5, matrix products, nt(): lax.dot_general(a, b, (((1,), (1,)), ((), ())), preferred_element_type=f32)  24 us
    dot_general x5, matrix products, tn(): lax.dot_general(a, b, (((0,), (0,)), ((), ())), preferred_element_type=f32)  19.8 us
  transfers between devices with their start and end apart: 62, of which 25 were waited for; matrix products, arithmetic and copies ran while one was open for 32% of the time, Pallas kernels for 21%

profile of v5, /device:TPU:0, one launch (start us, length us, event | category | flops | bytes accessed | tf_op | source)
XLA Modules:
  0.0 567.4 jit_solution(309013917155246710)
XLA Ops:
  8.0 5.5 concatenate.97
  13.4 6.2 %all-gather.1 = bf16[4,1,2304]{2,1,0:T(2,128)(2,1)S(1)} all-gather(bf16[1,1,2304]{2,1,0:T(2,128)(2,1)S(1)} %reshape.387), channel_id=2, replica_groups=mesh['dp'=8,'band'=4] {'band'}, dimensions={0}, use_global_device_ids=true | all-gather | bytes 23040 | tf_op jit(solution)/shard_map/all_gather | solution.py:215
  24.3 18.8 %all-gather.7.cloned.1.call-done = bf16[768,2304]{1,0:T(8,128)(2,1)} async-done(((bf16[192,2304]{1,0:T(8,128)(2,1)}), bf16[768,2304]{1,0:T(8,128)(2,1)}) %all-gather.7.cloned.1.call-update) | async-done | bytes 3538960 | tf_op jit(solution)/shard_map/all_gather | solution.py:250
  43.1 5.8 %fusion.62 = (bf16[1024,2304]{1,0:T(8,128)(2,1)S(1)}, f32[1024,2304]{1,0:T(8,128)S(1)}) fusion(bf16[1024,768]{1,0:T(8,128)(2,1)S(1)} %fusion.14, bf16[768,2304]{1,0:T(8,128)(2,1)} %all-gather.7.cloned.1.call-done), kind=kOutput, calls=%fused_computation.196 | convolution fusion | flops 3626237952 | bytes 19267584 | tf_op jit(solution)/shard_map/dot_general | solution.py:17
  53.7 18.5 %collective-permute-done.1.refs_3_.refs_7_.refs_6_.refs_10_ = bf16[512,768]{1,0:T(8,128)(2,1)S(1)} collective-permute-done((bf16[512,768]{1,0:T(8,128)(2,1)S(1)}, bf16[512,768]{1,0:T(8,128)(2,1)S(1)}, u32[]{:S(2)}, u32[]{:S(2)}) %collective-permute-start.1) | collective-permute-done | bytes 786464 | tf_op jit(solution)/shard_map/ppermute | solution.py:184
  81.9 13.3 %attn_fwd.4 = (bf16[512,384]{1,0:T(8,128)(2,1)}, f32[512,384]{1,0:T(8,128)}) custom-call(bf16[512,768]{1,0:T(8,128)(2,1)} %get-tuple-element.264.refs_0_, s32[512,1]{1,0:T(8,128)} %copy.41.refs_1_.refs_4_, bf16[512,768]{1,0:T(8,128)(2,1)} %copy-done.26, bf16[512,768]{1,0:T(8,128)(2,1)} %copy-done.55, bf16[512,768]{1,0:T(8,128)(2,1)} %copy-done.56, ...), custom_call_target="tpu_custom_call" | custom-call | flops 6442450944 | bytes 4718592 | tf_op jit(solution)/shard_map/attn_fwd/pallas_call | solution.py:90
  95.2 11.3 %collective-permute-done.refs_3_.refs_7_.refs_6_.refs_10_ = bf16[512,768]{1,0:T(8,128)(2,1)} collective-permute-done((bf16[512,768]{1,0:T(8,128)(2,1)}, bf16[512,768]{1,0:T(8,128)(2,1)}, u32[]{:S(2)}, u32[]{:S(2)}) %collective-permute-start) | collective-permute-done | bytes 786464 | tf_op jit(solution)/shard_map/ppermute | solution.py:184
  111.2 13.2 %attn_fwd.5 = (bf16[512,384]{1,0:T(8,128)(2,1)}, f32[512,384]{1,0:T(8,128)}) custom-call(bf16[512,768]{1,0:T(8,128)(2,1)} %get-tuple-element.264.refs_0_, s32[512,1]{1,0:T(8,128)} %copy.41.refs_1_.refs_4_, bf16[512,768]{1,0:T(8,128)(2,1)} %get-tuple-element.112.refs_2_.refs_6_.refs_5_.refs_9_, ...), custom_call_target="tpu_custom_call" | custom-call | flops 6442450944 | bytes 4718592 | tf_op jit(solution)/shard_map/attn_fwd/pallas_call | solution.py:90
  124.4 18.8 %collective-permute-done.4.refs_3_.refs_7_.refs_6_.refs_10_ = bf16[512,768]{1,0:T(8,128)(2,1)S(1)} collective-permute-done((bf16[512,768]{1,0:T(8,128)(2,1)S(1)}, bf16[512,768]{1,0:T(8,128)(2,1)S(1)}, u32[]{:S(2)}, u32[]{:S(2)}) %collective-permute-start.4) | collective-permute-done | bytes 786464 | tf_op jit(solution)/shard_map/ppermute | solution.py:184
  146.8 13.3 %attn_fwd.6 = (bf16[512,384]{1,0:T(8,128)(2,1)}, f32[512,384]{1,0:T(8,128)}) custom-call(bf16[512,768]{1,0:T(8,128)(2,1)} %get-tuple-element.265.refs_0_, s32[512,1]{1,0:T(8,128)} %copy.43.refs_1_.refs_4_, bf16[512,768]{1,0:T(8,128)(2,1)} %get-tuple-element.117.refs_2_.refs_6_.refs_5_.refs_9_, bf16[512,768]{1,0:T(8,128)(2,1)} %copy-done.54, ...), custom_call_target="tpu_custom_call" | custom-call | flops 6442450944 | bytes 4718592 | tf_op jit(solution)/shard_map/attn_fwd/pallas_call | solution.py:90
  160.1 8.7 %collective-permute-done.7.refs_3_.refs_7_.refs_6_.refs_10_ = bf16[512,768]{1,0:T(8,128)(2,1)} collective-permute-done((bf16[512,768]{1,0:T(8,128)(2,1)}, bf16[512,768]{1,0:T(8,128)(2,1)}, u32[]{:S(2)}, u32[]{:S(2)}) %collective-permute-start.7) | collective-permute-done | bytes 786464 | tf_op jit(solution)/shard_map/ppermute | solution.py:184
  173.1 13.1 %attn_fwd.7 = (bf16[512,384]{1,0:T(8,128)(2,1)}, f32[512,384]{1,0:T(8,128)}) custom-call(bf16[512,768]{1,0:T(8,128)(2,1)} %get-tuple-element.265.refs_0_, s32[512,1]{1,0:T(8,128)} %copy.43.refs_1_.refs_4_, bf16[512,768]{1,0:T(8,128)(2,1)} %get-tuple-element.121.refs_2_.refs_6_.refs_5_.refs_9_, ...), custom_call_target="tpu_custom_call" | custom-call | flops 6442450944 | bytes 4718592 | tf_op jit(solution)/shard_map/attn_fwd/pallas_call | solution.py:90
  186.3 3.4 fusion.63
  191.8 18.0 %fusion.5 = (f32[1024,3072]{1,0:T(8,128)}, bf16[1024,3072]{1,0:T(8,128)(2,1)S(1)}) fusion(f32[3072]{0:T(1024)S(1)} %reshape.361, bf16[768,3072]{1,0:T(8,128)(2,1)} %all-gather.11.cloned.1.call-done, f32[1024,768]{1,0:T(8,128)} %copy-done.4, f32[768]{0:T(1024)S(1)} %reshape.360, f32[768]{0:T(1024)S(1)} %reshape.359, f32[1024]{0:T(1024)S(1)} %fusion.44, ...), kind=kOutput, calls=%fused_computation.7 | convolution fusion | flops 4898684928 | bytes 26765312 | tf_op jit(solution)/shard_map/dot_general | solution.py:17
  209.8 5.5 convolution_convert_fusion.1
  219.5 9.5 %multiply_convert_fusion = bf16[1024,3072]{1,0:T(8,128)(2,1)S(1)} fusion(f32[1024,3072]{1,0:T(8,128)} %get-tuple-element.130, bf16[1024,768]{1,0:T(8,128)(2,1)S(1)} %copy-done.20, bf16[3072,768]{1,0:T(8,128)(2,1)} %all-gather.13.cloned.1.call-done), kind=kOutput, calls=%fused_computation.8 | convolution fusion | flops 4838129664 | bytes 25165824 | tf_op jit(solution)/shard_map/dot_general | solution.py:14
  229.0 6.6 %fusion.24 = (bf16[768,768]{1,0:T(8,128)(2,1)}, bf16[768,768]{1,0:T(8,128)(2,1)}) fusion(bf16[768,768]{1,0:T(8,128)(2,1)} %collective-permute-done.13, bf16[4,768,768]{2,1,0:T(8,128)(2,1)} %bitcast.205, s32[]{:T(128)S(6)} %select_n.135, bf16[768,768]{1,0:T(8,128)(2,1)} %collective-permute-done.12, s32[]{:T(128)S(6)} %select_n.133), kind=kLoop, calls=%fused_computation.52 | loop fusion | flops 4718592 | bytes 7077896 | tf_op jit(solution)/shard_map/convert_element_type | solution.py:201
  236.9 6.6 %convolution_convert_fusion = bf16[768,3072]{1,0:T(8,128)(2,1)S(1)} fusion(bf16[1024,3072]{1,0:T(8,128)(2,1)S(1)} %multiply_convert_fusion, f32[1024,768]{1,0:T(8,128)S(1)} %copy-done.5, f32[768]{0:T(1024)S(1)} %reshape.360, f32[768]{0:T(1024)S(1)} %reshape.359, f32[1024]{0:T(1024)S(1)} %fusion.44, f32[1024]{0:T(1024)S(1)} %broadcast_multiply_fusion), kind=kOutput, calls=%fused_computation.10 | convolution fusion | flops 4838129664 | bytes 14170112 | tf_op jit(solution)/shard_map/dot_general | solution.py:20
  244.2 8.6 %multiply_reduce_fusion = (bf16[768]{0:T(1024)(128)(2,1)}, f32[1024]{0:T(1024)S(1)}, bf16[768]{0:T(1024)(128)(2,1)}, f32[1024,768]{1,0:T(8,128)S(1)}) fusion(f32[1024,768]{1,0:T(8,128)S(1)} %copy-done.5, f32[1024]{0:T(1024)S(1)} %fusion.44, f32[1024]{0:T(1024)S(1)} %broadcast_multiply_fusion, f32[768]{0:T(1024)S(1)} %reshape.359, ...), kind=kOutput, calls=%fused_computation.37 | convolution fusion | flops 4838126592 | bytes 17319936 | tf_op jit(solution)/shard_map/dot_general | solution.py:14
  265.0 21.5 %attn_bwd.6 = (bf16[512,384]{1,0:T(8,128)(2,1)}, bf16[2,512,384]{2,1,0:T(8,128)(2,1)}, bf16[2,512,384]{2,1,0:T(8,128)(2,1)}, bf16[2,512,384]{2,1,0:T(8,128)(2,1)}, bf16[2,512,384]{2,1,0:T(8,128)(2,1)}) custom-call(bf16[512,768]{1,0:T(8,128)(2,1)} %get-tuple-element.264.refs_0_, bf16[512,768]{1,0:T(8,128)(2,1)} %get-tuple-element.143.refs_1_, ...), custom_call_target="tpu_custom_call" | custom-call | flops 16106127360 | bytes 8650752 | tf_op jit(solution)/shard_map/attn_bwd/pallas_call | solution.py:159
  288.2 2.9 add_convert_fusion.4
  294.4 21.8 %attn_bwd.4 = (bf16[512,384]{1,0:T(8,128)(2,1)}, bf16[2,512,384]{2,1,0:T(8,128)(2,1)}, bf16[2,512,384]{2,1,0:T(8,128)(2,1)}, bf16[2,512,384]{2,1,0:T(8,128)(2,1)}, bf16[2,512,384]{2,1,0:T(8,128)(2,1)}) custom-call(bf16[512,768]{1,0:T(8,128)(2,1)} %get-tuple-element.264.refs_0_, bf16[512,768]{1,0:T(8,128)(2,1)} %get-tuple-element.143.refs_1_, ...), custom_call_target="tpu_custom_call" | custom-call | flops 16106127360 | bytes 8650752 | tf_op jit(solution)/shard_map/attn_bwd/pallas_call | solution.py:159
  323.6 21.5 %attn_bwd.7 = (bf16[512,384]{1,0:T(8,128)(2,1)}, bf16[2,512,384]{2,1,0:T(8,128)(2,1)}, bf16[2,512,384]{2,1,0:T(8,128)(2,1)}, bf16[2,512,384]{2,1,0:T(8,128)(2,1)}, bf16[2,512,384]{2,1,0:T(8,128)(2,1)}) custom-call(bf16[512,768]{1,0:T(8,128)(2,1)} %get-tuple-element.265.refs_0_, bf16[512,768]{1,0:T(8,128)(2,1)} %get-tuple-element.164.refs_1_, ...), custom_call_target="tpu_custom_call" | custom-call | flops 16106127360 | bytes 8650752 | tf_op jit(solution)/shard_map/attn_bwd/pallas_call | solution.py:159
  351.7 2.7 add_convert_fusion.3
  354.4 21.5 %attn_bwd.5 = (bf16[512,384]{1,0:T(8,128)(2,1)}, bf16[2,512,384]{2,1,0:T(8,128)(2,1)}, bf16[2,512,384]{2,1,0:T(8,128)(2,1)}, bf16[2,512,384]{2,1,0:T(8,128)(2,1)}, bf16[2,512,384]{2,1,0:T(8,128)(2,1)}) custom-call(bf16[512,768]{1,0:T(8,128)(2,1)} %get-tuple-element.265.refs_0_, bf16[512,768]{1,0:T(8,128)(2,1)} %get-tuple-element.164.refs_1_, ...), custom_call_target="tpu_custom_call" | custom-call | flops 16106127360 | bytes 8650752 | tf_op jit(solution)/shard_map/attn_bwd/pallas_call | solution.py:159
  377.8 3.1 convolution_convert_fusion.4
  391.4 17.7 %collective-permute-done.41 = bf16[192,768]{1,0:T(8,128)(2,1)} collective-permute-done((bf16[192,768]{1,0:T(8,128)(2,1)S(1)}, bf16[192,768]{1,0:T(8,128)(2,1)}, u32[]{:S(2)}, u32[]{:S(2)}) %collective-permute-start.41) | collective-permute-done | bytes 294944 | tf_op jit(solution)/shard_map/ppermute | solution.py:184
  413.5 3.2 collective-permute-done.42
  420.8 6.4 %collective-permute-done.43 = bf16[48,768]{1,0:T(8,128)(2,1)S(1)} collective-permute-done((bf16[48,768]{1,0:T(8,128)(2,1)S(1)}, bf16[48,768]{1,0:T(8,128)(2,1)S(1)}, u32[]{:S(2)}, u32[]{:S(2)}) %collective-permute-start.43) | collective-permute-done | bytes 73760 | tf_op jit(solution)/shard_map/ppermute | solution.py:264
  429.6 3.8 collective-permute-done.44
  435.5 4.4 collective-permute-done.45
  441.4 3.8 collective-permute-done.46
  445.2 2.7 collective-permute-start.47
  447.9 9.7 %add_convert_fusion.1 = bf16[1024,768]{1,0:T(8,128)(2,1)} fusion(f32[1024,768]{1,0:T(8,128)S(1)} %copy-done.6, bf16[1024,3072]{1,0:T(8,128)(2,1)} %copy-done.58, bf16[3072,768]{1,0:T(8,128)(2,1)} %all-gather.13.cloned.1.call-done, f32[768]{0:T(1024)S(1)} %copy-done.49), kind=kOutput, calls=%fused_computation.39 | convolution fusion | flops 4834197504 | bytes 15731712 | tf_op jit(solution)/shard_map/dot_general | solution.py:17
  457.6 3.8 reduce.8
  466.3 19.0 %maximum_maximum_fusion = bf16[1024,1536]{1,0:T(8,128)(2,1)S(1)} fusion(bf16[512,384]{1,0:T(8,128)(2,1)S(1)} %get-tuple-element.283, bf16[512,384]{1,0:T(8,128)(2,1)S(1)} %get-tuple-element.281, bf16[512,384]{1,0:T(8,128)(2,1)S(1)} %get-tuple-element.282, bf16[512,384]{1,0:T(8,128)(2,1)S(1)} %get-tuple-element.280, ...), kind=kLoop, calls=%fused_computation.19 | loop fusion | flops 25165824 | bytes 6291456 | tf_op jit(solution)/shard_map/concatenate | solution.py:410
  485.4 3.2 convolution_convert_fusion.2
  488.7 2.6 fusion.20
  500.3 4.5 add_convert_fusion
  504.8 10.5 %collective-permute-done.50 = bf16[192,1536]{1,0:T(8,128)(2,1)S(1)} collective-permute-done((bf16[192,1536]{1,0:T(8,128)(2,1)S(1)}, bf16[192,1536]{1,0:T(8,128)(2,1)S(1)}, u32[]{:S(2)}, u32[]{:S(2)}) %collective-permute-start.50) | collective-permute-done | bytes 589856 | tf_op jit(solution)/shard_map/ppermute | solution.py:184
  518.4 6.4 %collective-permute-done.51 = bf16[96,1536]{1,0:T(8,128)(2,1)S(1)} collective-permute-done((bf16[96,1536]{1,0:T(8,128)(2,1)S(1)}, bf16[96,1536]{1,0:T(8,128)(2,1)S(1)}, u32[]{:S(2)}, u32[]{:S(2)}) %collective-permute-start.51) | collective-permute-done | bytes 294944 | tf_op jit(solution)/shard_map/ppermute | solution.py:264
  525.4 4.7 collective-permute-done.52
  532.7 4.3 collective-permute-done.53
  537.2 3.2 collective-permute-start.37
  540.3 3.0 collective-permute-done.54
  543.5 2.8 collective-permute-start.38
  546.3 2.8 collective-permute-done.55
  554.5 2.9 convert_element_type.781
  (364 shorter events, 126.8 us)
Async XLA Ops:
  7.2 35.9 %all-gather.7.cloned.1.call-start = ((), (), s32[]{:S(2)}) async-start(), calls=%async_computation | async-start | bytes 4423680 | tf_op jit(solution)/shard_map/all_gather | solution.py:250
  7.9 178.3 %all-gather.9.cloned.1.call-start = ((), (), s32[]{:S(2)}) async-start(), calls=%async_computation.1 | async-start | bytes 1474560 | tf_op jit(solution)/shard_map/all_gather | solution.py:250
  52.5 19.7 %collective-permute-start.1 = (bf16[512,768]{1,0:T(8,128)(2,1)S(1)}, bf16[512,768]{1,0:T(8,128)(2,1)S(1)}, u32[]{:S(2)}, u32[]{:S(2)}) collective-permute-start(bf16[512,768]{1,0:T(8,128)(2,1)S(1)} %get-tuple-element.104.refs_2_.refs_6_.refs_5_.refs_9_), channel_id=1, source_target_pairs={{0,2},{1,3},{2,0},{3,1},{4,6},{5,7},{6,4},{7,5},{8,10},{9,11},{10,... | collective-permute-start | bytes 2359304 | tf_op jit(solution)/shard_map/ppermute | solution.py:184
  53.5 18.8 %collective-permute-start.2 = (bf16[512,768]{1,0:T(8,128)(2,1)S(1)}, bf16[512,768]{1,0:T(8,128)(2,1)S(1)}, u32[]{:S(2)}, u32[]{:S(2)}) collective-permute-start(bf16[512,768]{1,0:T(8,128)(2,1)S(1)} %get-tuple-element.104.refs_2_.refs_6_.refs_5_.refs_9_), channel_id=1, source_target_pairs={{0,1},{1,0},{2,3},{3,2},{4,5},{5,4},{6,7},{7,6},{8,9},{9,8},{10,11... | collective-permute-start | bytes 2359304 | tf_op jit(solution)/shard_map/ppermute | solution.py:184
  74.7 117.1 %all-gather.11.cloned.1.call-start = ((), (), s32[]{:S(2)}) async-start(), calls=%async_computation.2 | async-start | bytes 5898240 | tf_op jit(solution)/shard_map/all_gather | solution.py:250
  75.4 144.1 %all-gather.13.cloned.1.call-start = ((), (), s32[]{:S(2)}) async-start(), calls=%async_computation.3 | async-start | bytes 5898240 | tf_op jit(solution)/shard_map/all_gather | solution.py:250
  80.3 26.2 %collective-permute-start = (bf16[512,768]{1,0:T(8,128)(2,1)}, bf16[512,768]{1,0:T(8,128)(2,1)}, u32[]{:S(2)}, u32[]{:S(2)}) collective-permute-start(bf16[512,768]{1,0:T(8,128)(2,1)} %get-tuple-element.112.refs_2_.refs_6_.refs_5_.refs_9_), channel_id=1, source_target_pairs={{0,2},{1,3},{2,0},{3,1},{4,6},{5,7},{6,4},{7,5},{8,10},{9,11},{10,... | collective-permute-start | bytes 2359304 | tf_op jit(solution)/shard_map/ppermute | solution.py:184
  107.0 36.1 %collective-permute-start.4 = (bf16[512,768]{1,0:T(8,128)(2,1)S(1)}, bf16[512,768]{1,0:T(8,128)(2,1)S(1)}, u32[]{:S(2)}, u32[]{:S(2)}) collective-permute-start(bf16[512,768]{1,0:T(8,128)(2,1)S(1)} %copy-done.25), channel_id=1, source_target_pairs={{0,2},{1,3},{2,0},{3,1},{4,6},{5,7},{6,4},{7,5},{8,10},{9,11},{10,... | collective-permute-start | bytes 2359304 | tf_op jit(solution)/shard_map/ppermute | solution.py:184
  143.7 25.1 %collective-permute-start.7 = (bf16[512,768]{1,0:T(8,128)(2,1)}, bf16[512,768]{1,0:T(8,128)(2,1)}, u32[]{:S(2)}, u32[]{:S(2)}) collective-permute-start(bf16[512,768]{1,0:T(8,128)(2,1)} %get-tuple-element.121.refs_2_.refs_6_.refs_5_.refs_9_), channel_id=1, source_target_pairs={{0,2},{1,3},{2,0},{3,1},{4,6},{5,7},{6,4},{7,5},{8,10},{9,11},{10,... | collective-permute-start | bytes 2359304 | tf_op jit(solution)/shard_map/ppermute | solution.py:184
  145.0 407.6 %all-reduce.4.cloned.1.call-start = ((), (), s32[]{:S(2)}) async-start(), calls=%async_computation.4 | async-start | bytes 5308416 | tf_op jit(solution)/shard_map/psum | solution.py:392
  219.0 10.0 %collective-permute-start.13 = (bf16[768,768]{1,0:T(8,128)(2,1)}, bf16[768,768]{1,0:T(8,128)(2,1)}, u32[]{:S(2)}, u32[]{:S(2)}) collective-permute-start(bf16[768,768]{1,0:T(8,128)(2,1)} %get-tuple-element.254), channel_id=1, source_target_pairs={{0,1},{1,0},{2,3},{3,2},{4,5},{5,4},{6,7},{7,6},{8,9},{9,8},{10,11... | collective-permute-start | bytes 3538952 | tf_op jit(solution)/shard_map/ppermute | solution.py:184
  219.2 9.9 %collective-permute-start.12 = (bf16[768,768]{1,0:T(8,128)(2,1)}, bf16[768,768]{1,0:T(8,128)(2,1)}, u32[]{:S(2)}, u32[]{:S(2)}) collective-permute-start(bf16[768,768]{1,0:T(8,128)(2,1)} %get-tuple-element.255), channel_id=1, source_target_pairs={{0,1},{1,0},{2,3},{3,2},{4,5},{5,4},{6,7},{7,6},{8,9},{9,8},{10,11... | collective-permute-start | bytes 3538952 | tf_op jit(solution)/shard_map/ppermute | solution.py:184
  235.6 52.1 %collective-permute-start.14 = (bf16[768,768]{1,0:T(8,128)(2,1)}, bf16[768,768]{1,0:T(8,128)(2,1)}, u32[]{:S(2)}, u32[]{:S(2)}) collective-permute-start(bf16[768,768]{1,0:T(8,128)(2,1)} %get-tuple-element.132), channel_id=1, source_target_pairs={{0,2},{1,3},{2,0},{3,1},{4,6},{5,7},{6,4},{7,5},{8,10},{9,11},{10,... | collective-permute-start | bytes 3538952 | tf_op jit(solution)/shard_map/ppermute | solution.py:184
  243.6 16.1 %collective-permute-start.16 = (bf16[192,3072]{1,0:T(8,128)(2,1)S(1)}, bf16[192,3072]{1,0:T(8,128)(2,1)S(1)}, u32[]{:S(2)}, u32[]{:S(2)}) collective-permute-start(bf16[192,3072]{1,0:T(8,128)(2,1)S(1)} %get-tuple-element.250), channel_id=1, source_target_pairs={{0,1},{1,0},{2,3},{3,2},{4,5},{5,4},{6,7},{7,6},{8,9},{9,8},{10,11... | collective-permute-start | bytes 3538952 | tf_op jit(solution)/shard_map/ppermute | solution.py:184
  243.7 16.0 %collective-permute-start.15 = (bf16[192,3072]{1,0:T(8,128)(2,1)S(1)}, bf16[192,3072]{1,0:T(8,128)(2,1)S(1)}, u32[]{:S(2)}, u32[]{:S(2)}) collective-permute-start(bf16[192,3072]{1,0:T(8,128)(2,1)S(1)} %get-tuple-element.251), channel_id=1, source_target_pairs={{0,1},{1,0},{2,3},{3,2},{4,5},{5,4},{6,7},{7,6},{8,9},{9,8},{10,11... | collective-permute-start | bytes 3538952 | tf_op jit(solution)/shard_map/ppermute | solution.py:184
  262.5 28.7 %collective-permute-start.18 = (bf16[192,768]{1,0:T(8,128)(2,1)}, bf16[192,768]{1,0:T(8,128)(2,1)}, u32[]{:S(2)}, u32[]{:S(2)}) collective-permute-start(bf16[192,768]{1,0:T(8,128)(2,1)} %get-tuple-element.274), channel_id=1, source_target_pairs={{0,1},{1,0},{2,3},{3,2},{4,5},{5,4},{6,7},{7,6},{8,9},{9,8},{10,11... | collective-permute-start | bytes 884744 | tf_op jit(solution)/shard_map/ppermute | solution.py:184
  262.5 28.6 %collective-permute-start.17 = (bf16[192,768]{1,0:T(8,128)(2,1)}, bf16[192,768]{1,0:T(8,128)(2,1)}, u32[]{:S(2)}, u32[]{:S(2)}) collective-permute-start(bf16[192,768]{1,0:T(8,128)(2,1)} %get-tuple-element.275), channel_id=1, source_target_pairs={{0,1},{1,0},{2,3},{3,2},{4,5},{5,4},{6,7},{7,6},{8,9},{9,8},{10,11... | collective-permute-start | bytes 884744 | tf_op jit(solution)/shard_map/ppermute | solution.py:184
  264.2 87.5 %collective-permute-start.19 = (bf16[192,3072]{1,0:T(8,128)(2,1)}, bf16[192,3072]{1,0:T(8,128)(2,1)}, u32[]{:S(2)}, u32[]{:S(2)}) collective-permute-start(bf16[192,3072]{1,0:T(8,128)(2,1)} %get-tuple-element.140), channel_id=1, source_target_pairs={{0,2},{1,3},{2,0},{3,1},{4,6},{5,7},{6,4},{7,5},{8,10},{9,11},{10,... | collective-permute-start | bytes 3538952 | tf_op jit(solution)/shard_map/ppermute | solution.py:184
  286.5 33.3 %collective-permute-start.25 = (bf16[2,512,384]{2,1,0:T(8,128)(2,1)}, bf16[2,512,384]{2,1,0:T(8,128)(2,1)}, u32[]{:S(2)}, u32[]{:S(2)}) collective-permute-start(bf16[2,512,384]{2,1,0:T(8,128)(2,1)} %get-tuple-element.161), channel_id=1, source_target_pairs={{0,1},{1,0},{2,3},{3,2},{4,5},{5,4},{6,7},{7,6},{8,9},{9,8},{10,11... | collective-permute-start | bytes 2359304 | tf_op jit(solution)/shard_map/ppermute | solution.py:184
  287.7 33.6 %collective-permute-start.26 = (bf16[2,512,384]{2,1,0:T(8,128)(2,1)}, bf16[2,512,384]{2,1,0:T(8,128)(2,1)}, u32[]{:S(2)}, u32[]{:S(2)}) collective-permute-start(bf16[2,512,384]{2,1,0:T(8,128)(2,1)} %get-tuple-element.163), channel_id=1, source_target_pairs={{0,1},{1,0},{2,3},{3,2},{4,5},{5,4},{6,7},{7,6},{8,9},{9,8},{10,11... | collective-permute-start | bytes 2359304 | tf_op jit(solution)/shard_map/ppermute | solution.py:184
  293.2 24.2 %collective-permute-start.20 = (bf16[192,768]{1,0:T(8,128)(2,1)}, bf16[192,768]{1,0:T(8,128)(2,1)}, u32[]{:S(2)}, u32[]{:S(2)}) collective-permute-start(bf16[192,768]{1,0:T(8,128)(2,1)} %get-tuple-element.142), channel_id=1, source_target_pairs={{0,2},{1,3},{2,0},{3,1},{4,6},{5,7},{6,4},{7,5},{8,10},{9,11},{10,... | collective-permute-start | bytes 884744 | tf_op jit(solution)/shard_map/ppermute | solution.py:184
  316.2 30.8 %collective-permute-start.21 = (bf16[2,512,384]{2,1,0:T(8,128)(2,1)}, bf16[2,512,384]{2,1,0:T(8,128)(2,1)}, u32[]{:S(2)}, u32[]{:S(2)}) collective-permute-start(bf16[2,512,384]{2,1,0:T(8,128)(2,1)} %get-tuple-element.146), channel_id=1, source_target_pairs={{0,1},{1,0},{2,3},{3,2},{4,5},{5,4},{6,7},{7,6},{8,9},{9,8},{10,11... | collective-permute-start | bytes 2359304 | tf_op jit(solution)/shard_map/ppermute | solution.py:184
  317.4 32.1 %collective-permute-start.22 = (bf16[2,512,384]{2,1,0:T(8,128)(2,1)}, bf16[2,512,384]{2,1,0:T(8,128)(2,1)}, u32[]{:S(2)}, u32[]{:S(2)}) collective-permute-start(bf16[2,512,384]{2,1,0:T(8,128)(2,1)} %get-tuple-element.148), channel_id=1, source_target_pairs={{0,1},{1,0},{2,3},{3,2},{4,5},{5,4},{6,7},{7,6},{8,9},{9,8},{10,11... | collective-permute-start | bytes 2359304 | tf_op jit(solution)/shard_map/ppermute | solution.py:184
  382.0 28.3 %collective-permute-start.27 = (bf16[2,512,384]{2,1,0:T(8,128)(2,1)}, bf16[2,512,384]{2,1,0:T(8,128)(2,1)}, u32[]{:S(2)}, u32[]{:S(2)}) collective-permute-start(bf16[2,512,384]{2,1,0:T(8,128)(2,1)} %add_convert_fusion.11), channel_id=1, source_target_pairs={{0,2},{1,3},{2,0},{3,1},{4,6},{5,7},{6,4},{7,5},{8,10},{9,11},{10,... | collective-permute-start | bytes 2359304 | tf_op jit(solution)/shard_map/ppermute | solution.py:184
  382.8 7.3 %collective-permute-start.39 = (bf16[192,768]{1,0:T(8,128)(2,1)}, bf16[192,768]{1,0:T(8,128)(2,1)}, u32[]{:S(2)}, u32[]{:S(2)}) collective-permute-start(bf16[192,768]{1,0:T(8,128)(2,1)} %get-tuple-element.270), channel_id=1, source_target_pairs={{0,1},{1,0},{2,3},{3,2},{4,5},{5,4},{6,7},{7,6},{8,9},{9,8},{10,11... | collective-permute-start | bytes 884744 | tf_op jit(solution)/shard_map/ppermute | solution.py:184
  383.5 25.6 %collective-permute-start.41 = (bf16[192,768]{1,0:T(8,128)(2,1)S(1)}, bf16[192,768]{1,0:T(8,128)(2,1)}, u32[]{:S(2)}, u32[]{:S(2)}) collective-permute-start(bf16[192,768]{1,0:T(8,128)(2,1)S(1)} %fusion.32), channel_id=1, source_target_pairs={{0,2},{1,3},{2,0},{3,1},{4,6},{5,7},{6,4},{7,5},{8,10},{9,11},{10,... | collective-permute-start | bytes 884744 | tf_op jit(solution)/shard_map/ppermute | solution.py:184
  387.5 29.2 %collective-permute-start.30 = (bf16[2,512,384]{2,1,0:T(8,128)(2,1)}, bf16[2,512,384]{2,1,0:T(8,128)(2,1)}, u32[]{:S(2)}, u32[]{:S(2)}) collective-permute-start(bf16[2,512,384]{2,1,0:T(8,128)(2,1)} %get-tuple-element.175), channel_id=1, source_target_pairs={{0,1},{1,0},{2,3},{3,2},{4,5},{5,4},{6,7},{7,6},{8,9},{9,8},{10,11... | collective-permute-start | bytes 2359304 | tf_op jit(solution)/shard_map/ppermute | solution.py:184
  387.7 75.0 %collective-permute-start.29 = (bf16[2,512,384]{2,1,0:T(8,128)(2,1)}, bf16[2,512,384]{2,1,0:T(8,128)(2,1)}, u32[]{:S(2)}, u32[]{:S(2)}) collective-permute-start(bf16[2,512,384]{2,1,0:T(8,128)(2,1)} %get-tuple-element.173), channel_id=1, source_target_pairs={{0,1},{1,0},{2,3},{3,2},{4,5},{5,4},{6,7},{7,6},{8,9},{9,8},{10,11... | collective-permute-start | bytes 2359304 | tf_op jit(solution)/shard_map/ppermute | solution.py:184
  390.1 38.1 %collective-permute-start.28 = (bf16[2,512,384]{2,1,0:T(8,128)(2,1)}, bf16[2,512,384]{2,1,0:T(8,128)(2,1)S(1)}, u32[]{:S(2)}, u32[]{:S(2)}) collective-permute-start(bf16[2,512,384]{2,1,0:T(8,128)(2,1)} %add_convert_fusion.15), channel_id=1, source_target_pairs={{0,2},{1,3},{2,0},{3,1},{4,6},{5,7},{6,4},{7,5},{8,10},{9,11},{10,... | collective-permute-start | bytes 2359304 | tf_op jit(solution)/shard_map/ppermute | solution.py:184
  409.0 25.4 %collective-permute-start.23 = (bf16[2,512,384]{2,1,0:T(8,128)(2,1)}, bf16[2,512,384]{2,1,0:T(8,128)(2,1)S(1)}, u32[]{:S(2)}, u32[]{:S(2)}) collective-permute-start(bf16[2,512,384]{2,1,0:T(8,128)(2,1)} %get-tuple-element.153), channel_id=1, source_target_pairs={{0,1},{1,0},{2,3},{3,2},{4,5},{5,4},{6,7},{7,6},{8,9},{9,8},{10,11... | collective-permute-start | bytes 2359304 | tf_op jit(solution)/shard_map/ppermute | solution.py:184
  410.4 6.3 %collective-permute-start.42 = (bf16[96,768]{1,0:T(8,128)(2,1)S(1)}, bf16[96,768]{1,0:T(8,128)(2,1)S(1)}, u32[]{:S(2)}, u32[]{:S(2)}) collective-permute-start(bf16[96,768]{1,0:T(8,128)(2,1)S(1)} %dynamic-slice_bitcast_fusion.12), channel_id=1, source_target_pairs={{0,4},{4,0},{8,12},{12,8},{16,20},{20,16},{24,28},{28,24},{1,5},{5... | collective-permute-start | bytes 442376 | tf_op jit(solution)/shard_map/ppermute | solution.py:264
  416.7 23.4 %collective-permute-start.24 = (bf16[2,512,384]{2,1,0:T(8,128)(2,1)S(1)}, bf16[2,512,384]{2,1,0:T(8,128)(2,1)S(1)}, u32[]{:S(2)}, u32[]{:S(2)}) collective-permute-start(bf16[2,512,384]{2,1,0:T(8,128)(2,1)S(1)} %copy-done.57), channel_id=1, source_target_pairs={{0,1},{1,0},{2,3},{3,2},{4,5},{5,4},{6,7},{7,6},{8,9},{9,8},{10,11... | collective-permute-start | bytes 2359304 | tf_op jit(solution)/shard_map/ppermute | solution.py:184
  416.8 10.4 %collective-permute-start.43 = (bf16[48,768]{1,0:T(8,128)(2,1)S(1)}, bf16[48,768]{1,0:T(8,128)(2,1)S(1)}, u32[]{:S(2)}, u32[]{:S(2)}) collective-permute-start(bf16[48,768]{1,0:T(8,128)(2,1)S(1)} %dynamic-slice_bitcast_fusion.14), channel_id=1, source_target_pairs={{0,8},{4,12},{8,0},{12,4},{16,24},{20,28},{24,16},{28,20},{1,9},{5... | collective-permute-start | bytes 221192 | tf_op jit(solution)/shard_map/ppermute | solution.py:264
  427.1 35.5 %collective-permute-start.31 = (bf16[2,512,384]{2,1,0:T(8,128)(2,1)}, bf16[2,512,384]{2,1,0:T(8,128)(2,1)}, u32[]{:S(2)}, u32[]{:S(2)}) collective-permute-start(bf16[2,512,384]{2,1,0:T(8,128)(2,1)} %add_convert_fusion.7), channel_id=1, source_target_pairs={{0,2},{1,3},{2,0},{3,1},{4,6},{5,7},{6,4},{7,5},{8,10},{9,11},{10,... | collective-permute-start | bytes 2359304 | tf_op jit(solution)/shard_map/ppermute | solution.py:184
  433.5 6.5 %collective-permute-start.45 = (bf16[24,768]{1,0:T(8,128)(2,1)S(1)}, bf16[24,768]{1,0:T(8,128)(2,1)S(1)}, u32[]{:S(2)}, u32[]{:S(2)}) collective-permute-start(bf16[24,768]{1,0:T(8,128)(2,1)S(1)} %fusion.42), channel_id=1, source_target_pairs={{0,16},{4,20},{8,24},{12,28},{16,0},{20,4},{24,8},{28,12},{1,17},{... | collective-permute-start | bytes 110600 | tf_op jit(solution)/shard_map/ppermute | solution.py:264
  441.1 23.4 %collective-permute-start.32 = (bf16[2,512,384]{2,1,0:T(8,128)(2,1)}, bf16[2,512,384]{2,1,0:T(8,128)(2,1)}, u32[]{:S(2)}, u32[]{:S(2)}) collective-permute-start(bf16[2,512,384]{2,1,0:T(8,128)(2,1)} %add_convert_fusion.13), channel_id=1, source_target_pairs={{0,2},{1,3},{2,0},{3,1},{4,6},{5,7},{6,4},{7,5},{8,10},{9,11},{10,... | collective-permute-start | bytes 2359304 | tf_op jit(solution)/shard_map/ppermute | solution.py:184
  445.2 16.2 %collective-permute-start.47 = (bf16[96,768]{1,0:T(8,128)(2,1)S(1)}, bf16[96,768]{1,0:T(8,128)(2,1)}, u32[]{:S(2)}, u32[]{:S(2)}) collective-permute-start(bf16[96,768]{1,0:T(8,128)(2,1)S(1)} %maximum_select_fusion.3), channel_id=1, source_target_pairs={{0,4},{4,0},{8,12},{12,8},{16,20},{20,16},{24,28},{28,24},{1,5},{5... | collective-permute-start | bytes 442376 | tf_op jit(solution)/shard_map/ppermute | solution.py:264
  498.0 6.8 %collective-permute-start.48 = (bf16[192,1536]{1,0:T(8,128)(2,1)}, bf16[192,1536]{1,0:T(8,128)(2,1)S(1)}, u32[]{:S(2)}, u32[]{:S(2)}) collective-permute-start(bf16[192,1536]{1,0:T(8,128)(2,1)} %get-tuple-element.260), channel_id=1, source_target_pairs={{0,1},{1,0},{2,3},{3,2},{4,5},{5,4},{6,7},{7,6},{8,9},{9,8},{10,11... | collective-permute-start | bytes 1769480 | tf_op jit(solution)/shard_map/ppermute | solution.py:184
  500.0 15.3 %collective-permute-start.50 = (bf16[192,1536]{1,0:T(8,128)(2,1)S(1)}, bf16[192,1536]{1,0:T(8,128)(2,1)S(1)}, u32[]{:S(2)}, u32[]{:S(2)}) collective-permute-start(bf16[192,1536]{1,0:T(8,128)(2,1)S(1)} %fusion.29), channel_id=1, source_target_pairs={{0,2},{1,3},{2,0},{3,1},{4,6},{5,7},{6,4},{7,5},{8,10},{9,11},{10,... | collective-permute-start | bytes 1769480 | tf_op jit(solution)/shard_map/ppermute | solution.py:184
  516.7 8.2 %collective-permute-start.51 = (bf16[96,1536]{1,0:T(8,128)(2,1)S(1)}, bf16[96,1536]{1,0:T(8,128)(2,1)S(1)}, u32[]{:S(2)}, u32[]{:S(2)}) collective-permute-start(bf16[96,1536]{1,0:T(8,128)(2,1)S(1)} %dynamic-slice_bitcast_fusion.6), channel_id=1, source_target_pairs={{0,4},{4,0},{8,12},{12,8},{16,20},{20,16},{24,28},{28,24},{1,5},{5... | collective-permute-start | bytes 884744 | tf_op jit(solution)/shard_map/ppermute | solution.py:264
  517.8 7.2 %collective-permute-start.34 = (bf16[16,1536]{1,0:T(8,128)(2,1)S(1)}, bf16[16,1536]{1,0:T(8,128)(2,1)S(1)}, u32[]{:S(2)}, u32[]{:S(2)}) collective-permute-start(bf16[16,1536]{1,0:T(8,128)(2,1)S(1)} %get-tuple-element.285), channel_id=1, source_target_pairs={{0,1},{1,0},{2,3},{3,2},{4,5},{5,4},{6,7},{7,6},{8,9},{9,8},{10,11... | collective-permute-start | bytes 147464 | tf_op jit(solution)/shard_map/ppermute | solution.py:184
  517.9 13.3 %collective-permute-start.33 = (bf16[16,1536]{1,0:T(8,128)(2,1)S(1)}, bf16[16,1536]{1,0:T(8,128)(2,1)S(1)}, u32[]{:S(2)}, u32[]{:S(2)}) collective-permute-start(bf16[16,1536]{1,0:T(8,128)(2,1)S(1)} %get-tuple-element.284), channel_id=1, source_target_pairs={{0,1},{1,0},{2,3},{3,2},{4,5},{5,4},{6,7},{7,6},{8,9},{9,8},{10,11... | collective-permute-start | bytes 147464 | tf_op jit(solution)/shard_map/ppermute | solution.py:184
  525.0 6.1 %collective-permute-start.35 = (bf16[16,1536]{1,0:T(8,128)(2,1)S(1)}, bf16[16,1536]{1,0:T(8,128)(2,1)S(1)}, u32[]{:S(2)}, u32[]{:S(2)}) collective-permute-start(bf16[16,1536]{1,0:T(8,128)(2,1)S(1)} %fusion.40), channel_id=1, source_target_pairs={{0,2},{1,3},{2,0},{3,1},{4,6},{5,7},{6,4},{7,5},{8,10},{9,11},{10,... | collective-permute-start | bytes 147464 | tf_op jit(solution)/shard_map/ppermute | solution.py:184
  530.2 6.8 %collective-permute-start.53 = (bf16[24,1536]{1,0:T(8,128)(2,1)S(1)}, bf16[24,1536]{1,0:T(8,128)(2,1)S(1)}, u32[]{:S(2)}, u32[]{:S(2)}) collective-permute-start(bf16[24,1536]{1,0:T(8,128)(2,1)S(1)} %dynamic-slice_bitcast_fusion.13), channel_id=1, source_target_pairs={{0,16},{4,20},{8,24},{12,28},{16,0},{20,4},{24,8},{28,12},{1,17},{... | collective-permute-start | bytes 221192 | tf_op jit(solution)/shard_map/ppermute | solution.py:264
  537.0 6.3 %collective-permute-start.54 = (bf16[24,1536]{1,0:T(8,128)(2,1)S(1)}, bf16[24,1536]{1,0:T(8,128)(2,1)S(1)}, u32[]{:S(2)}, u32[]{:S(2)}) collective-permute-start(bf16[24,1536]{1,0:T(8,128)(2,1)S(1)} %fusion.38), channel_id=1, source_target_pairs={{0,16},{4,20},{8,24},{12,28},{16,0},{20,4},{24,8},{28,12},{1,17},{... | collective-permute-start | bytes 221192 | tf_op jit(solution)/shard_map/ppermute | solution.py:264
  537.2 6.3 %collective-permute-start.37 = (bf16[16,1536]{1,0:T(8,128)(2,1)S(1)}, bf16[16,1536]{1,0:T(8,128)(2,1)S(1)}, u32[]{:S(2)}, u32[]{:S(2)}) collective-permute-start(bf16[16,1536]{1,0:T(8,128)(2,1)S(1)} %add_convert_fusion.22), channel_id=1, source_target_pairs={{0,8},{4,12},{8,0},{12,4},{16,24},{20,28},{24,16},{28,20},{1,9},{5... | collective-permute-start | bytes 147464 | tf_op jit(solution)/shard_map/ppermute | solution.py:264
  543.5 7.1 %collective-permute-start.38 = (bf16[16,1536]{1,0:T(8,128)(2,1)S(1)}, bf16[16,1536]{1,0:T(8,128)(2,1)S(1)}, u32[]{:S(2)}, u32[]{:S(2)}) collective-permute-start(bf16[16,1536]{1,0:T(8,128)(2,1)S(1)} %add_convert_fusion.21), channel_id=1, source_target_pairs={{0,16},{4,20},{8,24},{12,28},{16,0},{20,4},{24,8},{28,12},{1,17},{... | collective-permute-start | bytes 147464 | tf_op jit(solution)/shard_map/ppermute | solution.py:264
  549.2 9.8 %collective-permute-start.56 = (bf16[96,1536]{1,0:T(8,128)(2,1)S(1)}, bf16[96,1536]{1,0:T(8,128)(2,1)S(1)}, u32[]{:S(2)}, u32[]{:S(2)}) collective-permute-start(bf16[96,1536]{1,0:T(8,128)(2,1)S(1)} %maximum_select_fusion.2), channel_id=1, source_target_pairs={{0,4},{4,0},{8,12},{12,8},{16,20},{20,16},{24,28},{28,24},{1,5},{5... | collective-permute-start | bytes 884744 | tf_op jit(solution)/shard_map/ppermute | solution.py:264
  (77 other events, 688.6 us)
Sparse Core Ops, SparseCore 0:
  9.6 33.4 all-gather.6
  74.8 23.8 all-gather.8
  100.2 58.1 all-gather.10
  159.9 37.4 all-gather.12
  390.1 118.8 all-reduce.3

commit v6 on v4

--- a/solution.py
+++ b/solution.py
@@ -1,4 +1,5 @@
 import functools
+import math
 
 import jax
 import jax.numpy as jnp
@@ -175,8 +176,7 @@
     return center * lax.rsqrt(spread + 1e-06) * gain + shift
 
 
-def gelu_tanh(value):
-    return jax.nn.gelu(value, approximate=True)
+GELU = (2 / math.pi) ** 0.5
 
 
 def swap(x, flip):
@@ -350,8 +350,10 @@
     normed_mid, pull_two = jax.vjp(normed, hidden, gain_two, shift_two)
     mid_low = normed_mid.astype(bf)
     upward = nn(mid_low, w_rise) + bias_up
-    active, pull_gelu = jax.vjp(gelu_tanh, upward)
-    active_low = active.astype(bf)
+    bent = jnp.tanh(GELU * (upward + 0.044715 * upward * upward * upward))
+    active_low = (0.5 * upward * (1 + bent)).astype(bf)
+    slope = 0.5 * (1 + bent) + 0.5 * upward * (1 - bent * bent) * (GELU * (1 + 3 * 0.044715 * upward * upward))
+    active_low, slope = lax.optimization_barrier((active_low, slope))
 
     real = (seg.reshape(-1, 1) != 0).astype(f32)
     grad_y = cotangent.reshape(micro * tokens, width).astype(f32) * real
@@ -360,7 +362,7 @@
     grad_b_fall = jnp.sum(grad_m.astype(f32), axis=0)
     low_fall, grad_m = tie(grad_w_fall.astype(bf), grad_m)
     fall = reduce_core(low_fall)
-    grad_up = pull_gelu(nt(grad_m, w_fall))[0].astype(bf)
+    grad_up = (nt(grad_m, w_fall) * slope).astype(bf)
     fall, grad_up = tie(fall, grad_up)
     fall = reduce_chip(fall)
     grad_w_rise = tn(mid_low, grad_up)

time: 551 us -> 551 us (level)
    unnamed x132 -> x130, local copies, waits for them, and re-layouts: 14.6 us -> 14.7 us
where the time goes in v6:
time: 551 us; the launch traced here: 545 us
  waiting for transfers between devices  155 us (28%)
  Pallas kernels  139 us (25%)
  other arithmetic  81 us (15%)
  matrix products  78.3 us (14%)
  local copies, waits for them, and re-layouts  40.4 us (7%)
  starting transfers between devices  30.1 us (5%)
  between operations  15.2 us (3%)
  blocking collectives  6.24 us (1%)
    ppermute x39, waiting for transfers between devices, swap(): return lax.ppermute(x, 'band', [(i, i ^ flip) for i in range(parts)])  94.2 us
    pallas_call x4, Pallas kernels, attn_bwd(): pl.pallas_call(functools.partial(bwd_kernel, tq=min(tq, n), parts=parts),...  86.4 us
    pallas_call x4, Pallas kernels, attn_fwd(): pl.pallas_call(functools.partial(fwd_kernel, tq=min(tq, n), parts=parts),...  52.9 us
    convert_element_type x21, other arithmetic, fold(): (near.astype(f32) + swap(far, flip).astype(f32)).astype(bf)  45.3 us
    ppermute x9, waiting for transfers between devices, trade(): return lax.ppermute(x, 'dp', [(i, i ^ flip) for i in range(size)])  39.7 us
    dot_general x4, matrix products, nn(): lax.dot_general(a, b, (((1,), (0,)), ((), ())), preferred_element_type=f32)  36.7 us
    dot_general x4, matrix products, nt(): lax.dot_general(a, b, (((1,), (1,)), ((), ())), preferred_element_type=f32)  23.6 us
    all_gather x4, waiting for transfers between devices, gather_matrix(): return lax.all_gather(shard, 'band', axis=0, tiled=True)  19.3 us
  transfers between devices with their start and end apart: 53, of which 18 were waited for; matrix products, arithmetic and copies ran while one was open for 31% of the time, Pallas kernels for 26%

profile of v6, /device:TPU:0, one launch (start us, length us, event | category | flops | bytes accessed | tf_op | source)
XLA Modules:
  0.0 545.1 jit_solution(884855245274560207)
XLA Ops:
  8.0 5.5 %concatenate.60 = bf16[2304]{0:T(1024)(128)(2,1)S(1)} concatenate(bf16[192]{0:T(256)(128)(2,1)} %param.18, bf16[192]{0:T(256)(128)(2,1)} %param.19, bf16[384]{0:T(512)(128)(2,1)} %param.21, bf16[192]{0:T(256)(128)(2,1)} %param.23, bf16[192]{0:T(256)(128)(2,1)} %param.24, bf16[192]{0:T(256)(128)(2,1)} %param.25, bf16[768]{0:T(1024)(128)(2,1)} %param.27, bf16[192]{0:T(256)(128)(2,1)} %param.29), dimensions={0} | concatenate | bytes 9216 | tf_op jit(solution)/shard_map/concatenate | solution.py:214
  13.4 6.2 %all-gather.1 = bf16[4,1,2304]{2,1,0:T(2,128)(2,1)S(1)} all-gather(bf16[1,1,2304]{2,1,0:T(2,128)(2,1)S(1)} %reshape.372), channel_id=2, replica_groups=mesh['dp'=8,'band'=4] {'band'}, dimensions={0}, use_global_device_ids=true | all-gather | bytes 23040 | tf_op jit(solution)/shard_map/all_gather | solution.py:215
  23.8 19.3 %all-gather.7.cloned.1.call-done = bf16[768,2304]{1,0:T(8,128)(2,1)} async-done(((bf16[192,2304]{1,0:T(8,128)(2,1)}), bf16[768,2304]{1,0:T(8,128)(2,1)}) %all-gather.7.cloned.1.call-update) | async-done | bytes 3538960 | tf_op jit(solution)/shard_map/all_gather | solution.py:250
  43.1 5.8 %fusion.54 = (bf16[1024,2304]{1,0:T(8,128)(2,1)S(1)}, f32[1024,2304]{1,0:T(8,128)S(1)}) fusion(bf16[1024,768]{1,0:T(8,128)(2,1)S(1)} %fusion.14, bf16[768,2304]{1,0:T(8,128)(2,1)} %all-gather.7.cloned.1.call-done), kind=kOutput, calls=%fused_computation.169 | convolution fusion | flops 3626237952 | bytes 19267584 | tf_op jit(solution)/shard_map/dot_general | solution.py:17
  53.7 18.5 %collective-permute-done.1.refs_3_.refs_7_.refs_6_.refs_10_ = bf16[512,768]{1,0:T(8,128)(2,1)S(1)} collective-permute-done((bf16[512,768]{1,0:T(8,128)(2,1)S(1)}, bf16[512,768]{1,0:T(8,128)(2,1)S(1)}, u32[]{:S(2)}, u32[]{:S(2)}) %collective-permute-start.1) | collective-permute-done | bytes 786464 | tf_op jit(solution)/shard_map/ppermute | solution.py:184
  78.4 2.5 pad_maximum_fusion.3
  82.5 13.3 %attn_fwd.4 = (bf16[512,384]{1,0:T(8,128)(2,1)}, f32[512,384]{1,0:T(8,128)}) custom-call(bf16[512,768]{1,0:T(8,128)(2,1)} %get-tuple-element.272.refs_0_, s32[512,1]{1,0:T(8,128)} %copy.41.refs_1_.refs_4_, bf16[512,768]{1,0:T(8,128)(2,1)} %copy-done.21, bf16[512,768]{1,0:T(8,128)(2,1)} %copy-done.48, bf16[512,768]{1,0:T(8,128)(2,1)} %copy-done.49, ...), custom_call_target="tpu_custom_call" | custom-call | flops 6442450944 | bytes 4718592 | tf_op jit(solution)/shard_map/attn_fwd/pallas_call | solution.py:90
  95.8 11.3 %collective-permute-done.refs_3_.refs_7_.refs_6_.refs_10_ = bf16[512,768]{1,0:T(8,128)(2,1)} collective-permute-done((bf16[512,768]{1,0:T(8,128)(2,1)}, bf16[512,768]{1,0:T(8,128)(2,1)}, u32[]{:S(2)}, u32[]{:S(2)}) %collective-permute-start) | collective-permute-done | bytes 786464 | tf_op jit(solution)/shard_map/ppermute | solution.py:184
  112.5 13.2 %attn_fwd.5 = (bf16[512,384]{1,0:T(8,128)(2,1)}, f32[512,384]{1,0:T(8,128)}) custom-call(bf16[512,768]{1,0:T(8,128)(2,1)} %get-tuple-element.272.refs_0_, s32[512,1]{1,0:T(8,128)} %copy.41.refs_1_.refs_4_, bf16[512,768]{1,0:T(8,128)(2,1)} %get-tuple-element.116.refs_2_.refs_6_.refs_5_.refs_9_, ...), custom_call_target="tpu_custom_call" | custom-call | flops 6442450944 | bytes 4718592 | tf_op jit(solution)/shard_map/attn_fwd/pallas_call | solution.py:90
  125.7 18.5 %collective-permute-done.4.refs_3_.refs_7_.refs_6_.refs_10_ = bf16[512,768]{1,0:T(8,128)(2,1)S(1)} collective-permute-done((bf16[512,768]{1,0:T(8,128)(2,1)S(1)}, bf16[512,768]{1,0:T(8,128)(2,1)S(1)}, u32[]{:S(2)}, u32[]{:S(2)}) %collective-permute-start.4) | collective-permute-done | bytes 786464 | tf_op jit(solution)/shard_map/ppermute | solution.py:184
  147.9 13.3 %attn_fwd.6 = (bf16[512,384]{1,0:T(8,128)(2,1)}, f32[512,384]{1,0:T(8,128)}) custom-call(bf16[512,768]{1,0:T(8,128)(2,1)} %get-tuple-element.273.refs_0_, s32[512,1]{1,0:T(8,128)} %copy.43.refs_1_.refs_4_, bf16[512,768]{1,0:T(8,128)(2,1)} %get-tuple-element.121.refs_2_.refs_6_.refs_5_.refs_9_, bf16[512,768]{1,0:T(8,128)(2,1)} %copy-done.47, ...), custom_call_target="tpu_custom_call" | custom-call | flops 6442450944 | bytes 4718592 | tf_op jit(solution)/shard_map/attn_fwd/pallas_call | solution.py:90
  161.2 8.2 %collective-permute-done.7.refs_3_.refs_7_.refs_6_.refs_10_ = bf16[512,768]{1,0:T(8,128)(2,1)} collective-permute-done((bf16[512,768]{1,0:T(8,128)(2,1)}, bf16[512,768]{1,0:T(8,128)(2,1)}, u32[]{:S(2)}, u32[]{:S(2)}) %collective-permute-start.7) | collective-permute-done | bytes 786464 | tf_op jit(solution)/shard_map/ppermute | solution.py:184
  174.2 13.2 %attn_fwd.7 = (bf16[512,384]{1,0:T(8,128)(2,1)}, f32[512,384]{1,0:T(8,128)}) custom-call(bf16[512,768]{1,0:T(8,128)(2,1)} %get-tuple-element.273.refs_0_, s32[512,1]{1,0:T(8,128)} %copy.43.refs_1_.refs_4_, bf16[512,768]{1,0:T(8,128)(2,1)} %get-tuple-element.125.refs_2_.refs_6_.refs_5_.refs_9_, ...), custom_call_target="tpu_custom_call" | custom-call | flops 6442450944 | bytes 4718592 | tf_op jit(solution)/shard_map/attn_fwd/pallas_call | solution.py:90
  187.4 3.3 fusion.55
  192.9 17.9 %fusion.5 = (f32[1024,3072]{1,0:T(8,128)}, bf16[1024,3072]{1,0:T(8,128)(2,1)S(1)}) fusion(f32[3072]{0:T(1024)S(1)} %reshape.351, bf16[768,3072]{1,0:T(8,128)(2,1)} %all-gather.11.cloned.1.call-done, f32[1024,768]{1,0:T(8,128)} %copy-done.6, f32[768]{0:T(1024)S(1)} %reshape.350, f32[768]{0:T(1024)S(1)} %reshape.349, f32[1024]{0:T(1024)S(1)} %fusion.37, ...), kind=kOutput, calls=%fused_computation.7 | convolution fusion | flops 4898684928 | bytes 26765312 | tf_op jit(solution)/shard_map/dot_general | solution.py:17
  210.9 5.5 %convolution_convert_fusion.1 = bf16[3072,768]{1,0:T(8,128)(2,1)S(1)} fusion(bf16[1024,3072]{1,0:T(8,128)(2,1)S(1)} %get-tuple-element.160, bf16[1024,768]{1,0:T(8,128)(2,1)S(1)} %copy-done.16), kind=kOutput, calls=%fused_computation.11 | convolution fusion | flops 4834197504 | bytes 12582912 | tf_op jit(solution)/shard_map/dot_general | solution.py:20
  220.5 9.5 %multiply_convert_fusion = bf16[1024,3072]{1,0:T(8,128)(2,1)S(1)} fusion(f32[1024,3072]{1,0:T(8,128)} %get-tuple-element.134, bf16[1024,768]{1,0:T(8,128)(2,1)S(1)} %copy-done.16, bf16[3072,768]{1,0:T(8,128)(2,1)} %all-gather.13.cloned.1.call-done), kind=kOutput, calls=%fused_computation.8 | convolution fusion | flops 4838129664 | bytes 25165824 | tf_op jit(solution)/shard_map/dot_general | solution.py:14
  230.1 6.7 %fusion.22 = (bf16[768,768]{1,0:T(8,128)(2,1)}, bf16[768,768]{1,0:T(8,128)(2,1)}) fusion(bf16[768,768]{1,0:T(8,128)(2,1)} %collective-permute-done.13, bf16[4,768,768]{2,1,0:T(8,128)(2,1)} %bitcast.176, s32[]{:T(128)S(6)} %select_n.92, bf16[768,768]{1,0:T(8,128)(2,1)} %collective-permute-done.12, s32[]{:T(128)S(6)} %select_n.90), kind=kLoop, calls=%fused_computation.50 | loop fusion | flops 4718592 | bytes 7077896 | tf_op jit(solution)/shard_map/convert_element_type | solution.py:201
  237.5 6.9 %convolution_convert_fusion = bf16[768,3072]{1,0:T(8,128)(2,1)S(1)} fusion(bf16[1024,3072]{1,0:T(8,128)(2,1)S(1)} %multiply_convert_fusion, f32[1024,768]{1,0:T(8,128)S(1)} %copy-done.7, f32[768]{0:T(1024)S(1)} %reshape.350, f32[768]{0:T(1024)S(1)} %reshape.349, f32[1024]{0:T(1024)S(1)} %fusion.37, f32[1024]{0:T(1024)S(1)} %broadcast_multiply_fusion), kind=kOutput, calls=%fused_computation.10 | convolution fusion | flops 4838129664 | bytes 14170112 | tf_op jit(solution)/shard_map/dot_general | solution.py:20
  248.5 5.7 %multiply_reduce_fusion = (bf16[768]{0:T(1024)(128)(2,1)S(1)}, f32[1024]{0:T(1024)S(1)}, bf16[768]{0:T(1024)(128)(2,1)S(1)}, f32[1024,768]{1,0:T(8,128)S(1)}) fusion(f32[1024,768]{1,0:T(8,128)S(1)} %copy-done.7, f32[1024]{0:T(1024)S(1)} %fusion.37, f32[1024]{0:T(1024)S(1)} %broadcast_multiply_fusion, f32[768]{0:T(1024)S(1)} %reshape.349, ...), kind=kOutput, calls=%fused_computation.37 | convolution fusion | flops 4838126592 | bytes 17319936 | tf_op jit(solution)/shard_map/dot_general | solution.py:14
  259.5 2.8 convolution_convert_fusion.3
  263.8 4.7 fusion.20
  272.3 21.5 %attn_bwd.6 = (bf16[512,384]{1,0:T(8,128)(2,1)}, bf16[2,512,384]{2,1,0:T(8,128)(2,1)}, bf16[2,512,384]{2,1,0:T(8,128)(2,1)}, bf16[2,512,384]{2,1,0:T(8,128)(2,1)}, bf16[2,512,384]{2,1,0:T(8,128)(2,1)}) custom-call(bf16[512,768]{1,0:T(8,128)(2,1)} %get-tuple-element.272.refs_0_, bf16[512,768]{1,0:T(8,128)(2,1)} %get-tuple-element.147.refs_1_, ...), custom_call_target="tpu_custom_call" | custom-call | flops 16106127360 | bytes 8650752 | tf_op jit(solution)/shard_map/attn_bwd/pallas_call | solution.py:159
  294.4 2.9 add_convert_fusion.4
  299.9 21.5 %attn_bwd.4 = (bf16[512,384]{1,0:T(8,128)(2,1)}, bf16[2,512,384]{2,1,0:T(8,128)(2,1)}, bf16[2,512,384]{2,1,0:T(8,128)(2,1)}, bf16[2,512,384]{2,1,0:T(8,128)(2,1)}, bf16[2,512,384]{2,1,0:T(8,128)(2,1)}) custom-call(bf16[512,768]{1,0:T(8,128)(2,1)} %get-tuple-element.272.refs_0_, bf16[512,768]{1,0:T(8,128)(2,1)} %get-tuple-element.147.refs_1_, ...), custom_call_target="tpu_custom_call" | custom-call | flops 16106127360 | bytes 8650752 | tf_op jit(solution)/shard_map/attn_bwd/pallas_call | solution.py:159
  327.9 21.6 %attn_bwd.7 = (bf16[512,384]{1,0:T(8,128)(2,1)}, bf16[2,512,384]{2,1,0:T(8,128)(2,1)}, bf16[2,512,384]{2,1,0:T(8,128)(2,1)}, bf16[2,512,384]{2,1,0:T(8,128)(2,1)}, bf16[2,512,384]{2,1,0:T(8,128)(2,1)}) custom-call(bf16[512,768]{1,0:T(8,128)(2,1)} %get-tuple-element.273.refs_0_, bf16[512,768]{1,0:T(8,128)(2,1)} %get-tuple-element.170.refs_1_, ...), custom_call_target="tpu_custom_call" | custom-call | flops 16106127360 | bytes 8650752 | tf_op jit(solution)/shard_map/attn_bwd/pallas_call | solution.py:159
  350.1 2.5 add_convert_fusion.17
  352.6 2.5 add_convert_fusion.16
  355.8 2.7 add_convert_fusion.3
  358.5 21.8 %attn_bwd.5 = (bf16[512,384]{1,0:T(8,128)(2,1)}, bf16[2,512,384]{2,1,0:T(8,128)(2,1)}, bf16[2,512,384]{2,1,0:T(8,128)(2,1)}, bf16[2,512,384]{2,1,0:T(8,128)(2,1)}, bf16[2,512,384]{2,1,0:T(8,128)(2,1)}) custom-call(bf16[512,768]{1,0:T(8,128)(2,1)} %get-tuple-element.273.refs_0_, bf16[512,768]{1,0:T(8,128)(2,1)} %get-tuple-element.170.refs_1_, ...), custom_call_target="tpu_custom_call" | custom-call | flops 16106127360 | bytes 8650752 | tf_op jit(solution)/shard_map/attn_bwd/pallas_call | solution.py:159
  381.4 2.3 add_convert_fusion.8
  392.5 9.6 %add_convert_fusion.1 = bf16[1024,768]{1,0:T(8,128)(2,1)} fusion(f32[1024,768]{1,0:T(8,128)S(1)} %copy-done.8, bf16[1024,3072]{1,0:T(8,128)(2,1)} %copy-done.50, bf16[3072,768]{1,0:T(8,128)(2,1)} %all-gather.13.cloned.1.call-done, f32[768]{0:T(1024)S(1)} %copy-done.45), kind=kOutput, calls=%fused_computation.39 | convolution fusion | flops 4834197504 | bytes 15731712 | tf_op jit(solution)/shard_map/dot_general | solution.py:17
  402.1 4.4 reduce.7
  409.4 10.8 %collective-permute-done.32 = bf16[2,512,384]{2,1,0:T(8,128)(2,1)} collective-permute-done((bf16[2,512,384]{2,1,0:T(8,128)(2,1)}, bf16[2,512,384]{2,1,0:T(8,128)(2,1)}, u32[]{:S(2)}, u32[]{:S(2)}) %collective-permute-start.32) | collective-permute-done | bytes 786464 | tf_op jit(solution)/shard_map/ppermute | solution.py:184
  424.5 4.2 convolution_convert_fusion.2
  431.8 5.7 %fusion.43 = (bf16[768]{0:T(1024)(128)(2,1)S(1)}, f32[1024]{0:T(1024)S(1)}, f32[1024,768]{1,0:T(8,128)}) fusion(f32[768]{0:T(1024)S(1)} %copy-done.32, f32[1024]{0:T(1024)S(1)} %bitcast.200, bf16[2,1,512,768]{3,2,1,0:T(8,128)(2,1)S(1)} %copy-done.1, bf16[1024,2304]{1,0:T(8,128)(2,1)S(1)} %pad_maximum_fusion, bf16[768,2304]{1,0:T(8,128)(2,1)S(1)} %copy-done.46), kind=kOutput, calls=%fused_computation.159 | convolution fusion | flops 3628595456 | bytes 12988928 | tf_op jit(solution)/shard_map/dot_general | solution.py:14
  437.5 3.1 reduce.5
  440.6 3.0 fusion.15
  444.3 2.6 fusion.25
  449.0 19.8 %collective-permute-done.41 = bf16[192,2304]{1,0:T(8,128)(2,1)} collective-permute-done((bf16[192,2304]{1,0:T(8,128)(2,1)}, bf16[192,2304]{1,0:T(8,128)(2,1)}, u32[]{:S(2)}, u32[]{:S(2)}) %collective-permute-start.41) | collective-permute-done | bytes 884768 | tf_op jit(solution)/shard_map/ppermute | solution.py:184
  472.5 3.9 add_convert_fusion
  476.5 10.3 %collective-permute-done.42 = bf16[96,2304]{1,0:T(8,128)(2,1)S(1)} collective-permute-done((bf16[96,2304]{1,0:T(8,128)(2,1)S(1)}, bf16[96,2304]{1,0:T(8,128)(2,1)S(1)}, u32[]{:S(2)}, u32[]{:S(2)}) %collective-permute-start.42) | collective-permute-done | bytes 442400 | tf_op jit(solution)/shard_map/ppermute | solution.py:264
  490.1 11.1 %collective-permute-done.43 = bf16[48,2304]{1,0:T(8,128)(2,1)S(1)} collective-permute-done((bf16[48,2304]{1,0:T(8,128)(2,1)S(1)}, bf16[48,2304]{1,0:T(8,128)(2,1)S(1)}, u32[]{:S(2)}, u32[]{:S(2)}) %collective-permute-start.43) | collective-permute-done | bytes 221216 | tf_op jit(solution)/shard_map/ppermute | solution.py:264
  503.4 6.0 %collective-permute-done.44 = bf16[24,2304]{1,0:T(8,128)(2,1)S(1)} collective-permute-done((bf16[24,2304]{1,0:T(8,128)(2,1)S(1)}, bf16[24,2304]{1,0:T(8,128)(2,1)S(1)}, u32[]{:S(2)}, u32[]{:S(2)}) %collective-permute-start.44) | collective-permute-done | bytes 110624 | tf_op jit(solution)/shard_map/ppermute | solution.py:264
  511.7 4.9 collective-permute-done.45
  516.8 2.9 collective-permute-start.38
  519.6 6.0 %collective-permute-done.46 = bf16[48,2304]{1,0:T(8,128)(2,1)S(1)} collective-permute-done((bf16[48,2304]{1,0:T(8,128)(2,1)S(1)}, bf16[48,2304]{1,0:T(8,128)(2,1)S(1)}, u32[]{:S(2)}, u32[]{:S(2)}) %collective-permute-start.46) | collective-permute-done | bytes 221216 | tf_op jit(solution)/shard_map/ppermute | solution.py:264
  531.1 2.9 convert_element_type.683
  (322 shorter events, 107.7 us)
Async XLA Ops:
  7.2 35.9 %all-gather.7.cloned.1.call-start = ((), (), s32[]{:S(2)}) async-start(), calls=%async_computation | async-start | bytes 4423680 | tf_op jit(solution)/shard_map/all_gather | solution.py:250
  7.9 179.5 %all-gather.9.cloned.1.call-start = ((), (), s32[]{:S(2)}) async-start(), calls=%async_computation.1 | async-start | bytes 1474560 | tf_op jit(solution)/shard_map/all_gather | solution.py:250
  52.5 19.7 %collective-permute-start.1 = (bf16[512,768]{1,0:T(8,128)(2,1)S(1)}, bf16[512,768]{1,0:T(8,128)(2,1)S(1)}, u32[]{:S(2)}, u32[]{:S(2)}) collective-permute-start(bf16[512,768]{1,0:T(8,128)(2,1)S(1)} %get-tuple-element.108.refs_2_.refs_6_.refs_5_.refs_9_), channel_id=1, source_target_pairs={{0,2},{1,3},{2,0},{3,1},{4,6},{5,7},{6,4},{7,5},{8,10},{9,11},{10,... | collective-permute-start | bytes 2359304 | tf_op jit(solution)/shard_map/ppermute | solution.py:184
  53.5 18.8 %collective-permute-start.2 = (bf16[512,768]{1,0:T(8,128)(2,1)S(1)}, bf16[512,768]{1,0:T(8,128)(2,1)S(1)}, u32[]{:S(2)}, u32[]{:S(2)}) collective-permute-start(bf16[512,768]{1,0:T(8,128)(2,1)S(1)} %get-tuple-element.108.refs_2_.refs_6_.refs_5_.refs_9_), channel_id=1, source_target_pairs={{0,1},{1,0},{2,3},{3,2},{4,5},{5,4},{6,7},{7,6},{8,9},{9,8},{10,11... | collective-permute-start | bytes 2359304 | tf_op jit(solution)/shard_map/ppermute | solution.py:184
  74.7 118.3 %all-gather.11.cloned.1.call-start = ((), (), s32[]{:S(2)}) async-start(), calls=%async_computation.2 | async-start | bytes 5898240 | tf_op jit(solution)/shard_map/all_gather | solution.py:250
  75.4 145.2 %all-gather.13.cloned.1.call-start = ((), (), s32[]{:S(2)}) async-start(), calls=%async_computation.3 | async-start | bytes 5898240 | tf_op jit(solution)/shard_map/all_gather | solution.py:250
  80.9 26.2 %collective-permute-start = (bf16[512,768]{1,0:T(8,128)(2,1)}, bf16[512,768]{1,0:T(8,128)(2,1)}, u32[]{:S(2)}, u32[]{:S(2)}) collective-permute-start(bf16[512,768]{1,0:T(8,128)(2,1)} %get-tuple-element.116.refs_2_.refs_6_.refs_5_.refs_9_), channel_id=1, source_target_pairs={{0,2},{1,3},{2,0},{3,1},{4,6},{5,7},{6,4},{7,5},{8,10},{9,11},{10,... | collective-permute-start | bytes 2359304 | tf_op jit(solution)/shard_map/ppermute | solution.py:184
  107.2 5.3 collective-permute-start.6
  107.7 36.5 %collective-permute-start.4 = (bf16[512,768]{1,0:T(8,128)(2,1)S(1)}, bf16[512,768]{1,0:T(8,128)(2,1)S(1)}, u32[]{:S(2)}, u32[]{:S(2)}) collective-permute-start(bf16[512,768]{1,0:T(8,128)(2,1)S(1)} %copy-done.20), channel_id=1, source_target_pairs={{0,2},{1,3},{2,0},{3,1},{4,6},{5,7},{6,4},{7,5},{8,10},{9,11},{10,... | collective-permute-start | bytes 2359304 | tf_op jit(solution)/shard_map/ppermute | solution.py:184
  144.7 24.8 %collective-permute-start.7 = (bf16[512,768]{1,0:T(8,128)(2,1)}, bf16[512,768]{1,0:T(8,128)(2,1)}, u32[]{:S(2)}, u32[]{:S(2)}) collective-permute-start(bf16[512,768]{1,0:T(8,128)(2,1)} %get-tuple-element.125.refs_2_.refs_6_.refs_5_.refs_9_), channel_id=1, source_target_pairs={{0,2},{1,3},{2,0},{3,1},{4,6},{5,7},{6,4},{7,5},{8,10},{9,11},{10,... | collective-permute-start | bytes 2359304 | tf_op jit(solution)/shard_map/ppermute | solution.py:184
  145.8 383.4 %all-reduce.4.cloned.1.call-start = ((), (), s32[]{:S(2)}) async-start(), calls=%async_computation.4 | async-start | bytes 5308416 | tf_op jit(solution)/shard_map/psum | solution.py:392
  169.4 4.8 collective-permute-start.10
  220.0 10.0 %collective-permute-start.13 = (bf16[768,768]{1,0:T(8,128)(2,1)}, bf16[768,768]{1,0:T(8,128)(2,1)}, u32[]{:S(2)}, u32[]{:S(2)}) collective-permute-start(bf16[768,768]{1,0:T(8,128)(2,1)} %get-tuple-element.262), channel_id=1, source_target_pairs={{0,1},{1,0},{2,3},{3,2},{4,5},{5,4},{6,7},{7,6},{8,9},{9,8},{10,11... | collective-permute-start | bytes 3538952 | tf_op jit(solution)/shard_map/ppermute | solution.py:184
  220.0 10.0 %collective-permute-start.12 = (bf16[768,768]{1,0:T(8,128)(2,1)}, bf16[768,768]{1,0:T(8,128)(2,1)}, u32[]{:S(2)}, u32[]{:S(2)}) collective-permute-start(bf16[768,768]{1,0:T(8,128)(2,1)} %get-tuple-element.263), channel_id=1, source_target_pairs={{0,1},{1,0},{2,3},{3,2},{4,5},{5,4},{6,7},{7,6},{8,9},{9,8},{10,11... | collective-permute-start | bytes 3538952 | tf_op jit(solution)/shard_map/ppermute | solution.py:184
  236.8 57.1 %collective-permute-start.14 = (bf16[768,768]{1,0:T(8,128)(2,1)}, bf16[768,768]{1,0:T(8,128)(2,1)}, u32[]{:S(2)}, u32[]{:S(2)}) collective-permute-start(bf16[768,768]{1,0:T(8,128)(2,1)} %get-tuple-element.136), channel_id=1, source_target_pairs={{0,2},{1,3},{2,0},{3,1},{4,6},{5,7},{6,4},{7,5},{8,10},{9,11},{10,... | collective-permute-start | bytes 3538952 | tf_op jit(solution)/shard_map/ppermute | solution.py:184
  248.0 15.8 %collective-permute-start.16 = (bf16[192,3072]{1,0:T(8,128)(2,1)}, bf16[192,3072]{1,0:T(8,128)(2,1)}, u32[]{:S(2)}, u32[]{:S(2)}) collective-permute-start(bf16[192,3072]{1,0:T(8,128)(2,1)} %get-tuple-element.258), channel_id=1, source_target_pairs={{0,1},{1,0},{2,3},{3,2},{4,5},{5,4},{6,7},{7,6},{8,9},{9,8},{10,11... | collective-permute-start | bytes 3538952 | tf_op jit(solution)/shard_map/ppermute | solution.py:184
  248.0 15.8 %collective-permute-start.15 = (bf16[192,3072]{1,0:T(8,128)(2,1)}, bf16[192,3072]{1,0:T(8,128)(2,1)}, u32[]{:S(2)}, u32[]{:S(2)}) collective-permute-start(bf16[192,3072]{1,0:T(8,128)(2,1)} %get-tuple-element.259), channel_id=1, source_target_pairs={{0,1},{1,0},{2,3},{3,2},{4,5},{5,4},{6,7},{7,6},{8,9},{9,8},{10,11... | collective-permute-start | bytes 3538952 | tf_op jit(solution)/shard_map/ppermute | solution.py:184
  269.2 28.1 %collective-permute-start.18 = (bf16[192,768]{1,0:T(8,128)(2,1)}, bf16[192,768]{1,0:T(8,128)(2,1)S(1)}, u32[]{:S(2)}, u32[]{:S(2)}) collective-permute-start(bf16[192,768]{1,0:T(8,128)(2,1)} %get-tuple-element.280), channel_id=1, source_target_pairs={{0,1},{1,0},{2,3},{3,2},{4,5},{5,4},{6,7},{7,6},{8,9},{9,8},{10,11... | collective-permute-start | bytes 884744 | tf_op jit(solution)/shard_map/ppermute | solution.py:184
  269.3 28.0 %collective-permute-start.17 = (bf16[192,768]{1,0:T(8,128)(2,1)S(1)}, bf16[192,768]{1,0:T(8,128)(2,1)}, u32[]{:S(2)}, u32[]{:S(2)}) collective-permute-start(bf16[192,768]{1,0:T(8,128)(2,1)S(1)} %get-tuple-element.281), channel_id=1, source_target_pairs={{0,1},{1,0},{2,3},{3,2},{4,5},{5,4},{6,7},{7,6},{8,9},{9,8},{10,11... | collective-permute-start | bytes 884744 | tf_op jit(solution)/shard_map/ppermute | solution.py:184
  271.0 84.8 %collective-permute-start.19 = (bf16[192,3072]{1,0:T(8,128)(2,1)}, bf16[192,3072]{1,0:T(8,128)(2,1)}, u32[]{:S(2)}, u32[]{:S(2)}) collective-permute-start(bf16[192,3072]{1,0:T(8,128)(2,1)} %get-tuple-element.144), channel_id=1, source_target_pairs={{0,2},{1,3},{2,0},{3,1},{4,6},{5,7},{6,4},{7,5},{8,10},{9,11},{10,... | collective-permute-start | bytes 3538952 | tf_op jit(solution)/shard_map/ppermute | solution.py:184
  293.8 28.9 %collective-permute-start.25 = (bf16[2,512,384]{2,1,0:T(8,128)(2,1)}, bf16[2,512,384]{2,1,0:T(8,128)(2,1)}, u32[]{:S(2)}, u32[]{:S(2)}) collective-permute-start(bf16[2,512,384]{2,1,0:T(8,128)(2,1)} %get-tuple-element.163), channel_id=1, source_target_pairs={{0,1},{1,0},{2,3},{3,2},{4,5},{5,4},{6,7},{7,6},{8,9},{9,8},{10,11... | collective-permute-start | bytes 2359304 | tf_op jit(solution)/shard_map/ppermute | solution.py:184
  293.9 30.4 %collective-permute-start.26 = (bf16[2,512,384]{2,1,0:T(8,128)(2,1)}, bf16[2,512,384]{2,1,0:T(8,128)(2,1)}, u32[]{:S(2)}, u32[]{:S(2)}) collective-permute-start(bf16[2,512,384]{2,1,0:T(8,128)(2,1)} %get-tuple-element.165), channel_id=1, source_target_pairs={{0,1},{1,0},{2,3},{3,2},{4,5},{5,4},{6,7},{7,6},{8,9},{9,8},{10,11... | collective-permute-start | bytes 2359304 | tf_op jit(solution)/shard_map/ppermute | solution.py:184
  299.1 22.3 %collective-permute-start.20 = (bf16[192,768]{1,0:T(8,128)(2,1)}, bf16[192,768]{1,0:T(8,128)(2,1)S(1)}, u32[]{:S(2)}, u32[]{:S(2)}) collective-permute-start(bf16[192,768]{1,0:T(8,128)(2,1)} %get-tuple-element.146), channel_id=1, source_target_pairs={{0,2},{1,3},{2,0},{3,1},{4,6},{5,7},{6,4},{7,5},{8,10},{9,11},{10,... | collective-permute-start | bytes 884744 | tf_op jit(solution)/shard_map/ppermute | solution.py:184
  321.4 28.2 %collective-permute-start.21 = (bf16[2,512,384]{2,1,0:T(8,128)(2,1)}, bf16[2,512,384]{2,1,0:T(8,128)(2,1)}, u32[]{:S(2)}, u32[]{:S(2)}) collective-permute-start(bf16[2,512,384]{2,1,0:T(8,128)(2,1)} %get-tuple-element.150), channel_id=1, source_target_pairs={{0,1},{1,0},{2,3},{3,2},{4,5},{5,4},{6,7},{7,6},{8,9},{9,8},{10,11... | collective-permute-start | bytes 2359304 | tf_op jit(solution)/shard_map/ppermute | solution.py:184
  321.5 31.1 %collective-permute-start.22 = (bf16[2,512,384]{2,1,0:T(8,128)(2,1)}, bf16[2,512,384]{2,1,0:T(8,128)(2,1)}, u32[]{:S(2)}, u32[]{:S(2)}) collective-permute-start(bf16[2,512,384]{2,1,0:T(8,128)(2,1)} %get-tuple-element.152), channel_id=1, source_target_pairs={{0,1},{1,0},{2,3},{3,2},{4,5},{5,4},{6,7},{7,6},{8,9},{9,8},{10,11... | collective-permute-start | bytes 2359304 | tf_op jit(solution)/shard_map/ppermute | solution.py:184
  326.6 57.2 %collective-permute-start.27 = (bf16[2,512,384]{2,1,0:T(8,128)(2,1)}, bf16[2,512,384]{2,1,0:T(8,128)(2,1)}, u32[]{:S(2)}, u32[]{:S(2)}) collective-permute-start(bf16[2,512,384]{2,1,0:T(8,128)(2,1)} %add_convert_fusion.12), channel_id=1, source_target_pairs={{0,2},{1,3},{2,0},{3,1},{4,6},{5,7},{6,4},{7,5},{8,10},{9,11},{10,... | collective-permute-start | bytes 2359304 | tf_op jit(solution)/shard_map/ppermute | solution.py:184
  349.5 30.9 %collective-permute-start.30 = (bf16[2,512,384]{2,1,0:T(8,128)(2,1)}, bf16[2,512,384]{2,1,0:T(8,128)(2,1)}, u32[]{:S(2)}, u32[]{:S(2)}) collective-permute-start(bf16[2,512,384]{2,1,0:T(8,128)(2,1)} %get-tuple-element.175), channel_id=1, source_target_pairs={{0,1},{1,0},{2,3},{3,2},{4,5},{5,4},{6,7},{7,6},{8,9},{9,8},{10,11... | collective-permute-start | bytes 2359304 | tf_op jit(solution)/shard_map/ppermute | solution.py:184
  349.6 57.6 %collective-permute-start.29 = (bf16[2,512,384]{2,1,0:T(8,128)(2,1)}, bf16[2,512,384]{2,1,0:T(8,128)(2,1)}, u32[]{:S(2)}, u32[]{:S(2)}) collective-permute-start(bf16[2,512,384]{2,1,0:T(8,128)(2,1)} %get-tuple-element.173), channel_id=1, source_target_pairs={{0,1},{1,0},{2,3},{3,2},{4,5},{5,4},{6,7},{7,6},{8,9},{9,8},{10,11... | collective-permute-start | bytes 2359304 | tf_op jit(solution)/shard_map/ppermute | solution.py:184
  355.1 31.3 %collective-permute-start.28 = (bf16[2,512,384]{2,1,0:T(8,128)(2,1)}, bf16[2,512,384]{2,1,0:T(8,128)(2,1)}, u32[]{:S(2)}, u32[]{:S(2)}) collective-permute-start(bf16[2,512,384]{2,1,0:T(8,128)(2,1)} %add_convert_fusion.16), channel_id=1, source_target_pairs={{0,2},{1,3},{2,0},{3,1},{4,6},{5,7},{6,4},{7,5},{8,10},{9,11},{10,... | collective-permute-start | bytes 2359304 | tf_op jit(solution)/shard_map/ppermute | solution.py:184
  380.3 8.1 %collective-permute-start.23 = (bf16[2,512,384]{2,1,0:T(8,128)(2,1)}, bf16[2,512,384]{2,1,0:T(8,128)(2,1)}, u32[]{:S(2)}, u32[]{:S(2)}) collective-permute-start(bf16[2,512,384]{2,1,0:T(8,128)(2,1)} %get-tuple-element.157), channel_id=1, source_target_pairs={{0,1},{1,0},{2,3},{3,2},{4,5},{5,4},{6,7},{7,6},{8,9},{9,8},{10,11... | collective-permute-start | bytes 2359304 | tf_op jit(solution)/shard_map/ppermute | solution.py:184
  380.4 10.3 %collective-permute-start.24 = (bf16[2,512,384]{2,1,0:T(8,128)(2,1)}, bf16[2,512,384]{2,1,0:T(8,128)(2,1)S(1)}, u32[]{:S(2)}, u32[]{:S(2)}) collective-permute-start(bf16[2,512,384]{2,1,0:T(8,128)(2,1)} %get-tuple-element.159), channel_id=1, source_target_pairs={{0,1},{1,0},{2,3},{3,2},{4,5},{5,4},{6,7},{7,6},{8,9},{9,8},{10,11... | collective-permute-start | bytes 2359304 | tf_op jit(solution)/shard_map/ppermute | solution.py:184
  383.7 23.5 %collective-permute-start.31 = (bf16[2,512,384]{2,1,0:T(8,128)(2,1)}, bf16[2,512,384]{2,1,0:T(8,128)(2,1)}, u32[]{:S(2)}, u32[]{:S(2)}) collective-permute-start(bf16[2,512,384]{2,1,0:T(8,128)(2,1)} %add_convert_fusion.8), channel_id=1, source_target_pairs={{0,2},{1,3},{2,0},{3,1},{4,6},{5,7},{6,4},{7,5},{8,10},{9,11},{10,... | collective-permute-start | bytes 2359304 | tf_op jit(solution)/shard_map/ppermute | solution.py:184
  391.8 28.4 %collective-permute-start.32 = (bf16[2,512,384]{2,1,0:T(8,128)(2,1)}, bf16[2,512,384]{2,1,0:T(8,128)(2,1)}, u32[]{:S(2)}, u32[]{:S(2)}) collective-permute-start(bf16[2,512,384]{2,1,0:T(8,128)(2,1)} %add_convert_fusion.14), channel_id=1, source_target_pairs={{0,2},{1,3},{2,0},{3,1},{4,6},{5,7},{6,4},{7,5},{8,10},{9,11},{10,... | collective-permute-start | bytes 2359304 | tf_op jit(solution)/shard_map/ppermute | solution.py:184
  431.8 12.5 %collective-permute-start.40 = (bf16[192,2304]{1,0:T(8,128)(2,1)}, bf16[192,2304]{1,0:T(8,128)(2,1)}, u32[]{:S(2)}, u32[]{:S(2)}) collective-permute-start(bf16[192,2304]{1,0:T(8,128)(2,1)} %get-tuple-element.269), channel_id=1, source_target_pairs={{0,1},{1,0},{2,3},{3,2},{4,5},{5,4},{6,7},{7,6},{8,9},{9,8},{10,11... | collective-permute-start | bytes 2654216 | tf_op jit(solution)/shard_map/ppermute | solution.py:184
  443.8 5.2 collective-permute-start.39
  446.9 21.9 %collective-permute-start.41 = (bf16[192,2304]{1,0:T(8,128)(2,1)}, bf16[192,2304]{1,0:T(8,128)(2,1)}, u32[]{:S(2)}, u32[]{:S(2)}) collective-permute-start(bf16[192,2304]{1,0:T(8,128)(2,1)} %fusion.25), channel_id=1, source_target_pairs={{0,2},{1,3},{2,0},{3,1},{4,6},{5,7},{6,4},{7,5},{8,10},{9,11},{10,... | collective-permute-start | bytes 2654216 | tf_op jit(solution)/shard_map/ppermute | solution.py:184
  448.4 40.1 %collective-permute-start.34 = (bf16[16,2304]{1,0:T(8,128)(2,1)S(1)}, bf16[16,2304]{1,0:T(8,128)(2,1)S(1)}, u32[]{:S(2)}, u32[]{:S(2)}) collective-permute-start(bf16[16,2304]{1,0:T(8,128)(2,1)S(1)} %get-tuple-element.283), channel_id=1, source_target_pairs={{0,1},{1,0},{2,3},{3,2},{4,5},{5,4},{6,7},{7,6},{8,9},{9,8},{10,11... | collective-permute-start | bytes 221192 | tf_op jit(solution)/shard_map/ppermute | solution.py:184
  448.5 53.8 %collective-permute-start.33 = (bf16[16,2304]{1,0:T(8,128)(2,1)S(1)}, bf16[16,2304]{1,0:T(8,128)(2,1)S(1)}, u32[]{:S(2)}, u32[]{:S(2)}) collective-permute-start(bf16[16,2304]{1,0:T(8,128)(2,1)S(1)} %get-tuple-element.282), channel_id=1, source_target_pairs={{0,1},{1,0},{2,3},{3,2},{4,5},{5,4},{6,7},{7,6},{8,9},{9,8},{10,11... | collective-permute-start | bytes 221192 | tf_op jit(solution)/shard_map/ppermute | solution.py:184
  470.9 15.9 %collective-permute-start.42 = (bf16[96,2304]{1,0:T(8,128)(2,1)S(1)}, bf16[96,2304]{1,0:T(8,128)(2,1)S(1)}, u32[]{:S(2)}, u32[]{:S(2)}) collective-permute-start(bf16[96,2304]{1,0:T(8,128)(2,1)S(1)} %dynamic-slice_bitcast_fusion.6), channel_id=1, source_target_pairs={{0,4},{4,0},{8,12},{12,8},{16,20},{20,16},{24,28},{28,24},{1,5},{5... | collective-permute-start | bytes 1327112 | tf_op jit(solution)/shard_map/ppermute | solution.py:264
  487.0 14.3 %collective-permute-start.43 = (bf16[48,2304]{1,0:T(8,128)(2,1)S(1)}, bf16[48,2304]{1,0:T(8,128)(2,1)S(1)}, u32[]{:S(2)}, u32[]{:S(2)}) collective-permute-start(bf16[48,2304]{1,0:T(8,128)(2,1)S(1)} %dynamic-slice_bitcast_fusion.9), channel_id=1, source_target_pairs={{0,8},{4,12},{8,0},{12,4},{16,24},{20,28},{24,16},{28,20},{1,9},{5... | collective-permute-start | bytes 663560 | tf_op jit(solution)/shard_map/ppermute | solution.py:264
  488.5 13.7 %collective-permute-start.35 = (bf16[16,2304]{1,0:T(8,128)(2,1)S(1)}, bf16[16,2304]{1,0:T(8,128)(2,1)S(1)}, u32[]{:S(2)}, u32[]{:S(2)}) collective-permute-start(bf16[16,2304]{1,0:T(8,128)(2,1)S(1)} %fusion.34), channel_id=1, source_target_pairs={{0,2},{1,3},{2,0},{3,1},{4,6},{5,7},{6,4},{7,5},{8,10},{9,11},{10,... | collective-permute-start | bytes 221192 | tf_op jit(solution)/shard_map/ppermute | solution.py:184
  501.3 8.0 %collective-permute-start.44 = (bf16[24,2304]{1,0:T(8,128)(2,1)S(1)}, bf16[24,2304]{1,0:T(8,128)(2,1)S(1)}, u32[]{:S(2)}, u32[]{:S(2)}) collective-permute-start(bf16[24,2304]{1,0:T(8,128)(2,1)S(1)} %dynamic-slice_bitcast_fusion.10), channel_id=1, source_target_pairs={{0,16},{4,20},{8,24},{12,28},{16,0},{20,4},{24,8},{28,12},{1,17},{... | collective-permute-start | bytes 331784 | tf_op jit(solution)/shard_map/ppermute | solution.py:264
  502.3 7.2 %collective-permute-start.36 = (bf16[16,2304]{1,0:T(8,128)(2,1)S(1)}, bf16[16,2304]{1,0:T(8,128)(2,1)S(1)}, u32[]{:S(2)}, u32[]{:S(2)}) collective-permute-start(bf16[16,2304]{1,0:T(8,128)(2,1)S(1)} %add_convert_fusion.22), channel_id=1, source_target_pairs={{0,4},{4,0},{8,12},{12,8},{16,20},{20,16},{24,28},{28,24},{1,5},{5... | collective-permute-start | bytes 221192 | tf_op jit(solution)/shard_map/ppermute | solution.py:264
  509.4 7.2 %collective-permute-start.45 = (bf16[24,2304]{1,0:T(8,128)(2,1)S(1)}, bf16[24,2304]{1,0:T(8,128)(2,1)S(1)}, u32[]{:S(2)}, u32[]{:S(2)}) collective-permute-start(bf16[24,2304]{1,0:T(8,128)(2,1)S(1)} %fusion.33), channel_id=1, source_target_pairs={{0,16},{4,20},{8,24},{12,28},{16,0},{20,4},{24,8},{28,12},{1,17},{... | collective-permute-start | bytes 331784 | tf_op jit(solution)/shard_map/ppermute | solution.py:264
  509.5 7.2 %collective-permute-start.37 = (bf16[16,2304]{1,0:T(8,128)(2,1)S(1)}, bf16[16,2304]{1,0:T(8,128)(2,1)S(1)}, u32[]{:S(2)}, u32[]{:S(2)}) collective-permute-start(bf16[16,2304]{1,0:T(8,128)(2,1)S(1)} %add_convert_fusion.21), channel_id=1, source_target_pairs={{0,8},{4,12},{8,0},{12,4},{16,24},{20,28},{24,16},{28,20},{1,9},{5... | collective-permute-start | bytes 221192 | tf_op jit(solution)/shard_map/ppermute | solution.py:264
  516.6 9.0 %collective-permute-start.46 = (bf16[48,2304]{1,0:T(8,128)(2,1)S(1)}, bf16[48,2304]{1,0:T(8,128)(2,1)S(1)}, u32[]{:S(2)}, u32[]{:S(2)}) collective-permute-start(bf16[48,2304]{1,0:T(8,128)(2,1)S(1)} %maximum_select_fusion.2), channel_id=1, source_target_pairs={{0,8},{4,12},{8,0},{12,4},{16,24},{20,28},{24,16},{28,20},{1,9},{5... | collective-permute-start | bytes 663560 | tf_op jit(solution)/shard_map/ppermute | solution.py:264
  516.8 10.5 %collective-permute-start.38 = (bf16[16,2304]{1,0:T(8,128)(2,1)S(1)}, bf16[16,2304]{1,0:T(8,128)(2,1)S(1)}, u32[]{:S(2)}, u32[]{:S(2)}) collective-permute-start(bf16[16,2304]{1,0:T(8,128)(2,1)S(1)} %add_convert_fusion.20), channel_id=1, source_target_pairs={{0,16},{4,20},{8,24},{12,28},{16,0},{20,4},{24,8},{28,12},{1,17},{... | collective-permute-start | bytes 221192 | tf_op jit(solution)/shard_map/ppermute | solution.py:264
  525.7 11.3 %collective-permute-start.47 = (bf16[96,2304]{1,0:T(8,128)(2,1)S(1)}, bf16[96,2304]{1,0:T(8,128)(2,1)S(1)}, u32[]{:S(2)}, u32[]{:S(2)}) collective-permute-start(bf16[96,2304]{1,0:T(8,128)(2,1)S(1)} %maximum_select_fusion.1), channel_id=1, source_target_pairs={{0,4},{4,0},{8,12},{12,8},{16,20},{20,16},{24,28},{28,24},{1,5},{5... | collective-permute-start | bytes 1327112 | tf_op jit(solution)/shard_map/ppermute | solution.py:264
  (62 other events, 518.3 us)
Sparse Core Ops, SparseCore 0:
  9.6 33.4 all-gather.6
  74.8 23.8 all-gather.8
  100.2 58.5 all-gather.10
  160.2 37.4 all-gather.12
  380.5 119.7 all-reduce.3

commit v7 on v6

--- a/solution.py
+++ b/solution.py
@@ -230,7 +230,7 @@
     return [lax.dynamic_index_in_dim(array, me ^ i, 0, keepdims=False) for i in order]
 
 
-def reduce_last(matrix, grads, shards):
+def reduce_last(matrix, grads, shards, beside):
     parts, columns = lax.axis_size("band"), matrix.shape[1]
     packed = jnp.concatenate([g.reshape(parts, -1) for g in grads], axis=1).astype(bf)
     rows = -(-packed.shape[1] // (16 * columns)) * 16
@@ -238,12 +238,12 @@
     mine = reduce_chip(reduce_core(matrix))
     extra = reduce_relative(relative_rows(packed.reshape(parts, rows, columns)))
     vector = sum_small(extra).reshape(-1)
-    total = finish(mine, 1)
+    total, beside = finish(mine, 1, beside)
     out, at = [], 0
     for shard in shards:
         out.append(vector[at : at + shard.shape[0]])
         at += shard.shape[0]
-    return total, out
+    return total, out, beside
 
 
 def gather_matrix(shard):
@@ -278,15 +278,16 @@
     return jnp.where(bit == 0, jnp.concatenate([x, other]), jnp.concatenate([other, x]))
 
 
-def finish(x, flip):
+def finish(x, flip, beside):
     size = lax.axis_size("dp")
     while flip < size:
         x = halve(x, flip)
         flip *= 2
+    x, beside = tie(x, beside)
     while flip > 1:
         flip //= 2
         x = join(x, flip)
-    return x.astype(f32)
+    return x.astype(f32), [part.astype(f32) for part in beside]
 
 
 def sum_small(x):
@@ -393,7 +394,7 @@
         grad_q, *grad_blocks = attn_bwd(q, blocks, grad_out, mix, log_total, seg_q, first, count)
         halves.append(fold(grad_blocks, 1))
         grads_q.append(grad_q)
-    halves[-1], (active_low, grad_up) = tie(halves[-1], (active_low, grad_up))
+    grads_q[-2], (active_low, grad_up) = tie(grads_q[-2], (active_low, grad_up))
     output = (hidden + (nn(active_low, w_fall) + bias_down)).astype(bf)
     grad_b_rise = jnp.sum(grad_up.astype(f32), axis=0)
     pairs = []
@@ -409,7 +410,6 @@
         ]
     )
     grad_qkv = lax.optimization_barrier(grad_qkv)
-    wide = [part.astype(f32) for part in wide]
     grad_w_proj = tn(normed_low, grad_qkv)
     low_proj, grad_qkv = tie(grad_w_proj.astype(bf), grad_qkv)
     sums = jnp.sum(grad_qkv.astype(f32), axis=0)
@@ -417,10 +417,11 @@
     grad_norm_in, grad_gain_one, grad_shift_one = pull_one(nt(grad_qkv, w_proj))
     input_grad = (grad_hidden + grad_norm_in).astype(bf)
 
-    last, small = reduce_last(
+    last, small, wide = reduce_last(
         low_proj,
         (grad_gain_one, grad_shift_one, grad_b_proj, grad_b_mix, grad_gain_two, grad_shift_two, grad_b_rise, grad_b_fall),
         vectors,
+        wide,
     )
     return (
         output.reshape(inputs.shape),

time: 551 us -> 567 us (1.029)
  waiting for transfers between devices: 155 us -> 177 us
  other arithmetic: 81 us -> 73.3 us
    ppermute x39, waiting for transfers between devices: 94.2 us -> 133 us  [swap(): return lax.ppermute(x, 'band', [(i, i ^ flip) for i in range(parts)])]
    ppermute x9, waiting for transfers between devices: 39.7 us -> 22.8 us  [trade(): return lax.ppermute(x, 'dp', [(i, i ^ flip) for i in range(size)])]
    convert_element_type x21 -> x20, other arithmetic: 45.3 us -> 39.5 us  [fold(): (near.astype(f32) + swap(far, flip).astype(f32)).astype(bf)]
    unnamed x130 -> x126, local copies, waits for them, and re-layouts: 14.7 us -> 13.3 us
  transfers between devices with their start and end apart: 53 -> 53, of which waited for: 18 -> 21; matrix products, arithmetic and copies ran while one was open for 31% -> 27% of each run, Pallas kernels for 26% -> 25%
where the time goes in v7:
time: 567 us; the launch traced here: 561 us
  waiting for transfers between devices  177 us (31%)
  Pallas kernels  139 us (25%)
  matrix products  79.8 us (14%)
  other arithmetic  73.3 us (13%)
  local copies, waits for them, and re-layouts  38.8 us (7%)
  starting transfers between devices  31.3 us (6%)
  between operations  15.1 us (3%)
  blocking collectives  6.24 us (1%)
    ppermute x39, waiting for transfers between devices, swap(): return lax.ppermute(x, 'band', [(i, i ^ flip) for i in range(parts)])  133 us
    pallas_call x4, Pallas kernels, attn_bwd(): pl.pallas_call(functools.partial(bwd_kernel, tq=min(tq, n), parts=parts),...  86.4 us
    pallas_call x4, Pallas kernels, attn_fwd(): pl.pallas_call(functools.partial(fwd_kernel, tq=min(tq, n), parts=parts),...  52.9 us
    convert_element_type x20, other arithmetic, fold(): (near.astype(f32) + swap(far, flip).astype(f32)).astype(bf)  39.5 us
    dot_general x4, matrix products, nn(): lax.dot_general(a, b, (((1,), (0,)), ((), ())), preferred_element_type=f32)  37.1 us
    dot_general x4, matrix products, nt(): lax.dot_general(a, b, (((1,), (1,)), ((), ())), preferred_element_type=f32)  23.6 us
    ppermute x9, waiting for transfers between devices, trade(): return lax.ppermute(x, 'dp', [(i, i ^ flip) for i in range(size)])  22.8 us
    all_gather x4, waiting for transfers between devices, gather_matrix(): return lax.all_gather(shard, 'band', axis=0, tiled=True)  19.3 us
  transfers between devices with their start and end apart: 53, of which 21 were waited for; matrix products, arithmetic and copies ran while one was open for 27% of the time, Pallas kernels for 25%

profile of v7, /device:TPU:0, one launch (start us, length us, event | category | flops | bytes accessed | tf_op | source)
XLA Modules:
  0.0 560.5 jit_solution(5513571925393302522)
XLA Ops:
  8.0 5.5 concatenate.60
  13.4 6.2 %all-gather.1 = bf16[4,1,2304]{2,1,0:T(2,128)(2,1)S(1)} all-gather(bf16[1,1,2304]{2,1,0:T(2,128)(2,1)S(1)} %reshape.372), channel_id=2, replica_groups=mesh['dp'=8,'band'=4] {'band'}, dimensions={0}, use_global_device_ids=true | all-gather | bytes 23040 | tf_op jit(solution)/shard_map/all_gather | solution.py:215
  23.8 19.3 %all-gather.7.cloned.1.call-done = bf16[768,2304]{1,0:T(8,128)(2,1)} async-done(((bf16[192,2304]{1,0:T(8,128)(2,1)}), bf16[768,2304]{1,0:T(8,128)(2,1)}) %all-gather.7.cloned.1.call-update) | async-done | bytes 3538960 | tf_op jit(solution)/shard_map/all_gather | solution.py:250
  43.1 5.8 %fusion.54 = (bf16[1024,2304]{1,0:T(8,128)(2,1)S(1)}, f32[1024,2304]{1,0:T(8,128)S(1)}) fusion(bf16[1024,768]{1,0:T(8,128)(2,1)S(1)} %fusion.14, bf16[768,2304]{1,0:T(8,128)(2,1)} %all-gather.7.cloned.1.call-done), kind=kOutput, calls=%fused_computation.169 | convolution fusion | flops 3626237952 | bytes 19267584 | tf_op jit(solution)/shard_map/dot_general | solution.py:17
  53.7 18.5 %collective-permute-done.1.refs_3_.refs_7_.refs_6_.refs_10_ = bf16[512,768]{1,0:T(8,128)(2,1)S(1)} collective-permute-done((bf16[512,768]{1,0:T(8,128)(2,1)S(1)}, bf16[512,768]{1,0:T(8,128)(2,1)S(1)}, u32[]{:S(2)}, u32[]{:S(2)}) %collective-permute-start.1) | collective-permute-done | bytes 786464 | tf_op jit(solution)/shard_map/ppermute | solution.py:184
  82.5 13.2 %attn_fwd.4 = (bf16[512,384]{1,0:T(8,128)(2,1)}, f32[512,384]{1,0:T(8,128)}) custom-call(bf16[512,768]{1,0:T(8,128)(2,1)} %get-tuple-element.278.refs_0_, s32[512,1]{1,0:T(8,128)} %copy.41.refs_1_.refs_4_, bf16[512,768]{1,0:T(8,128)(2,1)} %copy-done.20, bf16[512,768]{1,0:T(8,128)(2,1)} %copy-done.46, bf16[512,768]{1,0:T(8,128)(2,1)} %copy-done.47, ...), custom_call_target="tpu_custom_call" | custom-call | flops 6442450944 | bytes 4718592 | tf_op jit(solution)/shard_map/attn_fwd/pallas_call | solution.py:90
  95.8 11.4 %collective-permute-done.refs_3_.refs_7_.refs_6_.refs_10_ = bf16[512,768]{1,0:T(8,128)(2,1)} collective-permute-done((bf16[512,768]{1,0:T(8,128)(2,1)}, bf16[512,768]{1,0:T(8,128)(2,1)}, u32[]{:S(2)}, u32[]{:S(2)}) %collective-permute-start) | collective-permute-done | bytes 786464 | tf_op jit(solution)/shard_map/ppermute | solution.py:184
  112.5 13.2 %attn_fwd.5 = (bf16[512,384]{1,0:T(8,128)(2,1)}, f32[512,384]{1,0:T(8,128)}) custom-call(bf16[512,768]{1,0:T(8,128)(2,1)} %get-tuple-element.278.refs_0_, s32[512,1]{1,0:T(8,128)} %copy.41.refs_1_.refs_4_, bf16[512,768]{1,0:T(8,128)(2,1)} %get-tuple-element.119.refs_2_.refs_6_.refs_5_.refs_9_, ...), custom_call_target="tpu_custom_call" | custom-call | flops 6442450944 | bytes 4718592 | tf_op jit(solution)/shard_map/attn_fwd/pallas_call | solution.py:90
  125.7 18.5 %collective-permute-done.4.refs_3_.refs_7_.refs_6_.refs_10_ = bf16[512,768]{1,0:T(8,128)(2,1)S(1)} collective-permute-done((bf16[512,768]{1,0:T(8,128)(2,1)S(1)}, bf16[512,768]{1,0:T(8,128)(2,1)S(1)}, u32[]{:S(2)}, u32[]{:S(2)}) %collective-permute-start.4) | collective-permute-done | bytes 786464 | tf_op jit(solution)/shard_map/ppermute | solution.py:184
  147.9 13.3 %attn_fwd.6 = (bf16[512,384]{1,0:T(8,128)(2,1)}, f32[512,384]{1,0:T(8,128)}) custom-call(bf16[512,768]{1,0:T(8,128)(2,1)} %get-tuple-element.279.refs_0_, s32[512,1]{1,0:T(8,128)} %copy.43.refs_1_.refs_4_, bf16[512,768]{1,0:T(8,128)(2,1)} %get-tuple-element.124.refs_2_.refs_6_.refs_5_.refs_9_, bf16[512,768]{1,0:T(8,128)(2,1)} %copy-done.45, ...), custom_call_target="tpu_custom_call" | custom-call | flops 6442450944 | bytes 4718592 | tf_op jit(solution)/shard_map/attn_fwd/pallas_call | solution.py:90
  161.2 8.2 %collective-permute-done.7.refs_3_.refs_7_.refs_6_.refs_10_ = bf16[512,768]{1,0:T(8,128)(2,1)} collective-permute-done((bf16[512,768]{1,0:T(8,128)(2,1)}, bf16[512,768]{1,0:T(8,128)(2,1)}, u32[]{:S(2)}, u32[]{:S(2)}) %collective-permute-start.7) | collective-permute-done | bytes 786464 | tf_op jit(solution)/shard_map/ppermute | solution.py:184
  174.2 13.2 %attn_fwd.7 = (bf16[512,384]{1,0:T(8,128)(2,1)}, f32[512,384]{1,0:T(8,128)}) custom-call(bf16[512,768]{1,0:T(8,128)(2,1)} %get-tuple-element.279.refs_0_, s32[512,1]{1,0:T(8,128)} %copy.43.refs_1_.refs_4_, bf16[512,768]{1,0:T(8,128)(2,1)} %get-tuple-element.128.refs_2_.refs_6_.refs_5_.refs_9_, ...), custom_call_target="tpu_custom_call" | custom-call | flops 6442450944 | bytes 4718592 | tf_op jit(solution)/shard_map/attn_fwd/pallas_call | solution.py:90
  187.4 3.3 fusion.55
  192.9 17.9 %fusion.5 = (f32[1024,3072]{1,0:T(8,128)}, bf16[1024,3072]{1,0:T(8,128)(2,1)S(1)}) fusion(f32[3072]{0:T(1024)S(1)} %reshape.351, bf16[768,3072]{1,0:T(8,128)(2,1)} %all-gather.11.cloned.1.call-done, f32[1024,768]{1,0:T(8,128)} %copy-done.6, f32[768]{0:T(1024)S(1)} %reshape.350, f32[768]{0:T(1024)S(1)} %reshape.349, f32[1024]{0:T(1024)S(1)} %fusion.37, ...), kind=kOutput, calls=%fused_computation.7 | convolution fusion | flops 4898684928 | bytes 26765312 | tf_op jit(solution)/shard_map/dot_general | solution.py:17
  210.9 5.5 convolution_convert_fusion.1
  220.6 9.5 %multiply_convert_fusion = bf16[1024,3072]{1,0:T(8,128)(2,1)S(1)} fusion(f32[1024,3072]{1,0:T(8,128)} %get-tuple-element.137, bf16[1024,768]{1,0:T(8,128)(2,1)S(1)} %copy-done.15, bf16[3072,768]{1,0:T(8,128)(2,1)} %all-gather.13.cloned.1.call-done), kind=kOutput, calls=%fused_computation.8 | convolution fusion | flops 4838129664 | bytes 25165824 | tf_op jit(solution)/shard_map/dot_general | solution.py:14
  230.1 6.6 %fusion.22 = (bf16[768,768]{1,0:T(8,128)(2,1)}, bf16[768,768]{1,0:T(8,128)(2,1)}) fusion(bf16[768,768]{1,0:T(8,128)(2,1)} %collective-permute-done.13, bf16[4,768,768]{2,1,0:T(8,128)(2,1)} %bitcast.176, s32[]{:T(128)S(6)} %select_n.92, bf16[768,768]{1,0:T(8,128)(2,1)} %collective-permute-done.12, s32[]{:T(128)S(6)} %select_n.90), kind=kLoop, calls=%fused_computation.50 | loop fusion | flops 4718592 | bytes 7077896 | tf_op jit(solution)/shard_map/convert_element_type | solution.py:201
  236.7 6.9 %convolution_convert_fusion = bf16[768,3072]{1,0:T(8,128)(2,1)S(1)} fusion(bf16[1024,3072]{1,0:T(8,128)(2,1)S(1)} %multiply_convert_fusion, f32[1024,768]{1,0:T(8,128)S(1)} %copy-done.7, f32[768]{0:T(1024)S(1)} %reshape.350, f32[768]{0:T(1024)S(1)} %reshape.349, f32[1024]{0:T(1024)S(1)} %fusion.37, f32[1024]{0:T(1024)S(1)} %broadcast_multiply_fusion), kind=kOutput, calls=%fused_computation.10 | convolution fusion | flops 4838129664 | bytes 14170112 | tf_op jit(solution)/shard_map/dot_general | solution.py:20
  247.8 5.7 %multiply_reduce_fusion = (bf16[768]{0:T(1024)(128)(2,1)S(1)}, f32[1024]{0:T(1024)S(1)}, bf16[768]{0:T(1024)(128)(2,1)S(1)}, f32[1024,768]{1,0:T(8,128)S(1)}) fusion(f32[1024,768]{1,0:T(8,128)S(1)} %copy-done.7, f32[1024]{0:T(1024)S(1)} %fusion.37, f32[1024]{0:T(1024)S(1)} %broadcast_multiply_fusion, f32[768]{0:T(1024)S(1)} %reshape.349, ...), kind=kOutput, calls=%fused_computation.37 | convolution fusion | flops 4838126592 | bytes 17319936 | tf_op jit(solution)/shard_map/dot_general | solution.py:14
  258.8 2.8 convolution_convert_fusion.3
  261.6 2.5 convolution_convert_fusion.4
  264.2 4.3 fusion.20
  269.7 21.4 %attn_bwd.4 = (bf16[512,384]{1,0:T(8,128)(2,1)}, bf16[2,512,384]{2,1,0:T(8,128)(2,1)}, bf16[2,512,384]{2,1,0:T(8,128)(2,1)}, bf16[2,512,384]{2,1,0:T(8,128)(2,1)}, bf16[2,512,384]{2,1,0:T(8,128)(2,1)}) custom-call(bf16[512,768]{1,0:T(8,128)(2,1)} %get-tuple-element.278.refs_0_, bf16[512,768]{1,0:T(8,128)(2,1)} %get-tuple-element.156.refs_1_, ...), custom_call_target="tpu_custom_call" | custom-call | flops 16106127360 | bytes 8650752 | tf_op jit(solution)/shard_map/attn_bwd/pallas_call | solution.py:159
  294.4 2.9 add_convert_fusion.4
  299.2 21.5 %attn_bwd.6 = (bf16[512,384]{1,0:T(8,128)(2,1)}, bf16[2,512,384]{2,1,0:T(8,128)(2,1)}, bf16[2,512,384]{2,1,0:T(8,128)(2,1)}, bf16[2,512,384]{2,1,0:T(8,128)(2,1)}, bf16[2,512,384]{2,1,0:T(8,128)(2,1)}) custom-call(bf16[512,768]{1,0:T(8,128)(2,1)} %get-tuple-element.278.refs_0_, bf16[512,768]{1,0:T(8,128)(2,1)} %get-tuple-element.156.refs_1_, ...), custom_call_target="tpu_custom_call" | custom-call | flops 16106127360 | bytes 8650752 | tf_op jit(solution)/shard_map/attn_bwd/pallas_call | solution.py:159
  320.8 7.0 %collective-permute-done.29 = bf16[192,768]{1,0:T(8,128)(2,1)S(1)} collective-permute-done((bf16[192,768]{1,0:T(8,128)(2,1)}, bf16[192,768]{1,0:T(8,128)(2,1)S(1)}, u32[]{:S(2)}, u32[]{:S(2)}) %collective-permute-start.29) | collective-permute-done | bytes 294944 | tf_op jit(solution)/shard_map/ppermute | solution.py:184
  332.4 21.7 %attn_bwd.5 = (bf16[512,384]{1,0:T(8,128)(2,1)}, bf16[2,512,384]{2,1,0:T(8,128)(2,1)}, bf16[2,512,384]{2,1,0:T(8,128)(2,1)}, bf16[2,512,384]{2,1,0:T(8,128)(2,1)}, bf16[2,512,384]{2,1,0:T(8,128)(2,1)}) custom-call(bf16[512,768]{1,0:T(8,128)(2,1)} %get-tuple-element.279.refs_0_, bf16[512,768]{1,0:T(8,128)(2,1)} %get-tuple-element.174.refs_1_, ...), custom_call_target="tpu_custom_call" | custom-call | flops 16106127360 | bytes 8650752 | tf_op jit(solution)/shard_map/attn_bwd/pallas_call | solution.py:159
  360.7 2.7 add_convert_fusion.3
  363.4 21.8 %attn_bwd.7 = (bf16[512,384]{1,0:T(8,128)(2,1)}, bf16[2,512,384]{2,1,0:T(8,128)(2,1)}, bf16[2,512,384]{2,1,0:T(8,128)(2,1)}, bf16[2,512,384]{2,1,0:T(8,128)(2,1)}, bf16[2,512,384]{2,1,0:T(8,128)(2,1)}) custom-call(bf16[512,768]{1,0:T(8,128)(2,1)} %get-tuple-element.279.refs_0_, bf16[512,768]{1,0:T(8,128)(2,1)} %get-tuple-element.174.refs_1_, ...), custom_call_target="tpu_custom_call" | custom-call | flops 16106127360 | bytes 8650752 | tf_op jit(solution)/shard_map/attn_bwd/pallas_call | solution.py:159
  385.5 10.0 %add_convert_fusion.1 = bf16[1024,768]{1,0:T(8,128)(2,1)} fusion(f32[1024,768]{1,0:T(8,128)} %copy-done.6, bf16[1024,3072]{1,0:T(8,128)(2,1)} %copy-done.48, bf16[3072,768]{1,0:T(8,128)(2,1)} %all-gather.13.cloned.1.call-done, f32[768]{0:T(1024)S(1)} %copy-done.43), kind=kOutput, calls=%fused_computation.39 | convolution fusion | flops 4834197504 | bytes 15731712 | tf_op jit(solution)/shard_map/dot_general | solution.py:17
  395.5 3.7 reduce.7
  407.5 12.6 %collective-permute-done.24 = bf16[2,512,384]{2,1,0:T(8,128)(2,1)} collective-permute-done((bf16[2,512,384]{2,1,0:T(8,128)(2,1)}, bf16[2,512,384]{2,1,0:T(8,128)(2,1)}, u32[]{:S(2)}, u32[]{:S(2)}) %collective-permute-start.24) | collective-permute-done | bytes 786464 | tf_op jit(solution)/shard_map/ppermute | solution.py:184
  421.4 15.4 %collective-permute-done.27 = bf16[2,512,384]{2,1,0:T(8,128)(2,1)S(1)} collective-permute-done((bf16[2,512,384]{2,1,0:T(8,128)(2,1)S(1)}, bf16[2,512,384]{2,1,0:T(8,128)(2,1)S(1)}, u32[]{:S(2)}, u32[]{:S(2)}) %collective-permute-start.27) | collective-permute-done | bytes 786464 | tf_op jit(solution)/shard_map/ppermute | solution.py:184
  438.4 14.6 %collective-permute-done.32 = bf16[2,512,384]{2,1,0:T(8,128)(2,1)S(1)} collective-permute-done((bf16[2,512,384]{2,1,0:T(8,128)(2,1)S(1)}, bf16[2,512,384]{2,1,0:T(8,128)(2,1)S(1)}, u32[]{:S(2)}, u32[]{:S(2)}) %collective-permute-start.32) | collective-permute-done | bytes 786464 | tf_op jit(solution)/shard_map/ppermute | solution.py:184
  456.2 4.2 convolution_convert_fusion.2
  463.6 5.7 %fusion.43 = (bf16[768]{0:T(1024)(128)(2,1)S(1)}, f32[1024]{0:T(1024)S(1)}, f32[1024,768]{1,0:T(8,128)}) fusion(f32[768]{0:T(1024)S(1)} %copy-done.30, f32[1024]{0:T(1024)S(1)} %bitcast.200, bf16[2,1,512,768]{3,2,1,0:T(8,128)(2,1)S(1)} %copy-done.1, bf16[1024,2304]{1,0:T(8,128)(2,1)S(1)} %pad_maximum_fusion, bf16[768,2304]{1,0:T(8,128)(2,1)S(1)} %copy-done.44), kind=kOutput, calls=%fused_computation.159 | convolution fusion | flops 3628595456 | bytes 12988928 | tf_op jit(solution)/shard_map/dot_general | solution.py:14
  469.3 3.1 reduce.5
  472.4 3.0 fusion.15
  476.1 2.5 fusion.25
  480.6 19.9 %collective-permute-done.41 = bf16[192,2304]{1,0:T(8,128)(2,1)} collective-permute-done((bf16[192,2304]{1,0:T(8,128)(2,1)}, bf16[192,2304]{1,0:T(8,128)(2,1)}, u32[]{:S(2)}, u32[]{:S(2)}) %collective-permute-start.41) | collective-permute-done | bytes 884768 | tf_op jit(solution)/shard_map/ppermute | solution.py:184
  504.1 4.1 add_convert_fusion
  508.3 5.6 %collective-permute-done.42 = bf16[96,2304]{1,0:T(8,128)(2,1)S(1)} collective-permute-done((bf16[96,2304]{1,0:T(8,128)(2,1)S(1)}, bf16[96,2304]{1,0:T(8,128)(2,1)S(1)}, u32[]{:S(2)}, u32[]{:S(2)}) %collective-permute-start.42) | collective-permute-done | bytes 442400 | tf_op jit(solution)/shard_map/ppermute | solution.py:264
  516.7 3.9 collective-permute-done.43
  520.7 3.1 collective-permute-start.44
  525.3 4.2 collective-permute-done.44
  529.7 2.9 collective-permute-start.37
  532.6 4.4 collective-permute-done.45
  539.7 4.1 collective-permute-done.46
  (317 shorter events, 108.0 us)
Async XLA Ops:
  7.2 35.9 %all-gather.7.cloned.1.call-start = ((), (), s32[]{:S(2)}) async-start(), calls=%async_computation | async-start | bytes 4423680 | tf_op jit(solution)/shard_map/all_gather | solution.py:250
  7.9 179.5 %all-gather.9.cloned.1.call-start = ((), (), s32[]{:S(2)}) async-start(), calls=%async_computation.1 | async-start | bytes 1474560 | tf_op jit(solution)/shard_map/all_gather | solution.py:250
  52.5 19.7 %collective-permute-start.1 = (bf16[512,768]{1,0:T(8,128)(2,1)S(1)}, bf16[512,768]{1,0:T(8,128)(2,1)S(1)}, u32[]{:S(2)}, u32[]{:S(2)}) collective-permute-start(bf16[512,768]{1,0:T(8,128)(2,1)S(1)} %get-tuple-element.111.refs_2_.refs_6_.refs_5_.refs_9_), channel_id=1, source_target_pairs={{0,2},{1,3},{2,0},{3,1},{4,6},{5,7},{6,4},{7,5},{8,10},{9,11},{10,... | collective-permute-start | bytes 2359304 | tf_op jit(solution)/shard_map/ppermute | solution.py:184
  53.5 18.8 %collective-permute-start.2 = (bf16[512,768]{1,0:T(8,128)(2,1)S(1)}, bf16[512,768]{1,0:T(8,128)(2,1)S(1)}, u32[]{:S(2)}, u32[]{:S(2)}) collective-permute-start(bf16[512,768]{1,0:T(8,128)(2,1)S(1)} %get-tuple-element.111.refs_2_.refs_6_.refs_5_.refs_9_), channel_id=1, source_target_pairs={{0,1},{1,0},{2,3},{3,2},{4,5},{5,4},{6,7},{7,6},{8,9},{9,8},{10,11... | collective-permute-start | bytes 2359304 | tf_op jit(solution)/shard_map/ppermute | solution.py:184
  74.7 118.2 %all-gather.11.cloned.1.call-start = ((), (), s32[]{:S(2)}) async-start(), calls=%async_computation.2 | async-start | bytes 5898240 | tf_op jit(solution)/shard_map/all_gather | solution.py:250
  75.4 145.2 %all-gather.13.cloned.1.call-start = ((), (), s32[]{:S(2)}) async-start(), calls=%async_computation.3 | async-start | bytes 5898240 | tf_op jit(solution)/shard_map/all_gather | solution.py:250
  80.9 26.2 %collective-permute-start = (bf16[512,768]{1,0:T(8,128)(2,1)}, bf16[512,768]{1,0:T(8,128)(2,1)}, u32[]{:S(2)}, u32[]{:S(2)}) collective-permute-start(bf16[512,768]{1,0:T(8,128)(2,1)} %get-tuple-element.119.refs_2_.refs_6_.refs_5_.refs_9_), channel_id=1, source_target_pairs={{0,2},{1,3},{2,0},{3,1},{4,6},{5,7},{6,4},{7,5},{8,10},{9,11},{10,... | collective-permute-start | bytes 2359304 | tf_op jit(solution)/shard_map/ppermute | solution.py:184
  107.2 5.3 collective-permute-start.6
  107.7 36.5 %collective-permute-start.4 = (bf16[512,768]{1,0:T(8,128)(2,1)S(1)}, bf16[512,768]{1,0:T(8,128)(2,1)S(1)}, u32[]{:S(2)}, u32[]{:S(2)}) collective-permute-start(bf16[512,768]{1,0:T(8,128)(2,1)S(1)} %copy-done.19), channel_id=1, source_target_pairs={{0,2},{1,3},{2,0},{3,1},{4,6},{5,7},{6,4},{7,5},{8,10},{9,11},{10,... | collective-permute-start | bytes 2359304 | tf_op jit(solution)/shard_map/ppermute | solution.py:184
  144.7 24.8 %collective-permute-start.7 = (bf16[512,768]{1,0:T(8,128)(2,1)}, bf16[512,768]{1,0:T(8,128)(2,1)}, u32[]{:S(2)}, u32[]{:S(2)}) collective-permute-start(bf16[512,768]{1,0:T(8,128)(2,1)} %get-tuple-element.128.refs_2_.refs_6_.refs_5_.refs_9_), channel_id=1, source_target_pairs={{0,2},{1,3},{2,0},{3,1},{4,6},{5,7},{6,4},{7,5},{8,10},{9,11},{10,... | collective-permute-start | bytes 2359304 | tf_op jit(solution)/shard_map/ppermute | solution.py:184
  145.8 383.7 %all-reduce.4.cloned.1.call-start = ((), (), s32[]{:S(2)}) async-start(), calls=%async_computation.4 | async-start | bytes 5308416 | tf_op jit(solution)/shard_map/psum | solution.py:393
  169.4 4.8 collective-permute-start.10
  169.4 4.8 collective-permute-start.11
  220.0 10.0 %collective-permute-start.13 = (bf16[768,768]{1,0:T(8,128)(2,1)}, bf16[768,768]{1,0:T(8,128)(2,1)}, u32[]{:S(2)}, u32[]{:S(2)}) collective-permute-start(bf16[768,768]{1,0:T(8,128)(2,1)} %get-tuple-element.268), channel_id=1, source_target_pairs={{0,1},{1,0},{2,3},{3,2},{4,5},{5,4},{6,7},{7,6},{8,9},{9,8},{10,11... | collective-permute-start | bytes 3538952 | tf_op jit(solution)/shard_map/ppermute | solution.py:184
  220.0 10.0 %collective-permute-start.12 = (bf16[768,768]{1,0:T(8,128)(2,1)}, bf16[768,768]{1,0:T(8,128)(2,1)}, u32[]{:S(2)}, u32[]{:S(2)}) collective-permute-start(bf16[768,768]{1,0:T(8,128)(2,1)} %get-tuple-element.269), channel_id=1, source_target_pairs={{0,1},{1,0},{2,3},{3,2},{4,5},{5,4},{6,7},{7,6},{8,9},{9,8},{10,11... | collective-permute-start | bytes 3538952 | tf_op jit(solution)/shard_map/ppermute | solution.py:184
  247.2 16.9 %collective-permute-start.15 = (bf16[192,3072]{1,0:T(8,128)(2,1)}, bf16[192,3072]{1,0:T(8,128)(2,1)}, u32[]{:S(2)}, u32[]{:S(2)}) collective-permute-start(bf16[192,3072]{1,0:T(8,128)(2,1)} %get-tuple-element.264), channel_id=1, source_target_pairs={{0,1},{1,0},{2,3},{3,2},{4,5},{5,4},{6,7},{7,6},{8,9},{9,8},{10,11... | collective-permute-start | bytes 3538952 | tf_op jit(solution)/shard_map/ppermute | solution.py:184
  247.2 16.9 %collective-permute-start.14 = (bf16[192,3072]{1,0:T(8,128)(2,1)}, bf16[192,3072]{1,0:T(8,128)(2,1)}, u32[]{:S(2)}, u32[]{:S(2)}) collective-permute-start(bf16[192,3072]{1,0:T(8,128)(2,1)} %get-tuple-element.265), channel_id=1, source_target_pairs={{0,1},{1,0},{2,3},{3,2},{4,5},{5,4},{6,7},{7,6},{8,9},{9,8},{10,11... | collective-permute-start | bytes 3538952 | tf_op jit(solution)/shard_map/ppermute | solution.py:184
  255.1 38.3 %collective-permute-start.19 = (bf16[768,768]{1,0:T(8,128)(2,1)}, bf16[768,768]{1,0:T(8,128)(2,1)}, u32[]{:S(2)}, u32[]{:S(2)}) collective-permute-start(bf16[768,768]{1,0:T(8,128)(2,1)} %get-tuple-element.154), channel_id=1, source_target_pairs={{0,2},{1,3},{2,0},{3,1},{4,6},{5,7},{6,4},{7,5},{8,10},{9,11},{10,... | collective-permute-start | bytes 3538952 | tf_op jit(solution)/shard_map/ppermute | solution.py:184
  291.1 37.5 %collective-permute-start.16 = (bf16[2,512,384]{2,1,0:T(8,128)(2,1)}, bf16[2,512,384]{2,1,0:T(8,128)(2,1)}, u32[]{:S(2)}, u32[]{:S(2)}) collective-permute-start(bf16[2,512,384]{2,1,0:T(8,128)(2,1)} %get-tuple-element.144), channel_id=1, source_target_pairs={{0,1},{1,0},{2,3},{3,2},{4,5},{5,4},{6,7},{7,6},{8,9},{9,8},{10,11... | collective-permute-start | bytes 2359304 | tf_op jit(solution)/shard_map/ppermute | solution.py:184
  291.2 39.0 %collective-permute-start.17 = (bf16[2,512,384]{2,1,0:T(8,128)(2,1)}, bf16[2,512,384]{2,1,0:T(8,128)(2,1)}, u32[]{:S(2)}, u32[]{:S(2)}) collective-permute-start(bf16[2,512,384]{2,1,0:T(8,128)(2,1)} %get-tuple-element.146), channel_id=1, source_target_pairs={{0,1},{1,0},{2,3},{3,2},{4,5},{5,4},{6,7},{7,6},{8,9},{9,8},{10,11... | collective-permute-start | bytes 2359304 | tf_op jit(solution)/shard_map/ppermute | solution.py:184
  292.8 4.5 collective-permute-start.21
  293.4 67.3 %collective-permute-start.28 = (bf16[192,3072]{1,0:T(8,128)(2,1)}, bf16[192,3072]{1,0:T(8,128)(2,1)}, u32[]{:S(2)}, u32[]{:S(2)}) collective-permute-start(bf16[192,3072]{1,0:T(8,128)(2,1)} %get-tuple-element.170), channel_id=1, source_target_pairs={{0,2},{1,3},{2,0},{3,1},{4,6},{5,7},{6,4},{7,5},{8,10},{9,11},{10,... | collective-permute-start | bytes 3538952 | tf_op jit(solution)/shard_map/ppermute | solution.py:184
  298.2 29.6 %collective-permute-start.29 = (bf16[192,768]{1,0:T(8,128)(2,1)}, bf16[192,768]{1,0:T(8,128)(2,1)S(1)}, u32[]{:S(2)}, u32[]{:S(2)}) collective-permute-start(bf16[192,768]{1,0:T(8,128)(2,1)} %get-tuple-element.172), channel_id=1, source_target_pairs={{0,2},{1,3},{2,0},{3,1},{4,6},{5,7},{6,4},{7,5},{8,10},{9,11},{10,... | collective-permute-start | bytes 884744 | tf_op jit(solution)/shard_map/ppermute | solution.py:184
  320.7 34.7 %collective-permute-start.22 = (bf16[2,512,384]{2,1,0:T(8,128)(2,1)}, bf16[2,512,384]{2,1,0:T(8,128)(2,1)}, u32[]{:S(2)}, u32[]{:S(2)}) collective-permute-start(bf16[2,512,384]{2,1,0:T(8,128)(2,1)} %get-tuple-element.159), channel_id=1, source_target_pairs={{0,1},{1,0},{2,3},{3,2},{4,5},{5,4},{6,7},{7,6},{8,9},{9,8},{10,11... | collective-permute-start | bytes 2359304 | tf_op jit(solution)/shard_map/ppermute | solution.py:184
  327.8 30.4 %collective-permute-start.23 = (bf16[2,512,384]{2,1,0:T(8,128)(2,1)}, bf16[2,512,384]{2,1,0:T(8,128)(2,1)}, u32[]{:S(2)}, u32[]{:S(2)}) collective-permute-start(bf16[2,512,384]{2,1,0:T(8,128)(2,1)} %get-tuple-element.161), channel_id=1, source_target_pairs={{0,1},{1,0},{2,3},{3,2},{4,5},{5,4},{6,7},{7,6},{8,9},{9,8},{10,11... | collective-permute-start | bytes 2359304 | tf_op jit(solution)/shard_map/ppermute | solution.py:184
  354.1 50.7 %collective-permute-start.18 = (bf16[2,512,384]{2,1,0:T(8,128)(2,1)}, bf16[2,512,384]{2,1,0:T(8,128)(2,1)}, u32[]{:S(2)}, u32[]{:S(2)}) collective-permute-start(bf16[2,512,384]{2,1,0:T(8,128)(2,1)} %add_convert_fusion.16), channel_id=1, source_target_pairs={{0,2},{1,3},{2,0},{3,1},{4,6},{5,7},{6,4},{7,5},{8,10},{9,11},{10,... | collective-permute-start | bytes 2359304 | tf_op jit(solution)/shard_map/ppermute | solution.py:184
  355.2 45.1 %collective-permute-start.26 = (bf16[2,512,384]{2,1,0:T(8,128)(2,1)}, bf16[2,512,384]{2,1,0:T(8,128)(2,1)}, u32[]{:S(2)}, u32[]{:S(2)}) collective-permute-start(bf16[2,512,384]{2,1,0:T(8,128)(2,1)} %get-tuple-element.167), channel_id=1, source_target_pairs={{0,1},{1,0},{2,3},{3,2},{4,5},{5,4},{6,7},{7,6},{8,9},{9,8},{10,11... | collective-permute-start | bytes 2359304 | tf_op jit(solution)/shard_map/ppermute | solution.py:184
  355.4 66.0 %collective-permute-start.25 = (bf16[2,512,384]{2,1,0:T(8,128)(2,1)}, bf16[2,512,384]{2,1,0:T(8,128)(2,1)}, u32[]{:S(2)}, u32[]{:S(2)}) collective-permute-start(bf16[2,512,384]{2,1,0:T(8,128)(2,1)} %get-tuple-element.165), channel_id=1, source_target_pairs={{0,1},{1,0},{2,3},{3,2},{4,5},{5,4},{6,7},{7,6},{8,9},{9,8},{10,11... | collective-permute-start | bytes 2359304 | tf_op jit(solution)/shard_map/ppermute | solution.py:184
  385.2 16.9 %collective-permute-start.31 = (bf16[2,512,384]{2,1,0:T(8,128)(2,1)}, bf16[2,512,384]{2,1,0:T(8,128)(2,1)}, u32[]{:S(2)}, u32[]{:S(2)}) collective-permute-start(bf16[2,512,384]{2,1,0:T(8,128)(2,1)} %get-tuple-element.179), channel_id=1, source_target_pairs={{0,1},{1,0},{2,3},{3,2},{4,5},{5,4},{6,7},{7,6},{8,9},{9,8},{10,11... | collective-permute-start | bytes 2359304 | tf_op jit(solution)/shard_map/ppermute | solution.py:184
  399.3 20.8 %collective-permute-start.24 = (bf16[2,512,384]{2,1,0:T(8,128)(2,1)}, bf16[2,512,384]{2,1,0:T(8,128)(2,1)}, u32[]{:S(2)}, u32[]{:S(2)}) collective-permute-start(bf16[2,512,384]{2,1,0:T(8,128)(2,1)} %add_convert_fusion.13), channel_id=1, source_target_pairs={{0,2},{1,3},{2,0},{3,1},{4,6},{5,7},{6,4},{7,5},{8,10},{9,11},{10,... | collective-permute-start | bytes 2359304 | tf_op jit(solution)/shard_map/ppermute | solution.py:184
  400.3 38.0 %collective-permute-start.30 = (bf16[2,512,384]{2,1,0:T(8,128)(2,1)}, bf16[2,512,384]{2,1,0:T(8,128)(2,1)S(1)}, u32[]{:S(2)}, u32[]{:S(2)}) collective-permute-start(bf16[2,512,384]{2,1,0:T(8,128)(2,1)} %get-tuple-element.177), channel_id=1, source_target_pairs={{0,1},{1,0},{2,3},{3,2},{4,5},{5,4},{6,7},{7,6},{8,9},{9,8},{10,11... | collective-permute-start | bytes 2359304 | tf_op jit(solution)/shard_map/ppermute | solution.py:184
  402.1 34.7 %collective-permute-start.27 = (bf16[2,512,384]{2,1,0:T(8,128)(2,1)S(1)}, bf16[2,512,384]{2,1,0:T(8,128)(2,1)S(1)}, u32[]{:S(2)}, u32[]{:S(2)}) collective-permute-start(bf16[2,512,384]{2,1,0:T(8,128)(2,1)S(1)} %add_convert_fusion.10), channel_id=1, source_target_pairs={{0,2},{1,3},{2,0},{3,1},{4,6},{5,7},{6,4},{7,5},{8,10},{9,11},{10,... | collective-permute-start | bytes 2359304 | tf_op jit(solution)/shard_map/ppermute | solution.py:184
  404.8 48.1 %collective-permute-start.32 = (bf16[2,512,384]{2,1,0:T(8,128)(2,1)S(1)}, bf16[2,512,384]{2,1,0:T(8,128)(2,1)S(1)}, u32[]{:S(2)}, u32[]{:S(2)}) collective-permute-start(bf16[2,512,384]{2,1,0:T(8,128)(2,1)S(1)} %add_convert_fusion.7), channel_id=1, source_target_pairs={{0,2},{1,3},{2,0},{3,1},{4,6},{5,7},{6,4},{7,5},{8,10},{9,11},{10,... | collective-permute-start | bytes 2359304 | tf_op jit(solution)/shard_map/ppermute | solution.py:184
  463.5 12.5 %collective-permute-start.40 = (bf16[192,2304]{1,0:T(8,128)(2,1)}, bf16[192,2304]{1,0:T(8,128)(2,1)}, u32[]{:S(2)}, u32[]{:S(2)}) collective-permute-start(bf16[192,2304]{1,0:T(8,128)(2,1)} %get-tuple-element.275), channel_id=1, source_target_pairs={{0,1},{1,0},{2,3},{3,2},{4,5},{5,4},{6,7},{7,6},{8,9},{9,8},{10,11... | collective-permute-start | bytes 2654216 | tf_op jit(solution)/shard_map/ppermute | solution.py:184
  475.6 5.0 collective-permute-start.39
  478.6 21.9 %collective-permute-start.41 = (bf16[192,2304]{1,0:T(8,128)(2,1)}, bf16[192,2304]{1,0:T(8,128)(2,1)}, u32[]{:S(2)}, u32[]{:S(2)}) collective-permute-start(bf16[192,2304]{1,0:T(8,128)(2,1)} %fusion.25), channel_id=1, source_target_pairs={{0,2},{1,3},{2,0},{3,1},{4,6},{5,7},{6,4},{7,5},{8,10},{9,11},{10,... | collective-permute-start | bytes 2654216 | tf_op jit(solution)/shard_map/ppermute | solution.py:184
  480.0 35.6 %collective-permute-start.34 = (bf16[16,2304]{1,0:T(8,128)(2,1)S(1)}, bf16[16,2304]{1,0:T(8,128)(2,1)S(1)}, u32[]{:S(2)}, u32[]{:S(2)}) collective-permute-start(bf16[16,2304]{1,0:T(8,128)(2,1)S(1)} %get-tuple-element.289), channel_id=1, source_target_pairs={{0,1},{1,0},{2,3},{3,2},{4,5},{5,4},{6,7},{7,6},{8,9},{9,8},{10,11... | collective-permute-start | bytes 221192 | tf_op jit(solution)/shard_map/ppermute | solution.py:184
  480.1 43.7 %collective-permute-start.33 = (bf16[16,2304]{1,0:T(8,128)(2,1)S(1)}, bf16[16,2304]{1,0:T(8,128)(2,1)S(1)}, u32[]{:S(2)}, u32[]{:S(2)}) collective-permute-start(bf16[16,2304]{1,0:T(8,128)(2,1)S(1)} %get-tuple-element.288), channel_id=1, source_target_pairs={{0,1},{1,0},{2,3},{3,2},{4,5},{5,4},{6,7},{7,6},{8,9},{9,8},{10,11... | collective-permute-start | bytes 221192 | tf_op jit(solution)/shard_map/ppermute | solution.py:184
  502.6 11.3 %collective-permute-start.42 = (bf16[96,2304]{1,0:T(8,128)(2,1)S(1)}, bf16[96,2304]{1,0:T(8,128)(2,1)S(1)}, u32[]{:S(2)}, u32[]{:S(2)}) collective-permute-start(bf16[96,2304]{1,0:T(8,128)(2,1)S(1)} %dynamic-slice_bitcast_fusion.6), channel_id=1, source_target_pairs={{0,4},{4,0},{8,12},{12,8},{16,20},{20,16},{24,28},{28,24},{1,5},{5... | collective-permute-start | bytes 1327112 | tf_op jit(solution)/shard_map/ppermute | solution.py:264
  514.0 6.6 %collective-permute-start.43 = (bf16[48,2304]{1,0:T(8,128)(2,1)S(1)}, bf16[48,2304]{1,0:T(8,128)(2,1)S(1)}, u32[]{:S(2)}, u32[]{:S(2)}) collective-permute-start(bf16[48,2304]{1,0:T(8,128)(2,1)S(1)} %dynamic-slice_bitcast_fusion.9), channel_id=1, source_target_pairs={{0,8},{4,12},{8,0},{12,4},{16,24},{20,28},{24,16},{28,20},{1,9},{5... | collective-permute-start | bytes 663560 | tf_op jit(solution)/shard_map/ppermute | solution.py:264
  515.6 8.2 %collective-permute-start.35 = (bf16[16,2304]{1,0:T(8,128)(2,1)S(1)}, bf16[16,2304]{1,0:T(8,128)(2,1)S(1)}, u32[]{:S(2)}, u32[]{:S(2)}) collective-permute-start(bf16[16,2304]{1,0:T(8,128)(2,1)S(1)} %fusion.34), channel_id=1, source_target_pairs={{0,2},{1,3},{2,0},{3,1},{4,6},{5,7},{6,4},{7,5},{8,10},{9,11},{10,... | collective-permute-start | bytes 221192 | tf_op jit(solution)/shard_map/ppermute | solution.py:184
  520.7 8.8 %collective-permute-start.44 = (bf16[24,2304]{1,0:T(8,128)(2,1)S(1)}, bf16[24,2304]{1,0:T(8,128)(2,1)S(1)}, u32[]{:S(2)}, u32[]{:S(2)}) collective-permute-start(bf16[24,2304]{1,0:T(8,128)(2,1)S(1)} %dynamic-slice_bitcast_fusion.10), channel_id=1, source_target_pairs={{0,16},{4,20},{8,24},{12,28},{16,0},{20,4},{24,8},{28,12},{1,17},{... | collective-permute-start | bytes 331784 | tf_op jit(solution)/shard_map/ppermute | solution.py:264
  523.8 5.8 %collective-permute-start.36 = (bf16[16,2304]{1,0:T(8,128)(2,1)S(1)}, bf16[16,2304]{1,0:T(8,128)(2,1)S(1)}, u32[]{:S(2)}, u32[]{:S(2)}) collective-permute-start(bf16[16,2304]{1,0:T(8,128)(2,1)S(1)} %add_convert_fusion.22), channel_id=1, source_target_pairs={{0,4},{4,0},{8,12},{12,8},{16,20},{20,16},{24,28},{28,24},{1,5},{5... | collective-permute-start | bytes 221192 | tf_op jit(solution)/shard_map/ppermute | solution.py:264
  529.6 7.4 %collective-permute-start.45 = (bf16[24,2304]{1,0:T(8,128)(2,1)S(1)}, bf16[24,2304]{1,0:T(8,128)(2,1)S(1)}, u32[]{:S(2)}, u32[]{:S(2)}) collective-permute-start(bf16[24,2304]{1,0:T(8,128)(2,1)S(1)} %fusion.33), channel_id=1, source_target_pairs={{0,16},{4,20},{8,24},{12,28},{16,0},{20,4},{24,8},{28,12},{1,17},{... | collective-permute-start | bytes 331784 | tf_op jit(solution)/shard_map/ppermute | solution.py:264
  529.7 7.9 %collective-permute-start.37 = (bf16[16,2304]{1,0:T(8,128)(2,1)S(1)}, bf16[16,2304]{1,0:T(8,128)(2,1)S(1)}, u32[]{:S(2)}, u32[]{:S(2)}) collective-permute-start(bf16[16,2304]{1,0:T(8,128)(2,1)S(1)} %add_convert_fusion.21), channel_id=1, source_target_pairs={{0,8},{4,12},{8,0},{12,4},{16,24},{20,28},{24,16},{28,20},{1,9},{5... | collective-permute-start | bytes 221192 | tf_op jit(solution)/shard_map/ppermute | solution.py:264
  537.1 6.8 %collective-permute-start.46 = (bf16[48,2304]{1,0:T(8,128)(2,1)S(1)}, bf16[48,2304]{1,0:T(8,128)(2,1)S(1)}, u32[]{:S(2)}, u32[]{:S(2)}) collective-permute-start(bf16[48,2304]{1,0:T(8,128)(2,1)S(1)} %maximum_select_fusion.2), channel_id=1, source_target_pairs={{0,8},{4,12},{8,0},{12,4},{16,24},{20,28},{24,16},{28,20},{1,9},{5... | collective-permute-start | bytes 663560 | tf_op jit(solution)/shard_map/ppermute | solution.py:264
  537.7 7.8 %collective-permute-start.38 = (bf16[16,2304]{1,0:T(8,128)(2,1)S(1)}, bf16[16,2304]{1,0:T(8,128)(2,1)S(1)}, u32[]{:S(2)}, u32[]{:S(2)}) collective-permute-start(bf16[16,2304]{1,0:T(8,128)(2,1)S(1)} %add_convert_fusion.20), channel_id=1, source_target_pairs={{0,16},{4,20},{8,24},{12,28},{16,0},{20,4},{24,8},{28,12},{1,17},{... | collective-permute-start | bytes 221192 | tf_op jit(solution)/shard_map/ppermute | solution.py:264
  543.9 8.5 %collective-permute-start.47 = (bf16[96,2304]{1,0:T(8,128)(2,1)S(1)}, bf16[96,2304]{1,0:T(8,128)(2,1)S(1)}, u32[]{:S(2)}, u32[]{:S(2)}) collective-permute-start(bf16[96,2304]{1,0:T(8,128)(2,1)S(1)} %maximum_select_fusion.1), channel_id=1, source_target_pairs={{0,4},{4,0},{8,12},{12,8},{16,20},{20,16},{24,28},{28,24},{1,5},{5... | collective-permute-start | bytes 1327112 | tf_op jit(solution)/shard_map/ppermute | solution.py:264
  (60 other events, 620.3 us)
Sparse Core Ops, SparseCore 0:
  9.6 33.4 all-gather.6
  74.8 23.8 all-gather.8
  100.2 58.5 all-gather.10
  160.2 37.4 all-gather.12
  400.5 116.8 all-reduce.3
